TPU v7x, 32 devices: a whole 2x2x4 slice. The times are simulated.
32 devices in a mesh: ep: 8 (over z, x), ctx: 4 (over y, core).
Axes of the slice: x: 2, y: 2, z: 4, core: 2. Of those that a mesh axis runs over, the one named last changes fastest.
Arguments:
- tokens: bfloat16 [8, 1536, 1024], P('ep', 'ctx'), may hold values from -6 to 6
- lengths: int32 [8], P('ep'), may hold values from 192 to 1536, as said below
- routes: int32 [8, 1536, 8], P('ep', 'ctx'), may hold values from 0 to 15, all different within a row; in each aligned block of 384 rows (0 to 383, 384 to 767, ..., all dimensions but the last counted through in order) at most 288 rows name the same one
- cotangent: bfloat16 [8, 1536, 1024], P('ep', 'ctx'), may hold values from -6 to 6
- attn_norm: float32 [1024], replicated, may hold values from 0.5 to 1.5
- w_query: bfloat16 [1024, 1024], replicated, may hold values from -0.21875 to 0.21875
- w_key: bfloat16 [1024, 512], replicated, may hold values from -0.21875 to 0.21875
- w_value: bfloat16 [1024, 512], replicated, may hold values from -0.1875 to 0.1875
- w_out: bfloat16 [1024, 1024], replicated, may hold values from -1.25 to 1.25
- ffn_norm: float32 [1024], replicated, may hold values from 0.5 to 1.5
- w_router: bfloat16 [1024, 16], replicated, may hold values from -0.09375 to 0.09375
- expert_gate_weight: bfloat16 [16, 1024, 512], P('ep'), may hold values from -0.1875 to 0.1875
- expert_up_weight: bfloat16 [16, 1024, 512], P('ep'), may hold values from -0.1875 to 0.1875
- expert_down_weight: bfloat16 [16, 512, 1024], P('ep'), may hold values from -1.5 to 1.5
Outputs:
- out: bfloat16 [8, 1536, 1024], P('ep', 'ctx')
- grad_tokens: bfloat16 [8, 1536, 1024], P('ep', 'ctx')
- grad_attn_norm: float32 [1024], replicated
- grad_w_query: float32 [1024, 1024], replicated
- grad_w_key: float32 [1024, 512], replicated
- grad_w_value: float32 [1024, 512], replicated
- grad_w_out: float32 [1024, 1024], replicated
- grad_ffn_norm: float32 [1024], replicated
- grad_w_router: float32 [1024, 16], replicated
- grad_w_gate: float32 [16, 1024, 512], P('ep')
- grad_w_up: float32 [16, 1024, 512], P('ep')
- grad_w_down: float32 [16, 512, 1024], P('ep')
Inputs may be any that keep to these rules, and one draw needn't show every extreme that they name: `routes`: within the 384 rows of one device (aligned blocks of the flattened positions), no expert is named by more than 288 rows, a bound that some block reaches; each row names 8 different experts. A sequence's valid positions are its first lengths ones; some sequence has all 1536.
All inputs are finite; a program needn't handle non-finite values.
Results may differ from a plain program's by a relative error of at most 0.024.
Values may be sent and summed in bfloat16 or wider, within the bound.
No kernel may reach another device: no remote copies, remote signals or barrier semaphores. Data moves between devices by JAX's collectives and lax.ppermute only.
A program may use at most 256 MiB of HBM per device.

v0:
```python
import jax
import jax.numpy as jnp
from jax import lax
from jax.sharding import PartitionSpec as P

HEAD_DIM = 64


EPS = 1e-06
THETA = 10000.0
NEG = -1e30


def rope_tables(positions, head_dim):
    half_dim = head_dim // 2
    inv_freq = THETA ** (-jnp.arange(half_dim, dtype=jnp.float32) / half_dim)
    angles = positions.astype(jnp.float32)[:, None] * inv_freq[None, :]
    return (jnp.cos(angles)[:, None, :], jnp.sin(angles)[:, None, :])


def rotate(values, cos_tab, sin_tab):
    half_dim = values.shape[-1] // 2
    front_half = values[..., :half_dim]
    back_half = values[..., half_dim:]
    return jnp.concatenate(
        [front_half * cos_tab - back_half * sin_tab, back_half * cos_tab + front_half * sin_tab], -1
    )


def rotate_back(grad_in, cos_tab, sin_tab):
    half_dim = grad_in.shape[-1] // 2
    front_half = grad_in[..., :half_dim]
    back_half = grad_in[..., half_dim:]
    return jnp.concatenate(
        [front_half * cos_tab + back_half * sin_tab, back_half * cos_tab - front_half * sin_tab], -1
    )


def norm_back(values, rms_scale, gain_vec, grad_in):
    weighted = grad_in * gain_vec
    mean_term = jnp.mean(weighted * values, -1, keepdims=True)
    grad_values = rms_scale * weighted - values * rms_scale**3 * mean_term
    grad_gain = jnp.sum(grad_in * values * rms_scale, 0)
    return (grad_values, grad_gain)


def slot_map(route_ids, experts, slot_cap):
    flat_ids = route_ids.reshape(-1)
    flat_count = flat_ids.shape[0]
    one_hot = (flat_ids[:, None] == jnp.arange(experts, dtype=jnp.int32)[None, :]).astype(jnp.int32)
    earlier = jnp.cumsum(one_hot, 0) - one_hot
    slot_rank = jnp.sum(earlier * one_hot, 1)
    slot_of = flat_ids * slot_cap + slot_rank
    slot_item = (
        jnp.zeros((experts * slot_cap,), jnp.int32)
        .at[slot_of]
        .set(jnp.arange(flat_count, dtype=jnp.int32))
    )
    slot_full = jnp.zeros((experts * slot_cap,), jnp.int32).at[slot_of].set(1)
    return (slot_of, slot_item, slot_full)


def attend(state_in, key_block, value_block, key_start, queries, query_pos, seq_len):
    running_max, running_sum, weighted = state_in
    score_scale = queries.shape[3] ** (-0.5)
    raw_scores = jnp.einsum(
        "qhgd,khd->hgqk", queries, key_block, preferred_element_type=jnp.float32
    )
    key_pos = key_start + jnp.arange(key_block.shape[0], dtype=jnp.int32)
    allowed = (key_pos[None, :] <= query_pos[:, None]) & (key_pos[None, :] < seq_len)
    scores = jnp.where(allowed, raw_scores * score_scale, NEG)
    new_max = jnp.maximum(running_max, jnp.max(scores, -1))
    weights = jnp.where(allowed, jnp.exp(scores - new_max[..., None]), 0.0)
    shrink = jnp.exp(running_max - new_max)
    running_sum = running_sum * shrink + jnp.sum(weights, -1)
    weighted = weighted * shrink[..., None] + jnp.einsum(
        "hgqk,khd->hgqd",
        weights.astype(jnp.bfloat16),
        value_block,
        preferred_element_type=jnp.float32,
    )
    return (new_max, running_sum, weighted)


def fold_keys(state_in, pieces, queries, query_pos, seq_len, block_len):
    key_piece, value_piece = pieces
    blocks = key_piece.shape[0] // block_len
    num_kv = queries.shape[1]
    head_dim = queries.shape[3]
    key_blocks = key_piece.reshape(blocks, block_len, num_kv, head_dim)
    value_blocks = value_piece.reshape(blocks, block_len, num_kv, head_dim)
    offsets = block_len * jnp.arange(blocks, dtype=jnp.int32)

    def visit_block(state_now, block_item):
        key_block, value_block, offset = block_item
        return (
            attend(state_now, key_block, value_block, offset, queries, query_pos, seq_len),
            None,
        )

    state_out, unused = lax.scan(visit_block, state_in, (key_blocks, value_blocks, offsets))
    return state_out


def attend_back(
    grad_q,
    key_block,
    value_block,
    key_start,
    queries,
    query_pos,
    seq_len,
    log_total,
    grad_heads,
    row_delta,
):
    score_scale = queries.shape[3] ** (-0.5)
    raw_scores = jnp.einsum(
        "qhgd,khd->hgqk", queries, key_block, preferred_element_type=jnp.float32
    )
    key_pos = key_start + jnp.arange(key_block.shape[0], dtype=jnp.int32)
    allowed = (key_pos[None, :] <= query_pos[:, None]) & (key_pos[None, :] < seq_len)
    scores = jnp.where(allowed, raw_scores * score_scale - log_total[..., None], NEG)
    probs = jnp.where(allowed, jnp.exp(scores), 0.0)
    grad_probs = jnp.einsum(
        "qhgd,khd->hgqk", grad_heads, value_block, preferred_element_type=jnp.float32
    )
    grad_raw = (probs * (grad_probs - row_delta[..., None]) * score_scale).astype(jnp.bfloat16)
    grad_q = grad_q + jnp.einsum(
        "hgqk,khd->qhgd", grad_raw, key_block, preferred_element_type=jnp.float32
    )
    grad_key = jnp.einsum("hgqk,qhgd->khd", grad_raw, queries, preferred_element_type=jnp.float32)
    grad_value = jnp.einsum(
        "hgqk,qhgd->khd", probs.astype(jnp.bfloat16), grad_heads, preferred_element_type=jnp.float32
    )
    return (grad_q, grad_key, grad_value)


def local(
    tokens,
    lengths,
    routes,
    cotangent,
    attn_norm,
    w_query,
    w_key,
    w_value,
    w_out,
    ffn_norm,
    w_router,
    expert_gate_weight,
    expert_up_weight,
    expert_down_weight,
):
    seq_rows = tokens.shape[1]
    model_dim = tokens.shape[2]
    top_k = routes.shape[2]
    experts = w_router.shape[1]
    local_experts = expert_gate_weight.shape[0]
    slot_cap = 3 * seq_rows * top_k // (2 * experts)
    num_heads = w_query.shape[1] // HEAD_DIM
    num_kv = w_key.shape[1] // HEAD_DIM
    group_size = num_heads // num_kv
    kv_width = num_kv * HEAD_DIM
    ctx_size = lax.axis_size("ctx")
    ep_size = lax.axis_size("ep")
    ctx_index = lax.axis_index("ctx")
    zero_low = jnp.zeros((), jnp.bfloat16)
    inputs = tokens[0].astype(jnp.float32)
    seq_len = lengths[0]
    positions = ctx_index * seq_rows + jnp.arange(seq_rows, dtype=jnp.int32)
    valid_rows = (positions < seq_len).astype(jnp.float32)[:, None]
    cos_tab, sin_tab = rope_tables(positions, HEAD_DIM)
    rms_attn = lax.rsqrt(jnp.mean(inputs * inputs, -1, keepdims=True) + EPS)
    normed = (inputs * rms_attn * attn_norm).astype(jnp.bfloat16)
    query_lin = jnp.dot(normed, w_query, preferred_element_type=jnp.float32).reshape(
        seq_rows, num_heads, HEAD_DIM
    )
    key_lin = jnp.dot(normed, w_key, preferred_element_type=jnp.float32).reshape(
        seq_rows, num_kv, HEAD_DIM
    )
    value_lin = jnp.dot(normed, w_value, preferred_element_type=jnp.float32)
    queries = (
        rotate(query_lin, cos_tab, sin_tab)
        .astype(jnp.bfloat16)
        .reshape(seq_rows, num_kv, group_size, HEAD_DIM)
    )
    key_rot = rotate(key_lin, cos_tab, sin_tab).astype(jnp.bfloat16).reshape(seq_rows, kv_width)
    value_rot = value_lin.astype(jnp.bfloat16)
    start_state = (
        jnp.full((num_kv, group_size, seq_rows), NEG, jnp.float32),
        jnp.zeros((num_kv, group_size, seq_rows), jnp.float32),
        jnp.zeros((num_kv, group_size, seq_rows, HEAD_DIM), jnp.float32),
    )
    running_max, running_sum, weighted = fold_keys(
        start_state,
        (
            lax.all_gather(key_rot, "ctx", axis=0, tiled=True),
            lax.all_gather(value_rot, "ctx", axis=0, tiled=True),
        ),
        queries,
        positions,
        seq_len,
        seq_rows,
    )
    log_total = running_max + jnp.log(running_sum)
    attended = (
        (weighted / running_sum[..., None])
        .transpose(2, 0, 1, 3)
        .reshape(seq_rows, num_heads * HEAD_DIM)
    )
    attended_low = attended.astype(jnp.bfloat16)
    branch = jnp.dot(attended_low, w_out, preferred_element_type=jnp.float32)
    hidden = inputs + branch
    rms_ffn = lax.rsqrt(jnp.mean(hidden * hidden, -1, keepdims=True) + EPS)
    mixed_in = (hidden * rms_ffn * ffn_norm).astype(jnp.bfloat16)
    logits = jnp.dot(mixed_in, w_router, preferred_element_type=jnp.float32)
    route_rows = routes[0]
    route_hot = (
        route_rows[:, :, None] == jnp.arange(experts, dtype=jnp.int32)[None, None, :]
    ).astype(jnp.float32)
    picked = jnp.sum(route_hot * logits[:, None, :], -1)
    gate_vals = jax.nn.softmax(picked, -1)
    slot_of, slot_item, slot_full = slot_map(route_rows, experts, slot_cap)
    occupied = slot_full[:, None] > 0
    outgoing = jnp.where(occupied, mixed_in[slot_item // top_k], zero_low).reshape(
        ep_size, local_experts, slot_cap, model_dim
    )
    holding_buffer = lax.all_to_all(outgoing, "ep", split_axis=0, concat_axis=0, tiled=True)
    gate_before_activation = jnp.einsum(
        "pvgh,vhm->pvgm", holding_buffer, expert_gate_weight, preferred_element_type=jnp.float32
    )
    up_before_activation = jnp.einsum(
        "pvgh,vhm->pvgm", holding_buffer, expert_up_weight, preferred_element_type=jnp.float32
    )
    inner_activation = (jax.nn.silu(gate_before_activation) * up_before_activation).astype(
        jnp.bfloat16
    )
    result = jnp.einsum(
        "uvoz,vzm->uvom", inner_activation, expert_down_weight, preferred_element_type=jnp.float32
    ).astype(jnp.bfloat16)
    result, gate_part, up_part = (result, gate_before_activation, up_before_activation)
    sent_back = lax.all_to_all(result, "ep", split_axis=0, concat_axis=0, tiled=True)
    route_out = sent_back.reshape(experts * slot_cap, model_dim)[slot_of].reshape(
        seq_rows, top_k, model_dim
    )
    expert_sum = jnp.zeros((seq_rows, model_dim), jnp.float32)
    for route_pos in range(top_k):
        expert_sum = expert_sum + gate_vals[:, route_pos : route_pos + 1] * route_out[
            :, route_pos
        ].astype(jnp.float32)
    result_out = (valid_rows * (hidden + expert_sum)).astype(jnp.bfloat16)
    grad_final = cotangent[0].astype(jnp.float32) * valid_rows
    grad_gates = jnp.stack(
        [
            jnp.sum(grad_final * route_out[:, route_pos].astype(jnp.float32), -1)
            for route_pos in range(top_k)
        ],
        1,
    )
    grad_routed = (
        (gate_vals[:, :, None] * grad_final[:, None, :])
        .astype(jnp.bfloat16)
        .reshape(seq_rows * top_k, model_dim)
    )
    grad_send = jnp.where(occupied, grad_routed[slot_item], zero_low).reshape(
        ep_size, local_experts, slot_cap, model_dim
    )
    gradient_received = lax.all_to_all(grad_send, "ep", split_axis=0, concat_axis=0, tiled=True)
    sig_gate = jax.nn.sigmoid(gate_part)
    silu_gate = gate_part * sig_gate
    inner_activation = (silu_gate * up_part).astype(jnp.bfloat16)
    grad_down = jnp.einsum(
        "wimr,wimq->irq", inner_activation, gradient_received, preferred_element_type=jnp.float32
    )
    gradient_inner_activation = jnp.einsum(
        "qyip,yzp->qyiz", gradient_received, expert_down_weight, preferred_element_type=jnp.float32
    )
    gradient_gate_before_activation = (
        gradient_inner_activation * up_part * sig_gate * (1.0 + gate_part * (1.0 - sig_gate))
    ).astype(jnp.bfloat16)
    gradient_up_before_activation = (gradient_inner_activation * silu_gate).astype(jnp.bfloat16)
    grad_gate_w = jnp.einsum(
        "chwm,chwu->hmu",
        holding_buffer,
        gradient_gate_before_activation,
        preferred_element_type=jnp.float32,
    )
    grad_up_w = jnp.einsum(
        "chwm,chwu->hmu",
        holding_buffer,
        gradient_up_before_activation,
        preferred_element_type=jnp.float32,
    )
    grad_expert_in = (
        jnp.einsum(
            "gkiw,kpw->gkip",
            gradient_gate_before_activation,
            expert_gate_weight,
            preferred_element_type=jnp.float32,
        )
        + jnp.einsum(
            "gkiw,kpw->gkip",
            gradient_up_before_activation,
            expert_up_weight,
            preferred_element_type=jnp.float32,
        )
    ).astype(jnp.bfloat16)
    grad_returned = lax.all_to_all(grad_expert_in, "ep", split_axis=0, concat_axis=0, tiled=True)
    expert_summed = (
        lax.psum(grad_gate_w.astype(jnp.bfloat16), "ctx").astype(jnp.float32),
        lax.psum(grad_up_w.astype(jnp.bfloat16), "ctx").astype(jnp.float32),
        lax.psum(grad_down.astype(jnp.bfloat16), "ctx").astype(jnp.float32),
    )
    grad_route_in = grad_returned.reshape(experts * slot_cap, model_dim)[slot_of].reshape(
        seq_rows, top_k, model_dim
    )
    grad_mixed = jnp.zeros((seq_rows, model_dim), jnp.float32)
    for route_pos in range(top_k):
        grad_mixed = grad_mixed + grad_route_in[:, route_pos].astype(jnp.float32)
    grad_picked = gate_vals * (grad_gates - jnp.sum(gate_vals * grad_gates, -1, keepdims=True))
    grad_logits = jnp.sum(route_hot * grad_picked[:, :, None], 1).astype(jnp.bfloat16)
    grad_router = jnp.einsum("td,te->de", mixed_in, grad_logits, preferred_element_type=jnp.float32)
    grad_mixed = grad_mixed + jnp.einsum(
        "te,de->td", grad_logits, w_router, preferred_element_type=jnp.float32
    )
    grad_hidden_norm, grad_ffn_norm = norm_back(hidden, rms_ffn, ffn_norm, grad_mixed)
    grad_hidden = grad_final + grad_hidden_norm
    grad_branch = grad_hidden.astype(jnp.bfloat16)
    grad_w_out = jnp.einsum(
        "tc,td->cd", attended_low, grad_branch, preferred_element_type=jnp.float32
    )
    grad_attended = jnp.einsum(
        "td,cd->tc", grad_branch, w_out, preferred_element_type=jnp.float32
    ).astype(jnp.bfloat16)
    grad_heads = grad_attended.reshape(seq_rows, num_kv, group_size, HEAD_DIM)
    row_delta = jnp.einsum(
        "qhgd,qhgd->hgq",
        grad_heads.astype(jnp.float32),
        attended.reshape(seq_rows, num_kv, group_size, HEAD_DIM),
    )
    key_every, value_every = (
        lax.all_gather(key_rot, "ctx", axis=0, tiled=True),
        lax.all_gather(value_rot, "ctx", axis=0, tiled=True),
    )
    key_blocks = key_every.reshape(ctx_size, seq_rows, num_kv, HEAD_DIM)
    value_blocks = value_every.reshape(ctx_size, seq_rows, num_kv, HEAD_DIM)
    block_starts = seq_rows * jnp.arange(ctx_size, dtype=jnp.int32)

    def visit_back(grad_q, block_item):
        key_block, value_block, offset = block_item
        grad_q, grad_key, grad_value = attend_back(
            grad_q,
            key_block,
            value_block,
            offset,
            queries,
            positions,
            seq_len,
            log_total,
            grad_heads,
            row_delta,
        )
        return (grad_q, (grad_key, grad_value))

    grad_start = jnp.zeros((seq_rows, num_kv, group_size, HEAD_DIM), jnp.float32)
    grad_queries, (key_terms, value_terms) = lax.scan(
        visit_back, grad_start, (key_blocks, value_blocks, block_starts)
    )
    grad_keys, grad_values = (
        lax.psum_scatter(
            key_terms.reshape(ctx_size * seq_rows, kv_width).astype(jnp.bfloat16),
            "ctx",
            scatter_dimension=0,
            tiled=True,
        ).astype(jnp.float32),
        lax.psum_scatter(
            value_terms.reshape(ctx_size * seq_rows, kv_width).astype(jnp.bfloat16),
            "ctx",
            scatter_dimension=0,
            tiled=True,
        ).astype(jnp.float32),
    )
    grad_query_lin = (
        rotate_back(grad_queries.reshape(seq_rows, num_heads, HEAD_DIM), cos_tab, sin_tab)
        .reshape(seq_rows, num_heads * HEAD_DIM)
        .astype(jnp.bfloat16)
    )
    grad_key_lin = (
        rotate_back(grad_keys.reshape(seq_rows, num_kv, HEAD_DIM), cos_tab, sin_tab)
        .reshape(seq_rows, kv_width)
        .astype(jnp.bfloat16)
    )
    grad_value_lin = grad_values.astype(jnp.bfloat16)
    grad_w_query = jnp.einsum(
        "td,tc->dc", normed, grad_query_lin, preferred_element_type=jnp.float32
    )
    grad_w_key = jnp.einsum("td,tc->dc", normed, grad_key_lin, preferred_element_type=jnp.float32)
    grad_w_value = jnp.einsum(
        "td,tc->dc", normed, grad_value_lin, preferred_element_type=jnp.float32
    )
    grad_normed = jnp.einsum(
        "tc,dc->td", grad_query_lin, w_query, preferred_element_type=jnp.float32
    )
    grad_normed = grad_normed + jnp.einsum(
        "tc,dc->td", grad_key_lin, w_key, preferred_element_type=jnp.float32
    )
    grad_normed = grad_normed + jnp.einsum(
        "tc,dc->td", grad_value_lin, w_value, preferred_element_type=jnp.float32
    )
    grad_input_norm, grad_attn_norm = norm_back(inputs, rms_attn, attn_norm, grad_normed)
    grad_inputs = (grad_hidden + grad_input_norm).astype(jnp.bfloat16)
    summed = lax.psum(
        (
            grad_w_query,
            grad_w_key,
            grad_w_value,
            grad_w_out,
            grad_router,
            grad_attn_norm,
            grad_ffn_norm,
        ),
        ("ep", "ctx"),
    )
    return (
        result_out[None],
        grad_inputs[None],
        summed[5],
        summed[0],
        summed[1],
        summed[2],
        summed[3],
        summed[6],
        summed[4],
        expert_summed[0],
        expert_summed[1],
        expert_summed[2],
    )


def solution(mesh):
    in_specs = (
        P("ep", "ctx", None),
        P("ep"),
        P("ep", "ctx", None),
        P("ep", "ctx", None),
        P(),
        P(),
        P(),
        P(),
        P(),
        P(),
        P(),
        P("ep", None, None),
        P("ep", None, None),
        P("ep", None, None),
    )
    out_specs = (
        P("ep", "ctx", None),
        P("ep", "ctx", None),
        P(),
        P(),
        P(),
        P(),
        P(),
        P(),
        P(),
        P("ep", None, None),
        P("ep", None, None),
        P("ep", None, None),
    )
    return jax.shard_map(local, mesh=mesh, in_specs=in_specs, out_specs=out_specs, check_vma=False)
```

profile of v0, /device:TPU:0, one launch (start us, length us, event | category | flops | bytes accessed | tf_op | source)
XLA Modules:
  0.0 1759.9 jit_solution(13814356557297036054)
XLA Ops:
  23.9 11.8 scatter_custom_fusion.1
  35.7 12.0 scatter_custom_fusion
  72.1 49.9 %while.30 = (s32[]{:T(128)}, f32[8,2,384]{2,1,0:T(2,128)S(1)}, f32[8,2,384]{2,1,0:T(2,128)S(1)}, f32[8,2,384,64]{2,3,1,0:T(8,128)}, s32[4]{0:T(128)S(1)}, /*inde...) while((s32[]{:T(128)}, f32[8,2,384]{2,1,0:T(2,128)S(1)}, ...), condition=%wide.region_4.5_spmd.clone, body=%wide.region_1.4_spmd.clone.sunk | while | flops 636157440 | bytes 46603236 | solution.py:101
  128.4 14.9 gather_fusion
  148.0 212.9 %all_to_all.20 = bf16[8,2,288,1024]{3,2,1,0:T(8,128)(2,1)S(1)} all-to-all(bf16[8,2,288,1024]{3,2,1,0:T(8,128)(2,1)S(1)} %broadcast_select_fusion.2), channel_id=1, replica_groups=mesh['ep'=8,'ctx'=4] {'ep'}, dimensions={0} | all-to-all | bytes 18874368 | tf_op jit(solution)/shard_map/all_to_all | solution.py:229
  360.9 7.5 fusion.72
  368.4 12.4 fusion.61
  380.8 10.0 convert_bitcast_fusion
  390.8 8.9 copy.138
  399.6 5.6 all-to-all-start.1
  406.4 203.5 %all-to-all-done.1 = bf16[8,2,288,1024]{3,2,1,0:T(8,128)(2,1)} async-done(((bf16[8,2,288,1024]{3,2,1,0:T(8,128)(2,1)}), bf16[8,2,288,1024]{3,2,1,0:T(8,128)(2,1)}, u32[]{:S(2)}, u32[]{:S(2)}) %all-to-all-start.1) | async-done | bytes 9437216 | tf_op jit(solution)/shard_map/all_to_all | solution.py:243
  609.9 20.8 %gather_fusion.1 = bf16[3072,1024]{1,0:T(8,128)(2,1)} fusion(bf16[4608,1024]{1,0:T(8,128)(2,1)} %bitcast.29, s32[3072]{0:T(1024)S(1)} %broadcast_clamp_fusion), kind=kCustom, calls=%fused_computation.1 | custom fusion | bytes 12595200 | tf_op jit(solution)/shard_map/gather | solution.py:244
  630.6 30.8 %fusion.169 = (bf16[384,1,1024]{2,1,0:T(2,128)(2,1)S(1)}, bf16[384,1,1024]{2,1,0:T(2,128)(2,1)S(1)}, bf16[384,1,1024]{2,1,0:T(2,128)(2,1)S(1)}, bf16[384,1,1024]...) fusion(bf16[384,8,1024]{2,1,0:T(8,128)(2,1)} %bitcast.438), kind=kLoop, calls=%fused_computation.278 | loop fusion | bytes 12582912 | tf_op jit(solution)/shard_map/slice | solution.py:249
  671.3 24.3 %gather_fusion.2 = bf16[4608,1024]{1,0:T(8,128)(2,1)} fusion(bf16[3072,1024]{1,0:T(8,128)(2,1)} %fusion.55, s32[5120]{0:T(1024)S(1)} %copy-done.60), kind=kCustom, calls=%fused_computation.2 | custom fusion | bytes 18892800 | tf_op jit(solution)/shard_map/gather | solution.py:266
  700.3 209.4 %all_to_all.21 = bf16[8,2,288,1024]{3,2,1,0:T(8,128)(2,1)} all-to-all(bf16[8,2,288,1024]{3,2,1,0:T(8,128)(2,1)S(1)} %broadcast_select_fusion.1), channel_id=1, replica_groups=mesh['ep'=8,'ctx'=4] {'ep'}, dimensions={0} | all-to-all | bytes 18874368 | tf_op jit(solution)/shard_map/all_to_all | solution.py:269
  909.6 16.1 fusion.60
  925.7 11.9 fusion.86
  937.6 12.7 fusion.56
  950.3 8.9 copy.149
  964.8 204.2 %all-to-all-done.3 = bf16[8,2,288,1024]{3,2,1,0:T(8,128)(2,1)} async-done(((bf16[8,2,288,1024]{3,2,1,0:T(8,128)(2,1)}), bf16[8,2,288,1024]{3,2,1,0:T(8,128)(2,1)}, u32[]{:S(2)}, u32[]{:S(2)}) %all-to-all-start.3) | async-done | bytes 9437216 | tf_op jit(solution)/shard_map/all_to_all | solution.py:309
  1168.9 20.8 %gather_fusion.3 = bf16[3072,1024]{1,0:T(8,128)(2,1)} fusion(bf16[4608,1024]{1,0:T(8,128)(2,1)} %bitcast.48, s32[3072]{0:T(1024)S(1)} %broadcast_clamp_fusion), kind=kCustom, calls=%fused_computation.3 | custom fusion | bytes 12595200 | tf_op jit(solution)/shard_map/gather | solution.py:315
  1189.7 31.0 %fusion.168 = (bf16[384,1,1024]{2,1,0:T(2,128)(2,1)S(1)}, bf16[384,1,1024]{2,1,0:T(2,128)(2,1)S(1)}, bf16[384,1,1024]{2,1,0:T(2,128)(2,1)S(1)}, bf16[384,1,1024]...) fusion(bf16[384,8,1024]{2,1,0:T(8,128)(2,1)} %bitcast.437), kind=kLoop, calls=%fused_computation.277 | loop fusion | bytes 12582912 | tf_op jit(solution)/shard_map/slice | solution.py:320
  1228.4 73.9 %while.31 = (s32[]{:T(128)}, f32[384,8,2,64]{0,3,2,1:T(8,128)}, bf16[4,384,8,64]{1,3,2,0:T(8,128)(2,1)}, bf16[4,384,8,64]{1,3,2,0:T(8,128)(2,1)}, bf16[4,384,8,6...) while((s32[]{:T(128)}, f32[384,8,2,64]{0,3,2,1:T(8,128)}, ...), condition=%wide.region_26.27_spmd.clone, body=%wide.region_25.26_spmd.clone.sunk | while | flops 1541703168 | bytes 89783416 | solution.py:367
  1316.5 5.5 reshape.625
  1322.1 11.0 bitcast_convert_fusion
  1333.1 10.2 bitcast_convert_fusion.1
  1343.4 6.3 bitcast_convert_fusion.2
  1364.0 6.8 reduce-scatter.9.cloned.1.call-done
  1374.7 9.3 fusion.138
  1384.0 109.7 %all-reduce.8.cloned.1.call-done = (bf16[2,1024,512]{2,1,0:T(8,128)(2,1)}, bf16[2,1024,512]{2,1,0:T(8,128)(2,1)}, bf16[2,512,1024]{2,1,0:T(8,128)(2,1)}) async-done(((bf16[2,1024,512]{2,1,0:T(8,128)(2,1)}, bf16[2,1024,512]{2,1,0:T(8,128)(2,1)}, bf16[2,512,1024]{2,1,0:T(8,128)(2,1)}), (bf16[2,1024,512]{2,1,0:T(8,128)(2,1)}, bf16[2,1024,512]{2,1,0:T(8,128)(2,1)}, ...) | async-done | bytes 6291472 | tf_op jit(solution)/shard_map/psum | solution.py:311
  1507.9 41.2 %all-reduce = (f32[1024]{0:T(1024)}, f32[1024]{0:T(1024)}) all-reduce(f32[1024]{0:T(1024)S(1)} %get-tuple-element.316, f32[1024]{0:T(1024)S(1)} %copy-done.75), channel_id=1, replica_groups=mesh['ep'=8,'ctx'=4] {'ep','ctx'}, use_global_device_ids=true, to_apply=%region_31.32 | all-reduce | flops 2048 | bytes 16384 | tf_op jit(solution)/shard_map/psum | solution.py:413
  1552.4 187.0 %all-reduce.6.cloned.1.call-done = (f32[1024,1024]{1,0:T(8,128)}, f32[1024,512]{1,0:T(8,128)}, f32[1024,512]{1,0:T(8,128)}, f32[1024,1024]{1,0:T(8,128)}, f32[1024,16]{0,1:T(8,128)}) async-done(((f32[1024,1024]{1,0:T(8,128)}, f32[1024,512]{1,0:T(8,128)}, f32[1024,512]{1,0:T(8,128)}, f32[1024,1024]{1,0:T(8,128)}, f32[1024,16]{0,1:T(8,128)}), (f32[1024,1024]{1,0:T(8,128)}, f32[1024,512]{1,0:T(8,128)}, ...) | async-done | bytes 12648464 | tf_op jit(solution)/shard_map/psum | solution.py:413
  (419 shorter events, 265.3 us)
Async XLA Ops:
  7.2 373.6 %copy-start = (bf16[2,512,1024]{2,1,0:T(8,128)(2,1)S(1)}, bf16[2,512,1024]{2,1,0:T(8,128)(2,1)}, u32[]{:S(2)}) copy-start(bf16[2,512,1024]{2,1,0:T(8,128)(2,1)} %param.31) | copy-start | bytes 6291460
  7.2 48.5 %all-gather.3.cloned.1.call-start = ((), (), s32[]{:S(2)}) async-start(), calls=%async_computation.6 | async-start | bytes 1966080 | tf_op jit(solution)/shard_map/all_gather | solution.py:198
  9.4 43.0 %copy-start.58 = (f32[384]{0:T(512)}, f32[384]{0:T(512)S(1)}, u32[]{:S(2)}) copy-start(f32[384]{0:T(512)S(1)} %get-tuple-element.432) | copy-start | bytes 4612
  11.9 43.4 %copy-start.47 = (f32[384,32]{0,1:T(8,128)}, f32[384,32]{0,1:T(8,128)S(1)}, u32[]{:S(2)}) copy-start(f32[384,32]{0,1:T(8,128)S(1)} %get-tuple-element.429) | copy-start | bytes 147460
  11.9 43.4 %copy-start.49 = (f32[384,32]{0,1:T(8,128)}, f32[384,32]{0,1:T(8,128)S(1)}, u32[]{:S(2)}) copy-start(f32[384,32]{0,1:T(8,128)S(1)} %get-tuple-element.430) | copy-start | bytes 147460
  14.9 47.6 %all-gather.5.cloned.1.call-start = ((), (), s32[]{:S(2)}) async-start(), calls=%async_computation.7 | async-start | bytes 1966080 | tf_op jit(solution)/shard_map/all_gather | solution.py:199
  23.8 27.9 %copy-start.62 = (s32[3072,1]{0,1:T(1,128)}, s32[3072,1]{0,1:T(1,128)S(1)}, u32[]{:S(2)}) copy-start(s32[3072,1]{0,1:T(1,128)S(1)} %compare_select_fusion) | copy-start | bytes 36868
  127.6 15.6 copy-start.69
  128.3 277.6 %copy-start.2 = (bf16[384,1024]{1,0:T(8,128)(2,1)}, bf16[384,1024]{1,0:T(8,128)(2,1)S(1)}, u32[]{:S(2)}) copy-start(bf16[384,1024]{1,0:T(8,128)(2,1)S(1)} %multiply_convert_fusion) | copy-start | bytes 2359300
  148.0 212.9 %copy-start.76 = (bf16[2,1024,512]{2,1,0:T(8,128)(2,1)S(1)}, bf16[2,1024,512]{2,1,0:T(8,128)(2,1)}, u32[]{:S(2)}) copy-start(bf16[2,1024,512]{2,1,0:T(8,128)(2,1)} %param.29) | copy-start | bytes 6291460
  360.9 7.5 copy-start.25
  399.6 6.6 copy-start.57
  399.6 210.3 %all-to-all-start.1 = ((bf16[8,2,288,1024]{3,2,1,0:T(8,128)(2,1)}), bf16[8,2,288,1024]{3,2,1,0:T(8,128)(2,1)}, u32[]{:S(2)}, u32[]{:S(2)}) async-start(bf16[8,2,288,1024]{3,2,1,0:T(8,128)(2,1)} %copy.138), calls=%async_computation.1 | async-start | bytes 18874368 | tf_op jit(solution)/shard_map/all_to_all | solution.py:243
  405.9 817.5 %copy-start.66 = (f32[384]{0:T(512)}, f32[384]{0:T(512)S(1)}, u32[]{:S(2)}) copy-start(f32[384]{0:T(512)S(1)} %fusion.162) | copy-start | bytes 4612
  630.6 30.9 %copy-start.30 = (bf16[1,384,1024]{2,1,0:T(8,128)(2,1)S(1)}, bf16[1,384,1024]{2,1,0:T(8,128)(2,1)}, u32[]{:S(2)}) copy-start(bf16[1,384,1024]{2,1,0:T(8,128)(2,1)} %param.21) | copy-start | bytes 2359300
  666.5 298.2 %copy-start.54 = (f32[384,8]{0,1:T(8,128)}, f32[384,8]{0,1:T(8,128)S(1)}, u32[]{:S(2)}) copy-start(f32[384,8]{0,1:T(8,128)S(1)} %get-tuple-element.393) | copy-start | bytes 36868
  925.7 11.9 copy-start.77
  959.2 209.8 %all-to-all-start.3 = ((bf16[8,2,288,1024]{3,2,1,0:T(8,128)(2,1)}), bf16[8,2,288,1024]{3,2,1,0:T(8,128)(2,1)}, u32[]{:S(2)}, u32[]{:S(2)}) async-start(bf16[8,2,288,1024]{3,2,1,0:T(8,128)(2,1)} %copy.149), calls=%async_computation.3 | async-start | bytes 18874368 | tf_op jit(solution)/shard_map/all_to_all | solution.py:309
  964.4 396.0 %reduce-scatter.7.cloned.1.call-start = ((), (), s32[]{:S(2)}) async-start(), calls=%async_computation.8 | async-start | bytes 1966080
  964.8 256.0 %copy-start.64 = (bf16[384,16]{0,1:T(8,128)(2,1)}, bf16[384,16]{0,1:T(8,128)(2,1)S(1)}, u32[]{:S(2)}) copy-start(bf16[384,16]{0,1:T(8,128)(2,1)S(1)} %select_reduce_fusion) | copy-start | bytes 36868
  1189.7 31.0 %copy-start.12 = (f32[384,1024]{1,0:T(8,128)S(1)}, f32[384,1024]{1,0:T(8,128)}, u32[]{:S(2)}) copy-start(f32[384,1024]{1,0:T(8,128)} %copy-done.11) | copy-start | bytes 4718596
  1189.7 31.0 %copy-start.70 = (f32[384]{0:T(512)S(1)}, f32[384]{0:T(512)}, u32[]{:S(2)}) copy-start(f32[384]{0:T(512)} %copy-done.69) | copy-start | bytes 4612
  1189.7 31.1 %copy-start.72 = (f32[1024]{0:T(1024)S(1)}, f32[1024]{0:T(1024)}, u32[]{:S(2)}) copy-start(f32[1024]{0:T(1024)} %param.27) | copy-start | bytes 12292
  1312.0 58.7 %reduce-scatter.9.cloned.1.call-start = ((), (), s32[]{:S(2)}) async-start(), calls=%async_computation.9 | async-start | bytes 1966080
  1322.0 171.7 %all-reduce.8.cloned.1.call-start = ((), (), s32[]{:S(2)}) async-start(), calls=%async_computation.11 | async-start | bytes 12582912 | tf_op jit(solution)/shard_map/psum | solution.py:311
  1322.1 21.2 %slice-start = ((s8[9437184]{0:T(1024)(128)(4,1)}), s8[4194304]{0:T(1024)(128)(4,1)S(1)}, s32[]{:S(2)}) async-start(s8[9437184]{0:T(1024)(128)(4,1)} %bitcast.443), calls=%async_computation.12 | async-start | bytes 8388608
  1322.1 21.2 %slice-start.1 = ((s8[9437184]{0:T(1024)(128)(4,1)}), s8[4194304]{0:T(1024)(128)(4,1)S(1)}, s32[]{:S(2)}) async-start(s8[9437184]{0:T(1024)(128)(4,1)} %bitcast.443), calls=%async_computation.13 | async-start | bytes 8388608
  1322.1 21.2 %slice-start.3 = ((s8[4718592]{0:T(1024)(128)(4,1)}), s8[4194304]{0:T(1024)(128)(4,1)S(1)}, s32[]{:S(2)}) async-start(s8[4718592]{0:T(1024)(128)(4,1)} %bitcast.467), calls=%async_computation.15 | async-start | bytes 8388608
  1333.1 10.2 slice-start.2
  1333.1 10.2 slice-start.4
  1349.7 389.7 %all-reduce.6.cloned.1.call-start = ((), (), s32[]{:S(2)}) async-start(), calls=%async_computation.10 | async-start | bytes 25296896 | tf_op jit(solution)/shard_map/psum | solution.py:413
  1505.8 43.3 %copy-start.73 = (f32[384]{0:T(512)S(1)}, f32[384]{0:T(512)}, u32[]{:S(2)}) copy-start(f32[384]{0:T(512)} %get-tuple-element.431) | copy-start | bytes 4612
  (85 other events, 252.4 us)
Sparse Core Ops, SparseCore 0:
  15.1 22.3 all-gather.2
  39.6 19.6 all-gather.4
  1312.2 27.2 reduce-scatter.6
  1342.6 28.1 reduce-scatter.8
  1373.7 119.9 all-reduce.7
  1501.2 238.1 all-reduce.5
where the time goes:
time: 1770 us; the launch traced here: 1760 us
  waiting for transfers between devices  711 us (40%)
  blocking collectives  463 us (26%)
  local copies, waits for them, and re-layouts  262 us (15%)
  matrix products  212 us (12%)
  other arithmetic  82.5 us (5%)
    all_to_all x1, blocking collectives, local(): lax.all_to_all(outgoing, 'ep', split_axis=0, concat_axis=0, tiled=True)  213 us
    all_to_all x1, blocking collectives, local(): lax.all_to_all(grad_send, 'ep', split_axis=0, concat_axis=0, tiled=True)  209 us
    all_to_all x1, waiting for transfers between devices, local(): lax.all_to_all(grad_expert_in, 'ep', split_axis=0, concat_axis=0, tiled=T...  204 us
    all_to_all x1, waiting for transfers between devices, local(): lax.all_to_all(result, 'ep', split_axis=0, concat_axis=0, tiled=True)  204 us
    psum x1, waiting for transfers between devices, local(): lax.psum((grad_w_query, grad_w_key, grad_w_value, grad_w_out, grad_router...  187 us
    psum x1, waiting for transfers between devices, local(): lax.psum(grad_gate_w.astype(jnp.bfloat16), 'ctx').astype(jnp.float32)  110 us
    unnamed x169, local copies, waits for them, and re-layouts  53.4 us
    psum x1, blocking collectives, local(): lax.psum((grad_w_query, grad_w_key, grad_w_value, grad_w_out, grad_router...  41.2 us
  transfers between devices with their start and end apart: 8, of which 5 were waited for; matrix products, arithmetic and copies ran while one was open for 7% of the time, Pallas kernels for 0%

commit v1 on v0

v1 whole, which is shorter than its diff:
```python
import functools

import jax
import jax.numpy as jnp
import numpy as np
from jax import lax
from jax.experimental import pallas as pl
from jax.experimental.pallas import tpu as pltpu
from jax.sharding import PartitionSpec as P

HEAD_DIM = 64
EPS = 1e-06
THETA = 10000.0
NEG = -1e30
LOG2E = 1.4426950408889634
NZ = 4
CORES = 2
F32 = jnp.float32
BF16 = jnp.bfloat16


def dot(a, b, ca, cb):
    return lax.dot_general(a, b, (((ca,), (cb,)), ((), ())), preferred_element_type=F32)


def params(semantics, mib):
    return pltpu.CompilerParams(
        dimension_semantics=semantics, vmem_limit_bytes=mib * 1024 * 1024
    )


def cost(flops, nbytes, trans=0):
    return pl.CostEstimate(flops=flops, bytes_accessed=nbytes, transcendentals=trans)


def rope_tables(ctx_index, ctx_size, rows):
    half = HEAD_DIM // 2
    inv = THETA ** (-np.arange(half, dtype=np.float64) / half)
    fine = np.arange(rows, dtype=np.float64)[:, None] * inv[None, :]
    coarse = (rows * np.arange(ctx_size, dtype=np.float64))[:, None] * inv[None, :]
    tile = lambda t: np.tile(t, (1, 128 // half)).astype(np.float32)
    pick = lambda t: lax.dynamic_slice_in_dim(jnp.asarray(tile(t)), ctx_index, 1, 0)
    cos_f, sin_f = jnp.asarray(tile(np.cos(fine))), jnp.asarray(tile(np.sin(fine)))
    cos_c, sin_c = pick(np.cos(coarse)), pick(np.sin(coarse))
    cos = cos_f * cos_c - sin_f * sin_c
    sin = sin_f * cos_c + cos_f * sin_c
    sign = np.where(np.arange(128) % HEAD_DIM < half, -1.0, 1.0).astype(np.float32)
    return cos, sin * jnp.asarray(sign)[None, :]


def swap_halves(x, roll):
    half = HEAD_DIM // 2
    width = x.shape[1]
    lane = lax.broadcasted_iota(jnp.int32, x.shape, 1)
    return jnp.where(lane % HEAD_DIM < half, roll(x, width - half), roll(x, half))


def project_body(x_ref, gain_ref, wq_ref, wk_ref, wv_ref, cos_ref, sin_ref, n_ref, q_ref, kv_ref):
    step = pl.program_id(0)
    nq = pl.num_programs(0) - 4

    @pl.when(step == 0)
    def _():
        x = x_ref[...].astype(F32)
        scale = lax.rsqrt(jnp.mean(x * x, -1, keepdims=True) + EPS)
        n_ref[...] = (x * scale * gain_ref[...]).astype(BF16)

    def rope(lin):
        cos = jnp.concatenate([cos_ref[...]] * 2, 1)
        sin = jnp.concatenate([sin_ref[...]] * 2, 1)
        return lin * cos + swap_halves(lin, lambda v, s: pltpu.roll(v, s, 1)) * sin

    @pl.when(step < nq)
    def _():
        lin = dot(n_ref[...], wq_ref[...], 1, 0)
        q_ref[...] = rope(lin).astype(BF16) * jnp.asarray(HEAD_DIM**-0.5, BF16)

    @pl.when((step >= nq) & (step < nq + 2))
    def _():
        kv_ref[...] = rope(dot(n_ref[...], wk_ref[...], 1, 0)).astype(BF16)[None]

    @pl.when(step >= nq + 2)
    def _():
        kv_ref[...] = dot(n_ref[...], wv_ref[...], 1, 0).astype(BF16)[None]


def project(x, gain, wq, wk, wv, cos, sin):
    rows, width = x.shape
    nq = wq.shape[1] // 256
    kvw = wk.shape[1]
    nk = kvw // 256
    clip = lambda v, hi: jnp.minimum(jnp.maximum(v, 0), hi)
    full = lambda shape: pl.BlockSpec(shape, lambda i: (0, 0))
    return pl.pallas_call(
        project_body,
        grid=(nq + 2 * nk,),
        in_specs=[
            full((rows, width)),
            full((1, width)),
            pl.BlockSpec((width, 256), lambda i: (0, clip(i, nq - 1))),
            pl.BlockSpec((width, 256), lambda i: (0, clip(i - nq, nk - 1))),
            pl.BlockSpec((width, 256), lambda i: (0, clip(i - nq - nk, nk - 1))),
            full((rows, 128)),
            full((rows, 128)),
        ],
        out_specs=[
            full((rows, width)),
            pl.BlockSpec((rows, 256), lambda i: (0, clip(i, nq - 1))),
            pl.BlockSpec(
                (1, rows, 256),
                lambda i: (clip(i - nq, 2 * nk - 1) // nk, 0, clip(i - nq, 2 * nk - 1) % nk),
            ),
        ],
        out_shape=[
            jax.ShapeDtypeStruct((rows, width), BF16),
            jax.ShapeDtypeStruct((rows, wq.shape[1]), BF16),
            jax.ShapeDtypeStruct((2, rows, kvw), BF16),
        ],
        compiler_params=params(("arbitrary",), 32),
        cost_estimate=cost(2 * rows * width * 2 * width, 6 * 1024 * 1024),
        name="project",
    )(x, gain, wq, wk, wv, cos, sin)


def split_heads(block):
    lane = lax.broadcasted_iota(jnp.int32, block.shape, 1)
    low = lane < HEAD_DIM
    zero = jnp.zeros_like(block)
    turned = jnp.concatenate([block[:, HEAD_DIM:], block[:, :HEAD_DIM]], 1)
    first = jnp.concatenate([jnp.where(low, block, zero), jnp.where(low, zero, turned)], 0)
    second = jnp.concatenate([jnp.where(low, turned, zero), jnp.where(low, zero, block)], 0)
    return first, second


def attend_body(roles, info_ref, q_ref, *refs):
    kv_refs = refs[:roles]
    wo_ref, x_ref, gain_ref, att_ref, lse_ref, hid_ref, mix_ref, acc, top, proj = refs[roles:]
    step = pl.program_id(0)
    rows = q_ref.shape[0]
    seq_len = info_ref[0]
    acc[...] = jnp.zeros_like(acc)
    top[...] = jnp.full_like(top, NEG)
    row = lax.broadcasted_iota(jnp.int32, (rows, rows), 0)
    col = lax.broadcasted_iota(jnp.int32, (rows, rows), 1)
    lane = lax.broadcasted_iota(jnp.int32, (rows, 128), 1)
    stack_row = lax.broadcasted_iota(jnp.int32, (2 * rows, 128), 0)
    stack_lane = lax.broadcasted_iota(jnp.int32, (2 * rows, 128), 1)
    ones = jnp.where((stack_lane == 0) == (stack_row < rows), 1.0, 0.0)
    ones = jnp.where(stack_lane < 2, ones, 0.0).astype(BF16)

    for role in range(roles):
        start, active, causal = (info_ref[1 + 3 * role + i] for i in range(3))

        @pl.when(active > 0)
        def _(role=role, start=start, causal=causal):
            keys = split_heads(kv_refs[role][0])
            values = split_heads(kv_refs[role][1])
            bad = col + start >= seq_len
            if role == 0:
                bad = bad | (col > row)
            bias = jnp.where(bad, NEG, 0.0)
            for pair in range(2):
                q = q_ref[:, pair * 128 : pair * 128 + 128]
                scores = dot(q, keys[pair], 1, 1)
                weights, shrinks, news = [], [], []
                for head in range(2):
                    part = scores[:, head * rows : (head + 1) * rows] + bias
                    old = top[:, 2 * pair + head : 2 * pair + head + 1]
                    new = jnp.maximum(old, jnp.max(part, 1, keepdims=True))
                    weights.append(jnp.exp2((part - new) * LOG2E).astype(BF16))
                    shrinks.append(jnp.exp2((old - new) * LOG2E))
                    top[:, 2 * pair + head : 2 * pair + head + 1] = new
                both = jnp.concatenate(weights, 1)
                full = jnp.concatenate([values[pair], ones], 1)
                fresh = dot(both, full, 1, 0)
                shrink = jnp.concatenate(
                    [
                        jnp.where(lane < HEAD_DIM, shrinks[0], shrinks[1]),
                        jnp.where(lane == 0, shrinks[0], shrinks[1]),
                    ],
                    1,
                )
                acc[pair] = acc[pair] * shrink + fresh

    for pair in range(2):
        sums = [acc[pair, :, 128 + head : 129 + head] for head in range(2)]
        total = jnp.where(lane < HEAD_DIM, sums[0], sums[1])
        att = (acc[pair, :, :128] / total).astype(BF16)
        att_ref[:, pair * 128 : pair * 128 + 128] = att
        for head in range(2):
            at = 2 * pair + head
            lse_ref[0, :, at : at + 1] = top[:, at : at + 1] * LOG2E + jnp.log2(sums[head])

    @pl.when(step == 0)
    def _():
        proj[...] = x_ref[...].astype(F32)

    proj[...] += dot(att_ref[...], wo_ref[...], 1, 0)

    @pl.when(step == pl.num_programs(0) - 1)
    def _():
        hidden = proj[...]
        scale = lax.rsqrt(jnp.mean(hidden * hidden, -1, keepdims=True) + EPS)
        hid_ref[...] = hidden
        mix_ref[...] = (hidden * scale * gain_ref[...]).astype(BF16)


def attend(info, q, blocks, wo, x, gain):
    rows, width = q.shape
    steps = width // 256
    roles = len(blocks)
    full = lambda shape: pl.BlockSpec(shape, lambda i, s: (0, 0))
    return pl.pallas_call(
        functools.partial(attend_body, roles),
        grid_spec=pltpu.PrefetchScalarGridSpec(
            num_scalar_prefetch=1,
            grid=(steps,),
            in_specs=[pl.BlockSpec((rows, 256), lambda i, s: (0, i))]
            + [pl.BlockSpec((2, rows, 128), lambda i, s: (0, 0, i))] * roles
            + [
                pl.BlockSpec((256, x.shape[1]), lambda i, s: (i, 0)),
                full(x.shape),
                full((1, x.shape[1])),
            ],
            out_specs=[
                pl.BlockSpec((rows, 256), lambda i, s: (0, i)),
                pl.BlockSpec((1, rows, 128), lambda i, s: (i, 0, 0)),
                full(x.shape),
                full(x.shape),
            ],
            scratch_shapes=[
                pltpu.VMEM((2, rows, 256), F32),
                pltpu.VMEM((rows, 128), F32),
                pltpu.VMEM(x.shape, F32),
            ],
        ),
        out_shape=[
            jax.ShapeDtypeStruct((rows, width), BF16),
            jax.ShapeDtypeStruct((steps, rows, 128), F32),
            jax.ShapeDtypeStruct(x.shape, F32),
            jax.ShapeDtypeStruct(x.shape, BF16),
        ],
        compiler_params=params(("arbitrary",), 40),
        cost_estimate=cost(16 * rows * rows * roles * width, 8 * 1024 * 1024),
        name="attend",
    )(info, q, *blocks, wo, x, gain)


def attend_back_body(roles, info_ref, q_ref, do_ref, lse_ref, delta_ref, *refs):
    kv_refs, dq_ref, dkv_refs = refs[:roles], refs[roles], refs[roles + 1 :]
    rows = q_ref.shape[0]
    seq_len = info_ref[0]
    dq_ref[...] = jnp.zeros_like(dq_ref)
    key = lax.broadcasted_iota(jnp.int32, (rows, rows), 0)
    query = lax.broadcasted_iota(jnp.int32, (rows, rows), 1)
    lane = lax.broadcasted_iota(jnp.int32, (rows, 128), 1)
    low = lane < HEAD_DIM

    for role in range(roles):
        start, active, causal = (info_ref[1 + 3 * role + i] for i in range(3))

        @pl.when(active == 0)
        def _(role=role):
            dkv_refs[role][...] = jnp.zeros_like(dkv_refs[role])

        @pl.when(active > 0)
        def _(role=role, start=start):
            keys = split_heads(kv_refs[role][0])
            values = split_heads(kv_refs[role][1])
            bad = key + start >= seq_len
            if role == 0:
                bad = bad | (key > query)
            bias = jnp.where(bad, NEG, 0.0)
            dks, dvs = [], []
            for pair in range(2):
                q = q_ref[:, pair * 128 : pair * 128 + 128]
                do = do_ref[:, pair * 128 : pair * 128 + 128]
                scores = dot(keys[pair], q, 1, 1)
                grads = dot(values[pair], do, 1, 1)
                probs, raws = [], []
                for head in range(2):
                    at = 2 * pair + head
                    part = scores[head * rows : (head + 1) * rows] * LOG2E + bias
                    prob = jnp.exp2(part - lse_ref[0, at : at + 1, :])
                    grad = grads[head * rows : (head + 1) * rows]
                    raws.append((prob * (grad - delta_ref[0, at : at + 1, :])).astype(BF16))
                    probs.append(prob.astype(BF16))
                raw = jnp.concatenate(raws, 0)
                dq_ref[:, pair * 128 : pair * 128 + 128] += dot(raw, keys[pair], 0, 0)
                dks.append(dot(raw, q, 1, 0))
                dvs.append(dot(jnp.concatenate(probs, 0), do, 1, 0))
            for which, parts in enumerate((dks, dvs)):
                top_a, bottom_a = parts[0][:rows], parts[0][rows:]
                top_b, bottom_b = parts[1][:rows], parts[1][rows:]
                turn = pltpu.roll(jnp.where(low, top_b, bottom_a), HEAD_DIM, 1)
                whole = jnp.where(low, top_a, bottom_b) + turn
                dkv_refs[role][which] = whole.astype(dkv_refs[role].dtype)


def attend_back(info, q, do, lse, delta, blocks):
    rows, width = q.shape
    steps = width // 256
    roles = len(blocks)
    kvw = blocks[0].shape[2]
    wide = pl.BlockSpec((rows, 256), lambda i, s: (0, i))
    heads = pl.BlockSpec((1, 8, rows), lambda i, s: (i, 0, 0))
    kv = pl.BlockSpec((2, rows, 128), lambda i, s: (0, 0, i))
    return pl.pallas_call(
        functools.partial(attend_back_body, roles),
        grid_spec=pltpu.PrefetchScalarGridSpec(
            num_scalar_prefetch=1,
            grid=(steps,),
            in_specs=[wide, wide, heads, heads] + [kv] * roles,
            out_specs=[wide] + [kv] * roles,
        ),
        out_shape=[jax.ShapeDtypeStruct((rows, width), F32)]
        + [jax.ShapeDtypeStruct((2, rows, kvw), F32)]
        + [jax.ShapeDtypeStruct((2, rows, kvw), BF16)] * (roles - 1),
        compiler_params=params(("arbitrary",), 40),
        cost_estimate=cost(40 * rows * rows * roles * width, 16 * 1024 * 1024),
        name="attend_back",
    )(info, q, do, lse, delta, *blocks)


def expert_body(own, remotes, experts, info_ref, x_ref, cot_ref, wr_ref, *refs):
    wg_hbm, wu_hbm, wd_hbm = refs[:3]
    far = refs[3 : 3 + remotes]
    outs = refs[3 + remotes :]
    if len(outs) == 18:
        outs = outs[5:]
    (gm_ref, gate_ref, out_ref, xs_ref, inner_ref, dg_ref, du_ref) = outs[:7]
    wbuf, sem, gm_acc, out_acc, gates, back = outs[7:]
    step = pl.program_id(0)
    total = own + remotes
    rows, width = x_ref.shape
    ff = width // 2
    slot = lax.rem(step, 2)

    def fetch(target, at):
        @pl.when(target < own)
        def _():
            src = (
                wg_hbm.at[target],
                wu_hbm.at[target],
                wd_hbm.at[target, :, pl.ds(0, ff)],
                wd_hbm.at[target, :, pl.ds(ff, ff)],
            )
            offsets = (0, width, 2 * width, 2 * width + ff)
            sizes = (width, width, ff, ff)
            for piece, (ref, off, size) in enumerate(zip(src, offsets, sizes)):
                pltpu.make_async_copy(
                    ref, wbuf.at[at, pl.ds(off, size)], sem.at[at, piece]
                ).start()

        for i in range(remotes):

            @pl.when(target == own + i)
            def _(i=i):
                offsets = (0, width, 2 * width, 2 * width + ff)
                sizes = (width, width, ff, ff)
                for piece, (off, size) in enumerate(zip(offsets, sizes)):
                    pltpu.make_async_copy(
                        far[i].at[pl.ds(off, size)],
                        wbuf.at[at, pl.ds(off, size)],
                        sem.at[at, piece],
                    ).start()

    @pl.when(step == 0)
    def _():
        fetch(jnp.int32(0), 0)

    @pl.when(step + 1 < total)
    def _():
        fetch(step + 1, lax.rem(step + 1, 2))

    lane = lax.broadcasted_iota(jnp.int32, (rows, 128), 1)

    @pl.when(step == 0)
    def _():
        logits = dot(x_ref[...], wr_ref[...], 1, 0)
        mask_t = cot_ref[pl.ds(rows, experts), :rows].astype(F32)
        mask_t = jnp.concatenate([mask_t, jnp.zeros((128 - experts, rows), F32)], 0)
        mask = jnp.transpose(mask_t) > 0.5
        high = jnp.max(jnp.where(mask, logits, NEG), 1, keepdims=True)
        raised = jnp.where(mask, jnp.exp(logits - high), 0.0)
        gates[...] = raised / jnp.sum(raised, 1, keepdims=True)
        gate_ref[...] = gates[...]
        back[...] = jnp.zeros_like(back)
        gm_acc[...] = jnp.zeros_like(gm_acc)
        out_acc[...] = jnp.zeros_like(out_acc)
        xs_ref[0] = x_ref[...]

    offsets = (0, width, 2 * width, 2 * width + ff)
    sizes = (width, width, ff, ff)
    for piece, (off, size) in enumerate(zip(offsets, sizes)):
        pltpu.make_async_copy(
            far[0].at[pl.ds(off, size)] if remotes else wg_hbm.at[0, pl.ds(0, size)],
            wbuf.at[slot, pl.ds(off, size)],
            sem.at[slot, piece],
        ).wait()

    wg = wbuf[slot, :width, :]
    wu = wbuf[slot, width : 2 * width, :]
    wd0 = wbuf[slot, 2 * width : 2 * width + ff, :]
    wd1 = wbuf[slot, 2 * width + ff :, :]
    which = info_ref[2] + info_ref[3 + step]
    x = x_ref[...]
    cot = cot_ref[pl.ds(0, rows), :]
    g = dot(x, wg, 1, 0)
    u = dot(x, wu, 1, 0)
    raw = dot(cot[:, :ff], wd0, 1, 1) + dot(cot[:, ff:], wd1, 1, 1)
    gate = jnp.sum(jnp.where(lane == which, gates[...], 0.0), 1, keepdims=True)
    sig = 1.0 / (1.0 + jnp.exp(-g))
    silu = g * sig
    inner = silu * u
    gg = jnp.sum(raw * inner, 1, keepdims=True)
    back[...] += jnp.where(lane == which, gg, 0.0)
    scaled = (gate * inner).astype(BF16)
    gi = gate * raw
    dg = (gi * u * (sig * (1.0 + g * (1.0 - sig)))).astype(BF16)
    du = (gi * silu).astype(BF16)
    inner_ref[0] = scaled
    dg_ref[0] = dg
    du_ref[0] = du
    out_acc[:, :ff] += dot(scaled, wd0, 1, 0)
    out_acc[:, ff:] += dot(scaled, wd1, 1, 0)
    gm_acc[...] += dot(dg, wg, 1, 1) + dot(du, wu, 1, 1)

    @pl.when(step == total - 1)
    def _():
        gm_ref[pl.ds(0, rows), :] = gm_acc[...].astype(BF16)
        back_t = jnp.transpose(back[...])[:experts, :].astype(BF16)
        pad = jnp.zeros((experts, width - rows), BF16)
        gm_ref[pl.ds(rows, experts), :] = jnp.concatenate([back_t, pad], 1)
        out_ref[0] = out_acc[...].astype(BF16)


def expert_call(info, x, cot_all, wr, own_weights, far, experts, kept):
    rows, width = x.shape
    own = own_weights[0].shape[0]
    remotes = len(far)
    total = own + remotes
    ff = width // 2
    ext = rows + experts
    full = lambda shape: pl.BlockSpec(shape, lambda i, s: (0, 0))
    anywhere = pl.BlockSpec(memory_space=pl.ANY)
    big = pl.BlockSpec((1, rows, width), lambda i, s: (s[0], 0, 0))
    part = pl.BlockSpec((1, rows, ff), lambda i, s: (s[0], 0, s[3 + i]))
    wide = jax.ShapeDtypeStruct((NZ, rows, width), BF16)
    hidden = jax.ShapeDtypeStruct((NZ, rows, total * ff), BF16)
    alias = {} if kept is None else {7 + remotes + i: 2 + i for i in range(5)}
    outs = pl.pallas_call(
        functools.partial(expert_body, own, remotes, experts),
        grid_spec=pltpu.PrefetchScalarGridSpec(
            num_scalar_prefetch=1,
            grid=(total,),
            in_specs=[
                full((rows, width)),
                pl.BlockSpec((ext, width), lambda i, s: (s[0], 0)),
                full(wr.shape),
            ]
            + [anywhere] * (3 + remotes + (0 if kept is None else 5)),
            out_specs=[full((ext, width)), full((rows, 128)), big, big, part, part, part],
            scratch_shapes=[
                pltpu.VMEM((2, 3 * width, ff), BF16),
                pltpu.SemaphoreType.DMA((2, 4)),
                pltpu.VMEM((rows, width), F32),
                pltpu.VMEM((rows, width), F32),
                pltpu.VMEM((rows, 128), F32),
                pltpu.VMEM((rows, 128), F32),
            ],
        ),
        out_shape=[
            jax.ShapeDtypeStruct((ext, width), BF16),
            jax.ShapeDtypeStruct((rows, 128), F32),
            wide,
            wide,
            hidden,
            hidden,
            hidden,
        ],
        input_output_aliases=alias,
        compiler_params=params(("arbitrary",), 40),
        cost_estimate=cost(12 * rows * width * ff * total, total * 6 * width * ff),
        name="experts",
    )(info, x, cot_all, wr, *own_weights, *far, *(kept or ()))
    return outs[0], outs[1], tuple(outs[2:])


def local(
    tokens,
    lengths,
    routes,
    cotangent,
    attn_norm,
    w_query,
    w_key,
    w_value,
    w_out,
    ffn_norm,
    w_router,
    expert_gate_weight,
    expert_up_weight,
    expert_down_weight,
):
    rows, width = tokens.shape[1:]
    experts = w_router.shape[1]
    own = expert_gate_weight.shape[0]
    ff = expert_gate_weight.shape[2]
    ctx_size, ep_size = lax.axis_size("ctx"), lax.axis_size("ep")
    ny, nx = ctx_size // CORES, ep_size // NZ
    ctx_index, ep_index = lax.axis_index("ctx"), lax.axis_index("ep")
    y, core = ctx_index // CORES, ctx_index % CORES
    z, xpos = ep_index // nx, ep_index % nx
    seq_len = lengths[0]
    low = tokens[0]
    positions = ctx_index * rows + jnp.arange(rows, dtype=jnp.int32)
    valid_flag = positions < seq_len
    valid = valid_flag.astype(F32)[:, None]

    core_swap = [(c, c ^ 1) for c in range(ctx_size)]
    core_up = [(c, c + 1) for c in range(0, ctx_size, CORES)]
    core_down = [(c + 1, c) for c in range(0, ctx_size, CORES)]
    y_up = lambda k: [(c, c + CORES * k) for c in range(ctx_size - CORES * k)]
    y_down = lambda k: [(b, a) for a, b in y_up(k)]
    zx = lambda pairs: [(a * nx + i, b * nx + i) for a, b in pairs for i in range(nx)]
    z_groups = [[i + nx * k for k in range(NZ)] for i in range(nx)]
    x_groups = [[nx * k + i for i in range(nx)] for k in range(NZ)]
    x_shift = lambda s: [(k * nx + i, k * nx + (i + s) % nx) for k in range(NZ) for i in range(nx)]

    sent = jnp.concatenate(
        [
            expert_gate_weight[core],
            expert_up_weight[core],
            expert_down_weight[core][:, :ff],
            expert_down_weight[core][:, ff:],
        ],
        0,
    )
    far, places = [], [xpos * own, xpos * own + 1]
    for shift in range(1, nx):
        arrived = lax.ppermute(sent, "ep", x_shift(shift))
        far += [arrived, lax.ppermute(arrived, "ctx", core_swap)]
        origin = (xpos - shift) % nx * own
        places += [origin + core, origin + 1 - core]

    cot_low = jnp.where(valid_flag[:, None], cotangent[0], jnp.zeros((), BF16))
    ids = jnp.arange(experts, dtype=jnp.int32)
    mask_t = jnp.any(routes[0][None] == ids[:, None, None], -1).astype(BF16)
    mask_t = jnp.pad(mask_t, ((0, 0), (0, width - rows)))
    cot_all = lax.all_gather(
        jnp.concatenate([cot_low, mask_t], 0), "ep", axis_index_groups=z_groups, tiled=True
    )

    cos, sin = rope_tables(ctx_index, ctx_size, rows)
    normed, q, kv = project(low, attn_norm[None], w_query, w_key, w_value, cos, sin)

    blocks = [kv, lax.ppermute(kv, "ctx", core_up)]
    facts = [(ctx_index * rows, True), ((ctx_index - 1) * rows, core == 1)]
    travelling = kv
    for back in range(1, ny):
        travelling = lax.ppermute(travelling, "ctx", y_up(1))
        blocks += [travelling, lax.ppermute(travelling, "ctx", core_swap)]
        base = (y - back) * CORES
        facts += [((base + core) * rows, y >= back), ((base + 1 - core) * rows, y >= back)]
    info = [seq_len]
    for start, reach in facts:
        info += [start, (jnp.asarray(reach) & (start < seq_len)).astype(jnp.int32), jnp.int32(0)]
    info = jnp.stack([jnp.asarray(v, jnp.int32) for v in info])

    attended, lse, hidden, mixed = attend(info, q, blocks, w_out, low, ffn_norm[None])

    near = lax.ppermute(mixed, "ep", zx([(0, 1), (1, 0), (2, 3), (3, 2)]))
    middle = lax.ppermute(mixed, "ep", zx([(1, 2), (2, 1)]))
    across = lax.ppermute(near, "ep", zx([(1, 2), (2, 1)]))
    outward = lax.ppermute(middle, "ep", zx([(1, 0), (2, 3)]))
    last = lax.ppermute(across, "ep", zx([(1, 0), (2, 3)]))
    inside = (z == 1) | (z == 2)
    shards = [
        (mixed, z),
        (near, z ^ 1),
        (jnp.where(inside, middle, outward), jnp.where(z < 2, 2, 1)),
        (jnp.where(inside, across, last), jnp.where(z < 2, 3, 0)),
    ]
    wr = jnp.pad(w_router, ((0, 0), (0, 128 - experts)))
    weights = (expert_gate_weight, expert_up_weight, expert_down_weight)
    kept, gms, gates = None, [], None
    for data, shard in shards:
        facts = [shard, jnp.int32(0), z * nx * own] + places
        facts = jnp.stack([jnp.asarray(v, jnp.int32) for v in facts])
        gm, gate, kept = expert_call(facts, data, cot_all, wr, weights, far, experts, kept)
        gms.append(gm)
        gates = gate if gates is None else gates

    add = lambda a, b: (a.astype(F32) + b.astype(F32)).astype(BF16)
    first = lax.ppermute(gms[3], "ep", zx([(0, 1), (3, 2)]))
    second = lax.ppermute(gms[2], "ep", zx([(0, 1), (3, 2)]))
    carried = lax.ppermute(add(gms[3], first), "ep", zx([(1, 2), (2, 1)]))
    third = lax.ppermute(gms[1], "ep", zx([(0, 1), (3, 2)]))
    turned = lax.ppermute(add(gms[2], second), "ep", zx([(1, 2), (2, 1)]))
    final = lax.ppermute(add(gms[1], carried), "ep", zx([(2, 3), (1, 0)]))
    summed = gms[0].astype(F32) + third.astype(F32) + turned.astype(F32) + final.astype(F32)

    out_all, x_all, inner_all, dg_all, du_all = kept
    cot_rows = cot_all.reshape(NZ, rows + experts, width)[:, :rows].reshape(NZ * rows, width)
    x_rows = x_all.reshape(NZ * rows, width)
    group = nx * own
    flat = lambda a: a.reshape(NZ * rows, group * ff)
    grad_gate_w = dot(x_rows, flat(dg_all), 0, 0).astype(BF16)
    grad_up_w = dot(x_rows, flat(du_all), 0, 0).astype(BF16)
    grad_down = dot(flat(inner_all), cot_rows, 0, 0).astype(BF16)
    stack = lambda w: w.reshape(width, nx, own, ff).transpose(1, 2, 0, 3).reshape(nx * own, width, ff)
    expert_grads = (stack(grad_gate_w), stack(grad_up_w), grad_down.reshape(nx * own, ff, width))
    expert_grads = tuple(
        lax.psum(
            lax.psum_scatter(
                g, "ep", scatter_dimension=0, axis_index_groups=x_groups, tiled=True
            ),
            "ctx",
        ).astype(F32)
        for g in expert_grads
    )
    expert_sum = lax.psum_scatter(
        out_all.reshape(NZ * rows, width),
        "ep",
        scatter_dimension=0,
        axis_index_groups=z_groups,
        tiled=True,
    ).astype(F32)
    result_out = (valid * (hidden + expert_sum)).astype(BF16)

    grad_mixed = summed[:rows]
    grad_gates = summed[rows:, :rows].T
    gates = gates[:, :experts]
    grad_logits = gates * (grad_gates - jnp.sum(gates * grad_gates, -1, keepdims=True))
    grad_logits = grad_logits.astype(BF16)
    grad_router = dot(mixed, grad_logits, 0, 0)
    grad_mixed = grad_mixed + dot(grad_logits, w_router, 1, 1)
    rms_ffn = lax.rsqrt(jnp.mean(hidden * hidden, -1, keepdims=True) + EPS)
    grad_ffn_norm = jnp.sum(grad_mixed * hidden * rms_ffn, 0)
    weighted = grad_mixed * ffn_norm
    mean_term = jnp.mean(weighted * hidden, -1, keepdims=True)
    grad_hidden = cot_low.astype(F32) + rms_ffn * weighted - hidden * rms_ffn**3 * mean_term
    grad_branch = grad_hidden.astype(BF16)
    grad_w_out = dot(attended, grad_branch, 0, 0)
    grad_attended = dot(grad_branch, w_out, 1, 1).astype(BF16)
    heads = w_query.shape[1] // HEAD_DIM
    delta = grad_attended.astype(F32) * attended.astype(F32)
    delta = jnp.sum(delta.reshape(rows, heads, HEAD_DIM), -1)
    to_rows = lambda a: jnp.pad(a, ((0, 0), (0, 4), (0, 0)))
    delta = to_rows(delta.T.reshape(heads // 4, 4, rows))
    lse = to_rows(lse[:, :, :4].transpose(0, 2, 1))
    dq, *dkvs = attend_back(info, q, grad_attended, lse, delta, blocks)

    dkv = dkvs[0] + lax.ppermute(dkvs[1], "ctx", core_down).astype(F32)
    for back in range(1, ny):
        same, other = dkvs[2 * back], dkvs[2 * back + 1]
        both = add(same, lax.ppermute(other, "ctx", core_swap))
        dkv = dkv + lax.ppermute(both, "ctx", y_down(back)).astype(F32)

    def rope_back(g):
        reps = g.shape[1] // 128
        swapped = swap_halves(g, lambda v, s: jnp.roll(v, s, 1))
        return (g * jnp.tile(cos, (1, reps)) - swapped * jnp.tile(sin, (1, reps))).astype(BF16)

    grad_query_lin = rope_back(dq * HEAD_DIM**-0.5)
    grad_key_lin = rope_back(dkv[0])
    grad_value_lin = dkv[1].astype(BF16)
    grad_w_query = dot(normed, grad_query_lin, 0, 0)
    grad_w_key = dot(normed, grad_key_lin, 0, 0)
    grad_w_value = dot(normed, grad_value_lin, 0, 0)
    grad_normed = (
        dot(grad_query_lin, w_query, 1, 1)
        + dot(grad_key_lin, w_key, 1, 1)
        + dot(grad_value_lin, w_value, 1, 1)
    )
    inputs = low.astype(F32)
    rms_attn = lax.rsqrt(jnp.mean(inputs * inputs, -1, keepdims=True) + EPS)
    grad_attn_norm = jnp.sum(grad_normed * inputs * rms_attn, 0)
    weighted = grad_normed * attn_norm
    mean_term = jnp.mean(weighted * inputs, -1, keepdims=True)
    grad_inputs = grad_hidden + rms_attn * weighted - inputs * rms_attn**3 * mean_term
    total = lax.psum(
        (
            grad_w_query,
            grad_w_key,
            grad_w_value,
            grad_w_out,
            grad_router,
            grad_attn_norm,
            grad_ffn_norm,
        ),
        ("ep", "ctx"),
    )
    return (
        result_out[None],
        grad_inputs.astype(BF16)[None],
        total[5],
        total[0],
        total[1],
        total[2],
        total[3],
        total[6],
        total[4],
        *expert_grads,
    )


def solution(mesh):
    rows, whole, split = P("ep", "ctx", None), P(), P("ep", None, None)
    return jax.shard_map(
        local,
        mesh=mesh,
        in_specs=(rows, P("ep"), rows, rows) + (whole,) * 7 + (split,) * 3,
        out_specs=(rows, rows) + (whole,) * 7 + (split,) * 3,
        check_vma=False,
    )
```

time: 1770 us -> 916 us (0.52)
  blocking collectives: 463 us -> 40.8 us
  waiting for transfers between devices: 711 us -> 525 us
  local copies, waits for them, and re-layouts: 262 us -> 85.5 us
  matrix products: 212 us -> 56.3 us
  Pallas kernels: 0 us -> 101 us
  other arithmetic: 82.5 us -> 42 us
  starting transfers between devices: 11.5 us -> 45.9 us
    all_to_all x2 -> x0, blocking collectives: 422 us -> none  [the longest x1 213 us: local(): lax.all_to_all(outgoing, 'ep', split_axis=0, concat_axis=0, tiled=True)]
    all_to_all x2 -> x0, waiting for transfers between devices: 408 us -> none  [the longest x1 204 us: local(): lax.all_to_all(grad_expert_in, 'ep', split_axis=0, concat_axis=0, tiled=T...]
    dot_general x52 -> x13, matrix products: 212 us -> 56.3 us  [dot(): lax.dot_general(a, b, (((ca,), (cb,)), ((), ())), preferred_element_type=...]
    ppermute x0 -> x19, waiting for transfers between devices: none -> 142 us  [the longest x1 34.9 us: local(): arrived = lax.ppermute(sent, 'ep', x_shift(shift))]
    pallas_call x0 -> x7, Pallas kernels: none -> 101 us  [the longest x4 67.4 us: expert_call(): pl.pallas_call(functools.partial(expert_body, own, remotes, experts), gri...]
    reduce_scatter x0 -> x4, waiting for transfers between devices: none -> 92.1 us  [the longest x3 92.1 us: local(): lax.psum_scatter(g, 'ep', scatter_dimension=0, axis_index_groups=x_groups...]
    gather x4 -> x0, local copies, waits for them, and re-layouts: 80.7 us -> none  [the longest x1 24.3 us: local(): grad_routed[slot_item]]
    slice x4 -> x5, local copies, waits for them, and re-layouts: 62.3 us -> 2.86 us  [the longest x4 2.79 us: rope_back(): swapped = swap_halves(g, lambda v, s: jnp.roll(v, s, 1))]
  transfers between devices with their start and end apart: 8 -> 26, of which waited for: 5 -> 13; matrix products, arithmetic and copies ran while one was open for 7% -> 15% of each run, Pallas kernels for 0% -> 4%
where the time goes in v1:
time: 916 us; the launch traced here: 912 us
  waiting for transfers between devices  525 us (57%)
  Pallas kernels  101 us (11%)
  local copies, waits for them, and re-layouts  85.5 us (9%)
  matrix products  56.3 us (6%)
  starting transfers between devices  45.9 us (5%)
  other arithmetic  42 us (5%)
  blocking collectives  40.8 us (4%)
  between operations  16.1 us (2%)
    psum x1, waiting for transfers between devices, local(): lax.psum((grad_w_query, grad_w_key, grad_w_value, grad_w_out, grad_router...  236 us
    reduce_scatter x3, waiting for transfers between devices, local(): lax.psum_scatter(g, 'ep', scatter_dimension=0, axis_index_groups=x_groups...  92.1 us
    pallas_call x4, Pallas kernels, expert_call(): pl.pallas_call(functools.partial(expert_body, own, remotes, experts), gri...  67.4 us
    dot_general x13, matrix products, dot(): lax.dot_general(a, b, (((ca,), (cb,)), ((), ())), preferred_element_type=...  56.3 us
    psum x1, waiting for transfers between devices, local(): lax.psum(lax.psum_scatter(g, 'ep', scatter_dimension=0, axis_index_groups...  54.2 us
    unnamed x162, local copies, waits for them, and re-layouts  46.8 us
    psum x1, blocking collectives, local(): lax.psum((grad_w_query, grad_w_key, grad_w_value, grad_w_out, grad_router...  40.8 us
    ppermute x1, waiting for transfers between devices, local(): arrived = lax.ppermute(sent, 'ep', x_shift(shift))  34.9 us
  transfers between devices with their start and end apart: 26, of which 13 were waited for; matrix products, arithmetic and copies ran while one was open for 15% of the time, Pallas kernels for 4%

profile of v1, /device:TPU:0, one launch (start us, length us, event | category | flops | bytes accessed | tf_op | source)
XLA Modules:
  0.0 911.8 jit_solution(271113281019192830)
XLA Ops:
  20.7 6.3 project.1
  38.6 9.5 %collective-permute-done.1.refs_2_ = bf16[2,384,512]{2,1,0:T(8,128)(2,1)} collective-permute-done((bf16[2,384,512]{2,1,0:T(8,128)(2,1)}, bf16[2,384,512]{2,1,0:T(8,128)(2,1)}, u32[]{:S(2)}, u32[]{:S(2)}) %collective-permute-start.1) | collective-permute-done | bytes 786464 | tf_op jit(solution)/shard_map/ppermute | solution.py:562
  48.2 34.9 %collective-permute-done.6.refs_3_ = bf16[3072,512]{1,0:T(8,128)(2,1)} collective-permute-done((bf16[3072,512]{1,0:T(8,128)(2,1)}, bf16[3072,512]{1,0:T(8,128)(2,1)}, u32[]{:S(2)}, u32[]{:S(2)}) %collective-permute-start.6) | collective-permute-done | bytes 3145760 | tf_op jit(solution)/shard_map/ppermute | solution.py:542
  87.0 15.0 %attend.1 = (bf16[384,1024]{1,0:T(8,128)(2,1)S(1)}, f32[4,384,128]{2,1,0:T(8,128)S(1)}, f32[384,1024]{1,0:T(8,128)S(1)}, bf16[384,1024]{1,0:T(8,128)(2,1)S(1)}) custom-call(s32[13]{0:T(128)S(1)} %stack.105.info_ref, bf16[384,1024]{1,0:T(8,128)(2,1)S(1)} %copy-done.46, bf16[2,384,512]{2,1,0:T(8,128)(2,1)} %get-tuple-element.50.refs_0_, ...), custom_call_target="tpu_custom_call" | custom-call | flops 9663676416 | bytes 8388608 | tf_op jit(solution)/shard_map/attend/pallas_call | solution.py:213
  109.2 7.8 collective-permute-done.3.x_ref
  125.1 9.6 %collective-permute-done.9 = bf16[384,1024]{1,0:T(8,128)(2,1)} collective-permute-done((bf16[384,1024]{1,0:T(8,128)(2,1)}, bf16[384,1024]{1,0:T(8,128)(2,1)}, u32[]{:S(2)}, u32[]{:S(2)}) %collective-permute-start.9) | collective-permute-done | bytes 786464 | tf_op jit(solution)/shard_map/ppermute | solution.py:576
  136.8 24.5 %collective-permute-done.5 = bf16[384,1024]{1,0:T(8,128)(2,1)} collective-permute-done((bf16[384,1024]{1,0:T(8,128)(2,1)}, bf16[384,1024]{1,0:T(8,128)(2,1)}, u32[]{:S(2)}, u32[]{:S(2)}) %collective-permute-start.5) | collective-permute-done | bytes 786464 | tf_op jit(solution)/shard_map/ppermute | solution.py:577
  168.4 16.6 %experts.4 = (bf16[400,1024]{1,0:T(8,128)(2,1)S(1)}, f32[384,128]{1,0:T(8,128)S(1)}, bf16[4,384,1024]{2,1,0:T(8,128)(2,1)}, bf16[4,384,1024]{2,1,0:T(8,128)(2,1)...) custom-call(s32[7]{0:T(128)S(1)} %copy-done.44, ...), custom_call_target="tpu_custom_call" | custom-call | flops 9663676416 | bytes 12582912 | tf_op jit(solution)/shard_map/experts/pallas_call | solution.py:452
  186.6 17.0 %experts.5 = (bf16[400,1024]{1,0:T(8,128)(2,1)}, f32[384,128]{1,0:T(8,128)}, bf16[4,384,1024]{2,1,0:T(8,128)(2,1)}, bf16[4,384,1024]{2,1,0:T(8,128)(2,1)}, bf16[...) custom-call(s32[7]{0:T(128)S(1)} %stack.116.info_ref, ...), custom_call_target="tpu_custom_call", output_to_operand_aliasing={{2}: (9, {}), {3}: (10, {}), {4}: (11, {}), {5}: (12, {}), ... | custom-call | flops 9663676416 | bytes 12582912 | tf_op jit(solution)/shard_map/experts/pallas_call | solution.py:452
  203.6 16.7 %experts.6 = (bf16[400,1024]{1,0:T(8,128)(2,1)S(1)}, f32[384,128]{1,0:T(8,128)}, bf16[4,384,1024]{2,1,0:T(8,128)(2,1)}, bf16[4,384,1024]{2,1,0:T(8,128)(2,1)}, b...) custom-call(s32[7]{0:T(128)S(1)} %stack.114.info_ref, ...), custom_call_target="tpu_custom_call", output_to_operand_aliasing={{2}: (9, {}), {3}: (10, {}), {4}: (11, {}), {5}: (12, {}), ... | custom-call | flops 9663676416 | bytes 12582912 | tf_op jit(solution)/shard_map/experts/pallas_call | solution.py:452
  221.1 17.1 %experts.7 = (bf16[400,1024]{1,0:T(8,128)(2,1)S(1)}, f32[384,128]{1,0:T(8,128)}, bf16[4,384,1024]{2,1,0:T(8,128)(2,1)}, bf16[4,384,1024]{2,1,0:T(8,128)(2,1)}, b...) custom-call(s32[7]{0:T(128)S(1)} %stack.112.info_ref, ...), custom_call_target="tpu_custom_call", output_to_operand_aliasing={{2}: (9, {}), {3}: (10, {}), {4}: (11, {}), {5}: (12, {}), ... | custom-call | flops 9663676416 | bytes 12582912 | tf_op jit(solution)/shard_map/experts/pallas_call | solution.py:452
  239.2 11.2 %bitcast_convert_fusion.1 = bf16[1024,2048]{1,0:T(8,128)(2,1)} fusion(bf16[4,384,1024]{2,1,0:T(8,128)(2,1)} %get-tuple-element.82, bf16[4,384,2048]{2,1,0:T(8,128)(2,1)} %get-tuple-element.84), kind=kOutput, calls=%fused_computation.1 | convolution fusion | flops 6444548096 | bytes 13631488 | tf_op jit(solution)/shard_map/dot_general | solution.py:23
  250.4 7.8 reshape.124
  258.2 5.0 copy.72
  263.3 11.4 %bitcast_convert_fusion.2 = bf16[1024,2048]{1,0:T(8,128)(2,1)} fusion(bf16[4,384,1024]{2,1,0:T(8,128)(2,1)} %get-tuple-element.82, bf16[4,384,2048]{2,1,0:T(8,128)(2,1)} %get-tuple-element.83), kind=kOutput, calls=%fused_computation.2 | convolution fusion | flops 6444548096 | bytes 13631488 | tf_op jit(solution)/shard_map/dot_general | solution.py:23
  274.6 7.8 reshape.122
  282.4 5.0 copy.70
  291.1 11.6 %bitcast_convert_fusion = bf16[2048,1024]{1,0:T(8,128)(2,1)} fusion(bf16[4,384,2048]{2,1,0:T(8,128)(2,1)} %get-tuple-element.85, bf16[4,400,1024]{2,1,0:T(8,128)(2,1)} %bitcast.130), kind=kOutput, calls=%fused_computation | convolution fusion | flops 6444548096 | bytes 13631488 | tf_op jit(solution)/shard_map/dot_general | solution.py:23
  305.2 20.3 %collective-permute-done.13 = bf16[400,1024]{1,0:T(8,128)(2,1)} collective-permute-done((bf16[400,1024]{1,0:T(8,128)(2,1)S(1)}, bf16[400,1024]{1,0:T(8,128)(2,1)}, u32[]{:S(2)}, u32[]{:S(2)}) %collective-permute-start.13) | collective-permute-done | bytes 819232 | tf_op jit(solution)/shard_map/ppermute | solution.py:596
  328.8 8.1 collective-permute-start.10
  336.9 16.9 %collective-permute-done.11 = bf16[400,1024]{1,0:T(8,128)(2,1)S(1)} collective-permute-done((bf16[400,1024]{1,0:T(8,128)(2,1)S(1)}, bf16[400,1024]{1,0:T(8,128)(2,1)S(1)}, u32[]{:S(2)}, u32[]{:S(2)}) %collective-permute-start.11) | collective-permute-done | bytes 819232 | tf_op jit(solution)/shard_map/ppermute | solution.py:597
  365.2 6.2 collective-permute-done.10
  371.5 12.2 %collective-permute-done.15 = bf16[400,1024]{1,0:T(8,128)(2,1)} collective-permute-done((bf16[400,1024]{1,0:T(8,128)(2,1)}, bf16[400,1024]{1,0:T(8,128)(2,1)}, u32[]{:S(2)}, u32[]{:S(2)}) %collective-permute-start.15) | collective-permute-done | bytes 819232 | tf_op jit(solution)/shard_map/ppermute | solution.py:601
  402.6 11.9 %attend_back.1 = (f32[384,1024]{1,0:T(8,128)S(1)}, f32[2,384,512]{2,1,0:T(8,128)S(1)}, bf16[2,384,512]{2,1,0:T(8,128)(2,1)}, bf16[2,384,512]{2,1,0:T(8,128)(2,1)S(1)}, bf16[2,384,512]{2,1,0:T(8,128)(2,1)S(1)}) custom-call(s32[13]{0:T(128)S(1)} %copy-done.43, bf16[384,1024]{1,0:T(8,128)(2,1)S(1)} %copy-done.47, ...), custom_call_target="tpu_custom_call" | custom-call | flops 24159191040 | bytes 16777216 | tf_op jit(solution)/shard_map/attend_back/pallas_call | solution.py:308
  414.5 9.6 %collective-permute-start.17 = (bf16[2,384,512]{2,1,0:T(8,128)(2,1)S(1)}, bf16[2,384,512]{2,1,0:T(8,128)(2,1)S(1)}, u32[]{:S(2)}, u32[]{:S(2)}) collective-permute-start(bf16[2,384,512]{2,1,0:T(8,128)(2,1)S(1)} %get-tuple-element.80), channel_id=1, source_target_pairs={{0,1},{1,0},{2,3},{3,2},{4,5},{5,4},{6,7},{7,6},{8,9},{9,8},{10,11... | collective-permute-start | bytes 2359304 | tf_op jit(solution)/shard_map/ppermute | solution.py:658
  430.4 35.0 %reduce-scatter.7.cloned.1.call-done = bf16[2,1024,512]{2,1,0:T(8,128)(2,1)} async-done(((bf16[4,1024,512]{2,1,0:T(8,128)(2,1)}), bf16[2,1024,512]{2,1,0:T(8,128)(2,1)}) %reduce-scatter.7.cloned.1.call-update) | async-done | bytes 2097168 | tf_op jit(solution)/shard_map/reduce_scatter | solution.py:616
  465.3 57.1 %reduce-scatter.11.cloned.1.call-done = bf16[2,512,1024]{2,1,0:T(8,128)(2,1)} async-done(((bf16[4,512,1024]{2,1,0:T(8,128)(2,1)}), bf16[2,512,1024]{2,1,0:T(8,128)(2,1)}) %reduce-scatter.11.cloned.1.call-update) | async-done | bytes 2097168 | tf_op jit(solution)/shard_map/reduce_scatter | solution.py:616
  548.1 40.8 %all-reduce.4 = (f32[1024]{0:T(1024)}, f32[1024]{0:T(1024)}) all-reduce(f32[1024]{0:T(1024)S(1)} %get-tuple-element.88, f32[1024]{0:T(1024)S(1)} %get-tuple-element.86), channel_id=1, replica_groups=mesh['ep'=8,'ctx'=4] {'ep','ctx'}, use_global_device_ids=true, to_apply=%region_9.10 | all-reduce | flops 2048 | bytes 16384 | tf_op jit(solution)/shard_map/psum | solution.py:683
  591.7 54.2 %all-reduce.12.cloned.1.call-done = (bf16[2,1024,512]{2,1,0:T(8,128)(2,1)}, bf16[2,1024,512]{2,1,0:T(8,128)(2,1)}, bf16[2,512,1024]{2,1,0:T(8,128)(2,1)}) async-done(((bf16[2,1024,512]{2,1,0:T(8,128)(2,1)}, bf16[2,1024,512]{2,1,0:T(8,128)(2,1)}, bf16[2,512,1024]{2,1,0:T(8,128)(2,1)}), (bf16[2,1024,512]{2,1,0:T(8,128)(2,1)}, bf16[2,1024,512]{2,1,0:T(8,128)(2,1)}, ...) | async-done | bytes 6291472 | tf_op jit(solution)/shard_map/psum | solution.py:615
  645.9 4.3 convert_element_type.164
  655.3 236.3 %all-reduce.10.cloned.1.call-done = (f32[1024,1024]{1,0:T(8,128)}, f32[1024,512]{1,0:T(8,128)}, f32[1024,512]{1,0:T(8,128)}, f32[1024,1024]{1,0:T(8,128)}, f32[1024,16]{0,1:T(8,128)}) async-done(((f32[1024,1024]{1,0:T(8,128)}, f32[1024,512]{1,0:T(8,128)}, f32[1024,512]{1,0:T(8,128)}, f32[1024,1024]{1,0:T(8,128)}, f32[1024,16]{0,1:T(8,128)}), (f32[1024,1024]{1,0:T(8,128)}, f32[1024,512]{1,0:T(8,128)}, ...) | async-done | bytes 12648464 | tf_op jit(solution)/shard_map/psum | solution.py:683
  891.7 4.9 copy.109
  (275 shorter events, 143.2 us)
Async XLA Ops:
  7.2 156.2 %all-gather.2.cloned.1.call-start = ((), (), s32[]{:S(2)}) async-start(), calls=%async_computation.4 | async-start | bytes 4096000 | tf_op jit(solution)/shard_map/all_gather | solution.py:551
  11.8 71.4 %collective-permute-start.6 = (bf16[3072,512]{1,0:T(8,128)(2,1)}, bf16[3072,512]{1,0:T(8,128)(2,1)}, u32[]{:S(2)}, u32[]{:S(2)}) collective-permute-start(bf16[3072,512]{1,0:T(8,128)(2,1)} %pad_maximum_fusion), channel_id=1, source_target_pairs={{0,4},{4,0},{8,12},{12,8},{16,20},{20,16},{24,28},{28,24},{1,5},{5... | collective-permute-start | bytes 9437192 | tf_op jit(solution)/shard_map/ppermute | solution.py:542
  27.9 20.2 %collective-permute-start.1 = (bf16[2,384,512]{2,1,0:T(8,128)(2,1)}, bf16[2,384,512]{2,1,0:T(8,128)(2,1)}, u32[]{:S(2)}, u32[]{:S(2)}) collective-permute-start(bf16[2,384,512]{2,1,0:T(8,128)(2,1)} %get-tuple-element.50.refs_0_), channel_id=1, source_target_pairs={{0,2},{1,3},{4,6},{5,7},{8,10},{9,11},{12,14},{13,15},{16,18},{17,... | collective-permute-start | bytes 2359304 | tf_op jit(solution)/shard_map/ppermute | solution.py:562
  35.1 48.0 %copy-start.39 = (f32[1024]{0:T(1024)S(1)}, f32[1024]{0:T(1024)}, u32[]{:S(2)}) copy-start(f32[1024]{0:T(1024)} %param.28) | copy-start | bytes 12292
  36.1 355.1 %reduce-scatter.5.cloned.1.call-start = ((), (), s32[]{:S(2)}) async-start(), calls=%async_computation.5 | async-start | bytes 3932160 | tf_op jit(solution)/shard_map/reduce_scatter | solution.py:623
  36.2 46.9 %collective-permute-start = (bf16[2,384,512]{2,1,0:T(8,128)(2,1)}, bf16[2,384,512]{2,1,0:T(8,128)(2,1)}, u32[]{:S(2)}, u32[]{:S(2)}) collective-permute-start(bf16[2,384,512]{2,1,0:T(8,128)(2,1)} %get-tuple-element.50.refs_0_), channel_id=1, source_target_pairs={{0,1},{2,3},{4,5},{6,7},{8,9},{10,11},{12,13},{14,15},{16,17},{18,... | collective-permute-start | bytes 2359304 | tf_op jit(solution)/shard_map/ppermute | solution.py:558
  48.1 35.0 %collective-permute-start.2 = (bf16[2,384,512]{2,1,0:T(8,128)(2,1)}, bf16[2,384,512]{2,1,0:T(8,128)(2,1)}, u32[]{:S(2)}, u32[]{:S(2)}) collective-permute-start(bf16[2,384,512]{2,1,0:T(8,128)(2,1)} %collective-permute-done.1.refs_2_), channel_id=1, source_target_pairs={{0,1},{1,0},{2,3},{3,2},{4,5},{5,4},{6,7},{7,6},{8,9},{9,8},{10,11... | collective-permute-start | bytes 2359304 | tf_op jit(solution)/shard_map/ppermute | solution.py:563
  48.2 53.8 %copy-start.42 = (s32[13]{0:T(128)}, s32[13]{0:T(128)S(1)}, u32[]{:S(2)}) copy-start(s32[13]{0:T(128)S(1)} %stack.105.info_ref) | copy-start | bytes 160
  83.1 80.3 %collective-permute-start.7 = (bf16[3072,512]{1,0:T(8,128)(2,1)}, bf16[3072,512]{1,0:T(8,128)(2,1)}, u32[]{:S(2)}, u32[]{:S(2)}) collective-permute-start(bf16[3072,512]{1,0:T(8,128)(2,1)} %collective-permute-done.6.refs_3_), channel_id=1, source_target_pairs={{0,1},{1,0},{2,3},{3,2},{4,5},{5,4},{6,7},{7,6},{8,9},{9,8},{10,11... | collective-permute-start | bytes 9437192 | tf_op jit(solution)/shard_map/ppermute | solution.py:543
  87.0 35.3 %copy-start.67 = (bf16[1024,16]{0,1:T(8,128)(2,1)S(1)}, bf16[1024,16]{0,1:T(8,128)(2,1)}, u32[]{:S(2)}) copy-start(bf16[1024,16]{0,1:T(8,128)(2,1)} %param.29) | copy-start | bytes 98308
  105.0 12.0 %collective-permute-start.3 = (bf16[384,1024]{1,0:T(8,128)(2,1)S(1)}, bf16[384,1024]{1,0:T(8,128)(2,1)S(1)}, u32[]{:S(2)}, u32[]{:S(2)}) collective-permute-start(bf16[384,1024]{1,0:T(8,128)(2,1)S(1)} %get-tuple-element.52.x_ref), channel_id=1, source_target_pairs={{0,8},{4,12},{8,0},{12,4},{16,24},{20,28},{24,16},{28,20},{1,9},{5... | collective-permute-start | bytes 2359304 | tf_op jit(solution)/shard_map/ppermute | solution.py:573
  106.8 12.6 %collective-permute-start.8 = (bf16[384,1024]{1,0:T(8,128)(2,1)S(1)}, bf16[384,1024]{1,0:T(8,128)(2,1)}, u32[]{:S(2)}, u32[]{:S(2)}) collective-permute-start(bf16[384,1024]{1,0:T(8,128)(2,1)S(1)} %get-tuple-element.52.x_ref), channel_id=1, source_target_pairs={{8,16},{12,20},{16,8},{20,12},{9,17},{13,21},{17,9},{21,13},{10,18... | collective-permute-start | bytes 2359304 | tf_op jit(solution)/shard_map/ppermute | solution.py:574
  116.9 3.7 collective-permute-start.4
  119.4 15.3 %collective-permute-start.9 = (bf16[384,1024]{1,0:T(8,128)(2,1)}, bf16[384,1024]{1,0:T(8,128)(2,1)}, u32[]{:S(2)}, u32[]{:S(2)}) collective-permute-start(bf16[384,1024]{1,0:T(8,128)(2,1)} %collective-permute-done.8), channel_id=1, source_target_pairs={{8,0},{12,4},{16,24},{20,28},{9,1},{13,5},{17,25},{21,29},{10,2},{... | collective-permute-start | bytes 2359304 | tf_op jit(solution)/shard_map/ppermute | solution.py:576
  120.7 40.6 %collective-permute-start.5 = (bf16[384,1024]{1,0:T(8,128)(2,1)}, bf16[384,1024]{1,0:T(8,128)(2,1)}, u32[]{:S(2)}, u32[]{:S(2)}) collective-permute-start(bf16[384,1024]{1,0:T(8,128)(2,1)} %collective-permute-done.4), channel_id=1, source_target_pairs={{8,0},{12,4},{16,24},{20,28},{9,1},{13,5},{17,25},{21,29},{10,2},{... | collective-permute-start | bytes 2359304 | tf_op jit(solution)/shard_map/ppermute | solution.py:577
  168.4 18.2 %copy-start.35 = (bf16[384,1024]{1,0:T(8,128)(2,1)S(1)}, bf16[384,1024]{1,0:T(8,128)(2,1)}, u32[]{:S(2)}) copy-start(bf16[384,1024]{1,0:T(8,128)(2,1)} %copy-done.34) | copy-start | bytes 2359300
  203.5 17.6 %copy-start.12 = (bf16[384,1024]{1,0:T(8,128)(2,1)S(1)}, bf16[384,1024]{1,0:T(8,128)(2,1)}, u32[]{:S(2)}) copy-start(bf16[384,1024]{1,0:T(8,128)(2,1)} %broadcast_select_fusion.1.x_ref) | copy-start | bytes 2359300
  239.2 191.2 %reduce-scatter.9.cloned.1.call-start = ((), (), s32[]{:S(2)}) async-start(), calls=%async_computation.7 | async-start | bytes 6291456 | tf_op jit(solution)/shard_map/reduce_scatter | solution.py:616
  263.2 202.1 %reduce-scatter.7.cloned.1.call-start = ((), (), s32[]{:S(2)}) async-start(), calls=%async_computation.6 | async-start | bytes 6291456 | tf_op jit(solution)/shard_map/reduce_scatter | solution.py:616
  287.5 234.9 %reduce-scatter.11.cloned.1.call-start = ((), (), s32[]{:S(2)}) async-start(), calls=%async_computation.8 | async-start | bytes 6291456 | tf_op jit(solution)/shard_map/reduce_scatter | solution.py:616
  288.6 36.8 %collective-permute-start.13 = (bf16[400,1024]{1,0:T(8,128)(2,1)S(1)}, bf16[400,1024]{1,0:T(8,128)(2,1)}, u32[]{:S(2)}, u32[]{:S(2)}) collective-permute-start(bf16[400,1024]{1,0:T(8,128)(2,1)S(1)} %copy-done.28), channel_id=1, source_target_pairs={{0,8},{4,12},{24,16},{28,20},{1,9},{5,13},{25,17},{29,21},{2,10},{... | collective-permute-start | bytes 2457608 | tf_op jit(solution)/shard_map/ppermute | solution.py:596
  302.7 343.1 %all-reduce.12.cloned.1.call-start = ((), (), s32[]{:S(2)}) async-start(), calls=%async_computation.10 | async-start | bytes 12582912 | tf_op jit(solution)/shard_map/psum | solution.py:615
  303.8 50.0 %collective-permute-start.11 = (bf16[400,1024]{1,0:T(8,128)(2,1)S(1)}, bf16[400,1024]{1,0:T(8,128)(2,1)S(1)}, u32[]{:S(2)}, u32[]{:S(2)}) collective-permute-start(bf16[400,1024]{1,0:T(8,128)(2,1)S(1)} %copy-done.26), channel_id=1, source_target_pairs={{0,8},{4,12},{24,16},{28,20},{1,9},{5,13},{25,17},{29,21},{2,10},{... | collective-permute-start | bytes 2457608 | tf_op jit(solution)/shard_map/ppermute | solution.py:597
  326.9 29.8 %collective-permute-start.14 = (bf16[400,1024]{1,0:T(8,128)(2,1)S(1)}, bf16[400,1024]{1,0:T(8,128)(2,1)S(1)}, u32[]{:S(2)}, u32[]{:S(2)}) collective-permute-start(bf16[400,1024]{1,0:T(8,128)(2,1)S(1)} %add_convert_fusion.1), channel_id=1, source_target_pairs={{8,16},{12,20},{16,8},{20,12},{9,17},{13,21},{17,9},{21,13},{10,18... | collective-permute-start | bytes 2457608 | tf_op jit(solution)/shard_map/ppermute | solution.py:598
  328.8 42.7 %collective-permute-start.10 = (bf16[400,1024]{1,0:T(8,128)(2,1)}, bf16[400,1024]{1,0:T(8,128)(2,1)}, u32[]{:S(2)}, u32[]{:S(2)}) collective-permute-start(bf16[400,1024]{1,0:T(8,128)(2,1)} %get-tuple-element.70), channel_id=1, source_target_pairs={{0,8},{4,12},{24,16},{28,20},{1,9},{5,13},{25,17},{29,21},{2,10},{... | collective-permute-start | bytes 2457608 | tf_op jit(solution)/shard_map/ppermute | solution.py:599
  355.0 16.5 %collective-permute-start.12 = (bf16[400,1024]{1,0:T(8,128)(2,1)}, bf16[400,1024]{1,0:T(8,128)(2,1)}, u32[]{:S(2)}, u32[]{:S(2)}) collective-permute-start(bf16[400,1024]{1,0:T(8,128)(2,1)} %add_convert_fusion.2), channel_id=1, source_target_pairs={{8,16},{12,20},{16,8},{20,12},{9,17},{13,21},{17,9},{21,13},{10,18... | collective-permute-start | bytes 2457608 | tf_op jit(solution)/shard_map/ppermute | solution.py:600
  359.1 24.6 %collective-permute-start.15 = (bf16[400,1024]{1,0:T(8,128)(2,1)}, bf16[400,1024]{1,0:T(8,128)(2,1)}, u32[]{:S(2)}, u32[]{:S(2)}) collective-permute-start(bf16[400,1024]{1,0:T(8,128)(2,1)} %add_convert_fusion), channel_id=1, source_target_pairs={{16,24},{20,28},{8,0},{12,4},{17,25},{21,29},{9,1},{13,5},{18,26},... | collective-permute-start | bytes 2457608 | tf_op jit(solution)/shard_map/ppermute | solution.py:601
  365.2 20.9 %copy-start.64 = (f32[384,128]{0,1:T(8,128)}, f32[384,128]{0,1:T(8,128)S(1)}, u32[]{:S(2)}) copy-start(f32[384,128]{0,1:T(8,128)S(1)} %copy.66) | copy-start | bytes 589828
  414.5 13.4 %collective-permute-start.17 = (bf16[2,384,512]{2,1,0:T(8,128)(2,1)S(1)}, bf16[2,384,512]{2,1,0:T(8,128)(2,1)S(1)}, u32[]{:S(2)}, u32[]{:S(2)}) collective-permute-start(bf16[2,384,512]{2,1,0:T(8,128)(2,1)S(1)} %get-tuple-element.80), channel_id=1, source_target_pairs={{0,1},{1,0},{2,3},{3,2},{4,5},{5,4},{6,7},{7,6},{8,9},{9,8},{10,11... | collective-permute-start | bytes 2359304 | tf_op jit(solution)/shard_map/ppermute | solution.py:658
  424.1 108.7 %collective-permute-start.16 = (bf16[2,384,512]{2,1,0:T(8,128)(2,1)}, bf16[2,384,512]{2,1,0:T(8,128)(2,1)}, u32[]{:S(2)}, u32[]{:S(2)}) collective-permute-start(bf16[2,384,512]{2,1,0:T(8,128)(2,1)} %get-tuple-element.78), channel_id=1, source_target_pairs={{1,0},{3,2},{5,4},{7,6},{9,8},{11,10},{13,12},{15,14},{17,16},{19,... | collective-permute-start | bytes 2359304 | tf_op jit(solution)/shard_map/ppermute | solution.py:655
  429.0 103.8 %collective-permute-start.18 = (bf16[2,384,512]{2,1,0:T(8,128)(2,1)}, bf16[2,384,512]{2,1,0:T(8,128)(2,1)}, u32[]{:S(2)}, u32[]{:S(2)}) collective-permute-start(bf16[2,384,512]{2,1,0:T(8,128)(2,1)} %add_convert_fusion.3), channel_id=1, source_target_pairs={{2,0},{3,1},{6,4},{7,5},{10,8},{11,9},{14,12},{15,13},{18,16},{19,... | collective-permute-start | bytes 2359304 | tf_op jit(solution)/shard_map/ppermute | solution.py:659
  522.4 369.2 %all-reduce.10.cloned.1.call-start = ((), (), s32[]{:S(2)}) async-start(), calls=%async_computation.9 | async-start | bytes 25296896 | tf_op jit(solution)/shard_map/psum | solution.py:683
  (72 other events, 197.9 us)
Sparse Core Ops, SparseCore 0:
  36.2 65.0 all-gather.1
  239.3 110.3 reduce-scatter.4
  352.5 55.5 reduce-scatter.8
  411.0 54.3 reduce-scatter.6
  468.0 54.3 reduce-scatter.10
  525.0 120.8 all-reduce.11
  654.6 237.0 all-reduce.9

commit v2 on v1

v2 whole, which is shorter than its diff:
```python
import functools

import jax
import jax.numpy as jnp
import numpy as np
from jax import lax
from jax.experimental import pallas as pl
from jax.experimental.pallas import tpu as pltpu
from jax.sharding import PartitionSpec as P

HEAD_DIM = 64
EPS = 1e-06
THETA = 10000.0
NEG = -1e30
LOG2E = 1.4426950408889634
NZ = 4
VMEM = 58 * 1024 * 1024
CORES = 2
F32 = jnp.float32
BF16 = jnp.bfloat16


def dot(a, b, ca, cb):
    return lax.dot_general(a, b, (((ca,), (cb,)), ((), ())), preferred_element_type=F32)


def params(semantics):
    return pltpu.CompilerParams(dimension_semantics=semantics, vmem_limit_bytes=VMEM)


COST = pl.CostEstimate(flops=1 << 20, bytes_accessed=1 << 20, transcendentals=0)


def cost(flops, nbytes):
    return pl.CostEstimate(flops=flops, bytes_accessed=nbytes, transcendentals=0)


def rope_constants(ctx_size, rows):
    half = HEAD_DIM // 2
    inv = THETA ** (-np.arange(half, dtype=np.float64) / half)
    fine = np.arange(rows, dtype=np.float64)[:, None] * inv[None, :]
    coarse = (rows * np.arange(ctx_size, dtype=np.float64))[:, None] * inv[None, :]
    tile = lambda t: jnp.asarray(np.tile(t, (1, 128 // half)).astype(np.float32))
    pad = np.zeros(((-2 * ctx_size) % 8, half))
    return (
        tile(np.concatenate([np.cos(fine), np.sin(fine)], 0)),
        tile(np.concatenate([np.cos(coarse), np.sin(coarse), pad], 0)),
    )


def swap_halves(x, roll):
    half = HEAD_DIM // 2
    width = x.shape[1]
    lane = lax.broadcasted_iota(jnp.int32, x.shape, 1)
    return jnp.where(lane % HEAD_DIM < half, roll(x, width - half), roll(x, half))


def prepare_body(experts, info_ref, r_ref, c_ref, wg, wu, wd, ext_ref, sent_ref, buf, sem):
    rows, width = c_ref.shape
    ff = width // 2
    core, count = info_ref[0], info_ref[1]
    pieces = [wg.at[core], wu.at[core]] + [wd.at[core, :, pl.ds(k * ff, ff)] for k in range(2)]
    spans = [pl.ds(0, width), pl.ds(width, width), pl.ds(2 * width, ff), pl.ds(2 * width + ff, ff)]
    into = [
        pltpu.make_async_copy(piece, buf.at[span], sem.at[0, k])
        for k, (piece, span) in enumerate(zip(pieces, spans))
    ]
    back = [
        pltpu.make_async_copy(buf.at[span], sent_ref.at[span], sem.at[1, k])
        for k, span in enumerate(spans)
    ]
    for copy in into:
        copy.start()
    row = lax.broadcasted_iota(jnp.int32, (rows, width), 0)
    ext_ref[:rows] = jnp.where(row < count, c_ref[...], jnp.zeros((), BF16))
    lane = lax.broadcasted_iota(jnp.int32, (rows, 128), 1)
    named = jnp.zeros((rows, 128), F32)
    for k in range(r_ref.shape[1]):
        named = jnp.where(lane == r_ref[:, k : k + 1], 1.0, named)
    named = jnp.transpose(named)[:experts]
    ext_ref[rows:] = jnp.concatenate(
        [named, jnp.zeros((experts, width - rows), F32)], 1
    ).astype(BF16)
    for k in range(4):
        into[k].wait()
        back[k].start()
    for copy in back:
        copy.wait()


def prepare(info, routes, cot, weights, experts):
    rows, width = cot.shape
    ff = width // 2
    anywhere = pl.BlockSpec(memory_space=pl.ANY)
    full = lambda shape: pl.BlockSpec(shape, lambda i, s: (0, 0))
    return pl.pallas_call(
        functools.partial(prepare_body, experts),
        grid_spec=pltpu.PrefetchScalarGridSpec(
            num_scalar_prefetch=1,
            grid=(1,),
            in_specs=[full(routes.shape), full(cot.shape)] + [anywhere] * 3,
            out_specs=[full((rows + experts, width)), anywhere],
            scratch_shapes=[
                pltpu.VMEM((3 * width, ff), BF16),
                pltpu.SemaphoreType.DMA((2, 4)),
            ],
        ),
        out_shape=[
            jax.ShapeDtypeStruct((rows + experts, width), BF16),
            jax.ShapeDtypeStruct((3 * width, ff), BF16),
        ],
        compiler_params=params(("arbitrary",)),
        cost_estimate=COST,
        name="prepare",
    )(info, routes, cot, *weights)


def project_body(blocks, info_ref, x_ref, gain_ref, wq_ref, wk_ref, wv_ref, fine_ref, start_ref,
                 n_ref, q_ref, kv_ref, cos_ref, sin_ref):
    step = pl.program_id(0)
    nq = pl.num_programs(0) - 4
    rows = x_ref.shape[0]

    @pl.when(step == 0)
    def _():
        x = x_ref[...].astype(F32)
        scale = lax.rsqrt(jnp.mean(x * x, -1, keepdims=True) + EPS)
        n_ref[...] = (x * scale * gain_ref[...]).astype(BF16)
        cos_f, sin_f = fine_ref[:rows], fine_ref[rows:]
        cos_c = start_ref[pl.ds(info_ref[0], 1), :]
        sin_c = start_ref[pl.ds(info_ref[0] + blocks, 1), :]
        lane = lax.broadcasted_iota(jnp.int32, (rows, 128), 1)
        sign = jnp.where(lane % HEAD_DIM < HEAD_DIM // 2, -1.0, 1.0)
        cos_ref[...] = cos_f * cos_c - sin_f * sin_c
        sin_ref[...] = (sin_f * cos_c + cos_f * sin_c) * sign

    def rope(lin):
        cos = jnp.concatenate([cos_ref[...]] * 2, 1)
        sin = jnp.concatenate([sin_ref[...]] * 2, 1)
        return lin * cos + swap_halves(lin, lambda v, s: pltpu.roll(v, s, 1)) * sin

    @pl.when(step < nq)
    def _():
        lin = dot(n_ref[...], wq_ref[...], 1, 0)
        q_ref[...] = rope(lin).astype(BF16) * jnp.asarray(HEAD_DIM**-0.5, BF16)

    @pl.when((step >= nq) & (step < nq + 2))
    def _():
        kv_ref[...] = rope(dot(n_ref[...], wk_ref[...], 1, 0)).astype(BF16)[None]

    @pl.when(step >= nq + 2)
    def _():
        kv_ref[...] = dot(n_ref[...], wv_ref[...], 1, 0).astype(BF16)[None]


def project(info, x, gain, wq, wk, wv, fine, starts, blocks):
    rows, width = x.shape
    nq = wq.shape[1] // 256
    kvw = wk.shape[1]
    nk = kvw // 256
    clip = lambda v, hi: jnp.minimum(jnp.maximum(v, 0), hi)
    full = lambda shape: pl.BlockSpec(shape, lambda i, s: (0, 0))
    return pl.pallas_call(
        functools.partial(project_body, blocks),
        grid_spec=pltpu.PrefetchScalarGridSpec(
            num_scalar_prefetch=1,
            grid=(nq + 2 * nk,),
            in_specs=[
                full((rows, width)),
                full((1, width)),
                pl.BlockSpec((width, 256), lambda i, s: (0, clip(i, nq - 1))),
                pl.BlockSpec((width, 256), lambda i, s: (0, clip(i - nq, nk - 1))),
                pl.BlockSpec((width, 256), lambda i, s: (0, clip(i - nq - nk, nk - 1))),
                full(fine.shape),
                full(starts.shape),
            ],
            out_specs=[
                full((rows, width)),
                pl.BlockSpec((rows, 256), lambda i, s: (0, clip(i, nq - 1))),
                pl.BlockSpec(
                    (1, rows, 256),
                    lambda i, s: (
                        clip(i - nq, 2 * nk - 1) // nk,
                        0,
                        clip(i - nq, 2 * nk - 1) % nk,
                    ),
                ),
                full((rows, 128)),
                full((rows, 128)),
            ],
        ),
        out_shape=[
            jax.ShapeDtypeStruct((rows, width), BF16),
            jax.ShapeDtypeStruct((rows, wq.shape[1]), BF16),
            jax.ShapeDtypeStruct((2, rows, kvw), BF16),
            jax.ShapeDtypeStruct((rows, 128), F32),
            jax.ShapeDtypeStruct((rows, 128), F32),
        ],
        compiler_params=params(("arbitrary",)),
        cost_estimate=COST,
        name="project",
    )(info, x, gain, wq, wk, wv, fine, starts)


def split_heads(block):
    lane = lax.broadcasted_iota(jnp.int32, block.shape, 1)
    low = lane < HEAD_DIM
    zero = jnp.zeros_like(block)
    turned = jnp.concatenate([block[:, HEAD_DIM:], block[:, :HEAD_DIM]], 1)
    first = jnp.concatenate([jnp.where(low, block, zero), jnp.where(low, zero, turned)], 0)
    second = jnp.concatenate([jnp.where(low, turned, zero), jnp.where(low, zero, block)], 0)
    return first, second


def attend_blocks(info_ref, q_ref, kv_refs, acc, top, low, diagonal):
    rows = q_ref.shape[0]
    seq_len = info_ref[0]
    key = lax.broadcasted_iota(jnp.int32, (rows, rows), 0)
    query = lax.broadcasted_iota(jnp.int32, (rows, rows), 1)

    for role in range(len(kv_refs)):
        start, active = (info_ref[1 + 2 * role + i] for i in range(2))

        @pl.when(active > 0)
        def _(role=role, start=start):
            keys = split_heads(kv_refs[role][0])
            values = split_heads(kv_refs[role][1])
            bad = key + start >= seq_len
            if diagonal and role == 0:
                bad = bad | (key > query)
            bias = jnp.where(bad, NEG, 0.0)
            for pair in range(2):
                q = q_ref[:, pair * 128 : pair * 128 + 128]
                scores = dot(keys[pair], q, 1, 1)
                weights, shrinks = [], []
                for head in range(2):
                    at = 2 * pair + head
                    part = scores[head * rows : (head + 1) * rows] * LOG2E + bias
                    old = top[0, at : at + 1, :]
                    new = jnp.maximum(old, jnp.max(part, 0, keepdims=True))
                    prob = jnp.exp2(part - new)
                    shrink = jnp.exp2(old - new)
                    top[0, at : at + 1, :] = new
                    fresh = jnp.sum(prob, 0, keepdims=True)
                    low[0, at : at + 1, :] = low[0, at : at + 1, :] * shrink + fresh
                    weights.append(prob.astype(BF16))
                    shrinks.append(jnp.broadcast_to(shrink, (HEAD_DIM, rows)))
                fresh = dot(values[pair], jnp.concatenate(weights, 0), 0, 0)
                acc[0, pair] = acc[0, pair] * jnp.concatenate(shrinks, 0) + fresh


def attend_start_body(roles, info_ref, q_ref, *refs):
    acc, top, low = refs[roles:]
    acc[...] = jnp.zeros_like(acc)
    top[...] = jnp.full_like(top, NEG)
    low[...] = jnp.zeros_like(low)
    attend_blocks(info_ref, q_ref, refs[:roles], acc, top, low, True)


def attend_finish_body(roles, info_ref, q_ref, *refs):
    acc_in, top_in, low_in, wo_ref, x_ref, gain_ref = refs[roles : roles + 6]
    att_ref, lse_ref, hid_ref, mix_ref, acc, top, low, proj = refs[roles + 6 :]
    step = pl.program_id(0)
    rows = q_ref.shape[0]
    acc[...] = acc_in[...]
    top[...] = top_in[...]
    low[...] = low_in[...]
    attend_blocks(info_ref, q_ref, refs[:roles], acc, top, low, False)
    for pair in range(2):
        sums = [low[0, 2 * pair + head : 2 * pair + head + 1, :] for head in range(2)]
        total = [jnp.broadcast_to(1.0 / s, (HEAD_DIM, rows)) for s in sums]
        att = acc[0, pair] * jnp.concatenate(total, 0)
        att_ref[:, pair * 128 : pair * 128 + 128] = jnp.transpose(att).astype(BF16)
    lse_ref[...] = top[...] + jnp.log2(jnp.maximum(low[...], 1e-30))

    @pl.when(step == 0)
    def _():
        proj[...] = x_ref[...].astype(F32)

    proj[...] += dot(att_ref[...], wo_ref[...], 1, 0)

    @pl.when(step == pl.num_programs(0) - 1)
    def _():
        hidden = proj[...]
        scale = lax.rsqrt(jnp.mean(hidden * hidden, -1, keepdims=True) + EPS)
        hid_ref[...] = hidden
        mix_ref[...] = (hidden * scale * gain_ref[...]).astype(BF16)


def attend(info, q, blocks, state, wo=None, x=None, gain=None):
    rows, width = q.shape
    steps = width // 256
    roles = len(blocks)
    full = lambda shape: pl.BlockSpec(shape, lambda i, s: (0, 0))
    wide = pl.BlockSpec((rows, 256), lambda i, s: (0, i))
    heads = pl.BlockSpec((1, 8, rows), lambda i, s: (i, 0, 0))
    accs = pl.BlockSpec((1, 2, 128, rows), lambda i, s: (i, 0, 0, 0))
    in_specs = [wide] + [pl.BlockSpec((2, rows, 128), lambda i, s: (0, 0, i))] * roles
    state_specs = [accs, heads, heads]
    state_shapes = [jax.ShapeDtypeStruct((steps, 2, 128, rows), F32)]
    state_shapes += [jax.ShapeDtypeStruct((steps, 8, rows), F32)] * 2
    args = [info, q, *blocks]
    scratch = []
    if state is None:
        body, out_specs, out_shape = attend_start_body, state_specs, state_shapes
    else:
        body = attend_finish_body
        args += [*state, wo, x, gain]
        in_specs += state_specs
        in_specs += [
            pl.BlockSpec((256, x.shape[1]), lambda i, s: (i, 0)),
            full(x.shape),
            full((1, x.shape[1])),
        ]
        out_specs = [wide, heads, full(x.shape), full(x.shape)]
        out_shape = [
            jax.ShapeDtypeStruct((rows, width), BF16),
            jax.ShapeDtypeStruct((steps, 8, rows), F32),
            jax.ShapeDtypeStruct(x.shape, F32),
            jax.ShapeDtypeStruct(x.shape, BF16),
        ]
        scratch = [
            pltpu.VMEM((1, 2, 128, rows), F32),
            pltpu.VMEM((1, 8, rows), F32),
            pltpu.VMEM((1, 8, rows), F32),
            pltpu.VMEM(x.shape, F32),
        ]
    return pl.pallas_call(
        functools.partial(body, roles),
        grid_spec=pltpu.PrefetchScalarGridSpec(
            num_scalar_prefetch=1,
            grid=(steps,),
            in_specs=in_specs,
            out_specs=out_specs,
            scratch_shapes=scratch,
        ),
        out_shape=out_shape,
        compiler_params=params(("arbitrary",)),
        cost_estimate=COST,
        name="attend",
    )(*args)


def attend_back_body(roles, diagonal, info_ref, q_ref, do_ref, lse_ref, delta_ref, *refs):
    kv_refs, (start_ref, dq_ref), dkv_refs = refs[:roles], refs[-roles - 2 : -roles], refs[-roles:]
    rows = q_ref.shape[0]
    seq_len = info_ref[0]
    if len(refs) > 2 * roles + 1:
        dq_ref[...] = start_ref[...]
    else:
        dq_ref[...] = jnp.zeros_like(dq_ref)
    key = lax.broadcasted_iota(jnp.int32, (rows, rows), 0)
    query = lax.broadcasted_iota(jnp.int32, (rows, rows), 1)
    lane = lax.broadcasted_iota(jnp.int32, (rows, 128), 1)
    low = lane < HEAD_DIM

    for role in range(roles):
        start, active = (info_ref[1 + 2 * role + i] for i in range(2))

        @pl.when(active == 0)
        def _(role=role):
            dkv_refs[role][...] = jnp.zeros_like(dkv_refs[role])

        @pl.when(active > 0)
        def _(role=role, start=start):
            keys = split_heads(kv_refs[role][0])
            values = split_heads(kv_refs[role][1])
            bad = key + start >= seq_len
            if diagonal and role == 0:
                bad = bad | (key > query)
            bias = jnp.where(bad, NEG, 0.0)
            dks, dvs = [], []
            for pair in range(2):
                q = q_ref[:, pair * 128 : pair * 128 + 128]
                do = do_ref[:, pair * 128 : pair * 128 + 128]
                scores = dot(keys[pair], q, 1, 1)
                grads = dot(values[pair], do, 1, 1)
                probs, raws = [], []
                for head in range(2):
                    at = 2 * pair + head
                    part = scores[head * rows : (head + 1) * rows] * LOG2E + bias
                    prob = jnp.exp2(part - lse_ref[0, at : at + 1, :])
                    grad = grads[head * rows : (head + 1) * rows]
                    raws.append((prob * (grad - delta_ref[0, at : at + 1, :])).astype(BF16))
                    probs.append(prob.astype(BF16))
                raw = jnp.concatenate(raws, 0)
                dq_ref[:, pair * 128 : pair * 128 + 128] += dot(raw, keys[pair], 0, 0)
                dks.append(dot(raw, q, 1, 0))
                dvs.append(dot(jnp.concatenate(probs, 0), do, 1, 0))
            for which, parts in enumerate((dks, dvs)):
                top_a, bottom_a = parts[0][:rows], parts[0][rows:]
                top_b, bottom_b = parts[1][:rows], parts[1][rows:]
                turn = pltpu.roll(jnp.where(low, top_b, bottom_a), HEAD_DIM, 1)
                whole = jnp.where(low, top_a, bottom_b) + turn
                dkv_refs[role][which] = whole.astype(dkv_refs[role].dtype)


def attend_back(info, q, do, lse, delta, blocks, before, diagonal):
    rows, width = q.shape
    steps = width // 256
    roles = len(blocks)
    kvw = blocks[0].shape[2]
    wide = pl.BlockSpec((rows, 256), lambda i, s: (0, i))
    heads = pl.BlockSpec((1, 8, rows), lambda i, s: (i, 0, 0))
    kv = pl.BlockSpec((2, rows, 128), lambda i, s: (0, 0, i))
    more = [] if before is None else [before]
    return pl.pallas_call(
        functools.partial(attend_back_body, roles, diagonal),
        grid_spec=pltpu.PrefetchScalarGridSpec(
            num_scalar_prefetch=1,
            grid=(steps,),
            in_specs=[wide, wide, heads, heads] + [kv] * roles + [wide] * len(more),
            out_specs=[wide] + [kv] * roles,
        ),
        out_shape=[jax.ShapeDtypeStruct((rows, width), F32)]
        + [jax.ShapeDtypeStruct((2, rows, kvw), BF16)] * roles,
        compiler_params=params(("arbitrary",)),
        cost_estimate=cost(40 * rows * rows * roles * width, 16 * 1024 * 1024),
        name="attend_back",
    )(info, q, do, lse, delta, *blocks, *more)


def expert_body(own, remotes, rows, low, half, first, carry, experts, info_ref, *refs):
    xa_hbm, xb_hbm, cot_hbm, wr_ref = refs[:4]
    near = refs[4 : 4 + (3 if own else 0)]
    at = 4 + len(near)
    far = refs[at : at + remotes]
    at += remotes
    before = refs[at] if carry else None
    outs = refs[-17 if first else -15 :]
    out_before = refs[at + 1] if carry else None
    gm_ref, gate_ref, out_ref, inner_ref, dg_ref, du_ref = outs[:6]
    copies = outs[6:8] if first else ()
    wbuf, sem, gm_acc, out_acc, gates, back, x_ref, cot_ref, row_sem = outs[-9:]
    step = pl.program_id(0)
    total = own + remotes
    width = x_ref.shape[1]
    shard_rows = 2 * half
    ff = width // 2
    slot = lax.rem(step, 2)
    offsets = (0, width, 2 * width, 2 * width + ff)
    sizes = (width, width, ff, ff)

    def fetch(target, where):
        def start(sources):
            for piece, (ref, off, size) in enumerate(zip(sources, offsets, sizes)):
                pltpu.make_async_copy(
                    ref, wbuf.at[where, pl.ds(off, size)], sem.at[where, piece]
                ).start()

        if own:

            @pl.when(target < own)
            def _():
                down = [near[2].at[target, :, pl.ds(k * ff, ff)] for k in range(2)]
                start([near[0].at[target], near[1].at[target]] + down)

        for i in range(remotes):

            @pl.when(target == own + i)
            def _(i=i):
                start([far[i].at[pl.ds(off, size)] for off, size in zip(offsets, sizes)])

    @pl.when(step == 0)
    def _():
        ext = shard_rows + experts
        block = pl.ds(pl.multiple_of(info_ref[0] * ext, 16), ext)
        cot_copy = pltpu.make_async_copy(cot_hbm.at[block], cot_ref, row_sem.at[0])

        @pl.when(info_ref[3] > 0)
        def _():
            pltpu.make_async_copy(xa_hbm, x_ref, row_sem.at[1]).start()

        @pl.when(info_ref[3] == 0)
        def _():
            pltpu.make_async_copy(xb_hbm, x_ref, row_sem.at[1]).start()

        cot_copy.start()
        fetch(jnp.int32(0), 0)
        pltpu.make_async_copy(xa_hbm, x_ref, row_sem.at[1]).wait()
        cot_copy.wait()

    @pl.when(step + 1 < total)
    def _():
        fetch(step + 1, lax.rem(step + 1, 2))

    lane = lax.broadcasted_iota(jnp.int32, (rows, 128), 1)

    @pl.when(step == 0)
    def _():
        logits = dot(x_ref[...], wr_ref[...], 1, 0)
        mask_t = cot_ref[pl.ds(shard_rows, experts), :shard_rows].astype(F32)
        mask_t = jnp.concatenate([mask_t, jnp.zeros((128 - experts, shard_rows), F32)], 0)
        mask = jnp.transpose(mask_t)[low : low + rows] > 0.5
        high = jnp.max(jnp.where(mask, logits, NEG), 1, keepdims=True)
        raised = jnp.where(mask, jnp.exp(logits - high), 0.0)
        gates[...] = raised / jnp.sum(raised, 1, keepdims=True)
        gate_ref[...] = gates[...]
        back[...] = jnp.zeros_like(back)
        gm_acc[...] = jnp.zeros_like(gm_acc)
        if carry:
            out_acc[...] = out_before[0].astype(F32)
        else:
            out_acc[...] = jnp.zeros_like(out_acc)
        if first:
            copies[0][0] = x_ref[...]
            copies[1][0] = cot_ref[pl.ds(low, rows), :]

    for piece, (off, size) in enumerate(zip(offsets, sizes)):
        place = wbuf.at[slot, pl.ds(off, size)]
        pltpu.make_async_copy(place, place, sem.at[slot, piece]).wait()

    wg = wbuf[slot, :width, :]
    wu = wbuf[slot, width : 2 * width, :]
    wd0 = wbuf[slot, 2 * width : 2 * width + ff, :]
    wd1 = wbuf[slot, 2 * width + ff :, :]
    which = info_ref[2] + info_ref[4 + step]
    x = x_ref[...]
    cot = cot_ref[pl.ds(low, rows), :]
    g = dot(x, wg, 1, 0)
    u = dot(x, wu, 1, 0)
    raw = dot(cot[:, :ff], wd0, 1, 1) + dot(cot[:, ff:], wd1, 1, 1)
    gate = jnp.sum(jnp.where(lane == which, gates[...], 0.0), 1, keepdims=True)
    sig = 1.0 / (1.0 + jnp.exp(-g))
    silu = g * sig
    inner = silu * u
    gg = jnp.sum(raw * inner, 1, keepdims=True)
    back[...] += jnp.where(lane == which, gg, 0.0)
    scaled = (gate * inner).astype(BF16)
    gi = gate * raw
    dg = (gi * u * (sig * (1.0 + g * (1.0 - sig)))).astype(BF16)
    du = (gi * silu).astype(BF16)
    inner_ref[0] = scaled
    dg_ref[0] = dg
    du_ref[0] = du
    out_acc[:, :ff] += dot(scaled, wd0, 1, 0)
    out_acc[:, ff:] += dot(scaled, wd1, 1, 0)
    gm_acc[...] += dot(dg, wg, 1, 1) + dot(du, wu, 1, 1)

    @pl.when(step == total - 1)
    def _():
        back_t = jnp.transpose(back[...])[:experts, :]
        for k in range(rows // half):
            body = gm_acc[k * half : (k + 1) * half, :]
            tail = back_t[:, k * half : (k + 1) * half]
            tail = jnp.concatenate([tail, jnp.zeros((experts, width - half), F32)], 1)
            if carry:
                body = body + before[k, :half, :].astype(F32)
                tail = tail + before[k, half:, :].astype(F32)
            gm_ref[k, :half, :] = body.astype(BF16)
            gm_ref[k, half:, :] = tail.astype(BF16)
        out_ref[0] = out_acc[...].astype(BF16)


def expert_call(info, xs, cot, wr, own_weights, far, experts, low, half, kept, before=None):
    rows, width = xs[0].shape
    shard_rows = 2 * half
    own = own_weights[0].shape[0] if own_weights else 0
    remotes = len(far)
    total = own + remotes
    carry = before is not None
    first = not carry
    ff = width // 2
    at = low // rows
    full = lambda shape: pl.BlockSpec(shape, lambda i, s: (0,) * len(shape))
    anywhere = pl.BlockSpec(memory_space=pl.ANY)
    big = pl.BlockSpec((1, rows, width), lambda i, s: (s[1], at, 0))
    part = pl.BlockSpec((1, rows, ff), lambda i, s: (s[1], at, s[4 + i]))
    count = 6 if first else 4
    fresh = isinstance(kept[0], jax.ShapeDtypeStruct)
    aliased = [] if fresh else list(kept[:count])
    inputs = [*xs, cot, wr, *own_weights, *far] + ([before] if carry else [])
    specs = [anywhere] * 3 + [full(wr.shape)]
    specs += [anywhere] * (len(own_weights) + remotes)
    specs += [full(before.shape)] if carry else []
    specs += [big if carry and k == 0 else anywhere for k in range(len(aliased))]
    gm_shape = (rows // half, half + experts, width)
    outs = pl.pallas_call(
        functools.partial(expert_body, own, remotes, rows, low, half, first, carry, experts),
        grid_spec=pltpu.PrefetchScalarGridSpec(
            num_scalar_prefetch=1,
            grid=(total,),
            in_specs=specs,
            out_specs=[full(gm_shape), full((rows, 128)), big, part, part, part]
            + ([big, big] if first else []),
            scratch_shapes=[
                pltpu.VMEM((2, 3 * width, ff), BF16),
                pltpu.SemaphoreType.DMA((2, 4)),
                pltpu.VMEM((rows, width), F32),
                pltpu.VMEM((rows, width), F32),
                pltpu.VMEM((rows, 128), F32),
                pltpu.VMEM((rows, 128), F32),
                pltpu.VMEM((rows, width), BF16),
                pltpu.VMEM((shard_rows + experts, width), BF16),
                pltpu.SemaphoreType.DMA((2,)),
            ],
        ),
        out_shape=[
            jax.ShapeDtypeStruct(gm_shape, BF16),
            jax.ShapeDtypeStruct((rows, 128), F32),
        ]
        + [jax.ShapeDtypeStruct(k.shape, k.dtype) for k in kept[:count]],
        input_output_aliases={1 + len(inputs) + k: 2 + k for k in range(len(aliased))},
        compiler_params=params(("arbitrary",)),
        cost_estimate=cost(12 * rows * width * ff * total, total * 6 * width * ff),
        name="experts",
    )(info, *inputs, *aliased)
    return outs[0], outs[1], tuple(outs[2:]) + tuple(kept[count:])


def expert_grads_body(info_ref, x_hbm, c_hbm, in_hbm, dg_hbm, du_hbm, o_ref, x, c, cols, sem):
    place, kind = pl.program_id(0), pl.program_id(1)
    step = place * 3 + kind
    ff = cols.shape[2]
    hidden = (dg_hbm, du_hbm, in_hbm)

    def fetch(target, start):
        at = lax.rem(target, 2)
        off = pl.ds(pl.multiple_of(info_ref[lax.div(target, 3)] * ff, 128), ff)
        for k, ref in enumerate(hidden):

            @pl.when(lax.rem(target, 3) == k)
            def _(ref=ref):
                pltpu.make_async_copy(ref.at[:, off], cols.at[at], sem.at[at]).start()

    @pl.when(step == 0)
    def _():
        pltpu.make_async_copy(x_hbm, x, sem.at[2]).start()
        fetch(step, True)
        pltpu.make_async_copy(c_hbm, c, sem.at[3]).start()
        pltpu.make_async_copy(x_hbm, x, sem.at[2]).wait()

    @pl.when(step + 1 < 3 * pl.num_programs(0))
    def _():
        fetch(step + 1, True)

    slot = lax.rem(step, 2)
    pltpu.make_async_copy(cols.at[slot], cols.at[slot], sem.at[slot]).wait()

    @pl.when(kind < 2)
    def _():
        o_ref[0, 0] = dot(x[...], cols[slot], 0, 0).astype(BF16)

    @pl.when(step == 2)
    def _():
        pltpu.make_async_copy(c_hbm, c, sem.at[3]).wait()

    @pl.when(kind == 2)
    def _():
        o_ref[0, 0, :ff] = dot(cols[slot], c[:, :ff], 0, 0).astype(BF16)
        o_ref[0, 0, ff:] = dot(cols[slot], c[:, ff:], 0, 0).astype(BF16)


def expert_grads(places, x, c, inner, dg, du):
    rows, width = x.shape
    ff = width // 2
    count = places.shape[0]
    anywhere = pl.BlockSpec(memory_space=pl.ANY)
    return pl.pallas_call(
        expert_grads_body,
        grid_spec=pltpu.PrefetchScalarGridSpec(
            num_scalar_prefetch=1,
            grid=(count, 3),
            in_specs=[anywhere] * 5,
            out_specs=pl.BlockSpec((1, 1, width, ff), lambda i, k, s: (i, k, 0, 0)),
            scratch_shapes=[
                pltpu.VMEM((rows, width), BF16),
                pltpu.VMEM((rows, width), BF16),
                pltpu.VMEM((2, rows, ff), BF16),
                pltpu.SemaphoreType.DMA((4,)),
            ],
        ),
        out_shape=jax.ShapeDtypeStruct((count, 3, width, ff), BF16),
        compiler_params=params(("arbitrary",) * 2),
        cost_estimate=cost(6 * rows * width * ff * count, 16 * 1024 * 1024),
        name="expert_grads",
    )(places, x, c, inner, dg, du)


def middle_body(experts, half, *refs):
    sums, refs = refs[:5], refs[5:]
    gate_ref, wr_ref, hid_ref, cot_ref, att_ref, mix_ref, gain_ref, wo_hbm = refs[:8]
    gh_ref, gb_ref, do_ref, delta_ref, ffn_ref, router_ref, wo, sem, deltas = refs[8:]
    step = pl.program_id(0)
    width = hid_ref.shape[1]

    @pl.when(step == 0)
    def _():
        pltpu.make_async_copy(wo_hbm, wo, sem).start()
        ffn_ref[...] = jnp.zeros_like(ffn_ref)
        router_ref[...] = jnp.zeros_like(router_ref)

    total = sums[0][0].astype(F32)
    for ref in sums[1:3]:
        total = total + ref[0].astype(F32)
    total = total + jnp.where(step == 0, sums[3][0].astype(F32), sums[4][0].astype(F32))
    wide = (half + 127) // 128 * 128
    gg = jnp.concatenate([total[half:, :wide], jnp.zeros((128 - experts, wide), F32)], 0)
    gg = jnp.transpose(gg)[:half]
    gates = gate_ref[...]
    gl = (gates * (gg - jnp.sum(gates * gg, 1, keepdims=True))).astype(BF16)
    router_ref[...] += dot(gl, mix_ref[...], 0, 0)
    hidden = hid_ref[...]
    grad_mixed = total[:half] + dot(gl, wr_ref[...], 1, 1)
    scale = lax.rsqrt(jnp.mean(hidden * hidden, -1, keepdims=True) + EPS)
    ffn_ref[...] += jnp.sum(grad_mixed * hidden * scale, 0, keepdims=True)
    weighted = grad_mixed * gain_ref[...]
    mean = jnp.mean(weighted * hidden, -1, keepdims=True)
    grad = cot_ref[...].astype(F32) + scale * weighted - hidden * (scale * scale * scale * mean)
    gh_ref[...] = grad
    low = grad.astype(BF16)
    gb_ref[...] = low

    @pl.when(step == 0)
    def _():
        pltpu.make_async_copy(wo_hbm, wo, sem).wait()

    do = dot(low, wo[...], 1, 1).astype(BF16)
    do_ref[...] = do
    both = do.astype(F32) * att_ref[...].astype(F32)
    lane = lax.broadcasted_iota(jnp.int32, (half, 128), 1)
    found = jnp.zeros((half, 128), F32)
    for block in range(both.shape[1] // 128):
        pair = both[:, block * 128 : block * 128 + 128]
        front = jnp.sum(jnp.where(lane < HEAD_DIM, pair, 0.0), 1, keepdims=True)
        back = jnp.sum(jnp.where(lane < HEAD_DIM, 0.0, pair), 1, keepdims=True)
        found = jnp.where(lane == 2 * block, front, found)
        found = jnp.where(lane == 2 * block + 1, back, found)
    deltas[pl.ds(pl.multiple_of(step * half, half), half), :] = found

    @pl.when(step == pl.num_programs(0) - 1)
    def _():
        turned = jnp.transpose(deltas[...])
        for group in range(delta_ref.shape[0]):
            delta_ref[group, :4, :] = turned[4 * group : 4 * group + 4]
            delta_ref[group, 4:, :] = jnp.zeros((4, turned.shape[1]), F32)


def middle(sums, gates, wr, hidden, cot_ext, attended, mixed, gain, wo, experts):
    rows, width = hidden.shape
    half = rows // 2
    ext = half + experts
    heads = attended.shape[1] // HEAD_DIM
    stacked = pl.BlockSpec((1, ext, width), lambda i: (i, 0, 0))
    alone = pl.BlockSpec((1, ext, width), lambda i: (0, 0, 0))
    row = lambda w: pl.BlockSpec((half, w), lambda i: (i, 0))
    full = lambda shape: pl.BlockSpec(shape, lambda i: (0,) * len(shape))
    return pl.pallas_call(
        functools.partial(middle_body, experts, half),
        grid=(2,),
        in_specs=[stacked] * 3
        + [alone] * 2
        + [
            row(128),
            full(wr.shape),
            row(width),
            row(width),
            row(attended.shape[1]),
            row(width),
            full((1, width)),
            pl.BlockSpec(memory_space=pl.ANY),
        ],
        out_specs=[
            row(width),
            row(width),
            row(attended.shape[1]),
            full((heads // 4, 8, rows)),
            full((1, width)),
            full((128, width)),
        ],
        out_shape=[
            jax.ShapeDtypeStruct((rows, width), F32),
            jax.ShapeDtypeStruct((rows, width), BF16),
            jax.ShapeDtypeStruct(attended.shape, BF16),
            jax.ShapeDtypeStruct((heads // 4, 8, rows), F32),
            jax.ShapeDtypeStruct((1, width), F32),
            jax.ShapeDtypeStruct((128, width), F32),
        ],
        scratch_shapes=[
            pltpu.VMEM(wo.shape, BF16),
            pltpu.SemaphoreType.DMA(()),
            pltpu.VMEM((rows, 128), F32),
        ],
        compiler_params=params(("arbitrary",)),
        cost_estimate=COST,
        name="middle",
    )(*sums, gates, wr, hidden, cot_ext, attended, mixed, gain, wo)


def early_body(experts, info_ref, att_ref, gb_ref, router_ref, ffn_ref, give_ref, keep_ref):
    size = att_ref.shape[1] // 2
    core = info_ref[0]
    width = gb_ref.shape[1]
    row = lax.broadcasted_iota(jnp.int32, (16, width), 0)
    extra = jnp.concatenate([router_ref[:experts], jnp.where(row == 0, ffn_ref[...], 0.0)], 0)
    for ref, half in ((keep_ref, core), (give_ref, 1 - core)):
        part = att_ref[:, pl.ds(pl.multiple_of(half * size, 128), size)]
        ref[:size] = dot(part, gb_ref[...], 0, 0).astype(BF16)
        ref[size : size + experts + 16] = jnp.where(half == 0, extra, 0.0).astype(BF16)
        rest = ref.shape[0] - (size + experts + 16)
        ref[size + experts + 16 :] = jnp.zeros((rest, width), BF16)


def early_grads(info, attended, gb, router, ffn, experts):
    rows, width = gb.shape
    count = attended.shape[1]
    col = lambda r: pl.BlockSpec((r, 256), lambda i, s: (0, i))
    size = count // 2 + count // 8
    return pl.pallas_call(
        functools.partial(early_body, experts),
        grid_spec=pltpu.PrefetchScalarGridSpec(
            num_scalar_prefetch=1,
            grid=(width // 256,),
            in_specs=[
                pl.BlockSpec(attended.shape, lambda i, s: (0, 0)),
                col(rows),
                col(router.shape[0]),
                col(1),
            ],
            out_specs=[col(size)] * 2,
        ),
        out_shape=[jax.ShapeDtypeStruct((size, width), BF16)] * 2,
        compiler_params=params(("arbitrary",)),
        cost_estimate=COST,
        name="early_grads",
    )(info, attended, gb, router, ffn)


def rope_back(g, cos_ref, sin_ref):
    cos = jnp.concatenate([cos_ref[...]] * (g.shape[1] // 128), 1)
    sin = jnp.concatenate([sin_ref[...]] * (g.shape[1] // 128), 1)
    return g * cos - swap_halves(g, lambda v, s: pltpu.roll(v, s, 1)) * sin


def split_rows(core, n_ref, lin, give_ref, keep_ref):
    size = n_ref.shape[1] // 2
    for ref, half in ((give_ref, 1 - core), (keep_ref, core)):
        part = n_ref[:, pl.ds(pl.multiple_of(half * size, 128), size)]
        ref[...] = dot(part, lin, 0, 0).astype(BF16)


def query_back_body(info_ref, dq_ref, n_ref, cos_ref, sin_ref, lin_ref, give_ref, keep_ref):
    lin = rope_back(dq_ref[...] * HEAD_DIM**-0.5, cos_ref, sin_ref).astype(BF16)
    lin_ref[...] = lin
    split_rows(info_ref[0], n_ref, lin, give_ref, keep_ref)


def query_back(info, dq, normed, cos, sin):
    rows, width = dq.shape
    col = lambda r: pl.BlockSpec((r, 256), lambda i, s: (0, i))
    full = lambda shape: pl.BlockSpec(shape, lambda i, s: (0, 0))
    size = normed.shape[1] // 2
    return pl.pallas_call(
        query_back_body,
        grid_spec=pltpu.PrefetchScalarGridSpec(
            num_scalar_prefetch=1,
            grid=(width // 256,),
            in_specs=[col(rows), full(normed.shape), full(cos.shape), full(sin.shape)],
            out_specs=[col(rows), col(size), col(size)],
        ),
        out_shape=[
            jax.ShapeDtypeStruct((rows, width), BF16),
            jax.ShapeDtypeStruct((size, width), BF16),
            jax.ShapeDtypeStruct((size, width), BF16),
        ],
        compiler_params=params(("arbitrary",)),
        cost_estimate=cost(2 * rows * width * width, 8 * 1024 * 1024),
        name="query_back",
    )(info, dq, normed, cos, sin)


def pair_back_body(parts, half_steps, info_ref, *refs):
    n_ref, cos_ref, sin_ref, lin_ref, give_ref, keep_ref = refs[parts:]
    step = pl.program_id(0)
    total = refs[0][0].astype(F32)
    for ref in refs[1:parts]:
        total = total + ref[0].astype(F32)

    @pl.when(step < half_steps)
    def _():
        lin_ref[...] = rope_back(total, cos_ref, sin_ref).astype(BF16)

    @pl.when(step >= half_steps)
    def _():
        lin_ref[...] = total.astype(BF16)

    split_rows(info_ref[0], n_ref, lin_ref[...], give_ref, keep_ref)


def pair_back(info, parts, normed, cos, sin):
    _, rows, kvw = parts[0].shape
    half_steps = kvw // 256
    col = lambda r: pl.BlockSpec((r, 256), lambda i, s: (0, i))
    full = lambda shape: pl.BlockSpec(shape, lambda i, s: (0, 0))
    part = pl.BlockSpec((1, rows, 256), lambda i, s: (i // half_steps, 0, i % half_steps))
    size = normed.shape[1] // 2
    return pl.pallas_call(
        functools.partial(pair_back_body, len(parts), half_steps),
        grid_spec=pltpu.PrefetchScalarGridSpec(
            num_scalar_prefetch=1,
            grid=(2 * half_steps,),
            in_specs=[part] * len(parts) + [full(normed.shape), full(cos.shape), full(sin.shape)],
            out_specs=[col(rows), col(size), col(size)],
        ),
        out_shape=[
            jax.ShapeDtypeStruct((rows, 2 * kvw), BF16),
            jax.ShapeDtypeStruct((size, 2 * kvw), BF16),
            jax.ShapeDtypeStruct((size, 2 * kvw), BF16),
        ],
        compiler_params=params(("arbitrary",)),
        cost_estimate=COST,
        name="pair_back",
    )(info, *parts, normed, cos, sin)


def tokens_back_body(lq_ref, lkv_ref, wq_ref, wk_ref, wv_ref, x_ref, gh_ref, gain_ref, o_ref):
    kvw = wk_ref.shape[1]
    grad = dot(lq_ref[...], wq_ref[...], 1, 1)
    grad = grad + dot(lkv_ref[:, :kvw], wk_ref[...], 1, 1)
    grad = grad + dot(lkv_ref[:, kvw:], wv_ref[...], 1, 1)
    x = x_ref[...].astype(F32)
    scale = lax.rsqrt(jnp.mean(x * x, -1, keepdims=True) + EPS)
    weighted = grad * gain_ref[...]
    mean = jnp.mean(weighted * x, -1, keepdims=True)
    total = gh_ref[...] + scale * weighted - x * (scale * scale * scale * mean)
    o_ref[...] = total.astype(BF16)


def tokens_back(lq, lkv, wq, wk, wv, x, gh, gain):
    rows, width = x.shape
    row = lambda w: pl.BlockSpec((rows // 4, w), lambda i: (i, 0))
    full = lambda shape: pl.BlockSpec(shape, lambda i: (0, 0))
    return pl.pallas_call(
        tokens_back_body,
        grid=(4,),
        in_specs=[
            row(lq.shape[1]),
            row(lkv.shape[1]),
            full(wq.shape),
            full(wk.shape),
            full(wv.shape),
            row(width),
            row(width),
            full((1, width)),
        ],
        out_specs=row(width),
        out_shape=jax.ShapeDtypeStruct((rows, width), BF16),
        compiler_params=params(("arbitrary",)),
        cost_estimate=COST,
        name="tokens_back",
    )(lq, lkv, wq, wk, wv, x, gh, gain)


def total_of(parts):
    total = parts[0].astype(F32)
    for part in parts[1:]:
        total = total + part.astype(F32)
    return total.astype(BF16)


def scatter_sum(buf, axis):
    name, size, pos, pairs = axis
    rows = buf.shape[0] // size
    take = lambda k: lax.dynamic_slice_in_dim(buf, k * rows, rows, 0)
    parts = [take(pos)]
    for shift in range(1, size):
        parts.append(lax.ppermute(take((pos + shift) % size), name, pairs(shift)))
    return total_of(parts)


def gather_rows(buf, axis):
    name, size, pos, pairs = axis
    rows = buf.shape[0]
    came = [lax.ppermute(buf, name, pairs(shift)) for shift in range(size - 1, 0, -1)]
    if size == 2:
        pick = lambda a, b: jnp.concatenate([a, b], 0)
        return jnp.where(pos == 0, pick(buf, came[0]), pick(came[0], buf))
    order = came + [buf]
    double = jnp.concatenate(order + order[:-1], 0)
    return lax.dynamic_slice_in_dim(double, (size - 1 - pos) * rows, size * rows, 0)


def local(
    tokens,
    lengths,
    routes,
    cotangent,
    attn_norm,
    w_query,
    w_key,
    w_value,
    w_out,
    ffn_norm,
    w_router,
    expert_gate_weight,
    expert_up_weight,
    expert_down_weight,
):
    rows, width = tokens.shape[1:]
    half = rows // 2
    experts = w_router.shape[1]
    own = expert_gate_weight.shape[0]
    ff = expert_gate_weight.shape[2]
    kvw = w_key.shape[1]
    ctx_size, ep_size = lax.axis_size("ctx"), lax.axis_size("ep")
    ny, nx = ctx_size // CORES, ep_size // NZ
    ctx_index, ep_index = lax.axis_index("ctx"), lax.axis_index("ep")
    y, core = ctx_index // CORES, ctx_index % CORES
    z, xpos = ep_index // nx, ep_index % nx
    seq_len = lengths[0]
    tokens = tokens[0]
    valid_flag = ctx_index * rows + jnp.arange(rows, dtype=jnp.int32) < seq_len
    valid = valid_flag.astype(F32)[:, None]
    tie = lax.optimization_barrier
    ints = lambda values: jnp.stack([jnp.asarray(v, jnp.int32) for v in values])

    core_swap = [(c, c ^ 1) for c in range(ctx_size)]
    core_up = [(c, c + 1) for c in range(0, ctx_size, CORES)]
    core_down = [(c + 1, c) for c in range(0, ctx_size, CORES)]
    y_up = lambda k: [(c, c + CORES * k) for c in range(ctx_size - CORES * k)]
    y_down = lambda k: [(b, a) for a, b in y_up(k)]
    zx = lambda pairs: [(a * nx + i, b * nx + i) for a, b in pairs for i in range(nx)]
    z_groups = [[i + nx * k for k in range(NZ)] for i in range(nx)]
    x_shift = lambda s: [(k * nx + i, k * nx + (i + s) % nx) for k in range(NZ) for i in range(nx)]
    y_ring = lambda s: [(c, (c + CORES * s) % ctx_size) for c in range(ctx_size)]
    core_axis = ("ctx", CORES, core, lambda s: core_swap)
    y_axis = ("ctx", ny, y, y_ring)
    x_axis = ("ep", nx, xpos, x_shift)
    z_axis = ("ep", NZ, z, lambda s: zx([(k, (k + s) % NZ) for k in range(NZ)]))

    weights = (expert_gate_weight, expert_up_weight, expert_down_weight)
    count = jnp.clip(seq_len - ctx_index * rows, 0, rows)
    cot_ext, sent = prepare(ints([core, count]), routes[0], cotangent[0], weights, experts)
    cot_all = lax.all_gather(cot_ext, "ep", axis_index_groups=z_groups, tiled=True)
    arrived, far_places = [], []
    for shift in range(1, nx):
        arrived.append(lax.ppermute(sent, "ep", x_shift(shift)))
        origin = (xpos - shift) % nx * own
        far_places += [origin + core, origin + 1 - core]
    own_places = [xpos * own + i for i in range(own)]

    tokens, cot_ext, sent = tie((tokens, cot_ext, sent))
    fine, starts = rope_constants(ctx_size, rows)
    normed, q, kv, cos, sin = project(
        ints([ctx_index]), tokens, attn_norm[None], w_query, w_key, w_value, fine, starts, ctx_size
    )

    blocks = [kv, lax.ppermute(kv, "ctx", core_up)]
    facts = [(ctx_index * rows, True), ((ctx_index - 1) * rows, core == 1)]
    travelling = kv
    for back in range(1, ny):
        travelling = lax.ppermute(travelling, "ctx", y_up(1))
        blocks.append(travelling)
        base = (y - back) * CORES
        facts += [((base + core) * rows, y >= back), ((base + 1 - core) * rows, y >= back)]
    facts = [[start, (jnp.asarray(reach) & (start < seq_len))] for start, reach in facts]
    info_of = lambda part: ints([seq_len] + sum(part, []))
    state = attend(info_of(facts[:2]), q, blocks[:2], None)
    came = tie((*blocks[2:], *state))
    came, state = came[: ny - 1], came[ny - 1 :]
    blocks = blocks[:2]
    for piece in came:
        blocks += [piece, lax.ppermute(piece, "ctx", core_swap)]
    attended, lse, hidden, mixed = attend(
        info_of(facts[2:]), q, blocks[2:], state, w_out, tokens, ffn_norm[None]
    )

    wr = jnp.pad(w_router, ((0, 0), (0, 128 - experts)))
    group = nx * own
    widths = (width, group * ff, group * ff, group * ff, width, width)
    kept = tuple(jax.ShapeDtypeStruct((NZ, rows, w), BF16) for w in widths)

    def run(data, pick, cot, block, shard, near, far, low, kept, before=None):
        places = (own_places if near else []) + (far_places if far else [])
        facts = ints([block, shard, z * group, pick] + places)
        return expert_call(facts, data, cot, wr, near, far, experts, low, half, kept, before)

    shard_b, shard_c, shard_d = z ^ 1, jnp.where(z < 2, 2, 1), jnp.where(z < 2, 3, 0)
    inside = (z == 1) | (z == 2)
    swap, mid, out = [(0, 1), (1, 0), (2, 3), (3, 2)], [(1, 2), (2, 1)], [(1, 0), (2, 3)]
    halves = lambda a: [a[:half], a[half:]]
    near = lax.ppermute(mixed, "ep", zx(swap))
    middle_rows = lax.ppermute(mixed, "ep", zx(mid))
    gm_a, gates, kept = run((mixed, mixed), 1, cot_ext, 0, z, weights, [], 0, kept)
    near, middle_rows, arrived, kept = tie((near, middle_rows, arrived, kept))
    across = [lax.ppermute(part, "ep", zx(mid)) for part in halves(near)]
    outward = lax.ppermute(middle_rows, "ep", zx(out))
    far = []
    for piece in arrived:
        far += [piece, lax.ppermute(piece, "ctx", core_swap)]
    gm_a, _, kept = run((mixed, mixed), 1, cot_all, z, z, (), far, 0, kept, gm_a)
    across, outward, kept = tie((across, outward, kept))
    last = [lax.ppermute(part, "ep", zx(out)) for part in across]
    gm_b, _, kept = run((near, near), 1, cot_all, shard_b, shard_b, weights, far, 0, kept)
    ends, away = [(0, 1), (3, 2)], [(2, 3), (1, 0)]
    third = lax.ppermute(gm_b, "ep", zx(ends))
    last, kept = tie((last, kept))
    gm_c, _, kept = run(
        (middle_rows, outward), inside, cot_all, shard_c, shard_c, weights, far, 0, kept
    )
    second = lax.ppermute(gm_c, "ep", zx(ends))
    third, kept = tie((third, kept))
    gm_d0, _, kept = run(
        (across[0], last[0]), inside, cot_all, shard_d, shard_d, weights, far, 0, kept
    )
    first = [lax.ppermute(gm_d0, "ep", zx(ends))]
    second, kept = tie((second, kept))
    gm_d1, _, kept = run(
        (across[1], last[1]), inside, cot_all, shard_d, shard_d, weights, far, half, kept
    )
    first.append(lax.ppermute(gm_d1, "ep", zx(ends)))

    add = lambda a, b: (a.astype(F32) + b.astype(F32)).astype(BF16)
    first[0], kept = tie((first[0], kept))
    carried = [lax.ppermute(add(gm_d0, first[0]), "ep", zx(mid))]
    turned = lax.ppermute(add(gm_c, second), "ep", zx(mid))
    line = lambda a: a.reshape(NZ * rows, a.shape[2])
    turn = lambda i: ints([(xpos + j) % nx * own + i for j in range(nx)])
    saved = lambda kept: [line(kept[k]) for k in (4, 5, 1, 2, 3)]
    give = expert_grads(turn(1 - core), *saved(kept))
    first[1], carried[0], give, kept = tie((first[1], carried[0], give, kept))
    carried.append(lax.ppermute(add(gm_d1, first[1]), "ep", zx(mid)))
    final = [lax.ppermute(add(gm_b[:1], carried[0]), "ep", zx(away))]
    came = lax.ppermute(give, "ctx", core_swap)
    keep = expert_grads(turn(core), *saved(kept))
    carried[1], final[0], keep, came = tie((carried[1], final[0], keep, came))
    final.append(lax.ppermute(add(gm_b[1:], carried[1]), "ep", zx(away)))
    size = 3 * width // 2
    kept_p = [add(keep[j], came[j]).reshape(3 * width, ff)[:size] for j in range(nx)]
    kept_q = [add(keep[j], came[j]).reshape(3 * width, ff)[size:] for j in range(nx)]
    final, kept_p, kept_q = tie((final, kept_p, kept_q))
    sum_p = [lax.ppermute(kept_p[s], "ep", x_shift(s)) for s in range(1, nx)]
    rows_q = size // ny
    take_q = lambda s: jnp.concatenate(
        [lax.dynamic_slice_in_dim(k, (y + s) % ny * rows_q, rows_q, 0) for k in kept_q], 0
    )
    sum_q = [lax.ppermute(take_q(s), "ctx", y_ring(s)) for s in range(1, ny)]

    sums = [gm_a, third, turned, *final]
    gh, gb, do, delta, grad_ffn, grad_router = middle(
        sums, gates, wr, hidden, cot_ext, attended, mixed, ffn_norm[None], w_out, experts
    )
    which = ints([core])
    give, keep = early_grads(which, attended, gb, grad_router, grad_ffn, experts)
    give, keep, do = tie((give, keep, do))
    out_all = kept[0]
    out_all, do = tie((out_all, do))
    expert_sum = lax.psum_scatter(
        line(out_all), "ep", scatter_dimension=0, axis_index_groups=z_groups, tiled=True
    )

    came = lax.ppermute(give, "ctx", core_swap)
    dq = None
    homeward = []
    if ny > 1:
        far_info = info_of(facts[2:])
        dq, *far_dkv = attend_back(far_info, q, do, lse, delta, blocks[2:], None, False)
        for back in range(1, ny):
            same, other = far_dkv[2 * back - 2], far_dkv[2 * back - 1]
            homeward.append(add(same, lax.ppermute(other, "ctx", core_swap)))
    homeward, dq, came, sum_p, sum_q = tie((homeward, dq, came, sum_p, sum_q))
    homeward = [lax.ppermute(h, "ctx", y_down(k + 1)) for k, h in enumerate(homeward)]
    early = add(keep, came)
    part = early.shape[0] // 2
    early = [scatter_sum(early[:part], y_axis), scatter_sum(early[part:], x_axis)]
    half_q = total_of([take_q(0)] + sum_q)
    send_q = [half_q[s * rows_q : (s + 1) * rows_q] for s in range(nx)]
    sum_q = [lax.ppermute(send_q[s], "ep", x_shift(s)) for s in range(1, nx)]
    dq, *near_dkv = attend_back(info_of(facts[:2]), q, do, lse, delta, blocks[:2], dq, True)
    early, dq, homeward, sum_q, near_dkv = tie((early, dq, homeward, sum_q, near_dkv))
    parts = [near_dkv[0], lax.ppermute(near_dkv[1], "ctx", core_down), *homeward]
    early = [scatter_sum(early[0], x_axis), scatter_sum(early[1], y_axis)]
    sum_p = scatter_sum(total_of([kept_p[0]] + sum_p), y_axis)
    sum_q = total_of([send_q[0]] + sum_q)

    lin_q, give, keep = query_back(which, dq, normed, cos, sin)
    half_q = [keep, lax.ppermute(give, "ctx", core_swap)]
    parts, lin_q = tie((parts, lin_q))
    lin_kv, give, keep = pair_back(which, parts, normed, cos, sin)
    half_kv = [keep, lax.ppermute(give, "ctx", core_swap)]
    half_q, half_kv, early, sum_p, sum_q = tie((half_q, half_kv, early, sum_p, sum_q))
    one, two = scatter_sum(add(*half_q), y_axis), scatter_sum(add(*half_kv), x_axis)
    grad_tokens = tokens_back(
        lin_q, lin_kv, w_query, w_key, w_value, tokens, gh, attn_norm[None]
    )
    one, two, grad_tokens = tie((one, two, grad_tokens))
    one, two = scatter_sum(one, x_axis), scatter_sum(two, y_axis)
    one, two = tie((one, two))
    grads = jnp.concatenate([sum_p, sum_q], 0)
    grads = gather_rows(grads, y_axis)
    both = jnp.concatenate([one, early[0], two, early[1]], 0)
    both = gather_rows(scatter_sum(both, z_axis), z_axis)
    both, grads, expert_sum = tie((both, grads, expert_sum))
    result_out = (valid * (hidden + expert_sum.astype(F32))).astype(BF16)
    size = both.shape[0] // 2
    one, two = gather_rows(both[:size], x_axis), gather_rows(both[size:], y_axis)
    grads = gather_rows(grads.reshape(ny, 2 * rows_q, ff), core_axis)
    grads = grads.reshape(own, ny, 2, rows_q, ff).transpose(0, 2, 1, 3, 4).reshape(own, 3, width, ff)
    down = jnp.concatenate([grads[:, 2, :ff], grads[:, 2, ff:]], -1)
    expert_out = tuple(g.astype(F32) for g in (grads[:, 0], grads[:, 1], down))
    one, two, result_out, expert_out = tie((one, two, result_out, expert_out))
    one, two = gather_rows(one, y_axis), gather_rows(two, x_axis)

    wide = width // (CORES * ny * nx)
    late = gather_rows(jnp.concatenate([one, two], 0), core_axis)
    late = late.reshape(CORES, 2, ny * nx, size, width)
    late_q = late[:, 0, :, :wide].reshape(width, width).astype(F32)
    late_kv = late[:, 1, :, :wide].reshape(width, width).astype(F32)
    late_k, late_v = late_kv[:, :kvw], late_kv[:, kvw:]
    late_out = late[:, :, :, wide:].reshape(CORES, -1, width)
    w_out_sum = late_out[:, : width // 2].reshape(width, width).astype(F32)
    small = late_out[0, width // 2 :].astype(F32)
    paired = lambda w, g: jnp.sum(w.astype(F32) * g, 1)
    grad_attn_norm = paired(w_query, late_q) + paired(w_key, late_k) + paired(w_value, late_v)
    return (
        result_out[None],
        grad_tokens[None],
        grad_attn_norm / attn_norm,
        late_q,
        late_k,
        late_v,
        w_out_sum,
        small[experts],
        small[:experts].T,
        *expert_out,
    )


def solution(mesh):
    rows, whole, split = P("ep", "ctx", None), P(), P("ep", None, None)
    return jax.shard_map(
        local,
        mesh=mesh,
        in_specs=(rows, P("ep"), rows, rows) + (whole,) * 7 + (split,) * 3,
        out_specs=(rows, rows) + (whole,) * 7 + (split,) * 3,
        check_vma=False,
    )
```

time: 916 us -> 576 us (0.63)
  waiting for transfers between devices: 525 us -> 179 us
  Pallas kernels: 101 us -> 206 us
  local copies, waits for them, and re-layouts: 85.5 us -> 23.6 us
  matrix products: 56.3 us -> 0 us
  blocking collectives: 40.8 us -> 0 us
  starting transfers between devices: 45.9 us -> 77.7 us
  other arithmetic: 42 us -> 64.6 us
    psum x2 -> x0, waiting for transfers between devices: 291 us -> none  [the longest x1 236 us: local(): lax.psum((grad_w_query, grad_w_key, grad_w_value, grad_w_out, grad_router...]
    pallas_call x7 -> x19, Pallas kernels: 101 us -> 206 us  [the longest x6 92.1 us: expert_call(): pl.pallas_call(functools.partial(expert_body, own, remotes, rows, low, ha...]
    reduce_scatter x4 -> x1, waiting for transfers between devices: 92.1 us -> 0.02 us  [local(): lax.psum_scatter(line(out_all), 'ep', scatter_dimension=0, axis_index_gro...]
    dot_general x13 -> x0, matrix products: 56.3 us -> none  [dot(): lax.dot_general(a, b, (((ca,), (cb,)), ((), ())), preferred_element_type=...]
    unnamed x162 -> x79, local copies, waits for them, and re-layouts: 46.8 us -> 5.33 us
    psum x1 -> x0, blocking collectives: 40.8 us -> none  [local(): lax.psum((grad_w_query, grad_w_key, grad_w_value, grad_w_out, grad_router...]
    ppermute x17 -> x51, waiting for transfers between devices: 132 us -> 173 us  [the longest x10 47.8 us: gather_rows(): lax.ppermute(buf, name, pairs(shift))]
    ppermute x17 -> x51, starting transfers between devices: 38.7 us -> 71 us  [the longest x10 15 us: gather_rows(): lax.ppermute(buf, name, pairs(shift))]
  transfers between devices with their start and end apart: 26 -> 55, of which waited for: 13 -> 24; matrix products, arithmetic and copies ran while one was open for 15% -> 9% of each run, Pallas kernels for 4% -> 35%
where the time goes in v2:
time: 576 us; the launch traced here: 567 us
  Pallas kernels  206 us (36%)
  waiting for transfers between devices  179 us (31%)
  starting transfers between devices  77.7 us (13%)
  other arithmetic  64.6 us (11%)
  local copies, waits for them, and re-layouts  23.6 us (4%)
  between operations  16.5 us (3%)
    pallas_call x6, Pallas kernels, expert_call(): pl.pallas_call(functools.partial(expert_body, own, remotes, rows, low, ha...  92.1 us
    ppermute x10, waiting for transfers between devices, gather_rows(): lax.ppermute(buf, name, pairs(shift))  47.8 us
    ppermute x1, waiting for transfers between devices, local(): near = lax.ppermute(mixed, 'ep', zx(swap))  36 us
    ppermute x12, waiting for transfers between devices, scatter_sum(): parts.append(lax.ppermute(take((pos + shift) % size), name, pairs(shift)))  34.8 us
    pallas_call x2, Pallas kernels, expert_grads(): pl.pallas_call(expert_grads_body, grid_spec=pltpu.PrefetchScalarGridSpec(...  30.6 us
    ppermute x1, waiting for transfers between devices, local(): sum_p = [lax.ppermute(kept_p[s], 'ep', x_shift(s)) for s in range(1, nx)]  17.6 us
    ppermute x1, waiting for transfers between devices, local(): final.append(lax.ppermute(add(gm_b[1:], carried[1]), 'ep', zx(away)))  16.8 us
    pallas_call x2, Pallas kernels, attend_back(): pl.pallas_call(functools.partial(attend_back_body, roles, diagonal), grid...  16.6 us
  transfers between devices with their start and end apart: 55, of which 24 were waited for; matrix products, arithmetic and copies ran while one was open for 9% of the time, Pallas kernels for 35%

profile of v2, /device:TPU:0, one launch (start us, length us, event | category | flops | bytes accessed | tf_op | source)
XLA Modules:
  0.0 567.1 jit_solution(5357420475279810202)
XLA Ops:
  10.0 5.8 %prepare.1 = (bf16[400,1024]{1,0:T(8,128)(2,1)}, bf16[3072,512]{1,0:T(8,128)(2,1)}) custom-call(s32[2]{0:T(128)} %pad_add_fusion.info_ref, s32[384,8]{1,0:T(8,128)} %bitcast.117, bf16[384,1024]{1,0:T(8,128)(2,1)} %bitcast.115, bf16[2,1024,512]{2,1,0:T(8,128)(2,1)} %refs_4_.9, bf16[2,1024,512]{2,1,0:T(8,128)(2,1)} %refs_5_.11, bf16[2,512,1024]{2,1,0:T(8,128)(2,1)} %refs_6_.9), custom_call_target="tpu_custom_call" | custom-call | flops 1048576 | bytes 1048576 | tf_op jit(solution)/shard_map/prepare/pallas_call | solution.py:96
  18.8 9.4 %project.1 = (bf16[384,1024]{1,0:T(8,128)(2,1)}, bf16[384,1024]{1,0:T(8,128)(2,1)}, bf16[2,384,512]{2,1,0:T(8,128)(2,1)}, f32[384,128]{1,0:T(8,128)}, f32[384,128]{1,0:T(8,128)}) custom-call(s32[1]{0:T(128)} %bitcast.6.info_ref, bf16[384,1024]{1,0:T(8,128)(2,1)} %bitcast.112, f32[1,1024]{1,0:T(1,128)} %bitcast.119, bf16[1024,1024]{1,0:T(8,128)(2,1)} %wq_ref.3, ...), custom_call_target="tpu_custom_call" | custom-call | flops 1048576 | bytes 1048576 | tf_op jit(solution)/shard_map/project/pallas_call | solution.py:163
  35.5 8.2 %attend.2 = (f32[4,2,128,384]{3,2,1,0:T(8,128)}, f32[4,8,384]{2,1,0:T(8,128)}, f32[4,8,384]{2,1,0:T(8,128)}) custom-call(s32[5]{0:T(128)} %stack.179.info_ref, bf16[384,1024]{1,0:T(8,128)(2,1)} %get-tuple-element.205.q_ref, bf16[2,384,512]{2,1,0:T(8,128)(2,1)} %get-tuple-element.206.refs_0_, bf16[2,384,512]{2,1,0:T(8,128)(2,1)} %collective-permute-done.1.refs_1_), custom_call_target="tpu_custom_call" | custom-call | flops 1048576 | bytes 1048576 | tf_op jit(solution)/shard_map/attend/pallas_call | solution.py:328
  43.7 6.0 %collective-permute-done.refs_0_ = bf16[2,384,512]{2,1,0:T(8,128)(2,1)} collective-permute-done((bf16[2,384,512]{2,1,0:T(8,128)(2,1)}, bf16[2,384,512]{2,1,0:T(8,128)(2,1)}, u32[]{:S(2)}, u32[]{:S(2)}) %collective-permute-start) | collective-permute-done | bytes 786464 | tf_op jit(solution)/shard_map/ppermute | solution.py:1052
  52.3 7.9 %attend.3 = (bf16[384,1024]{1,0:T(8,128)(2,1)}, f32[4,8,384]{2,1,0:T(8,128)}, f32[384,1024]{1,0:T(8,128)}, bf16[384,1024]{1,0:T(8,128)(2,1)}) custom-call(s32[5]{0:T(128)} %stack.169.info_ref, bf16[384,1024]{1,0:T(8,128)(2,1)} %get-tuple-element.205.q_ref, bf16[2,384,512]{2,1,0:T(8,128)(2,1)} %collective-permute-done.refs_0_, ...), custom_call_target="tpu_custom_call" | custom-call | flops 1048576 | bytes 1048576 | tf_op jit(solution)/shard_map/attend/pallas_call | solution.py:328
  65.2 13.0 %experts.6 = (bf16[2,208,1024]{2,1,0:T(8,128)(2,1)}, f32[384,128]{1,0:T(8,128)}, bf16[4,384,1024]{2,1,0:T(8,128)(2,1)}, bf16[4,384,2048]{2,1,0:T(8,128)(2,1)}, b...) custom-call(s32[6]{0:T(128)} %stack.187.info_ref, ...), custom_call_target="tpu_custom_call" | custom-call | flops 4831838208 | bytes 6291456 | tf_op jit(solution)/shard_map/experts/pallas_call | solution.py:578
  78.3 36.0 %collective-permute-done.3.refs_0_.refs_1_ = bf16[384,1024]{1,0:T(8,128)(2,1)} collective-permute-done((bf16[384,1024]{1,0:T(8,128)(2,1)}, bf16[384,1024]{1,0:T(8,128)(2,1)}, u32[]{:S(2)}, u32[]{:S(2)}) %collective-permute-start.3) | collective-permute-done | bytes 786464 | tf_op jit(solution)/shard_map/ppermute | solution.py:1082
  122.0 13.1 %experts.7 = (bf16[2,208,1024]{2,1,0:T(8,128)(2,1)}, f32[384,128]{1,0:T(8,128)}, bf16[4,384,1024]{2,1,0:T(8,128)(2,1)}, bf16[4,384,2048]{2,1,0:T(8,128)(2,1)}, b...) custom-call(s32[6]{0:T(128)} %stack.184.info_ref, ...), custom_call_target="tpu_custom_call", output_to_operand_aliasing={{2}: (8, {}), {3}: (9, {}), {4}: (10, {}), {5}: (11, {})} | custom-call | flops 4831838208 | bytes 6291456 | tf_op jit(solution)/shard_map/experts/pallas_call | solution.py:578
  139.3 19.0 %experts.8 = (bf16[2,208,1024]{2,1,0:T(8,128)(2,1)}, f32[384,128]{1,0:T(8,128)}, bf16[4,384,1024]{2,1,0:T(8,128)(2,1)}, bf16[4,384,2048]{2,1,0:T(8,128)(2,1)}, b...) custom-call(s32[8]{0:T(128)} %stack.189.info_ref, ...), custom_call_target="tpu_custom_call", output_to_operand_aliasing={{2}: (10, {}), {3}: (11, {}), {4}: (12, {}), {5}: (13, {}),... | custom-call | flops 9663676416 | bytes 12582912 | tf_op jit(solution)/shard_map/experts/pallas_call | solution.py:578
  158.2 10.9 %collective-permute-start.10 = (bf16[2,208,1024]{2,1,0:T(8,128)(2,1)}, bf16[2,208,1024]{2,1,0:T(8,128)(2,1)S(1)}, u32[]{:S(2)}, u32[]{:S(2)}) collective-permute-start(bf16[2,208,1024]{2,1,0:T(8,128)(2,1)} %get-tuple-element.244), channel_id=1, source_target_pairs={{0,8},{4,12},{24,16},{28,20},{1,9},{5,13},{25,17},{29,21},{2,10},{... | collective-permute-start | bytes 2555912 | tf_op jit(solution)/shard_map/ppermute | solution.py:1096
  169.2 19.0 %experts.9 = (bf16[2,208,1024]{2,1,0:T(8,128)(2,1)}, f32[384,128]{1,0:T(8,128)}, bf16[4,384,1024]{2,1,0:T(8,128)(2,1)}, bf16[4,384,2048]{2,1,0:T(8,128)(2,1)}, b...) custom-call(s32[8]{0:T(128)} %stack.193.info_ref, ...), custom_call_target="tpu_custom_call", output_to_operand_aliasing={{2}: (10, {}), {3}: (11, {}), {4}: (12, {}), {5}: (13, {}),... | custom-call | flops 9663676416 | bytes 12582912 | tf_op jit(solution)/shard_map/experts/pallas_call | solution.py:578
  190.7 14.0 %experts.10 = (bf16[1,208,1024]{2,1,0:T(8,128)(2,1)}, f32[192,128]{1,0:T(8,128)}, bf16[4,384,1024]{2,1,0:T(8,128)(2,1)}, bf16[4,384,2048]{2,1,0:T(8,128)(2,1)}, ...) custom-call(s32[8]{0:T(128)} %stack.195.info_ref, ...), custom_call_target="tpu_custom_call", output_to_operand_aliasing={{2}: (10, {}), {3}: (11, {}), {4}: (12, {}), {5}: (13, {}),... | custom-call | flops 4831838208 | bytes 12582912 | tf_op jit(solution)/shard_map/experts/pallas_call | solution.py:578
  209.2 14.1 %experts.11 = (bf16[1,208,1024]{2,1,0:T(8,128)(2,1)}, f32[192,128]{1,0:T(8,128)}, bf16[4,384,1024]{2,1,0:T(8,128)(2,1)}, bf16[4,384,2048]{2,1,0:T(8,128)(2,1)}, ...) custom-call(s32[8]{0:T(128)} %stack.195.info_ref, ...), custom_call_target="tpu_custom_call", output_to_operand_aliasing={{2}: (10, {}), {3}: (11, {}), {4}: (12, {}), {5}: (13, {}),... | custom-call | flops 4831838208 | bytes 12582912 | tf_op jit(solution)/shard_map/experts/pallas_call | solution.py:578
  229.2 15.4 %expert_grads.2 = bf16[2,3,1024,512]{3,2,1,0:T(8,128)(2,1)} custom-call(s32[2]{0:T(128)} %pad_add_fusion.1.info_ref, bf16[1536,1024]{1,0:T(8,128)(2,1)} %bitcast.97, bf16[1536,1024]{1,0:T(8,128)(2,1)} %bitcast.99, bf16[1536,2048]{1,0:T(8,128)(2,1)} %bitcast.90, bf16[1536,2048]{1,0:T(8,128)(2,1)} %bitcast.92, bf16[1536,2048]{1,0:T(8,128)(2,1)} %bitcast.94), custom_call_target="tpu_custom_call" | custom-call | flops 9663676416 | bytes 16777216 | tf_op jit(solution)/shard_map/expert_grads/pallas_call | solution.py:659
  249.9 15.3 %expert_grads.3 = bf16[2,3,1024,512]{3,2,1,0:T(8,128)(2,1)} custom-call(s32[2]{0:T(128)} %pad_add_fusion.2.info_ref, bf16[1536,1024]{1,0:T(8,128)(2,1)} %bitcast.98, bf16[1536,1024]{1,0:T(8,128)(2,1)} %bitcast.100, bf16[1536,2048]{1,0:T(8,128)(2,1)} %bitcast.91, bf16[1536,2048]{1,0:T(8,128)(2,1)} %bitcast.93, bf16[1536,2048]{1,0:T(8,128)(2,1)} %bitcast.95), custom_call_target="tpu_custom_call" | custom-call | flops 9663676416 | bytes 16777216 | tf_op jit(solution)/shard_map/expert_grads/pallas_call | solution.py:659
  266.6 5.6 add_convert_fusion
  273.8 16.8 %collective-permute-done.21.refs_4_ = bf16[1,208,1024]{2,1,0:T(8,128)(2,1)S(1)} collective-permute-done((bf16[1,208,1024]{2,1,0:T(8,128)(2,1)S(1)}, bf16[1,208,1024]{2,1,0:T(8,128)(2,1)S(1)}, u32[]{:S(2)}, u32[]{:S(2)}) %collective-permute-start.21) | collective-permute-done | bytes 426016 | tf_op jit(solution)/shard_map/ppermute | solution.py:1127
  294.9 8.8 %middle.1 = (f32[384,1024]{1,0:T(8,128)}, bf16[384,1024]{1,0:T(8,128)(2,1)}, bf16[384,1024]{1,0:T(8,128)(2,1)}, f32[4,8,384]{2,1,0:T(8,128)}, f32[1,1024]{1,0:T(1,128)}, /*index=5*/f32[128,1024]{1,0:T(8,128)}) custom-call(bf16[2,208,1024]{2,1,0:T(8,128)(2,1)} %get-tuple-element.229.refs_0_, bf16[2,208,1024]{2,1,0:T(8,128)(2,1)} %copy-done.18, ...), custom_call_target="tpu_custom_call" | custom-call | flops 1048576 | bytes 1048576 | tf_op jit(solution)/shard_map/middle/pallas_call | solution.py:748
  320.8 7.5 %collective-permute-done.25 = bf16[1536,512]{1,0:T(8,128)(2,1)} collective-permute-done((bf16[1536,512]{1,0:T(8,128)(2,1)}, bf16[1536,512]{1,0:T(8,128)(2,1)}, u32[]{:S(2)}, u32[]{:S(2)}) %collective-permute-start.25) | collective-permute-done | bytes 1572896 | tf_op jit(solution)/shard_map/ppermute | solution.py:1137
  328.4 17.6 %collective-permute-done.24 = bf16[1536,512]{1,0:T(8,128)(2,1)} collective-permute-done((bf16[1536,512]{1,0:T(8,128)(2,1)}, bf16[1536,512]{1,0:T(8,128)(2,1)}, u32[]{:S(2)}, u32[]{:S(2)}) %collective-permute-start.24) | collective-permute-done | bytes 1572896 | tf_op jit(solution)/shard_map/ppermute | solution.py:1132
  355.2 11.5 %attend_back.3 = (f32[384,1024]{1,0:T(8,128)}, bf16[2,384,512]{2,1,0:T(8,128)(2,1)}, bf16[2,384,512]{2,1,0:T(8,128)(2,1)}) custom-call(s32[5]{0:T(128)} %stack.179.info_ref, bf16[384,1024]{1,0:T(8,128)(2,1)} %get-tuple-element.205.q_ref, bf16[384,1024]{1,0:T(8,128)(2,1)} %get-tuple-element.329.do_ref, f32[4,8,384]{2,1,0:T(8,128)} %get-tuple-element.330.lse_ref, ...), custom_call_target="tpu_custom_call" | custom-call | flops 12079595520 | bytes 16777216 | tf_op jit(solution)/shard_map/attend_back/pallas_call | solution.py:407
  366.6 7.7 %collective-permute-done.27 = bf16[160,1024]{1,0:T(8,128)(2,1)} collective-permute-done((bf16[160,1024]{1,0:T(8,128)(2,1)S(1)}, bf16[160,1024]{1,0:T(8,128)(2,1)}, u32[]{:S(2)}, u32[]{:S(2)}) %collective-permute-start.27) | collective-permute-done | bytes 327712 | tf_op jit(solution)/shard_map/ppermute | solution.py:967
  384.5 5.7 %query_back.1 = (bf16[384,1024]{1,0:T(8,128)(2,1)}, bf16[512,1024]{1,0:T(8,128)(2,1)}, bf16[512,1024]{1,0:T(8,128)(2,1)}) custom-call(s32[1]{0:T(128)} %bitcast.info_ref, f32[384,1024]{1,0:T(8,128)} %get-tuple-element.346.dq_ref, bf16[384,1024]{1,0:T(8,128)(2,1)} %get-tuple-element.347.n_ref.refs_3_, f32[384,128]{1,0:T(8,128)} %get-tuple-element.348.cos_ref.refs_4_, ...), custom_call_target="tpu_custom_call" | custom-call | flops 805306368 | bytes 8388608 | tf_op jit(solution)/shard_map/query_back/pallas_call | solution.py:853
  391.8 6.2 %pair_back.1 = (bf16[384,1024]{1,0:T(8,128)(2,1)}, bf16[512,1024]{1,0:T(8,128)(2,1)}, bf16[512,1024]{1,0:T(8,128)(2,1)}) custom-call(s32[1]{0:T(128)} %bitcast.info_ref, bf16[2,384,512]{2,1,0:T(8,128)(2,1)} %get-tuple-element.356.refs_0_, bf16[2,384,512]{2,1,0:T(8,128)(2,1)} %collective-permute-done.31.refs_1_, bf16[2,384,512]{2,1,0:T(8,128)(2,1)} %copy-done.23, ...), custom_call_target="tpu_custom_call" | custom-call | flops 1048576 | bytes 1048576 | tf_op jit(solution)/shard_map/pair_back/pallas_call | solution.py:897
  411.2 9.6 %tokens_back.1 = bf16[384,1024]{1,0:T(8,128)(2,1)} custom-call(bf16[384,1024]{1,0:T(8,128)(2,1)} %get-tuple-element.370.lq_ref, bf16[384,1024]{1,0:T(8,128)(2,1)} %get-tuple-element.371.lkv_ref, bf16[1024,1024]{1,0:T(8,128)(2,1)} %wq_ref.3, bf16[1024,512]{1,0:T(8,128)(2,1)} %wk_ref.3, bf16[1024,512]{1,0:T(8,128)(2,1)} %wv_ref.3, ...), custom_call_target="tpu_custom_call" | custom-call | flops 1048576 | bytes 1048576 | tf_op jit(solution)/shard_map/tokens_back/pallas_call | solution.py:933
  429.0 7.1 %collective-permute-done.39 = bf16[128,1024]{1,0:T(8,128)(2,1)} collective-permute-done((bf16[128,1024]{1,0:T(8,128)(2,1)S(1)}, bf16[128,1024]{1,0:T(8,128)(2,1)}, u32[]{:S(2)}, u32[]{:S(2)}) %collective-permute-start.39) | collective-permute-done | bytes 262176 | tf_op jit(solution)/shard_map/ppermute | solution.py:967
  449.6 8.0 %collective-permute-done.41 = bf16[104,1024]{1,0:T(8,128)(2,1)} collective-permute-done((bf16[104,1024]{1,0:T(8,128)(2,1)}, bf16[104,1024]{1,0:T(8,128)(2,1)}, u32[]{:S(2)}, u32[]{:S(2)}) %collective-permute-start.41) | collective-permute-done | bytes 213024 | tf_op jit(solution)/shard_map/ppermute | solution.py:967
  458.9 5.1 collective-permute-start.43
  469.8 13.0 %collective-permute-done.44 = bf16[104,1024]{1,0:T(8,128)(2,1)S(1)} collective-permute-done((bf16[104,1024]{1,0:T(8,128)(2,1)S(1)}, bf16[104,1024]{1,0:T(8,128)(2,1)S(1)}, u32[]{:S(2)}, u32[]{:S(2)}) %collective-permute-start.44) | collective-permute-done | bytes 213024 | tf_op jit(solution)/shard_map/ppermute | solution.py:974
  494.6 6.3 %collective-permute-done.48 = bf16[208,1024]{1,0:T(8,128)(2,1)} collective-permute-done((bf16[208,1024]{1,0:T(8,128)(2,1)}, bf16[208,1024]{1,0:T(8,128)(2,1)}, u32[]{:S(2)}, u32[]{:S(2)}) %collective-permute-start.48) | collective-permute-done | bytes 426016 | tf_op jit(solution)/shard_map/ppermute | solution.py:974
  518.2 17.0 %collective-permute-done.50 = bf16[416,1024]{1,0:T(8,128)(2,1)S(1)} collective-permute-done((bf16[416,1024]{1,0:T(8,128)(2,1)S(1)}, bf16[416,1024]{1,0:T(8,128)(2,1)S(1)}, u32[]{:S(2)}, u32[]{:S(2)}) %collective-permute-start.50) | collective-permute-done | bytes 852000 | tf_op jit(solution)/shard_map/ppermute | solution.py:974
  538.0 6.0 %collective-permute-done.52 = bf16[1664,1024]{1,0:T(8,128)(2,1)S(1)} collective-permute-done((bf16[1664,1024]{1,0:T(8,128)(2,1)S(1)}, bf16[1664,1024]{1,0:T(8,128)(2,1)S(1)}, u32[]{:S(2)}, u32[]{:S(2)}) %collective-permute-start.52) | collective-permute-done | bytes 3407904 | tf_op jit(solution)/shard_map/ppermute | solution.py:974
  (259 shorter events, 184.2 us)
Async XLA Ops:
  7.2 114.8 %all-gather.2.cloned.1.call-start = ((), (), s32[]{:S(2)}) async-start(), calls=%async_computation.1 | async-start | bytes 4096000 | tf_op jit(solution)/shard_map/all_gather | solution.py:1034
  15.8 98.6 %collective-permute-start.5 = (bf16[3072,512]{1,0:T(8,128)(2,1)}, bf16[3072,512]{1,0:T(8,128)(2,1)S(1)}, u32[]{:S(2)}, u32[]{:S(2)}) collective-permute-start(bf16[3072,512]{1,0:T(8,128)(2,1)} %get-tuple-element.203), channel_id=1, source_target_pairs={{0,4},{4,0},{8,12},{12,8},{16,20},{20,16},{24,28},{28,24},{1,5},{5... | collective-permute-start | bytes 9437192 | tf_op jit(solution)/shard_map/ppermute | solution.py:1037
  30.5 19.2 %collective-permute-start = (bf16[2,384,512]{2,1,0:T(8,128)(2,1)}, bf16[2,384,512]{2,1,0:T(8,128)(2,1)}, u32[]{:S(2)}, u32[]{:S(2)}) collective-permute-start(bf16[2,384,512]{2,1,0:T(8,128)(2,1)} %get-tuple-element.206.refs_0_), channel_id=1, source_target_pairs={{0,2},{1,3},{4,6},{5,7},{8,10},{9,11},{12,14},{13,15},{16,18},{17,... | collective-permute-start | bytes 2359304 | tf_op jit(solution)/shard_map/ppermute | solution.py:1052
  34.8 451.3 %reduce-scatter.2.cloned.1.call-start = ((), (), s32[]{:S(2)}) async-start(), calls=%async_computation.2 | async-start | bytes 3932160 | tf_op jit(solution)/shard_map/reduce_scatter | solution.py:1148
  60.2 54.1 %collective-permute-start.3 = (bf16[384,1024]{1,0:T(8,128)(2,1)}, bf16[384,1024]{1,0:T(8,128)(2,1)}, u32[]{:S(2)}, u32[]{:S(2)}) collective-permute-start(bf16[384,1024]{1,0:T(8,128)(2,1)} %get-tuple-element.215.refs_0_.refs_1_.refs_10_), channel_id=1, source_target_pairs={{0,8},{4,12},{8,0},{12,4},{16,24},{20,28},{24,16},{28,20},{1,9},{5... | collective-permute-start | bytes 2359304 | tf_op jit(solution)/shard_map/ppermute | solution.py:1082
  61.9 52.4 %collective-permute-start.4 = (bf16[384,1024]{1,0:T(8,128)(2,1)}, bf16[384,1024]{1,0:T(8,128)(2,1)}, u32[]{:S(2)}, u32[]{:S(2)}) collective-permute-start(bf16[384,1024]{1,0:T(8,128)(2,1)} %get-tuple-element.215.refs_0_.refs_1_.refs_10_), channel_id=1, source_target_pairs={{8,16},{12,20},{16,8},{20,12},{9,17},{13,21},{17,9},{21,13},{10,18... | collective-permute-start | bytes 2359304 | tf_op jit(solution)/shard_map/ppermute | solution.py:1083
  114.5 22.2 %collective-permute-start.9 = (bf16[384,1024]{1,0:T(8,128)(2,1)}, bf16[384,1024]{1,0:T(8,128)(2,1)}, u32[]{:S(2)}, u32[]{:S(2)}) collective-permute-start(bf16[384,1024]{1,0:T(8,128)(2,1)} %collective-permute-done.4.refs_0_), channel_id=1, source_target_pairs={{8,0},{12,4},{16,24},{20,28},{9,1},{13,5},{17,25},{21,29},{10,2},{... | collective-permute-start | bytes 2359304 | tf_op jit(solution)/shard_map/ppermute | solution.py:1087
  136.7 32.5 %collective-permute-start.11 = (bf16[192,1024]{1,0:T(8,128)(2,1)}, bf16[192,1024]{1,0:T(8,128)(2,1)S(1)}, u32[]{:S(2)}, u32[]{:S(2)}) collective-permute-start(bf16[192,1024]{1,0:T(8,128)(2,1)} %collective-permute-done.7.refs_0_), channel_id=1, source_target_pairs={{8,0},{12,4},{16,24},{20,28},{9,1},{13,5},{17,25},{21,29},{10,2},{... | collective-permute-start | bytes 1179656 | tf_op jit(solution)/shard_map/ppermute | solution.py:1093
  138.0 31.2 %collective-permute-start.12 = (bf16[192,1024]{1,0:T(8,128)(2,1)S(1)}, bf16[192,1024]{1,0:T(8,128)(2,1)S(1)}, u32[]{:S(2)}, u32[]{:S(2)}) collective-permute-start(bf16[192,1024]{1,0:T(8,128)(2,1)S(1)} %collective-permute-done.8.refs_0_), channel_id=1, source_target_pairs={{8,0},{12,4},{16,24},{20,28},{9,1},{13,5},{17,25},{21,29},{10,2},{... | collective-permute-start | bytes 1179656 | tf_op jit(solution)/shard_map/ppermute | solution.py:1093
  158.2 32.5 %collective-permute-start.10 = (bf16[2,208,1024]{2,1,0:T(8,128)(2,1)}, bf16[2,208,1024]{2,1,0:T(8,128)(2,1)S(1)}, u32[]{:S(2)}, u32[]{:S(2)}) collective-permute-start(bf16[2,208,1024]{2,1,0:T(8,128)(2,1)} %get-tuple-element.244), channel_id=1, source_target_pairs={{0,8},{4,12},{24,16},{28,20},{1,9},{5,13},{25,17},{29,21},{2,10},{... | collective-permute-start | bytes 2555912 | tf_op jit(solution)/shard_map/ppermute | solution.py:1096
  188.2 21.0 %collective-permute-start.13 = (bf16[2,208,1024]{2,1,0:T(8,128)(2,1)}, bf16[2,208,1024]{2,1,0:T(8,128)(2,1)S(1)}, u32[]{:S(2)}, u32[]{:S(2)}) collective-permute-start(bf16[2,208,1024]{2,1,0:T(8,128)(2,1)} %get-tuple-element.267), channel_id=1, source_target_pairs={{0,8},{4,12},{24,16},{28,20},{1,9},{5,13},{25,17},{29,21},{2,10},{... | collective-permute-start | bytes 2555912 | tf_op jit(solution)/shard_map/ppermute | solution.py:1101
  204.7 22.9 %collective-permute-start.16 = (bf16[1,208,1024]{2,1,0:T(8,128)(2,1)}, bf16[1,208,1024]{2,1,0:T(8,128)(2,1)S(1)}, u32[]{:S(2)}, u32[]{:S(2)}) collective-permute-start(bf16[1,208,1024]{2,1,0:T(8,128)(2,1)} %get-tuple-element.290), channel_id=1, source_target_pairs={{0,8},{4,12},{24,16},{28,20},{1,9},{5,13},{25,17},{29,21},{2,10},{... | collective-permute-start | bytes 1277960 | tf_op jit(solution)/shard_map/ppermute | solution.py:1106
  223.2 21.3 %collective-permute-start.15 = (bf16[1,208,1024]{2,1,0:T(8,128)(2,1)}, bf16[1,208,1024]{2,1,0:T(8,128)(2,1)S(1)}, u32[]{:S(2)}, u32[]{:S(2)}) collective-permute-start(bf16[1,208,1024]{2,1,0:T(8,128)(2,1)} %get-tuple-element.289), channel_id=1, source_target_pairs={{0,8},{4,12},{24,16},{28,20},{1,9},{5,13},{25,17},{29,21},{2,10},{... | collective-permute-start | bytes 1277960 | tf_op jit(solution)/shard_map/ppermute | solution.py:1111
  244.6 20.6 %collective-permute-start.20 = (bf16[2,3,1024,512]{3,2,1,0:T(8,128)(2,1)}, bf16[2,3,1024,512]{3,2,1,0:T(8,128)(2,1)}, u32[]{:S(2)}, u32[]{:S(2)}) collective-permute-start(bf16[2,3,1024,512]{3,2,1,0:T(8,128)(2,1)} %expert_grads.2), channel_id=1, source_target_pairs={{0,1},{1,0},{2,3},{3,2},{4,5},{5,4},{6,7},{7,6},{8,9},{9,8},{10,11... | collective-permute-start | bytes 18874376 | tf_op jit(solution)/shard_map/ppermute | solution.py:1124
  245.7 48.3 %collective-permute-start.14 = (bf16[2,208,1024]{2,1,0:T(8,128)(2,1)S(1)}, bf16[2,208,1024]{2,1,0:T(8,128)(2,1)S(1)}, u32[]{:S(2)}, u32[]{:S(2)}) collective-permute-start(bf16[2,208,1024]{2,1,0:T(8,128)(2,1)S(1)} %add_convert_fusion.7), channel_id=1, source_target_pairs={{8,16},{12,20},{16,8},{20,12},{9,17},{13,21},{17,9},{21,13},{10,18... | collective-permute-start | bytes 2555912 | tf_op jit(solution)/shard_map/ppermute | solution.py:1116
  247.6 17.6 %collective-permute-start.19 = (bf16[1,208,1024]{2,1,0:T(8,128)(2,1)S(1)}, bf16[1,208,1024]{2,1,0:T(8,128)(2,1)S(1)}, u32[]{:S(2)}, u32[]{:S(2)}) collective-permute-start(bf16[1,208,1024]{2,1,0:T(8,128)(2,1)S(1)} %add_convert_fusion.14), channel_id=1, source_target_pairs={{16,24},{20,28},{8,0},{12,4},{17,25},{21,29},{9,1},{13,5},{18,26},... | collective-permute-start | bytes 1277960 | tf_op jit(solution)/shard_map/ppermute | solution.py:1123
  265.3 25.3 %collective-permute-start.21 = (bf16[1,208,1024]{2,1,0:T(8,128)(2,1)S(1)}, bf16[1,208,1024]{2,1,0:T(8,128)(2,1)S(1)}, u32[]{:S(2)}, u32[]{:S(2)}) collective-permute-start(bf16[1,208,1024]{2,1,0:T(8,128)(2,1)S(1)} %add_convert_fusion.13), channel_id=1, source_target_pairs={{16,24},{20,28},{8,0},{12,4},{17,25},{21,29},{9,1},{13,5},{18,26},... | collective-permute-start | bytes 1277960 | tf_op jit(solution)/shard_map/ppermute | solution.py:1127
  292.7 35.7 %collective-permute-start.25 = (bf16[1536,512]{1,0:T(8,128)(2,1)}, bf16[1536,512]{1,0:T(8,128)(2,1)}, u32[]{:S(2)}, u32[]{:S(2)}) collective-permute-start(bf16[1536,512]{1,0:T(8,128)(2,1)} %pad_maximum_fusion.1), channel_id=1, source_target_pairs={{0,2},{1,3},{2,0},{3,1},{4,6},{5,7},{6,4},{7,5},{8,10},{9,11},{10,... | collective-permute-start | bytes 4718600 | tf_op jit(solution)/shard_map/ppermute | solution.py:1137
  308.9 37.1 %collective-permute-start.24 = (bf16[1536,512]{1,0:T(8,128)(2,1)}, bf16[1536,512]{1,0:T(8,128)(2,1)}, u32[]{:S(2)}, u32[]{:S(2)}) collective-permute-start(bf16[1536,512]{1,0:T(8,128)(2,1)} %get-tuple-element.336), channel_id=1, source_target_pairs={{0,4},{4,0},{8,12},{12,8},{16,20},{20,16},{24,28},{28,24},{1,5},{5... | collective-permute-start | bytes 4718600 | tf_op jit(solution)/shard_map/ppermute | solution.py:1132
  348.0 28.2 %collective-permute-start.29 = (bf16[768,512]{1,0:T(8,128)(2,1)S(1)}, bf16[768,512]{1,0:T(8,128)(2,1)S(1)}, u32[]{:S(2)}, u32[]{:S(2)}) collective-permute-start(bf16[768,512]{1,0:T(8,128)(2,1)S(1)} %slice.139), channel_id=1, source_target_pairs={{0,4},{4,0},{8,12},{12,8},{16,20},{20,16},{24,28},{28,24},{1,5},{5... | collective-permute-start | bytes 2359304 | tf_op jit(solution)/shard_map/ppermute | solution.py:1168
  351.7 22.6 %collective-permute-start.27 = (bf16[160,1024]{1,0:T(8,128)(2,1)S(1)}, bf16[160,1024]{1,0:T(8,128)(2,1)}, u32[]{:S(2)}, u32[]{:S(2)}) collective-permute-start(bf16[160,1024]{1,0:T(8,128)(2,1)S(1)} %constant_dynamic-slice_fusion.13), channel_id=1, source_target_pairs={{0,4},{4,0},{8,12},{12,8},{16,20},{20,16},{24,28},{28,24},{1,5},{5... | collective-permute-start | bytes 983048 | tf_op jit(solution)/shard_map/ppermute | solution.py:967
  352.9 22.4 %collective-permute-start.26 = (bf16[160,1024]{1,0:T(8,128)(2,1)}, bf16[160,1024]{1,0:T(8,128)(2,1)S(1)}, u32[]{:S(2)}, u32[]{:S(2)}) collective-permute-start(bf16[160,1024]{1,0:T(8,128)(2,1)} %constant_dynamic-slice_fusion.14), channel_id=1, source_target_pairs={{0,2},{1,3},{2,0},{3,1},{4,6},{5,7},{6,4},{7,5},{8,10},{9,11},{10,... | collective-permute-start | bytes 983048 | tf_op jit(solution)/shard_map/ppermute | solution.py:967
  353.7 25.4 %collective-permute-start.28 = (bf16[2,384,512]{2,1,0:T(8,128)(2,1)}, bf16[2,384,512]{2,1,0:T(8,128)(2,1)S(1)}, u32[]{:S(2)}, u32[]{:S(2)}) collective-permute-start(bf16[2,384,512]{2,1,0:T(8,128)(2,1)} %add_convert_fusion.10), channel_id=1, source_target_pairs={{2,0},{3,1},{6,4},{7,5},{10,8},{11,9},{14,12},{15,13},{18,16},{19,... | collective-permute-start | bytes 2359304 | tf_op jit(solution)/shard_map/ppermute | solution.py:1162
  382.2 19.5 %collective-permute-start.35 = (bf16[768,512]{1,0:T(8,128)(2,1)S(1)}, bf16[768,512]{1,0:T(8,128)(2,1)}, u32[]{:S(2)}, u32[]{:S(2)}) collective-permute-start(bf16[768,512]{1,0:T(8,128)(2,1)S(1)} %constant_dynamic-slice_fusion.8), channel_id=1, source_target_pairs={{0,2},{1,3},{2,0},{3,1},{4,6},{5,7},{6,4},{7,5},{8,10},{9,11},{10,... | collective-permute-start | bytes 2359304 | tf_op jit(solution)/shard_map/ppermute | solution.py:967
  382.4 22.7 %collective-permute-start.34 = (bf16[80,1024]{1,0:T(8,128)(2,1)S(1)}, bf16[80,1024]{1,0:T(8,128)(2,1)S(1)}, u32[]{:S(2)}, u32[]{:S(2)}) collective-permute-start(bf16[80,1024]{1,0:T(8,128)(2,1)S(1)} %constant_dynamic-slice_fusion.9), channel_id=1, source_target_pairs={{0,2},{1,3},{2,0},{3,1},{4,6},{5,7},{6,4},{7,5},{8,10},{9,11},{10,... | collective-permute-start | bytes 491528 | tf_op jit(solution)/shard_map/ppermute | solution.py:967
  439.1 18.4 %collective-permute-start.41 = (bf16[104,1024]{1,0:T(8,128)(2,1)}, bf16[104,1024]{1,0:T(8,128)(2,1)}, u32[]{:S(2)}, u32[]{:S(2)}) collective-permute-start(bf16[104,1024]{1,0:T(8,128)(2,1)} %get-tuple-element.422), channel_id=1, source_target_pairs={{0,16},{4,20},{8,24},{12,28},{16,0},{20,4},{24,8},{28,12},{1,17},{... | collective-permute-start | bytes 638984 | tf_op jit(solution)/shard_map/ppermute | solution.py:967
  443.0 40.8 %collective-permute-start.46 = (bf16[1536,512]{1,0:T(8,128)(2,1)S(1)}, bf16[1536,512]{1,0:T(8,128)(2,1)}, u32[]{:S(2)}, u32[]{:S(2)}) collective-permute-start(bf16[1536,512]{1,0:T(8,128)(2,1)S(1)} %pad_maximum_fusion.2), channel_id=1, source_target_pairs={{0,2},{1,3},{2,0},{3,1},{4,6},{5,7},{6,4},{7,5},{8,10},{9,11},{10,... | collective-permute-start | bytes 4718600 | tf_op jit(solution)/shard_map/ppermute | solution.py:974
  464.0 18.7 %collective-permute-start.44 = (bf16[104,1024]{1,0:T(8,128)(2,1)S(1)}, bf16[104,1024]{1,0:T(8,128)(2,1)S(1)}, u32[]{:S(2)}, u32[]{:S(2)}) collective-permute-start(bf16[104,1024]{1,0:T(8,128)(2,1)S(1)} %add_convert_fusion.21), channel_id=1, source_target_pairs={{0,16},{4,20},{8,24},{12,28},{16,0},{20,4},{24,8},{28,12},{1,17},{... | collective-permute-start | bytes 638984 | tf_op jit(solution)/shard_map/ppermute | solution.py:974
  464.7 18.1 %collective-permute-start.45 = (bf16[104,1024]{1,0:T(8,128)(2,1)S(1)}, bf16[104,1024]{1,0:T(8,128)(2,1)S(1)}, u32[]{:S(2)}, u32[]{:S(2)}) collective-permute-start(bf16[104,1024]{1,0:T(8,128)(2,1)S(1)} %add_convert_fusion.21), channel_id=1, source_target_pairs={{0,8},{4,12},{8,16},{12,20},{16,24},{20,28},{24,0},{28,4},{1,9},{5... | collective-permute-start | bytes 638984 | tf_op jit(solution)/shard_map/ppermute | solution.py:974
  486.2 16.9 %collective-permute-start.49 = (bf16[2,1536,512]{2,1,0:T(8,128)(2,1)S(1)}, bf16[2,1536,512]{2,1,0:T(8,128)(2,1)}, u32[]{:S(2)}, u32[]{:S(2)}) collective-permute-start(bf16[2,1536,512]{2,1,0:T(8,128)(2,1)S(1)} %bitcast.108), channel_id=1, source_target_pairs={{0,1},{1,0},{2,3},{3,2},{4,5},{5,4},{6,7},{7,6},{8,9},{9,8},{10,11... | collective-permute-start | bytes 9437192 | tf_op jit(solution)/shard_map/ppermute | solution.py:974
  514.7 20.6 %collective-permute-start.50 = (bf16[416,1024]{1,0:T(8,128)(2,1)S(1)}, bf16[416,1024]{1,0:T(8,128)(2,1)S(1)}, u32[]{:S(2)}, u32[]{:S(2)}) collective-permute-start(bf16[416,1024]{1,0:T(8,128)(2,1)S(1)} %maximum_select_fusion.5), channel_id=1, source_target_pairs={{0,2},{1,3},{2,0},{3,1},{4,6},{5,7},{6,4},{7,5},{8,10},{9,11},{10,... | collective-permute-start | bytes 2555912 | tf_op jit(solution)/shard_map/ppermute | solution.py:974
  516.1 20.7 %collective-permute-start.51 = (bf16[416,1024]{1,0:T(8,128)(2,1)S(1)}, bf16[416,1024]{1,0:T(8,128)(2,1)S(1)}, u32[]{:S(2)}, u32[]{:S(2)}) collective-permute-start(bf16[416,1024]{1,0:T(8,128)(2,1)S(1)} %maximum_select_fusion.6), channel_id=1, source_target_pairs={{0,4},{4,0},{8,12},{12,8},{16,20},{20,16},{24,28},{28,24},{1,5},{5... | collective-permute-start | bytes 2555912 | tf_op jit(solution)/shard_map/ppermute | solution.py:974
  (57 other events, 644.4 us)
Sparse Core Ops, SparseCore 0:
  35.0 80.9 all-gather.1
  382.5 61.0 reduce-scatter.1

commit v3 on v2

v3 whole, which is shorter than its diff:
```python
import functools

import jax
import jax.numpy as jnp
import numpy as np
from jax import lax
from jax.experimental import pallas as pl
from jax.experimental.pallas import tpu as pltpu
from jax.sharding import PartitionSpec as P

HEAD_DIM = 64
EPS = 1e-06
THETA = 10000.0
NEG = -1e30
LOG2E = 1.4426950408889634
NZ = 4
VMEM = 58 * 1024 * 1024
CORES = 2
F32 = jnp.float32
BF16 = jnp.bfloat16


def dot(a, b, ca, cb):
    return lax.dot_general(a, b, (((ca,), (cb,)), ((), ())), preferred_element_type=F32)


def params(semantics):
    return pltpu.CompilerParams(dimension_semantics=semantics, vmem_limit_bytes=VMEM)


COST = pl.CostEstimate(flops=1 << 20, bytes_accessed=1 << 20, transcendentals=0)


def cost(flops, nbytes):
    return pl.CostEstimate(flops=flops, bytes_accessed=nbytes, transcendentals=0)


def rope_constants(ctx_size, rows):
    half = HEAD_DIM // 2
    inv = THETA ** (-np.arange(half, dtype=np.float64) / half)
    fine = np.arange(rows, dtype=np.float64)[:, None] * inv[None, :]
    coarse = (rows * np.arange(ctx_size, dtype=np.float64))[:, None] * inv[None, :]
    tile = lambda t: jnp.asarray(np.tile(t, (1, 128 // half)).astype(np.float32))
    pad = np.zeros(((-2 * ctx_size) % 8, half))
    return (
        tile(np.concatenate([np.cos(fine), np.sin(fine)], 0)),
        tile(np.concatenate([np.cos(coarse), np.sin(coarse), pad], 0)),
    )


def swap_halves(x, roll):
    half = HEAD_DIM // 2
    width = x.shape[1]
    lane = lax.broadcasted_iota(jnp.int32, x.shape, 1)
    return jnp.where(lane % HEAD_DIM < half, roll(x, width - half), roll(x, half))


def prepare_body(experts, info_ref, len_ref, r_ref, c_ref, wg, wu, wd, ext_ref, sent_ref, buf, sem):
    rows, width = c_ref.shape
    ff = width // 2
    core = info_ref[0]
    count = len_ref[0] - info_ref[1] * rows
    pieces = [wg.at[core], wu.at[core]] + [wd.at[core, :, pl.ds(k * ff, ff)] for k in range(2)]
    spans = [pl.ds(0, width), pl.ds(width, width), pl.ds(2 * width, ff), pl.ds(2 * width + ff, ff)]
    into = [
        pltpu.make_async_copy(piece, buf.at[span], sem.at[0, k])
        for k, (piece, span) in enumerate(zip(pieces, spans))
    ]
    back = [
        pltpu.make_async_copy(buf.at[span], sent_ref.at[span], sem.at[1, k])
        for k, span in enumerate(spans)
    ]
    for copy in into:
        copy.start()
    row = lax.broadcasted_iota(jnp.int32, (rows, width), 0)
    ext_ref[:rows] = jnp.where(row < count, c_ref[...], jnp.zeros((), BF16))
    expert = lax.broadcasted_iota(jnp.int32, (experts, rows), 0)
    named = jnp.zeros((experts, rows), F32)
    for k in range(r_ref.shape[0]):
        named = jnp.where(expert == r_ref[k : k + 1, :], 1.0, named)
    ext_ref[rows:] = jnp.concatenate(
        [named, jnp.zeros((experts, width - rows), F32)], 1
    ).astype(BF16)
    for k in range(4):
        into[k].wait()
        back[k].start()
    for copy in back:
        copy.wait()


def prepare(facts, routes, cot, weights, experts):
    rows, width = cot.shape
    ff = width // 2
    anywhere = pl.BlockSpec(memory_space=pl.ANY)
    full = lambda shape: pl.BlockSpec(shape, lambda i, *s: (0, 0))
    return pl.pallas_call(
        functools.partial(prepare_body, experts),
        grid_spec=pltpu.PrefetchScalarGridSpec(
            num_scalar_prefetch=2,
            grid=(1,),
            in_specs=[full(routes.shape), full(cot.shape)] + [anywhere] * 3,
            out_specs=[full((rows + experts, width)), anywhere],
            scratch_shapes=[
                pltpu.VMEM((3 * width, ff), BF16),
                pltpu.SemaphoreType.DMA((2, 4)),
            ],
        ),
        out_shape=[
            jax.ShapeDtypeStruct((rows + experts, width), BF16),
            jax.ShapeDtypeStruct((3 * width, ff), BF16),
        ],
        compiler_params=params(("arbitrary",)),
        cost_estimate=COST,
        name="prepare",
    )(*facts, routes, cot, *weights)


def project_body(blocks, info_ref, len_ref, x_ref, gain_ref, wq_ref, wk_ref, wv_ref, fine_ref, start_ref,
                 n_ref, q_ref, kv_ref, cos_ref, sin_ref):
    step = pl.program_id(0)
    wide = q_ref.shape[1]
    nq = pl.num_programs(0) - 2
    rows = x_ref.shape[0]

    @pl.when(step == 0)
    def _():
        x = x_ref[...].astype(F32)
        scale = lax.rsqrt(jnp.mean(x * x, -1, keepdims=True) + EPS)
        n_ref[...] = (x * scale * gain_ref[...]).astype(BF16)
        cos_f, sin_f = fine_ref[:rows], fine_ref[rows:]
        cos_c = start_ref[pl.ds(info_ref[1], 1), :]
        sin_c = start_ref[pl.ds(info_ref[1] + blocks, 1), :]
        lane = lax.broadcasted_iota(jnp.int32, (rows, 128), 1)
        sign = jnp.where(lane % HEAD_DIM < HEAD_DIM // 2, -1.0, 1.0)
        cos_ref[...] = cos_f * cos_c - sin_f * sin_c
        sin_ref[...] = (sin_f * cos_c + cos_f * sin_c) * sign

    def rope(lin):
        cos = jnp.concatenate([cos_ref[...]] * (wide // 128), 1)
        sin = jnp.concatenate([sin_ref[...]] * (wide // 128), 1)
        return lin * cos + swap_halves(lin, lambda v, s: pltpu.roll(v, s, 1)) * sin

    @pl.when(step < nq)
    def _():
        lin = dot(n_ref[...], wq_ref[...], 1, 0)
        q_ref[...] = rope(lin).astype(BF16) * jnp.asarray(HEAD_DIM**-0.5, BF16)

    @pl.when(step == nq)
    def _():
        kv_ref[...] = rope(dot(n_ref[...], wk_ref[...], 1, 0)).astype(BF16)[None]

    @pl.when(step == nq + 1)
    def _():
        kv_ref[...] = dot(n_ref[...], wv_ref[...], 1, 0).astype(BF16)[None]


def project(facts, x, gain, wq, wk, wv, fine, starts, blocks):
    rows, width = x.shape
    kvw = wk.shape[1]
    nq = wq.shape[1] // kvw
    clip = lambda v, hi: jnp.minimum(jnp.maximum(v, 0), hi)
    full = lambda shape: pl.BlockSpec(shape, lambda i, *s: (0, 0))
    return pl.pallas_call(
        functools.partial(project_body, blocks),
        grid_spec=pltpu.PrefetchScalarGridSpec(
            num_scalar_prefetch=2,
            grid=(nq + 2,),
            in_specs=[
                full((rows, width)),
                full((1, width)),
                pl.BlockSpec((width, kvw), lambda i, *s: (0, clip(i, nq - 1))),
                full((width, kvw)),
                full((width, kvw)),
                full(fine.shape),
                full(starts.shape),
            ],
            out_specs=[
                full((rows, width)),
                pl.BlockSpec((rows, kvw), lambda i, *s: (0, clip(i, nq - 1))),
                pl.BlockSpec((1, rows, kvw), lambda i, *s: (clip(i - nq, 1), 0, 0)),
                full((rows, 128)),
                full((rows, 128)),
            ],
        ),
        out_shape=[
            jax.ShapeDtypeStruct((rows, width), BF16),
            jax.ShapeDtypeStruct((rows, wq.shape[1]), BF16),
            jax.ShapeDtypeStruct((2, rows, kvw), BF16),
            jax.ShapeDtypeStruct((rows, 128), F32),
            jax.ShapeDtypeStruct((rows, 128), F32),
        ],
        compiler_params=params(("arbitrary",)),
        cost_estimate=COST,
        name="project",
    )(*facts, x, gain, wq, wk, wv, fine, starts)


def split_heads(block):
    lane = lax.broadcasted_iota(jnp.int32, block.shape, 1)
    low = lane < HEAD_DIM
    zero = jnp.zeros_like(block)
    turned = jnp.concatenate([block[:, HEAD_DIM:], block[:, :HEAD_DIM]], 1)
    first = jnp.concatenate([jnp.where(low, block, zero), jnp.where(low, zero, turned)], 0)
    second = jnp.concatenate([jnp.where(low, turned, zero), jnp.where(low, zero, block)], 0)
    return first, second


def attend_blocks(info_ref, len_ref, base, q_ref, kv_refs, acc, top, low, diagonal):
    rows = q_ref.shape[0]
    seq_len = len_ref[0]
    key = lax.broadcasted_iota(jnp.int32, (rows, rows), 0)
    query = lax.broadcasted_iota(jnp.int32, (rows, rows), 1)

    for role in range(len(kv_refs)):
        start = info_ref[base + 2 * role]
        active = (info_ref[base + 2 * role + 1] > 0) & (start < seq_len)

        @pl.when(active)
        def _(role=role, start=start):
            keys = split_heads(kv_refs[role][0])
            values = split_heads(kv_refs[role][1])
            bad = key + start >= seq_len
            if diagonal and role == 0:
                bad = bad | (key > query)
            bias = jnp.where(bad, NEG, 0.0)
            for pair in range(2):
                q = q_ref[:, pair * 128 : pair * 128 + 128]
                scores = dot(keys[pair], q, 1, 1)
                weights, shrinks = [], []
                for head in range(2):
                    at = 2 * pair + head
                    part = scores[head * rows : (head + 1) * rows] * LOG2E + bias
                    old = top[0, at : at + 1, :]
                    new = jnp.maximum(old, jnp.max(part, 0, keepdims=True))
                    prob = jnp.exp2(part - new)
                    shrink = jnp.exp2(old - new)
                    top[0, at : at + 1, :] = new
                    fresh = jnp.sum(prob, 0, keepdims=True)
                    low[0, at : at + 1, :] = low[0, at : at + 1, :] * shrink + fresh
                    weights.append(prob.astype(BF16))
                    shrinks.append(jnp.broadcast_to(shrink, (HEAD_DIM, rows)))
                fresh = dot(values[pair], jnp.concatenate(weights, 0), 0, 0)
                acc[0, pair] = acc[0, pair] * jnp.concatenate(shrinks, 0) + fresh


def attend_start_body(base, roles, info_ref, len_ref, q_ref, *refs):
    acc, top, low = refs[roles:]
    acc[...] = jnp.zeros_like(acc)
    top[...] = jnp.full_like(top, NEG)
    low[...] = jnp.zeros_like(low)
    attend_blocks(info_ref, len_ref, base, q_ref, refs[:roles], acc, top, low, True)


def attend_finish_body(base, roles, info_ref, len_ref, q_ref, *refs):
    acc_in, top_in, low_in, wo_ref, x_ref, gain_ref = refs[roles : roles + 6]
    att_ref, lse_ref, hid_ref, mix_ref, acc, top, low, proj = refs[roles + 6 :]
    step = pl.program_id(0)
    rows = q_ref.shape[0]
    acc[...] = acc_in[...]
    top[...] = top_in[...]
    low[...] = low_in[...]
    attend_blocks(info_ref, len_ref, base, q_ref, refs[:roles], acc, top, low, False)
    for pair in range(2):
        sums = [low[0, 2 * pair + head : 2 * pair + head + 1, :] for head in range(2)]
        total = [jnp.broadcast_to(1.0 / s, (HEAD_DIM, rows)) for s in sums]
        att = acc[0, pair] * jnp.concatenate(total, 0)
        att_ref[:, pair * 128 : pair * 128 + 128] = jnp.transpose(att).astype(BF16)
    lse_ref[...] = top[...] + jnp.log2(jnp.maximum(low[...], 1e-30))

    @pl.when(step == 0)
    def _():
        proj[...] = x_ref[...].astype(F32)

    proj[...] += dot(att_ref[...], wo_ref[...], 1, 0)

    @pl.when(step == pl.num_programs(0) - 1)
    def _():
        hidden = proj[...]
        scale = lax.rsqrt(jnp.mean(hidden * hidden, -1, keepdims=True) + EPS)
        hid_ref[...] = hidden
        mix_ref[...] = (hidden * scale * gain_ref[...]).astype(BF16)


def attend(facts, base, q, blocks, state, wo=None, x=None, gain=None):
    rows, width = q.shape
    steps = width // 256
    roles = len(blocks)
    full = lambda shape: pl.BlockSpec(shape, lambda i, *s: (0, 0))
    wide = pl.BlockSpec((rows, 256), lambda i, *s: (0, i))
    heads = pl.BlockSpec((1, 8, rows), lambda i, *s: (i, 0, 0))
    accs = pl.BlockSpec((1, 2, 128, rows), lambda i, *s: (i, 0, 0, 0))
    in_specs = [wide] + [pl.BlockSpec((2, rows, 128), lambda i, *s: (0, 0, i))] * roles
    state_specs = [accs, heads, heads]
    state_shapes = [jax.ShapeDtypeStruct((steps, 2, 128, rows), F32)]
    state_shapes += [jax.ShapeDtypeStruct((steps, 8, rows), F32)] * 2
    args = [*facts, q, *blocks]
    scratch = []
    if state is None:
        body, out_specs, out_shape = attend_start_body, state_specs, state_shapes
    else:
        body = attend_finish_body
        args += [*state, wo, x, gain]
        in_specs += state_specs
        in_specs += [
            pl.BlockSpec((256, x.shape[1]), lambda i, *s: (i, 0)),
            full(x.shape),
            full((1, x.shape[1])),
        ]
        out_specs = [wide, heads, full(x.shape), full(x.shape)]
        out_shape = [
            jax.ShapeDtypeStruct((rows, width), BF16),
            jax.ShapeDtypeStruct((steps, 8, rows), F32),
            jax.ShapeDtypeStruct(x.shape, F32),
            jax.ShapeDtypeStruct(x.shape, BF16),
        ]
        scratch = [
            pltpu.VMEM((1, 2, 128, rows), F32),
            pltpu.VMEM((1, 8, rows), F32),
            pltpu.VMEM((1, 8, rows), F32),
            pltpu.VMEM(x.shape, F32),
        ]
    return pl.pallas_call(
        functools.partial(body, base, roles),
        grid_spec=pltpu.PrefetchScalarGridSpec(
            num_scalar_prefetch=2,
            grid=(steps,),
            in_specs=in_specs,
            out_specs=out_specs,
            scratch_shapes=scratch,
        ),
        out_shape=out_shape,
        compiler_params=params(("arbitrary",)),
        cost_estimate=COST,
        name="attend",
    )(*args)


def attend_back_body(base, roles, diagonal, info_ref, len_ref, q_ref, do_ref, lse_ref, delta_ref, *refs):
    kv_refs, (start_ref, dq_ref), dkv_refs = refs[:roles], refs[-roles - 2 : -roles], refs[-roles:]
    rows = q_ref.shape[0]
    seq_len = len_ref[0]
    if len(refs) > 2 * roles + 1:
        dq_ref[...] = start_ref[...]
    else:
        dq_ref[...] = jnp.zeros_like(dq_ref)
    key = lax.broadcasted_iota(jnp.int32, (rows, rows), 0)
    query = lax.broadcasted_iota(jnp.int32, (rows, rows), 1)
    lane = lax.broadcasted_iota(jnp.int32, (rows, 128), 1)
    low = lane < HEAD_DIM

    for role in range(roles):
        start = info_ref[base + 2 * role]
        active = (info_ref[base + 2 * role + 1] > 0) & (start < seq_len)

        @pl.when(jnp.logical_not(active))
        def _(role=role):
            dkv_refs[role][...] = jnp.zeros_like(dkv_refs[role])

        @pl.when(active)
        def _(role=role, start=start):
            keys = split_heads(kv_refs[role][0])
            values = split_heads(kv_refs[role][1])
            bad = key + start >= seq_len
            if diagonal and role == 0:
                bad = bad | (key > query)
            bias = jnp.where(bad, NEG, 0.0)
            dks, dvs = [], []
            for pair in range(2):
                q = q_ref[:, pair * 128 : pair * 128 + 128]
                do = do_ref[:, pair * 128 : pair * 128 + 128]
                scores = dot(keys[pair], q, 1, 1)
                grads = dot(values[pair], do, 1, 1)
                probs, raws = [], []
                for head in range(2):
                    at = 2 * pair + head
                    part = scores[head * rows : (head + 1) * rows] * LOG2E + bias
                    prob = jnp.exp2(part - lse_ref[0, at : at + 1, :])
                    grad = grads[head * rows : (head + 1) * rows]
                    raws.append((prob * (grad - delta_ref[0, at : at + 1, :])).astype(BF16))
                    probs.append(prob.astype(BF16))
                raw = jnp.concatenate(raws, 0)
                dq_ref[:, pair * 128 : pair * 128 + 128] += dot(raw, keys[pair], 0, 0)
                dks.append(dot(raw, q, 1, 0))
                dvs.append(dot(jnp.concatenate(probs, 0), do, 1, 0))
            for which, parts in enumerate((dks, dvs)):
                top_a, bottom_a = parts[0][:rows], parts[0][rows:]
                top_b, bottom_b = parts[1][:rows], parts[1][rows:]
                turn = pltpu.roll(jnp.where(low, top_b, bottom_a), HEAD_DIM, 1)
                whole = jnp.where(low, top_a, bottom_b) + turn
                dkv_refs[role][which] = whole.astype(dkv_refs[role].dtype)


def attend_back(facts, base, q, do, lse, delta, blocks, before, diagonal):
    rows, width = q.shape
    steps = width // 256
    roles = len(blocks)
    kvw = blocks[0].shape[2]
    wide = pl.BlockSpec((rows, 256), lambda i, *s: (0, i))
    heads = pl.BlockSpec((1, 8, rows), lambda i, *s: (i, 0, 0))
    kv = pl.BlockSpec((2, rows, 128), lambda i, *s: (0, 0, i))
    more = [] if before is None else [before]
    return pl.pallas_call(
        functools.partial(attend_back_body, base, roles, diagonal),
        grid_spec=pltpu.PrefetchScalarGridSpec(
            num_scalar_prefetch=2,
            grid=(steps,),
            in_specs=[wide, wide, heads, heads] + [kv] * roles + [wide] * len(more),
            out_specs=[wide] + [kv] * roles,
        ),
        out_shape=[jax.ShapeDtypeStruct((rows, width), F32)]
        + [jax.ShapeDtypeStruct((2, rows, kvw), BF16)] * roles,
        compiler_params=params(("arbitrary",)),
        cost_estimate=cost(40 * rows * rows * roles * width, 16 * 1024 * 1024),
        name="attend_back",
    )(*facts, q, do, lse, delta, *blocks, *more)


def expert_body(base, own, remotes, twins, first, carry, experts, info_ref, len_ref, *refs):
    x_refs, c_refs, wr_ref = refs[:twins], refs[twins : 2 * twins], refs[2 * twins]
    at = 2 * twins + 1
    near = refs[at : at + (3 if own else 0)]
    at += len(near)
    far = refs[at : at + remotes]
    at += remotes
    before, out_before = (refs[at], refs[at + 1]) if carry else (None, None)
    outs = refs[-15 if first else -13 :]
    gm_ref, gate_ref, out_ref, inner_ref, dg_ref, du_ref = outs[:6]
    copies = outs[6:8] if first else ()
    wbuf, sem, gm_acc, out_acc, gates, back, picked = outs[-7:]
    step = pl.program_id(0)
    total = own + remotes
    rows, width = x_refs[0].shape
    ff = width // 2
    slot = lax.rem(step, 2)
    offsets = (0, width, 2 * width, 2 * width + ff)
    sizes = (width, width, ff, ff)

    def fetch(target, where):
        def start(sources):
            for piece, (ref, off, size) in enumerate(zip(sources, offsets, sizes)):
                pltpu.make_async_copy(
                    ref, wbuf.at[where, pl.ds(off, size)], sem.at[where, piece]
                ).start()

        if own:

            @pl.when(target < own)
            def _():
                down = [near[2].at[target, :, pl.ds(k * ff, ff)] for k in range(2)]
                start([near[0].at[target], near[1].at[target]] + down)

        for i in range(remotes):

            @pl.when(target == own + i)
            def _(i=i):
                start([far[i].at[pl.ds(off, size)] for off, size in zip(offsets, sizes)])

    @pl.when(step == 0)
    def _():
        fetch(jnp.int32(0), 0)

    @pl.when(step + 1 < total)
    def _():
        fetch(step + 1, lax.rem(step + 1, 2))

    lane = lax.broadcasted_iota(jnp.int32, (rows, 128), 1)
    if twins == 2:
        x_ref, cot_ref = picked.at[0, pl.ds(0, rows)], picked.at[1]
    else:
        x_ref, cot_ref = x_refs[0], c_refs[0]

    @pl.when(step == 0)
    def _():
        if twins == 2:
            use = info_ref[base + 3] > 0
            picked[0, :rows] = jnp.where(use, x_refs[0][...], x_refs[1][...])
            picked[1] = jnp.where(use, c_refs[0][...], c_refs[1][...])
        logits = dot(x_ref[...], wr_ref[...], 1, 0)
        mask_t = cot_ref[pl.ds(rows, experts), :rows].astype(F32)
        mask_t = jnp.concatenate([mask_t, jnp.zeros((128 - experts, rows), F32)], 0)
        mask = jnp.transpose(mask_t) > 0.5
        high = jnp.max(jnp.where(mask, logits, NEG), 1, keepdims=True)
        raised = jnp.where(mask, jnp.exp(logits - high), 0.0)
        gates[...] = raised / jnp.sum(raised, 1, keepdims=True)
        gate_ref[...] = gates[...]
        back[...] = jnp.zeros_like(back)
        if carry:
            out_acc[...] = out_before[0].astype(F32)
            gm_acc[...] = before[:rows, :].astype(F32)
        else:
            out_acc[...] = jnp.zeros_like(out_acc)
            gm_acc[...] = jnp.zeros_like(gm_acc)
        if first:
            copies[0][0] = x_ref[...]
            copies[1][0] = cot_ref[pl.ds(0, rows), :]

    for piece, (off, size) in enumerate(zip(offsets, sizes)):
        place = wbuf.at[slot, pl.ds(off, size)]
        pltpu.make_async_copy(place, place, sem.at[slot, piece]).wait()

    wg = wbuf[slot, :width, :]
    wu = wbuf[slot, width : 2 * width, :]
    wd0 = wbuf[slot, 2 * width : 2 * width + ff, :]
    wd1 = wbuf[slot, 2 * width + ff :, :]
    which = info_ref[base + 2] + info_ref[base + 4 + step]
    x = x_ref[...]
    cot = cot_ref[pl.ds(0, rows), :]
    g = dot(x, wg, 1, 0)
    u = dot(x, wu, 1, 0)
    raw = dot(cot[:, :ff], wd0, 1, 1) + dot(cot[:, ff:], wd1, 1, 1)
    gate = jnp.sum(jnp.where(lane == which, gates[...], 0.0), 1, keepdims=True)
    sig = 1.0 / (1.0 + jnp.exp(-g))
    silu = g * sig
    inner = silu * u
    gg = jnp.sum(raw * inner, 1, keepdims=True)
    back[...] += jnp.where(lane == which, gg, 0.0)
    scaled = (gate * inner).astype(BF16)
    gi = gate * raw
    dg = (gi * u * (sig * (1.0 + g * (1.0 - sig)))).astype(BF16)
    du = (gi * silu).astype(BF16)
    inner_ref[0] = scaled
    dg_ref[0] = dg
    du_ref[0] = du
    out_acc[:, :ff] += dot(scaled, wd0, 1, 0)
    out_acc[:, ff:] += dot(scaled, wd1, 1, 0)
    gm_acc[...] += dot(dg, wg, 1, 1) + dot(du, wu, 1, 1)

    @pl.when(step == total - 1)
    def _():
        tail = jnp.transpose(back[...])[:experts, :]
        tail = jnp.concatenate([tail, jnp.zeros((experts, width - rows), F32)], 1)
        if carry:
            tail = tail + before[rows:, :].astype(F32)
        gm_ref[:rows, :] = gm_acc[...].astype(BF16)
        gm_ref[rows:, :] = tail.astype(BF16)
        out_ref[0] = out_acc[...].astype(BF16)


def expert_call(facts, base, xs, cots, wr, own_weights, far, experts, kept, before=None):
    rows, width = xs[0].shape
    own = own_weights[0].shape[0] if own_weights else 0
    remotes = len(far)
    total = own + remotes
    twins = len(xs)
    carry = before is not None
    first = not carry
    ff = width // 2
    full = lambda shape: pl.BlockSpec(shape, lambda i, *s: (0,) * len(shape))
    anywhere = pl.BlockSpec(memory_space=pl.ANY)
    big = pl.BlockSpec((1, rows, width), lambda i, s, n: (s[base + 1], 0, 0))
    part = pl.BlockSpec((1, rows, ff), lambda i, s, n: (s[base + 1], 0, s[base + 4 + i]))
    count = 6 if first else 4
    fresh = isinstance(kept[0], jax.ShapeDtypeStruct)
    aliased = [] if fresh else list(kept[:count])
    inputs = [*xs, *cots, wr, *own_weights, *far] + ([before] if carry else [])
    specs = [full((rows, width))] * twins + [full(cots[0].shape)] * twins + [full(wr.shape)]
    specs += [anywhere] * (len(own_weights) + remotes)
    specs += [full(before.shape)] if carry else []
    specs += [big if carry and k == 0 else anywhere for k in range(len(aliased))]
    gm_shape = (rows + experts, width)
    outs = pl.pallas_call(
        functools.partial(expert_body, base, own, remotes, twins, first, carry, experts),
        grid_spec=pltpu.PrefetchScalarGridSpec(
            num_scalar_prefetch=2,
            grid=(total,),
            in_specs=specs,
            out_specs=[full(gm_shape), full((rows, 128)), big, part, part, part]
            + ([big, big] if first else []),
            scratch_shapes=[
                pltpu.VMEM((2, 3 * width, ff), BF16),
                pltpu.SemaphoreType.DMA((2, 4)),
                pltpu.VMEM((rows, width), F32),
                pltpu.VMEM((rows, width), F32),
                pltpu.VMEM((rows, 128), F32),
                pltpu.VMEM((rows, 128), F32),
                pltpu.VMEM((2,) + gm_shape, BF16),
            ],
        ),
        out_shape=[
            jax.ShapeDtypeStruct(gm_shape, BF16),
            jax.ShapeDtypeStruct((rows, 128), F32),
        ]
        + [jax.ShapeDtypeStruct(k.shape, k.dtype) for k in kept[:count]],
        input_output_aliases={2 + len(inputs) + k: 2 + k for k in range(len(aliased))},
        compiler_params=params(("arbitrary",)),
        cost_estimate=COST
        if not far
        else cost(12 * rows * width * ff * total, total * 6 * width * ff),
        name="experts",
    )(*facts, *inputs, *aliased)
    return outs[0], outs[1], tuple(outs[2:]) + tuple(kept[count:])


def expert_grads_body(base, info_ref, len_ref, x_hbm, c_hbm, in_hbm, dg_hbm, du_hbm, o_ref, x, c, cols, sem):
    place, kind = pl.program_id(0), pl.program_id(1)
    step = place * 3 + kind
    ff = cols.shape[2]
    hidden = (dg_hbm, du_hbm, in_hbm)

    def fetch(target, start):
        at = lax.rem(target, 2)
        off = pl.ds(pl.multiple_of(info_ref[base + lax.div(target, 3)] * ff, 128), ff)
        for k, ref in enumerate(hidden):

            @pl.when(lax.rem(target, 3) == k)
            def _(ref=ref):
                pltpu.make_async_copy(ref.at[:, off], cols.at[at], sem.at[at]).start()

    @pl.when(step == 0)
    def _():
        pltpu.make_async_copy(x_hbm, x, sem.at[2]).start()
        fetch(step, True)
        pltpu.make_async_copy(c_hbm, c, sem.at[3]).start()
        pltpu.make_async_copy(x_hbm, x, sem.at[2]).wait()

    @pl.when(step + 1 < 3 * pl.num_programs(0))
    def _():
        fetch(step + 1, True)

    slot = lax.rem(step, 2)
    pltpu.make_async_copy(cols.at[slot], cols.at[slot], sem.at[slot]).wait()

    @pl.when(kind < 2)
    def _():
        o_ref[0, 0] = dot(x[...], cols[slot], 0, 0).astype(BF16)

    @pl.when(step == 2)
    def _():
        pltpu.make_async_copy(c_hbm, c, sem.at[3]).wait()

    @pl.when(kind == 2)
    def _():
        o_ref[0, 0, :ff] = dot(cols[slot], c[:, :ff], 0, 0).astype(BF16)
        o_ref[0, 0, ff:] = dot(cols[slot], c[:, ff:], 0, 0).astype(BF16)


def expert_grads(facts, base, count, x, c, inner, dg, du):
    rows, width = x.shape
    ff = width // 2
    anywhere = pl.BlockSpec(memory_space=pl.ANY)
    return pl.pallas_call(
        functools.partial(expert_grads_body, base),
        grid_spec=pltpu.PrefetchScalarGridSpec(
            num_scalar_prefetch=2,
            grid=(count, 3),
            in_specs=[anywhere] * 5,
            out_specs=pl.BlockSpec((1, 1, width, ff), lambda i, k, *s: (i, k, 0, 0)),
            scratch_shapes=[
                pltpu.VMEM((rows, width), BF16),
                pltpu.VMEM((rows, width), BF16),
                pltpu.VMEM((2, rows, ff), BF16),
                pltpu.SemaphoreType.DMA((4,)),
            ],
        ),
        out_shape=jax.ShapeDtypeStruct((count, 3, width, ff), BF16),
        compiler_params=params(("arbitrary",) * 2),
        cost_estimate=cost(6 * rows * width * ff * count, 16 * 1024 * 1024),
        name="expert_grads",
    )(*facts, x, c, inner, dg, du)


def middle_body(experts, *refs):
    sums, ends, refs = refs[:4], refs[4:8], refs[8:]
    gate_ref, wr_ref, hid_ref, cot_ref, att_ref, mix_ref, gain_ref, wo_hbm = refs[:8]
    gh_ref, gb_ref, do_ref, delta_ref, ffn_ref, router_ref, wo, sem, deltas, logit = refs[8:]
    step = pl.program_id(0)
    part, width = hid_ref.shape
    rows = gate_ref.shape[0]
    span = pl.ds(pl.multiple_of(step * part, part), part)

    @pl.when(step == 0)
    def _():
        pltpu.make_async_copy(wo_hbm, wo, sem).start()
        ffn_ref[...] = jnp.zeros_like(ffn_ref)
        router_ref[...] = jnp.zeros_like(router_ref)
        gg = ends[0][:, :rows].astype(F32)
        for ref in ends[1:]:
            gg = gg + ref[:, :rows].astype(F32)
        gg = jnp.transpose(jnp.concatenate([gg, jnp.zeros((128 - experts, rows), F32)], 0))
        gates = gate_ref[...]
        logit[...] = (gates * (gg - jnp.sum(gates * gg, 1, keepdims=True))).astype(BF16)

    total = sums[0][...].astype(F32)
    for ref in sums[1:]:
        total = total + ref[...].astype(F32)
    gl = logit[span, :]
    router_ref[...] += dot(gl, mix_ref[...], 0, 0)
    hidden = hid_ref[...]
    grad_mixed = total + dot(gl, wr_ref[...], 1, 1)
    scale = lax.rsqrt(jnp.mean(hidden * hidden, -1, keepdims=True) + EPS)
    ffn_ref[...] += jnp.sum(grad_mixed * hidden * scale, 0, keepdims=True)
    weighted = grad_mixed * gain_ref[...]
    mean = jnp.mean(weighted * hidden, -1, keepdims=True)
    grad = cot_ref[...].astype(F32) + scale * weighted - hidden * (scale * scale * scale * mean)
    gh_ref[...] = grad
    low = grad.astype(BF16)
    gb_ref[...] = low

    @pl.when(step == 0)
    def _():
        pltpu.make_async_copy(wo_hbm, wo, sem).wait()

    do = dot(low, wo[...], 1, 1).astype(BF16)
    do_ref[...] = do
    both = do.astype(F32) * att_ref[...].astype(F32)
    lane = lax.broadcasted_iota(jnp.int32, (part, 128), 1)
    found = jnp.zeros((part, 128), F32)
    for block in range(both.shape[1] // 128):
        pair = both[:, block * 128 : block * 128 + 128]
        front = jnp.sum(jnp.where(lane < HEAD_DIM, pair, 0.0), 1, keepdims=True)
        back = jnp.sum(jnp.where(lane < HEAD_DIM, 0.0, pair), 1, keepdims=True)
        found = jnp.where(lane == 2 * block, front, found)
        found = jnp.where(lane == 2 * block + 1, back, found)
    deltas[span, :] = found

    @pl.when(step == pl.num_programs(0) - 1)
    def _():
        turned = jnp.transpose(deltas[...])
        for group in range(delta_ref.shape[0]):
            delta_ref[group, :4, :] = turned[4 * group : 4 * group + 4]
            delta_ref[group, 4:, :] = jnp.zeros((4, rows), F32)


def middle(sums, gates, wr, hidden, cot_ext, attended, mixed, gain, wo, experts):
    rows, width = hidden.shape
    steps = 3
    heads = attended.shape[1] // HEAD_DIM
    row = lambda w: pl.BlockSpec((rows // steps, w), lambda i: (i, 0))
    end = pl.BlockSpec((experts, width), lambda i: (rows // experts, 0))
    full = lambda shape: pl.BlockSpec(shape, lambda i: (0,) * len(shape))
    return pl.pallas_call(
        functools.partial(middle_body, experts),
        grid=(steps,),
        in_specs=[row(width)] * 4
        + [end] * 4
        + [
            full((rows, 128)),
            full(wr.shape),
            row(width),
            row(width),
            row(attended.shape[1]),
            row(width),
            full((1, width)),
            pl.BlockSpec(memory_space=pl.ANY),
        ],
        out_specs=[
            row(width),
            row(width),
            row(attended.shape[1]),
            full((heads // 4, 8, rows)),
            full((1, width)),
            full((128, width)),
        ],
        out_shape=[
            jax.ShapeDtypeStruct((rows, width), F32),
            jax.ShapeDtypeStruct((rows, width), BF16),
            jax.ShapeDtypeStruct(attended.shape, BF16),
            jax.ShapeDtypeStruct((heads // 4, 8, rows), F32),
            jax.ShapeDtypeStruct((1, width), F32),
            jax.ShapeDtypeStruct((128, width), F32),
        ],
        scratch_shapes=[
            pltpu.VMEM(wo.shape, BF16),
            pltpu.SemaphoreType.DMA(()),
            pltpu.VMEM((rows, 128), F32),
            pltpu.VMEM((rows, 128), BF16),
        ],
        compiler_params=params(("arbitrary",)),
        cost_estimate=COST,
        name="middle",
    )(*sums, *sums, gates, wr, hidden, cot_ext, attended, mixed, gain, wo)


def early_body(experts, info_ref, len_ref, att_ref, gb_ref, router_ref, ffn_ref, give_ref, keep_ref):
    size = att_ref.shape[1] // 2
    core = info_ref[0]
    width = gb_ref.shape[1]
    row = lax.broadcasted_iota(jnp.int32, (16, width), 0)
    extra = jnp.concatenate([router_ref[:experts], jnp.where(row == 0, ffn_ref[...], 0.0)], 0)
    for ref, half in ((keep_ref, core), (give_ref, 1 - core)):
        part = att_ref[:, pl.ds(pl.multiple_of(half * size, 128), size)]
        ref[:size] = dot(part, gb_ref[...], 0, 0).astype(BF16)
        ref[size : size + experts + 16] = jnp.where(half == 0, extra, 0.0).astype(BF16)
        rest = ref.shape[0] - (size + experts + 16)
        ref[size + experts + 16 :] = jnp.zeros((rest, width), BF16)


def early_grads(facts, attended, gb, router, ffn, experts):
    rows, width = gb.shape
    count = attended.shape[1]
    col = lambda r: pl.BlockSpec((r, 256), lambda i, *s: (0, i))
    size = count // 2 + count // 8
    return pl.pallas_call(
        functools.partial(early_body, experts),
        grid_spec=pltpu.PrefetchScalarGridSpec(
            num_scalar_prefetch=2,
            grid=(width // 256,),
            in_specs=[
                pl.BlockSpec(attended.shape, lambda i, *s: (0, 0)),
                col(rows),
                col(router.shape[0]),
                col(1),
            ],
            out_specs=[col(size)] * 2,
        ),
        out_shape=[jax.ShapeDtypeStruct((size, width), BF16)] * 2,
        compiler_params=params(("arbitrary",)),
        cost_estimate=COST,
        name="early_grads",
    )(*facts, attended, gb, router, ffn)


def rope_back(g, cos_ref, sin_ref):
    cos = jnp.concatenate([cos_ref[...]] * (g.shape[1] // 128), 1)
    sin = jnp.concatenate([sin_ref[...]] * (g.shape[1] // 128), 1)
    return g * cos - swap_halves(g, lambda v, s: pltpu.roll(v, s, 1)) * sin


def split_rows(core, n_ref, lin, give_ref, keep_ref):
    size = n_ref.shape[1] // 2
    for ref, half in ((give_ref, 1 - core), (keep_ref, core)):
        part = n_ref[:, pl.ds(pl.multiple_of(half * size, 128), size)]
        ref[...] = dot(part, lin, 0, 0).astype(BF16)


def query_back_body(info_ref, len_ref, dq_ref, n_ref, cos_ref, sin_ref, lin_ref, give_ref, keep_ref):
    lin = rope_back(dq_ref[...] * HEAD_DIM**-0.5, cos_ref, sin_ref).astype(BF16)
    lin_ref[...] = lin
    split_rows(info_ref[0], n_ref, lin, give_ref, keep_ref)


def query_back(facts, dq, normed, cos, sin):
    rows, width = dq.shape
    col = lambda r: pl.BlockSpec((r, 256), lambda i, *s: (0, i))
    full = lambda shape: pl.BlockSpec(shape, lambda i, *s: (0, 0))
    size = normed.shape[1] // 2
    return pl.pallas_call(
        query_back_body,
        grid_spec=pltpu.PrefetchScalarGridSpec(
            num_scalar_prefetch=2,
            grid=(width // 256,),
            in_specs=[col(rows), full(normed.shape), full(cos.shape), full(sin.shape)],
            out_specs=[col(rows), col(size), col(size)],
        ),
        out_shape=[
            jax.ShapeDtypeStruct((rows, width), BF16),
            jax.ShapeDtypeStruct((size, width), BF16),
            jax.ShapeDtypeStruct((size, width), BF16),
        ],
        compiler_params=params(("arbitrary",)),
        cost_estimate=cost(2 * rows * width * width, 8 * 1024 * 1024),
        name="query_back",
    )(*facts, dq, normed, cos, sin)


def pair_back_body(parts, half_steps, info_ref, len_ref, *refs):
    n_ref, cos_ref, sin_ref, lin_ref, give_ref, keep_ref = refs[parts:]
    step = pl.program_id(0)
    total = refs[0][0].astype(F32)
    for ref in refs[1:parts]:
        total = total + ref[0].astype(F32)

    @pl.when(step < half_steps)
    def _():
        lin_ref[...] = rope_back(total, cos_ref, sin_ref).astype(BF16)

    @pl.when(step >= half_steps)
    def _():
        lin_ref[...] = total.astype(BF16)

    split_rows(info_ref[0], n_ref, lin_ref[...], give_ref, keep_ref)


def pair_back(facts, parts, normed, cos, sin):
    _, rows, kvw = parts[0].shape
    half_steps = kvw // 256
    col = lambda r: pl.BlockSpec((r, 256), lambda i, *s: (0, i))
    full = lambda shape: pl.BlockSpec(shape, lambda i, *s: (0, 0))
    part = pl.BlockSpec((1, rows, 256), lambda i, *s: (i // half_steps, 0, i % half_steps))
    size = normed.shape[1] // 2
    return pl.pallas_call(
        functools.partial(pair_back_body, len(parts), half_steps),
        grid_spec=pltpu.PrefetchScalarGridSpec(
            num_scalar_prefetch=2,
            grid=(2 * half_steps,),
            in_specs=[part] * len(parts) + [full(normed.shape), full(cos.shape), full(sin.shape)],
            out_specs=[col(rows), col(size), col(size)],
        ),
        out_shape=[
            jax.ShapeDtypeStruct((rows, 2 * kvw), BF16),
            jax.ShapeDtypeStruct((size, 2 * kvw), BF16),
            jax.ShapeDtypeStruct((size, 2 * kvw), BF16),
        ],
        compiler_params=params(("arbitrary",)),
        cost_estimate=COST,
        name="pair_back",
    )(*facts, *parts, normed, cos, sin)


def tokens_back_body(lq_ref, lkv_ref, wq_ref, wk_ref, wv_ref, x_ref, gh_ref, gain_ref, o_ref):
    kvw = wk_ref.shape[1]
    grad = dot(lq_ref[...], wq_ref[...], 1, 1)
    grad = grad + dot(lkv_ref[:, :kvw], wk_ref[...], 1, 1)
    grad = grad + dot(lkv_ref[:, kvw:], wv_ref[...], 1, 1)
    x = x_ref[...].astype(F32)
    scale = lax.rsqrt(jnp.mean(x * x, -1, keepdims=True) + EPS)
    weighted = grad * gain_ref[...]
    mean = jnp.mean(weighted * x, -1, keepdims=True)
    total = gh_ref[...] + scale * weighted - x * (scale * scale * scale * mean)
    o_ref[...] = total.astype(BF16)


def tokens_back(lq, lkv, wq, wk, wv, x, gh, gain):
    rows, width = x.shape
    row = lambda w: pl.BlockSpec((rows // 4, w), lambda i: (i, 0))
    full = lambda shape: pl.BlockSpec(shape, lambda i: (0, 0))
    return pl.pallas_call(
        tokens_back_body,
        grid=(4,),
        in_specs=[
            row(lq.shape[1]),
            row(lkv.shape[1]),
            full(wq.shape),
            full(wk.shape),
            full(wv.shape),
            row(width),
            row(width),
            full((1, width)),
        ],
        out_specs=row(width),
        out_shape=jax.ShapeDtypeStruct((rows, width), BF16),
        compiler_params=params(("arbitrary",)),
        cost_estimate=COST,
        name="tokens_back",
    )(lq, lkv, wq, wk, wv, x, gh, gain)


def finish_body(info_ref, len_ref, qa, qb, pa, pb, wq_ref, wk_ref, wv_ref, gain_ref, q_ref, k_ref, v_ref, n_ref):
    mine = pl.program_id(0) // (pl.num_programs(0) // 2) == info_ref[0]
    q = jnp.where(mine, qa[...].astype(F32), qb[...].astype(F32))
    pair = jnp.where(mine, pa[...].astype(F32), pb[...].astype(F32))
    kvw = k_ref.shape[1]
    q_ref[...] = q
    k_ref[...] = pair[:, :kvw]
    v_ref[...] = pair[:, kvw:]
    gain = jnp.sum(q * wq_ref[...].astype(F32), 1, keepdims=True)
    gain = gain + jnp.sum(pair[:, :kvw] * wk_ref[...].astype(F32), 1, keepdims=True)
    gain = gain + jnp.sum(pair[:, kvw:] * wv_ref[...].astype(F32), 1, keepdims=True)
    turned = jnp.transpose(jnp.broadcast_to(gain, (gain.shape[0], 128)))
    n_ref[...] = turned[:1] / gain_ref[...]


def finish(facts, qa, qb, pa, pb, wq, wk, wv, gain):
    width = wq.shape[0]
    part = width // 4
    half = lambda w: pl.BlockSpec((part, w), lambda i, *s: (i % 2, 0))
    row = lambda w: pl.BlockSpec((part, w), lambda i, *s: (i, 0))
    line = pl.BlockSpec((1, part), lambda i, *s: (0, i))
    return pl.pallas_call(
        finish_body,
        grid_spec=pltpu.PrefetchScalarGridSpec(
            num_scalar_prefetch=2,
            grid=(4,),
            in_specs=[half(width)] * 4
            + [row(wq.shape[1]), row(wk.shape[1]), row(wv.shape[1]), line],
            out_specs=[row(wq.shape[1]), row(wk.shape[1]), row(wv.shape[1]), line],
        ),
        out_shape=[
            jax.ShapeDtypeStruct(wq.shape, F32),
            jax.ShapeDtypeStruct(wk.shape, F32),
            jax.ShapeDtypeStruct(wv.shape, F32),
            jax.ShapeDtypeStruct((1, width), F32),
        ],
        compiler_params=params(("arbitrary",)),
        cost_estimate=COST,
        name="finish",
    )(*facts, qa, qb, pa, pb, wq, wk, wv, gain)


def total_of(parts):
    total = parts[0].astype(F32)
    for part in parts[1:]:
        total = total + part.astype(F32)
    return total.astype(BF16)


def scatter_start(buf, axis):
    name, size, pos, pairs = axis
    rows = buf.shape[0] // size
    take = lambda k: lax.dynamic_slice_in_dim(buf, k * rows, rows, 0)
    parts = [take(pos)]
    for shift in range(1, size):
        parts.append(lax.ppermute(take((pos + shift) % size), name, pairs(shift)))
    return parts


def gather_start(buf, axis):
    name, size, pos, pairs = axis
    return [lax.ppermute(buf, name, pairs(shift)) for shift in range(size - 1, 0, -1)] + [buf]


def gather_end(order, axis):
    name, size, pos, pairs = axis
    rows = order[0].shape[0]
    if size == 2:
        pick = lambda a, b: jnp.concatenate([a, b], 0)
        return jnp.where(pos == 0, pick(order[1], order[0]), pick(order[0], order[1]))
    double = jnp.concatenate(order + order[:-1], 0)
    return lax.dynamic_slice_in_dim(double, (size - 1 - pos) * rows, size * rows, 0)


def device_facts(nx, ny, own, rows, ep_index, ctx_index):
    group = nx * own
    table = np.zeros((NZ * nx, ny * CORES, 160), np.int32)
    for ep in range(NZ * nx):
        for ctx in range(ny * CORES):
            z, x, y, core = ep // nx, ep % nx, ctx // CORES, ctx % CORES
            out = table[ep, ctx]
            out[0], out[1] = core, ctx
            out[16:20] = ctx * rows, 1, (ctx - 1) * rows, core
            for back in range(1, ny):
                at, block = 16 + 4 * back, (y - back) * CORES
                out[at : at + 4] = (block + core) * rows, y >= back, (block + 1 - core) * rows, y >= back
            near = [x * own + i for i in range(own)]
            far = [(x - s) % nx * own + i for s in range(1, nx) for i in (core, 1 - core)]
            shard_c, shard_d, inside = (2, 2, 1, 1)[z], (3, 3, 0, 0)[z], int(z in (1, 2))
            calls = [(z, 1, near), (z, 1, far), (z ^ 1, 1, near + far)]
            calls += [(shard_c, inside, near + far), (shard_d, inside, near + far)]
            for k, (shard, pick, places) in enumerate(calls):
                out[48 + 16 * k : 52 + 16 * k] = 0, shard, z * group, pick
                out[52 + 16 * k : 52 + 16 * k + len(places)] = places
            for j in range(nx):
                out[128 + j] = (x + j) % nx * own + 1 - core
                out[144 + j] = (x + j) % nx * own + core
    line = lax.dynamic_slice(
        jnp.asarray(table), (ep_index, ctx_index, jnp.int32(0)), (1, 1, table.shape[2])
    )
    return line.reshape(-1)


def local(
    tokens,
    lengths,
    routes,
    cotangent,
    attn_norm,
    w_query,
    w_key,
    w_value,
    w_out,
    ffn_norm,
    w_router,
    expert_gate_weight,
    expert_up_weight,
    expert_down_weight,
):
    rows, width = tokens.shape[1:]
    half = rows // 2
    experts = w_router.shape[1]
    own = expert_gate_weight.shape[0]
    ff = expert_gate_weight.shape[2]
    kvw = w_key.shape[1]
    ctx_size, ep_size = lax.axis_size("ctx"), lax.axis_size("ep")
    ny, nx = ctx_size // CORES, ep_size // NZ
    ctx_index, ep_index = lax.axis_index("ctx"), lax.axis_index("ep")
    y, core = ctx_index // CORES, ctx_index % CORES
    z, xpos = ep_index // nx, ep_index % nx
    seq_len = lengths[0]
    tokens = tokens[0]
    valid_flag = ctx_index * rows + jnp.arange(rows, dtype=jnp.int32) < seq_len
    valid = valid_flag.astype(F32)[:, None]
    tie = lax.optimization_barrier

    core_swap = [(c, c ^ 1) for c in range(ctx_size)]
    core_up = [(c, c + 1) for c in range(0, ctx_size, CORES)]
    core_down = [(c + 1, c) for c in range(0, ctx_size, CORES)]
    y_up = lambda k: [(c, c + CORES * k) for c in range(ctx_size - CORES * k)]
    y_down = lambda k: [(b, a) for a, b in y_up(k)]
    zx = lambda pairs: [(a * nx + i, b * nx + i) for a, b in pairs for i in range(nx)]
    z_groups = [[i + nx * k for k in range(NZ)] for i in range(nx)]
    x_shift = lambda s: [(k * nx + i, k * nx + (i + s) % nx) for k in range(NZ) for i in range(nx)]
    y_ring = lambda s: [(c, (c + CORES * s) % ctx_size) for c in range(ctx_size)]
    core_axis = ("ctx", CORES, core, lambda s: core_swap)
    y_axis = ("ctx", ny, y, y_ring)
    x_axis = ("ep", nx, xpos, x_shift)
    z_axis = ("ep", NZ, z, lambda s: zx([(k, (k + s) % NZ) for k in range(NZ)]))

    weights = (expert_gate_weight, expert_up_weight, expert_down_weight)
    facts = (device_facts(nx, ny, own, rows, ep_index, ctx_index), lengths)
    cot_ext, sent = prepare(facts, routes[0].T, cotangent[0], weights, experts)
    arrived = [lax.ppermute(sent, "ep", x_shift(shift)) for shift in range(1, nx)]

    swap, mid, out = [(0, 1), (1, 0), (2, 3), (3, 2)], [(1, 2), (2, 1)], [(1, 0), (2, 3)]
    cot_near = lax.ppermute(cot_ext, "ep", zx(swap))
    cot_middle = lax.ppermute(cot_ext, "ep", zx(mid))
    tokens, cot_ext, sent = tie((tokens, cot_ext, sent))
    fine, starts = rope_constants(ctx_size, rows)
    normed, q, kv, cos, sin = project(
        facts, tokens, attn_norm[None], w_query, w_key, w_value, fine, starts, ctx_size
    )

    blocks = [kv, lax.ppermute(kv, "ctx", core_up)]
    travelling = kv
    for back in range(1, ny):
        travelling = lax.ppermute(travelling, "ctx", y_up(1))
        blocks.append(travelling)
    near_row, far_row = 16, 20
    state = attend(facts, near_row, q, blocks[:2], None)
    came, state, cot_near, cot_middle = tie((blocks[2:], state, cot_near, cot_middle))
    cot_across = lax.ppermute(cot_near, "ep", zx(mid))
    cot_outward = lax.ppermute(cot_middle, "ep", zx(out))
    blocks = blocks[:2]
    for piece in came:
        blocks += [piece, lax.ppermute(piece, "ctx", core_swap)]
    attended, lse, hidden, mixed = attend(
        facts, far_row, q, blocks[2:], state, w_out, tokens, ffn_norm[None]
    )

    wr = jnp.pad(w_router, ((0, 0), (0, 128 - experts)))
    group = nx * own
    widths = (width, group * ff, group * ff, group * ff, width, width)
    kept = tuple(jax.ShapeDtypeStruct((NZ, rows, w), BF16) for w in widths)

    def run(call, data, cots, near, far, kept, before=None):
        return expert_call(
            facts, 48 + 16 * call, data, cots, wr, near, far, experts, kept, before
        )

    ends, away = [(0, 1), (3, 2)], [(2, 3), (1, 0)]
    near = lax.ppermute(mixed, "ep", zx(swap))
    middle_rows = lax.ppermute(mixed, "ep", zx(mid))
    mixed, cot_across, cot_outward = tie((mixed, cot_across, cot_outward))
    gm_a, gates, kept = run(0, (mixed,), (cot_ext,), weights, [], kept)
    near, middle_rows, arrived, kept = tie((near, middle_rows, arrived, kept))
    across = lax.ppermute(near, "ep", zx(mid))
    outward = lax.ppermute(middle_rows, "ep", zx(out))
    far = []
    for piece in arrived:
        far += [piece, lax.ppermute(piece, "ctx", core_swap)]
    gm_a, _, kept = run(1, (mixed,), (cot_ext,), (), far, kept, gm_a)
    across, outward, kept = tie((across, outward, kept))
    last = lax.ppermute(across, "ep", zx(out))
    gm_b, _, kept = run(2, (near,), (cot_near,), weights, far, kept)
    third = lax.ppermute(gm_b, "ep", zx(ends))
    last, kept, cot_across = tie((last, kept, cot_across))
    cot_last = lax.ppermute(cot_across, "ep", zx(out))
    cots = (cot_middle, cot_outward)
    gm_c, _, kept = run(3, (middle_rows, outward), cots, weights, far, kept)
    second = lax.ppermute(gm_c, "ep", zx(ends))
    third, cot_last, kept = tie((third, cot_last, kept))
    cots = (cot_across, cot_last)
    gm_d, _, kept = run(4, (across, last), cots, weights, far, kept)
    first = lax.ppermute(gm_d, "ep", zx(ends))

    add = lambda a, b: (a.astype(F32) + b.astype(F32)).astype(BF16)
    line = lambda a: a.reshape(NZ * rows, a.shape[2])
    saved = lambda kept: [line(kept[k]) for k in (4, 5, 1, 2, 3)]
    second, kept = tie((second, kept))
    turned = lax.ppermute(add(gm_c, second), "ep", zx(mid))
    give = expert_grads(facts, 128, nx, *saved(kept))
    first, turned, give, kept = tie((first, turned, give, kept))
    carried = lax.ppermute(add(gm_d, first), "ep", zx(mid))
    came = lax.ppermute(give, "ctx", core_swap)
    keep = expert_grads(facts, 144, nx, *saved(kept))
    carried, keep, came = tie((carried, keep, came))
    send, keep, came = tie((add(gm_b, carried), keep, came))
    final = lax.ppermute(send, "ep", zx(away))
    total = [[add(keep[j, 0], came[j, 0]) for j in range(nx)]]
    total, keep, came = tie((total, keep, came))
    total += [[add(keep[j, k], came[j, k]) for j in range(nx)] for k in (1, 2)]
    over_x = lambda k: [lax.ppermute(total[k][s], "ep", x_shift(s)) for s in range(1, nx)]
    x_came = [over_x(0)]

    sums = [gm_a, third, turned, final]
    gh, gb, do, delta, grad_ffn, grad_router = middle(
        sums, gates, wr, hidden, cot_ext, attended, mixed, ffn_norm[None], w_out, experts
    )
    give, early = early_grads(facts, attended, gb, grad_router, grad_ffn, experts)
    give, early, do, x_came, out_all = tie((give, early, do, x_came, kept[0]))
    expert_sum = lax.psum_scatter(
        line(out_all), "ep", scatter_dimension=0, axis_index_groups=z_groups, tiled=True
    )

    y_parts = [scatter_start(total_of([total[0][0]] + x_came[0]), y_axis)]
    x_came.append(over_x(1))
    early = [early, lax.ppermute(give, "ctx", core_swap)]
    dq = None
    far_dkv = []
    if ny > 1:
        dq, *far_dkv = attend_back(facts, far_row, q, do, lse, delta, blocks[2:], None, False)
    dq, far_dkv, y_parts, x_came, early = tie((dq, far_dkv, y_parts, x_came, early))

    homeward = [
        lax.ppermute(add(far_dkv[2 * k], lax.ppermute(far_dkv[2 * k + 1], "ctx", core_swap)), "ctx", y_down(k + 1))
        for k in range(ny - 1)
    ]
    x_came.append(over_x(2))
    early = total_of(early)
    dq, *near_dkv = attend_back(facts, near_row, q, do, lse, delta, blocks[:2], dq, True)
    dq, homeward, x_came, near_dkv, early = tie((dq, homeward, x_came, near_dkv, early))

    parts = [near_dkv[0], lax.ppermute(near_dkv[1], "ctx", core_down), *homeward]
    y_parts.append(scatter_start(total_of([total[1][0]] + x_came[1]), y_axis))
    early = scatter_start(early, x_axis)
    lin_q, give, keep = query_back(facts, dq, normed, cos, sin)
    parts, lin_q, give, keep = tie((parts, lin_q, give, keep))

    half_q = [keep, lax.ppermute(give, "ctx", core_swap)]
    lin_kv, give, keep = pair_back(facts, parts, normed, cos, sin)
    half_q, lin_kv, give, keep, y_parts, early, expert_sum = tie(
        (half_q, lin_kv, give, keep, y_parts, early, expert_sum)
    )

    half_kv = [keep, lax.ppermute(give, "ctx", core_swap)]
    one = scatter_start(total_of(half_q), y_axis)
    two = scatter_start(total_of(half_kv), x_axis)
    early = scatter_start(total_of(early), z_axis)
    grad_tokens = tokens_back(
        lin_q, lin_kv, w_query, w_key, w_value, tokens, gh, attn_norm[None]
    )
    one, two, early, grad_tokens = tie((one, two, early, grad_tokens))
    one = scatter_start(total_of(one), x_axis)
    two = scatter_start(total_of(two), y_axis)
    early = scatter_start(total_of(early), y_axis)
    y_parts.append(scatter_start(total_of([total[2][0]] + x_came[2]), y_axis))
    one, two, early = tie((one, two, early))
    both = scatter_start(jnp.concatenate([total_of(one), total_of(two)], 0), z_axis)
    early = gather_start(total_of(early), y_axis)
    grads = [gather_start(total_of(y_parts[0]), y_axis)]
    both, early, y_parts = tie((both, early, y_parts))
    both = gather_start(total_of(both), z_axis)
    grads.append(gather_start(total_of(y_parts[1]), y_axis))
    both, early, grads[0] = tie((both, early, grads[0]))
    both = gather_end(both, z_axis)
    size = both.shape[0] // 2
    one, two = gather_start(both[:size], x_axis), gather_start(both[size:], y_axis)
    early = gather_start(gather_end(early, y_axis), z_axis)
    result_out = (valid * (hidden + expert_sum.astype(F32))).astype(BF16)
    one, two, result_out, grads = tie((one, two, result_out, grads))
    one = gather_start(gather_end(one, x_axis), y_axis)
    two = gather_start(gather_end(two, y_axis), x_axis)
    whole = lambda g: gather_end(gather_start(gather_end(g, y_axis)[None], core_axis), core_axis)
    ready = [whole(g).reshape(own, width, ff).astype(F32) for g in grads]
    grads = gather_start(total_of(y_parts[2]), y_axis)
    one, two, ready, early = tie((one, two, ready, early))
    one, two = gather_end(one, y_axis), gather_end(two, x_axis)
    swapped = lax.ppermute(one, "ctx", core_swap), lax.ppermute(two, "ctx", core_swap)
    early = gather_start(gather_end(early, z_axis), x_axis)
    swapped, one, two = tie((swapped, one, two))
    late_q, late_k, late_v, gain = finish(
        facts, one, swapped[0], two, swapped[1], w_query, w_key, w_value, attn_norm[None]
    )
    early, late_q, grads = tie((early, late_q, grads))
    early = gather_end(early, x_axis)
    down = gather_end(grads, y_axis)
    early = gather_end(gather_start(early[None], core_axis), core_axis)
    w_out_sum = early[:, : width // 2].reshape(width, width).astype(F32)
    small = early[0, width // 2 :].astype(F32)
    down = gather_end(gather_start(down[None], core_axis), core_axis).reshape(own, width, ff)
    down = jnp.concatenate([down[:, :ff], down[:, ff:]], -1).astype(F32)
    return (
        result_out[None],
        grad_tokens[None],
        gain[0],
        late_q,
        late_k,
        late_v,
        w_out_sum,
        small[experts],
        small[:experts].T,
        *ready,
        down,
    )


def solution(mesh):
    rows, whole, split = P("ep", "ctx", None), P(), P("ep", None, None)
    return jax.shard_map(
        local,
        mesh=mesh,
        in_specs=(rows, P("ep"), rows, rows) + (whole,) * 7 + (split,) * 3,
        out_specs=(rows, rows) + (whole,) * 7 + (split,) * 3,
        check_vma=False,
    )
```

time: 576 us -> 505 us (0.88)
  waiting for transfers between devices: 179 us -> 123 us
  other arithmetic: 64.6 us -> 40.6 us
  starting transfers between devices: 77.7 us -> 95.3 us
  local copies, waits for them, and re-layouts: 23.6 us -> 16.9 us
    ppermute x1, waiting for transfers between devices: 36 us -> 4.26 us  [local(): near = lax.ppermute(mixed, 'ep', zx(swap))]
    ppermute x38 -> x53, waiting for transfers between devices: 130 us -> 105 us  [the longest x19 28.4 us: gather_start(): lax.ppermute(buf, name, pairs(shift))]
    ppermute x38 -> x53, starting transfers between devices: 50.2 us -> 69.2 us  [the longest x15 27.4 us: scatter_start(): parts.append(lax.ppermute(take((pos + shift) % size), name, pairs(shift)))]
    select_n x7 -> x11, other arithmetic: 13.7 us -> 6.38 us  [gather_end(): jnp.where(pos == 0, pick(order[1], order[0]), pick(order[0], order[1]))]
    ppermute x1, starting transfers between devices: 10.9 us -> 4.64 us  [local(): third = lax.ppermute(gm_b, 'ep', zx(ends))]
    convert_element_type x10 -> x6, other arithmetic: 13.9 us -> 7.64 us  [local(): add = lambda a, b: (a.astype(F32) + b.astype(F32)).astype(BF16)]
    convert_element_type x13 -> x15, other arithmetic: 15 us -> 13.3 us  [total_of(): return total.astype(BF16)]
  transfers between devices with their start and end apart: 55 -> 68, of which waited for: 24 -> 23; matrix products, arithmetic and copies ran while one was open for 9% -> 8% of each run, Pallas kernels for 35% -> 40%
where the time goes in v3:
time: 505 us; the launch traced here: 497 us
  Pallas kernels  204 us (40%)
  waiting for transfers between devices  123 us (24%)
  starting transfers between devices  95.3 us (19%)
  other arithmetic  40.6 us (8%)
  local copies, waits for them, and re-layouts  16.9 us (3%)
  between operations  16.5 us (3%)
    pallas_call x5, Pallas kernels, expert_call(): pl.pallas_call(functools.partial(expert_body, base, own, remotes, twins,...  79.9 us
    pallas_call x2, Pallas kernels, expert_grads(): pl.pallas_call(functools.partial(expert_grads_body, base), grid_spec=pltp...  30.6 us
    ppermute x19, waiting for transfers between devices, gather_start(): lax.ppermute(buf, name, pairs(shift))  28.4 us
    ppermute x15, starting transfers between devices, scatter_start(): parts.append(lax.ppermute(take((pos + shift) % size), name, pairs(shift)))  27.4 us
    ppermute x1, waiting for transfers between devices, local(): final = lax.ppermute(send, 'ep', zx(away))  26.5 us
    ppermute x3, waiting for transfers between devices, local(): lax.ppermute(total[k][s], 'ep', x_shift(s))  20 us
    ppermute x15, waiting for transfers between devices, scatter_start(): parts.append(lax.ppermute(take((pos + shift) % size), name, pairs(shift)))  19 us
    ppermute x19, starting transfers between devices, gather_start(): lax.ppermute(buf, name, pairs(shift))  17 us
  transfers between devices with their start and end apart: 68, of which 23 were waited for; matrix products, arithmetic and copies ran while one was open for 8% of the time, Pallas kernels for 40%

profile of v3, /device:TPU:0, one launch (start us, length us, event | category | flops | bytes accessed | tf_op | source)
XLA Modules:
  0.0 496.7 jit_solution(1040625529537739616)
XLA Ops:
  9.1 5.7 %prepare.1 = (bf16[400,1024]{1,0:T(8,128)(2,1)}, bf16[3072,512]{1,0:T(8,128)(2,1)}) custom-call(s32[160]{0:T(256)} %bitcast.83, s32[1]{0:T(128)} %copy.86.len_ref, s32[8,384]{1,0:T(8,128)} %bitcast.105, bf16[384,1024]{1,0:T(8,128)(2,1)} %bitcast.77, bf16[2,1024,512]{2,1,0:T(8,128)(2,1)} %refs_5_.9, bf16[2,1024,512]{2,1,0:T(8,128)(2,1)} %refs_6_.3, ...), custom_call_target="tpu_custom_call" | custom-call | flops 1048576 | bytes 1048576 | tf_op jit(solution)/shard_map/prepare/pallas_call | solution.py:96
  21.0 8.3 %project.1 = (bf16[384,1024]{1,0:T(8,128)(2,1)}, bf16[384,1024]{1,0:T(8,128)(2,1)}, bf16[2,384,512]{2,1,0:T(8,128)(2,1)}, f32[384,128]{1,0:T(8,128)}, f32[384,128]{1,0:T(8,128)}) custom-call(s32[160]{0:T(256)} %bitcast.84, s32[1]{0:T(128)} %copy.86.len_ref, bf16[384,1024]{1,0:T(8,128)(2,1)} %bitcast.69, f32[1,1024]{1,0:T(1,128)} %bitcast.100, ...), custom_call_target="tpu_custom_call" | custom-call | flops 1048576 | bytes 1048576 | tf_op jit(solution)/shard_map/project/pallas_call | solution.py:163
  35.0 8.2 %attend.2 = (f32[4,2,128,384]{3,2,1,0:T(8,128)}, f32[4,8,384]{2,1,0:T(8,128)}, f32[4,8,384]{2,1,0:T(8,128)}) custom-call(s32[160]{0:T(256)} %bitcast.85, s32[1]{0:T(128)} %copy.86.len_ref, bf16[384,1024]{1,0:T(8,128)(2,1)} %get-tuple-element.256.q_ref, bf16[2,384,512]{2,1,0:T(8,128)(2,1)} %get-tuple-element.257.refs_0_, bf16[2,384,512]{2,1,0:T(8,128)(2,1)} %copy-done.23), custom_call_target="tpu_custom_call" | custom-call | flops 1048576 | bytes 1048576 | tf_op jit(solution)/shard_map/attend/pallas_call | solution.py:322
  43.2 7.3 %collective-permute-done.refs_0_ = bf16[2,384,512]{2,1,0:T(8,128)(2,1)S(1)} collective-permute-done((bf16[2,384,512]{2,1,0:T(8,128)(2,1)}, bf16[2,384,512]{2,1,0:T(8,128)(2,1)S(1)}, u32[]{:S(2)}, u32[]{:S(2)}) %collective-permute-start) | collective-permute-done | bytes 786464 | tf_op jit(solution)/shard_map/ppermute | solution.py:1105
  54.4 7.9 %attend.3 = (bf16[384,1024]{1,0:T(8,128)(2,1)}, f32[4,8,384]{2,1,0:T(8,128)}, f32[384,1024]{1,0:T(8,128)}, bf16[384,1024]{1,0:T(8,128)(2,1)}) custom-call(s32[160]{0:T(256)} %bitcast.86, s32[1]{0:T(128)} %copy.86.len_ref, bf16[384,1024]{1,0:T(8,128)(2,1)} %get-tuple-element.256.q_ref, bf16[2,384,512]{2,1,0:T(8,128)(2,1)} %copy-done.25, ...), custom_call_target="tpu_custom_call" | custom-call | flops 1048576 | bytes 1048576 | tf_op jit(solution)/shard_map/attend/pallas_call | solution.py:322
  62.3 4.8 collective-permute-start.7
  69.8 6.9 %collective-permute-done.6.refs_3_ = bf16[400,1024]{1,0:T(8,128)(2,1)} collective-permute-done((bf16[400,1024]{1,0:T(8,128)(2,1)}, bf16[400,1024]{1,0:T(8,128)(2,1)}, u32[]{:S(2)}, u32[]{:S(2)}) %collective-permute-start.6) | collective-permute-done | bytes 819232 | tf_op jit(solution)/shard_map/ppermute | solution.py:1111
  76.7 12.2 %experts.5 = (bf16[400,1024]{1,0:T(8,128)(2,1)}, f32[384,128]{1,0:T(8,128)}, bf16[4,384,1024]{2,1,0:T(8,128)(2,1)}, bf16[4,384,2048]{2,1,0:T(8,128)(2,1)}, bf16[...) custom-call(s32[160]{0:T(256)} %bitcast.87, ...), custom_call_target="tpu_custom_call" | custom-call | flops 1048576 | bytes 1048576 | tf_op jit(solution)/shard_map/experts/pallas_call | solution.py:561
  100.5 12.2 %experts.6 = (bf16[400,1024]{1,0:T(8,128)(2,1)}, f32[384,128]{1,0:T(8,128)}, bf16[4,384,1024]{2,1,0:T(8,128)(2,1)}, bf16[4,384,2048]{2,1,0:T(8,128)(2,1)}, bf16[...) custom-call(s32[160]{0:T(256)} %bitcast.88, ...), custom_call_target="tpu_custom_call", output_to_operand_aliasing={{2}: (8, {}), {3}: (9, {}), {4}: (10, {}), {5}: (11, {})} | custom-call | flops 4831838208 | bytes 6291456 | tf_op jit(solution)/shard_map/experts/pallas_call | solution.py:561
  117.2 18.1 %experts.7 = (bf16[400,1024]{1,0:T(8,128)(2,1)}, f32[384,128]{1,0:T(8,128)}, bf16[4,384,1024]{2,1,0:T(8,128)(2,1)}, bf16[4,384,2048]{2,1,0:T(8,128)(2,1)}, bf16[...) custom-call(s32[160]{0:T(256)} %bitcast.89, ...), custom_call_target="tpu_custom_call", output_to_operand_aliasing={{2}: (10, {}), {3}: (11, {}), {4}: (12, {}), {5}: (13, {}),... | custom-call | flops 9663676416 | bytes 12582912 | tf_op jit(solution)/shard_map/experts/pallas_call | solution.py:561
  141.8 18.6 %experts.8 = (bf16[400,1024]{1,0:T(8,128)(2,1)}, f32[384,128]{1,0:T(8,128)}, bf16[4,384,1024]{2,1,0:T(8,128)(2,1)}, bf16[4,384,2048]{2,1,0:T(8,128)(2,1)}, bf16[...) custom-call(s32[160]{0:T(256)} %bitcast.90, ...), custom_call_target="tpu_custom_call", output_to_operand_aliasing={{2}: (12, {}), {3}: (13, {}), {4}: (14, {}), {5}: (15, {}),... | custom-call | flops 9663676416 | bytes 12582912 | tf_op jit(solution)/shard_map/experts/pallas_call | solution.py:561
  166.0 18.8 %experts.9 = (bf16[400,1024]{1,0:T(8,128)(2,1)}, f32[384,128]{1,0:T(8,128)}, bf16[4,384,1024]{2,1,0:T(8,128)(2,1)}, bf16[4,384,2048]{2,1,0:T(8,128)(2,1)}, bf16[...) custom-call(s32[160]{0:T(256)} %bitcast.91, ...), custom_call_target="tpu_custom_call", output_to_operand_aliasing={{2}: (12, {}), {3}: (13, {}), {4}: (14, {}), {5}: (15, {}),... | custom-call | flops 9663676416 | bytes 12582912 | tf_op jit(solution)/shard_map/experts/pallas_call | solution.py:561
  190.2 15.2 %expert_grads.2 = bf16[2,3,1024,512]{3,2,1,0:T(8,128)(2,1)} custom-call(s32[160]{0:T(256)} %bitcast.92, s32[1]{0:T(128)} %copy.86.len_ref, bf16[1536,1024]{1,0:T(8,128)(2,1)} %bitcast.65, bf16[1536,1024]{1,0:T(8,128)(2,1)} %bitcast.67, bf16[1536,2048]{1,0:T(8,128)(2,1)} %bitcast.58, bf16[1536,2048]{1,0:T(8,128)(2,1)} %bitcast.60, bf16[1536,2048]{1,0:T(8,128)(2,1)} %bitcast.62), custom_call_target="tpu_custom_call" | custom-call | flops 9663676416 | bytes 16777216 | tf_op jit(solution)/shard_map/expert_grads/pallas_call | solution.py:641
  207.5 15.4 %expert_grads.3 = bf16[2,3,1024,512]{3,2,1,0:T(8,128)(2,1)} custom-call(s32[160]{0:T(256)} %bitcast.93, s32[1]{0:T(128)} %copy.86.len_ref, bf16[1536,1024]{1,0:T(8,128)(2,1)} %bitcast.66, bf16[1536,1024]{1,0:T(8,128)(2,1)} %bitcast.68, bf16[1536,2048]{1,0:T(8,128)(2,1)} %bitcast.59, bf16[1536,2048]{1,0:T(8,128)(2,1)} %bitcast.61, bf16[1536,2048]{1,0:T(8,128)(2,1)} %bitcast.63), custom_call_target="tpu_custom_call" | custom-call | flops 9663676416 | bytes 16777216 | tf_op jit(solution)/shard_map/expert_grads/pallas_call | solution.py:641
  227.9 26.5 %collective-permute-done.21.refs_3_.refs_7_ = bf16[400,1024]{1,0:T(8,128)(2,1)S(1)} collective-permute-done((bf16[400,1024]{1,0:T(8,128)(2,1)S(1)}, bf16[400,1024]{1,0:T(8,128)(2,1)S(1)}, u32[]{:S(2)}, u32[]{:S(2)}) %collective-permute-start.21) | collective-permute-done | bytes 819232 | tf_op jit(solution)/shard_map/ppermute | solution.py:1167
  255.4 9.4 %middle.1 = (f32[384,1024]{1,0:T(8,128)}, bf16[384,1024]{1,0:T(8,128)(2,1)}, bf16[384,1024]{1,0:T(8,128)(2,1)}, f32[4,8,384]{2,1,0:T(8,128)}, f32[1,1024]{1,0:T(1,128)}, /*index=5*/f32[128,1024]{1,0:T(8,128)}) custom-call(bf16[400,1024]{1,0:T(8,128)(2,1)} %get-tuple-element.283.refs_0_.refs_4_, bf16[400,1024]{1,0:T(8,128)(2,1)} %copy-done.5, ...), custom_call_target="tpu_custom_call" | custom-call | flops 1048576 | bytes 1048576 | tf_op jit(solution)/shard_map/middle/pallas_call | solution.py:731
  264.8 5.8 %early_grads.1 = (bf16[640,1024]{1,0:T(8,128)(2,1)}, bf16[640,1024]{1,0:T(8,128)(2,1)}) custom-call(s32[160]{0:T(256)} %bitcast.94, s32[1]{0:T(128)} %copy.86.len_ref, bf16[384,1024]{1,0:T(8,128)(2,1)} %get-tuple-element.265.refs_12_.att_ref, bf16[384,1024]{1,0:T(8,128)(2,1)} %get-tuple-element.360.gb_ref, f32[128,1024]{1,0:T(8,128)} %get-tuple-element.361.router_ref, ...), custom_call_target="tpu_custom_call" | custom-call | flops 1048576 | bytes 1048576 | tf_op jit(solution)/shard_map/early_grads/pallas_call | solution.py:793
  276.3 6.7 %collective-permute-start.23 = (bf16[512,512]{1,0:T(8,128)(2,1)S(1)}, bf16[512,512]{1,0:T(8,128)(2,1)S(1)}, u32[]{:S(2)}, u32[]{:S(2)}) collective-permute-start(bf16[512,512]{1,0:T(8,128)(2,1)S(1)} %get-tuple-element.512), channel_id=1, source_target_pairs={{0,2},{1,3},{2,0},{3,1},{4,6},{5,7},{6,4},{7,5},{8,10},{9,11},{10,... | collective-permute-start | bytes 1572872 | tf_op jit(solution)/shard_map/ppermute | solution.py:993
  283.0 5.3 %attend_back.2 = (f32[384,1024]{1,0:T(8,128)}, bf16[2,384,512]{2,1,0:T(8,128)(2,1)}, bf16[2,384,512]{2,1,0:T(8,128)(2,1)}) custom-call(s32[160]{0:T(256)} %bitcast.95, s32[1]{0:T(128)} %copy.86.len_ref, bf16[384,1024]{1,0:T(8,128)(2,1)} %get-tuple-element.256.q_ref, bf16[384,1024]{1,0:T(8,128)(2,1)} %get-tuple-element.370.do_ref, ...), custom_call_target="tpu_custom_call" | custom-call | flops 12079595520 | bytes 16777216 | tf_op jit(solution)/shard_map/attend_back/pallas_call | solution.py:402
  288.3 10.2 %collective-permute-done.24 = bf16[1024,512]{1,0:T(8,128)(2,1)} collective-permute-done((bf16[1024,512]{1,0:T(8,128)(2,1)S(1)}, bf16[1024,512]{1,0:T(8,128)(2,1)}, u32[]{:S(2)}, u32[]{:S(2)}) %collective-permute-start.24) | collective-permute-done | bytes 1048608 | tf_op jit(solution)/shard_map/ppermute | solution.py:1171
  303.0 11.5 %attend_back.3 = (f32[384,1024]{1,0:T(8,128)}, bf16[2,384,512]{2,1,0:T(8,128)(2,1)}, bf16[2,384,512]{2,1,0:T(8,128)(2,1)}) custom-call(s32[160]{0:T(256)} %bitcast.96, s32[1]{0:T(128)} %copy.86.len_ref, bf16[384,1024]{1,0:T(8,128)(2,1)} %get-tuple-element.256.q_ref, bf16[384,1024]{1,0:T(8,128)(2,1)} %get-tuple-element.370.do_ref, ...), custom_call_target="tpu_custom_call" | custom-call | flops 12079595520 | bytes 16777216 | tf_op jit(solution)/shard_map/attend_back/pallas_call | solution.py:402
  314.5 9.8 %collective-permute-done.28 = bf16[1024,512]{1,0:T(8,128)(2,1)S(1)} collective-permute-done((bf16[1024,512]{1,0:T(8,128)(2,1)}, bf16[1024,512]{1,0:T(8,128)(2,1)S(1)}, u32[]{:S(2)}, u32[]{:S(2)}) %collective-permute-start.28) | collective-permute-done | bytes 1048608 | tf_op jit(solution)/shard_map/ppermute | solution.py:1171
  328.6 6.3 %query_back.1 = (bf16[384,1024]{1,0:T(8,128)(2,1)}, bf16[512,1024]{1,0:T(8,128)(2,1)}, bf16[512,1024]{1,0:T(8,128)(2,1)}) custom-call(s32[160]{0:T(256)} %bitcast.97, s32[1]{0:T(128)} %copy.86.len_ref, f32[384,1024]{1,0:T(8,128)} %get-tuple-element.394.dq_ref, bf16[384,1024]{1,0:T(8,128)(2,1)} %get-tuple-element.395.n_ref.refs_3_, ...), custom_call_target="tpu_custom_call" | custom-call | flops 805306368 | bytes 8388608 | tf_op jit(solution)/shard_map/query_back/pallas_call | solution.py:837
  346.8 6.8 %pair_back.1 = (bf16[384,1024]{1,0:T(8,128)(2,1)}, bf16[512,1024]{1,0:T(8,128)(2,1)}, bf16[512,1024]{1,0:T(8,128)(2,1)}) custom-call(s32[160]{0:T(256)} %bitcast.98, s32[1]{0:T(128)} %copy.86.len_ref, bf16[2,384,512]{2,1,0:T(8,128)(2,1)} %get-tuple-element.403.refs_0_, bf16[2,384,512]{2,1,0:T(8,128)(2,1)} %collective-permute-done.29.refs_1_, ...), custom_call_target="tpu_custom_call" | custom-call | flops 1048576 | bytes 1048576 | tf_op jit(solution)/shard_map/pair_back/pallas_call | solution.py:881
  353.6 5.0 %collective-permute-done.31 = bf16[512,512]{1,0:T(8,128)(2,1)S(1)} collective-permute-done((bf16[512,512]{1,0:T(8,128)(2,1)S(1)}, bf16[512,512]{1,0:T(8,128)(2,1)S(1)}, u32[]{:S(2)}, u32[]{:S(2)}) %collective-permute-start.31) | collective-permute-done | bytes 524320 | tf_op jit(solution)/shard_map/ppermute | solution.py:993
  373.3 9.5 %tokens_back.1 = bf16[384,1024]{1,0:T(8,128)(2,1)} custom-call(bf16[384,1024]{1,0:T(8,128)(2,1)} %get-tuple-element.420.lq_ref, bf16[384,1024]{1,0:T(8,128)(2,1)} %get-tuple-element.421.lkv_ref, bf16[1024,1024]{1,0:T(8,128)(2,1)} %wq_ref.5, bf16[1024,512]{1,0:T(8,128)(2,1)} %wk_ref.5, bf16[1024,512]{1,0:T(8,128)(2,1)} %wv_ref.5, bf16[384,1024]{1,0:T(8,128)(2,1)} %bitcast.71, ...), custom_call_target="tpu_custom_call" | custom-call | flops 1048576 | bytes 1048576 | tf_op jit(solution)/shard_map/tokens_back/pallas_call | solution.py:917
  391.5 8.0 %collective-permute-done.41 = bf16[40,1024]{1,0:T(8,128)(2,1)S(1)} collective-permute-done((bf16[40,1024]{1,0:T(8,128)(2,1)S(1)}, bf16[40,1024]{1,0:T(8,128)(2,1)S(1)}, u32[]{:S(2)}, u32[]{:S(2)}) %collective-permute-start.41) | collective-permute-done | bytes 81952 | tf_op jit(solution)/shard_map/ppermute | solution.py:993
  399.5 5.6 %collective-permute-done.40 = bf16[128,1024]{1,0:T(8,128)(2,1)S(1)} collective-permute-done((bf16[128,1024]{1,0:T(8,128)(2,1)S(1)}, bf16[128,1024]{1,0:T(8,128)(2,1)S(1)}, u32[]{:S(2)}, u32[]{:S(2)}) %collective-permute-start.40) | collective-permute-done | bytes 262176 | tf_op jit(solution)/shard_map/ppermute | solution.py:993
  411.5 4.8 collective-permute-done.45
  422.3 7.3 %collective-permute-done.48 = bf16[64,1024]{1,0:T(8,128)(2,1)S(1)} collective-permute-done((bf16[64,1024]{1,0:T(8,128)(2,1)S(1)}, bf16[64,1024]{1,0:T(8,128)(2,1)S(1)}, u32[]{:S(2)}, u32[]{:S(2)}) %collective-permute-start.48) | collective-permute-done | bytes 131104 | tf_op jit(solution)/shard_map/ppermute | solution.py:999
  453.8 6.2 %collective-permute-done.59 = bf16[80,1024]{1,0:T(8,128)(2,1)S(1)} collective-permute-done((bf16[80,1024]{1,0:T(8,128)(2,1)S(1)}, bf16[80,1024]{1,0:T(8,128)(2,1)S(1)}, u32[]{:S(2)}, u32[]{:S(2)}) %collective-permute-start.59) | collective-permute-done | bytes 163872 | tf_op jit(solution)/shard_map/ppermute | solution.py:999
  467.3 9.0 %finish.1 = (f32[1024,1024]{1,0:T(8,128)}, f32[1024,512]{1,0:T(8,128)}, f32[1024,512]{1,0:T(8,128)}, f32[1,1024]{1,0:T(1,128)}) custom-call(s32[160]{0:T(256)} %bitcast.99, s32[1]{0:T(128)} %copy.86.len_ref, bf16[512,1024]{1,0:T(8,128)(2,1)} %copy-done.4, bf16[512,1024]{1,0:T(8,128)(2,1)} %copy-done.17, bf16[512,1024]{1,0:T(8,128)(2,1)} %copy-done.3, ...), custom_call_target="tpu_custom_call" | custom-call | flops 1048576 | bytes 1048576 | tf_op jit(solution)/shard_map/finish/pallas_call | solution.py:959
  (277 shorter events, 166.8 us)
Async XLA Ops:
  7.2 352.2 %reduce-scatter.2.cloned.1.call-start = ((), (), s32[]{:S(2)}) async-start(), calls=%async_computation.1 | async-start | bytes 3932160 | tf_op jit(solution)/shard_map/reduce_scatter | solution.py:1180
  14.9 78.2 %collective-permute-start.9 = (bf16[3072,512]{1,0:T(8,128)(2,1)}, bf16[3072,512]{1,0:T(8,128)(2,1)S(1)}, u32[]{:S(2)}, u32[]{:S(2)}) collective-permute-start(bf16[3072,512]{1,0:T(8,128)(2,1)} %get-tuple-element.254), channel_id=1, source_target_pairs={{0,4},{4,0},{8,12},{12,8},{16,20},{20,16},{24,28},{28,24},{1,5},{5... | collective-permute-start | bytes 9437192 | tf_op jit(solution)/shard_map/ppermute | solution.py:1091
  17.9 32.7 %collective-permute-start.2 = (bf16[400,1024]{1,0:T(8,128)(2,1)}, bf16[400,1024]{1,0:T(8,128)(2,1)}, u32[]{:S(2)}, u32[]{:S(2)}) collective-permute-start(bf16[400,1024]{1,0:T(8,128)(2,1)} %get-tuple-element.270.refs_1_.refs_11_), channel_id=1, source_target_pairs={{0,8},{4,12},{8,0},{12,4},{16,24},{20,28},{24,16},{28,20},{1,9},{5... | collective-permute-start | bytes 2457608 | tf_op jit(solution)/shard_map/ppermute | solution.py:1094
  19.4 31.1 %collective-permute-start.3 = (bf16[400,1024]{1,0:T(8,128)(2,1)}, bf16[400,1024]{1,0:T(8,128)(2,1)}, u32[]{:S(2)}, u32[]{:S(2)}) collective-permute-start(bf16[400,1024]{1,0:T(8,128)(2,1)} %get-tuple-element.270.refs_1_.refs_11_), channel_id=1, source_target_pairs={{8,16},{12,20},{16,8},{20,12},{9,17},{13,21},{17,9},{21,13},{10,18... | collective-permute-start | bytes 2457608 | tf_op jit(solution)/shard_map/ppermute | solution.py:1095
  30.6 19.9 %collective-permute-start = (bf16[2,384,512]{2,1,0:T(8,128)(2,1)}, bf16[2,384,512]{2,1,0:T(8,128)(2,1)S(1)}, u32[]{:S(2)}, u32[]{:S(2)}) collective-permute-start(bf16[2,384,512]{2,1,0:T(8,128)(2,1)} %get-tuple-element.257.refs_0_), channel_id=1, source_target_pairs={{0,2},{1,3},{4,6},{5,7},{8,10},{9,11},{12,14},{13,15},{16,18},{17,... | collective-permute-start | bytes 2359304 | tf_op jit(solution)/shard_map/ppermute | solution.py:1105
  50.6 19.2 %collective-permute-start.5 = (bf16[400,1024]{1,0:T(8,128)(2,1)}, bf16[400,1024]{1,0:T(8,128)(2,1)}, u32[]{:S(2)}, u32[]{:S(2)}) collective-permute-start(bf16[400,1024]{1,0:T(8,128)(2,1)} %collective-permute-done.2.refs_1_), channel_id=1, source_target_pairs={{8,16},{12,20},{16,8},{20,12},{9,17},{13,21},{17,9},{21,13},{10,18... | collective-permute-start | bytes 2457608 | tf_op jit(solution)/shard_map/ppermute | solution.py:1110
  52.2 24.5 %collective-permute-start.6 = (bf16[400,1024]{1,0:T(8,128)(2,1)}, bf16[400,1024]{1,0:T(8,128)(2,1)}, u32[]{:S(2)}, u32[]{:S(2)}) collective-permute-start(bf16[400,1024]{1,0:T(8,128)(2,1)} %collective-permute-done.3.refs_2_), channel_id=1, source_target_pairs={{8,0},{12,4},{16,24},{20,28},{9,1},{13,5},{17,25},{21,29},{10,2},{... | collective-permute-start | bytes 2457608 | tf_op jit(solution)/shard_map/ppermute | solution.py:1111
  62.3 30.8 %collective-permute-start.7 = (bf16[384,1024]{1,0:T(8,128)(2,1)}, bf16[384,1024]{1,0:T(8,128)(2,1)}, u32[]{:S(2)}, u32[]{:S(2)}) collective-permute-start(bf16[384,1024]{1,0:T(8,128)(2,1)} %get-tuple-element.269.refs_0_.refs_13_), channel_id=1, source_target_pairs={{0,8},{4,12},{8,0},{12,4},{16,24},{20,28},{24,16},{28,20},{1,9},{5... | collective-permute-start | bytes 2359304 | tf_op jit(solution)/shard_map/ppermute | solution.py:1130
  67.1 26.0 %collective-permute-start.8 = (bf16[384,1024]{1,0:T(8,128)(2,1)}, bf16[384,1024]{1,0:T(8,128)(2,1)}, u32[]{:S(2)}, u32[]{:S(2)}) collective-permute-start(bf16[384,1024]{1,0:T(8,128)(2,1)} %get-tuple-element.269.refs_0_.refs_13_), channel_id=1, source_target_pairs={{8,16},{12,20},{16,8},{20,12},{9,17},{13,21},{17,9},{21,13},{10,18... | collective-permute-start | bytes 2359304 | tf_op jit(solution)/shard_map/ppermute | solution.py:1131
  93.2 19.5 %collective-permute-start.11 = (bf16[384,1024]{1,0:T(8,128)(2,1)}, bf16[384,1024]{1,0:T(8,128)(2,1)S(1)}, u32[]{:S(2)}, u32[]{:S(2)}) collective-permute-start(bf16[384,1024]{1,0:T(8,128)(2,1)} %collective-permute-done.7.refs_0_), channel_id=1, source_target_pairs={{8,16},{12,20},{16,8},{20,12},{9,17},{13,21},{17,9},{21,13},{10,18... | collective-permute-start | bytes 2359304 | tf_op jit(solution)/shard_map/ppermute | solution.py:1135
  93.9 22.0 %collective-permute-start.12 = (bf16[384,1024]{1,0:T(8,128)(2,1)}, bf16[384,1024]{1,0:T(8,128)(2,1)S(1)}, u32[]{:S(2)}, u32[]{:S(2)}) collective-permute-start(bf16[384,1024]{1,0:T(8,128)(2,1)} %collective-permute-done.8.refs_0_), channel_id=1, source_target_pairs={{8,0},{12,4},{16,24},{20,28},{9,1},{13,5},{17,25},{21,29},{10,2},{... | collective-permute-start | bytes 2359304 | tf_op jit(solution)/shard_map/ppermute | solution.py:1136
  115.9 24.1 %collective-permute-start.14 = (bf16[384,1024]{1,0:T(8,128)(2,1)S(1)}, bf16[384,1024]{1,0:T(8,128)(2,1)S(1)}, u32[]{:S(2)}, u32[]{:S(2)}) collective-permute-start(bf16[384,1024]{1,0:T(8,128)(2,1)S(1)} %collective-permute-done.11.refs_0_), channel_id=1, source_target_pairs={{8,0},{12,4},{16,24},{20,28},{9,1},{13,5},{17,25},{21,29},{10,2},{... | collective-permute-start | bytes 2359304 | tf_op jit(solution)/shard_map/ppermute | solution.py:1142
  135.4 29.7 %collective-permute-start.13 = (bf16[400,1024]{1,0:T(8,128)(2,1)}, bf16[400,1024]{1,0:T(8,128)(2,1)S(1)}, u32[]{:S(2)}, u32[]{:S(2)}) collective-permute-start(bf16[400,1024]{1,0:T(8,128)(2,1)} %get-tuple-element.298), channel_id=1, source_target_pairs={{0,8},{4,12},{24,16},{28,20},{1,9},{5,13},{25,17},{29,21},{2,10},{... | collective-permute-start | bytes 2457608 | tf_op jit(solution)/shard_map/ppermute | solution.py:1144
  140.1 25.0 %collective-permute-start.15 = (bf16[400,1024]{1,0:T(8,128)(2,1)}, bf16[400,1024]{1,0:T(8,128)(2,1)S(1)}, u32[]{:S(2)}, u32[]{:S(2)}) collective-permute-start(bf16[400,1024]{1,0:T(8,128)(2,1)} %collective-permute-done.5.refs_2_), channel_id=1, source_target_pairs={{8,0},{12,4},{16,24},{20,28},{9,1},{13,5},{17,25},{21,29},{10,2},{... | collective-permute-start | bytes 2457608 | tf_op jit(solution)/shard_map/ppermute | solution.py:1146
  160.4 24.4 %collective-permute-start.17 = (bf16[400,1024]{1,0:T(8,128)(2,1)}, bf16[400,1024]{1,0:T(8,128)(2,1)S(1)}, u32[]{:S(2)}, u32[]{:S(2)}) collective-permute-start(bf16[400,1024]{1,0:T(8,128)(2,1)} %get-tuple-element.332), channel_id=1, source_target_pairs={{0,8},{4,12},{24,16},{28,20},{1,9},{5,13},{25,17},{29,21},{2,10},{... | collective-permute-start | bytes 2457608 | tf_op jit(solution)/shard_map/ppermute | solution.py:1149
  185.2 20.2 %collective-permute-start.18 = (bf16[400,1024]{1,0:T(8,128)(2,1)S(1)}, bf16[400,1024]{1,0:T(8,128)(2,1)S(1)}, u32[]{:S(2)}, u32[]{:S(2)}) collective-permute-start(bf16[400,1024]{1,0:T(8,128)(2,1)S(1)} %add_convert_fusion.12), channel_id=1, source_target_pairs={{8,16},{12,20},{16,8},{20,12},{9,17},{13,21},{17,9},{21,13},{10,18... | collective-permute-start | bytes 2457608 | tf_op jit(solution)/shard_map/ppermute | solution.py:1159
  185.9 20.3 %collective-permute-start.16 = (bf16[400,1024]{1,0:T(8,128)(2,1)S(1)}, bf16[400,1024]{1,0:T(8,128)(2,1)S(1)}, u32[]{:S(2)}, u32[]{:S(2)}) collective-permute-start(bf16[400,1024]{1,0:T(8,128)(2,1)S(1)} %copy-done.21), channel_id=1, source_target_pairs={{0,8},{4,12},{24,16},{28,20},{1,9},{5,13},{25,17},{29,21},{2,10},{... | collective-permute-start | bytes 2457608 | tf_op jit(solution)/shard_map/ppermute | solution.py:1153
  226.0 44.6 %collective-permute-start.22 = (bf16[1024,512]{1,0:T(8,128)(2,1)S(1)}, bf16[1024,512]{1,0:T(8,128)(2,1)S(1)}, u32[]{:S(2)}, u32[]{:S(2)}) collective-permute-start(bf16[1024,512]{1,0:T(8,128)(2,1)S(1)} %get-tuple-element.368), channel_id=1, source_target_pairs={{0,4},{4,0},{8,12},{12,8},{16,20},{20,16},{24,28},{28,24},{1,5},{5... | collective-permute-start | bytes 3145736 | tf_op jit(solution)/shard_map/ppermute | solution.py:1171
  226.6 27.8 %collective-permute-start.21 = (bf16[400,1024]{1,0:T(8,128)(2,1)S(1)}, bf16[400,1024]{1,0:T(8,128)(2,1)S(1)}, u32[]{:S(2)}, u32[]{:S(2)}) collective-permute-start(bf16[400,1024]{1,0:T(8,128)(2,1)S(1)} %add_convert_fusion.10), channel_id=1, source_target_pairs={{16,24},{20,28},{8,0},{12,4},{17,25},{21,29},{9,1},{13,5},{18,26},... | collective-permute-start | bytes 2457608 | tf_op jit(solution)/shard_map/ppermute | solution.py:1167
  274.4 24.0 %collective-permute-start.24 = (bf16[1024,512]{1,0:T(8,128)(2,1)S(1)}, bf16[1024,512]{1,0:T(8,128)(2,1)}, u32[]{:S(2)}, u32[]{:S(2)}) collective-permute-start(bf16[1024,512]{1,0:T(8,128)(2,1)S(1)} %get-tuple-element.497), channel_id=1, source_target_pairs={{0,4},{4,0},{8,12},{12,8},{16,20},{20,16},{24,28},{28,24},{1,5},{5... | collective-permute-start | bytes 3145736 | tf_op jit(solution)/shard_map/ppermute | solution.py:1171
  275.9 22.5 %collective-permute-start.25 = (bf16[640,1024]{1,0:T(8,128)(2,1)}, bf16[640,1024]{1,0:T(8,128)(2,1)S(1)}, u32[]{:S(2)}, u32[]{:S(2)}) collective-permute-start(bf16[640,1024]{1,0:T(8,128)(2,1)} %get-tuple-element.381), channel_id=1, source_target_pairs={{0,1},{1,0},{2,3},{3,2},{4,5},{5,4},{6,7},{7,6},{8,9},{9,8},{10,11... | collective-permute-start | bytes 3932168 | tf_op jit(solution)/shard_map/ppermute | solution.py:1186
  276.3 22.1 %collective-permute-start.23 = (bf16[512,512]{1,0:T(8,128)(2,1)S(1)}, bf16[512,512]{1,0:T(8,128)(2,1)S(1)}, u32[]{:S(2)}, u32[]{:S(2)}) collective-permute-start(bf16[512,512]{1,0:T(8,128)(2,1)S(1)} %get-tuple-element.512), channel_id=1, source_target_pairs={{0,2},{1,3},{2,0},{3,1},{4,6},{5,7},{6,4},{7,5},{8,10},{9,11},{10,... | collective-permute-start | bytes 1572872 | tf_op jit(solution)/shard_map/ppermute | solution.py:993
  299.2 25.1 %collective-permute-start.28 = (bf16[1024,512]{1,0:T(8,128)(2,1)}, bf16[1024,512]{1,0:T(8,128)(2,1)S(1)}, u32[]{:S(2)}, u32[]{:S(2)}) collective-permute-start(bf16[1024,512]{1,0:T(8,128)(2,1)} %get-tuple-element.496), channel_id=1, source_target_pairs={{0,4},{4,0},{8,12},{12,8},{16,20},{20,16},{24,28},{28,24},{1,5},{5... | collective-permute-start | bytes 3145736 | tf_op jit(solution)/shard_map/ppermute | solution.py:1171
  301.5 25.8 %collective-permute-start.27 = (bf16[2,384,512]{2,1,0:T(8,128)(2,1)S(1)}, bf16[2,384,512]{2,1,0:T(8,128)(2,1)}, u32[]{:S(2)}, u32[]{:S(2)}) collective-permute-start(bf16[2,384,512]{2,1,0:T(8,128)(2,1)S(1)} %add_convert_fusion.13), channel_id=1, source_target_pairs={{2,0},{3,1},{6,4},{7,5},{10,8},{11,9},{14,12},{15,13},{18,16},{19,... | collective-permute-start | bytes 2359304 | tf_op jit(solution)/shard_map/ppermute | solution.py:1194
  335.0 24.5 %collective-permute-start.30 = (bf16[512,1024]{1,0:T(8,128)(2,1)}, bf16[512,1024]{1,0:T(8,128)(2,1)}, u32[]{:S(2)}, u32[]{:S(2)}) collective-permute-start(bf16[512,1024]{1,0:T(8,128)(2,1)} %get-tuple-element.402), channel_id=1, source_target_pairs={{0,1},{1,0},{2,3},{3,2},{4,5},{5,4},{6,7},{7,6},{8,9},{9,8},{10,11... | collective-permute-start | bytes 3145736 | tf_op jit(solution)/shard_map/ppermute | solution.py:1208
  337.1 21.5 %collective-permute-start.32 = (bf16[320,1024]{1,0:T(8,128)(2,1)S(1)}, bf16[320,1024]{1,0:T(8,128)(2,1)}, u32[]{:S(2)}, u32[]{:S(2)}) collective-permute-start(bf16[320,1024]{1,0:T(8,128)(2,1)S(1)} %get-tuple-element.502), channel_id=1, source_target_pairs={{0,4},{4,0},{8,12},{12,8},{16,20},{20,16},{24,28},{28,24},{1,5},{5... | collective-permute-start | bytes 1966088 | tf_op jit(solution)/shard_map/ppermute | solution.py:993
  362.1 21.4 %collective-permute-start.33 = (bf16[256,1024]{1,0:T(8,128)(2,1)}, bf16[256,1024]{1,0:T(8,128)(2,1)S(1)}, u32[]{:S(2)}, u32[]{:S(2)}) collective-permute-start(bf16[256,1024]{1,0:T(8,128)(2,1)} %get-tuple-element.508), channel_id=1, source_target_pairs={{0,2},{1,3},{2,0},{3,1},{4,6},{5,7},{6,4},{7,5},{8,10},{9,11},{10,... | collective-permute-start | bytes 1572872 | tf_op jit(solution)/shard_map/ppermute | solution.py:993
  382.8 28.3 %collective-permute-start.46 = (bf16[512,512]{1,0:T(8,128)(2,1)S(1)}, bf16[512,512]{1,0:T(8,128)(2,1)}, u32[]{:S(2)}, u32[]{:S(2)}) collective-permute-start(bf16[512,512]{1,0:T(8,128)(2,1)S(1)} %get-tuple-element.504), channel_id=1, source_target_pairs={{0,2},{1,3},{2,0},{3,1},{4,6},{5,7},{6,4},{7,5},{8,10},{9,11},{10,... | collective-permute-start | bytes 1572872 | tf_op jit(solution)/shard_map/ppermute | solution.py:993
  387.6 17.5 %collective-permute-start.40 = (bf16[128,1024]{1,0:T(8,128)(2,1)S(1)}, bf16[128,1024]{1,0:T(8,128)(2,1)S(1)}, u32[]{:S(2)}, u32[]{:S(2)}) collective-permute-start(bf16[128,1024]{1,0:T(8,128)(2,1)S(1)} %get-tuple-element.524), channel_id=1, source_target_pairs={{0,2},{1,3},{2,0},{3,1},{4,6},{5,7},{6,4},{7,5},{8,10},{9,11},{10,... | collective-permute-start | bytes 786440 | tf_op jit(solution)/shard_map/ppermute | solution.py:993
  390.1 30.7 %collective-permute-start.50 = (bf16[512,512]{1,0:T(8,128)(2,1)S(1)}, bf16[512,512]{1,0:T(8,128)(2,1)S(1)}, u32[]{:S(2)}, u32[]{:S(2)}) collective-permute-start(bf16[512,512]{1,0:T(8,128)(2,1)S(1)} %add_convert_fusion.17), channel_id=1, source_target_pairs={{0,2},{1,3},{2,0},{3,1},{4,6},{5,7},{6,4},{7,5},{8,10},{9,11},{10,... | collective-permute-start | bytes 1572872 | tf_op jit(solution)/shard_map/ppermute | solution.py:999
  420.4 17.3 %collective-permute-start.53 = (bf16[512,512]{1,0:T(8,128)(2,1)S(1)}, bf16[512,512]{1,0:T(8,128)(2,1)S(1)}, u32[]{:S(2)}, u32[]{:S(2)}) collective-permute-start(bf16[512,512]{1,0:T(8,128)(2,1)S(1)} %add_convert_fusion.16), channel_id=1, source_target_pairs={{0,2},{1,3},{2,0},{3,1},{4,6},{5,7},{6,4},{7,5},{8,10},{9,11},{10,... | collective-permute-start | bytes 1572872 | tf_op jit(solution)/shard_map/ppermute | solution.py:999
  440.7 19.3 %collective-permute-start.55 = (bf16[256,1024]{1,0:T(8,128)(2,1)S(1)}, bf16[256,1024]{1,0:T(8,128)(2,1)S(1)}, u32[]{:S(2)}, u32[]{:S(2)}) collective-permute-start(bf16[256,1024]{1,0:T(8,128)(2,1)S(1)} %maximum_select_fusion.11), channel_id=1, source_target_pairs={{0,4},{4,0},{8,12},{12,8},{16,20},{20,16},{24,28},{28,24},{1,5},{5... | collective-permute-start | bytes 1572872 | tf_op jit(solution)/shard_map/ppermute | solution.py:999
  (76 other events, 747.7 us)
Sparse Core Ops, SparseCore 0:
  270.8 65.6 reduce-scatter.1

commit v4 on v3

--- a/solution.py
+++ b/solution.py
@@ -13,6 +13,7 @@
 THETA = 10000.0
 NEG = -1e30
 LOG2E = 1.4426950408889634
+PER_STEP = 2
 NZ = 4
 VMEM = 58 * 1024 * 1024
 CORES = 2
@@ -143,7 +144,7 @@
     @pl.when(step < nq)
     def _():
         lin = dot(n_ref[...], wq_ref[...], 1, 0)
-        q_ref[...] = rope(lin).astype(BF16) * jnp.asarray(HEAD_DIM**-0.5, BF16)
+        q_ref[...] = (rope(lin) * (LOG2E * HEAD_DIM**-0.5)).astype(BF16)
 
     @pl.when(step == nq)
     def _():
@@ -205,42 +206,61 @@
     return first, second
 
 
+def with_mask(active, start, rows, seq_len, diagonal, work):
+    if diagonal:
+        pl.when(active)(lambda: work(True))
+        return
+    whole = start + rows <= seq_len
+    pl.when(active & whole)(lambda: work(False))
+    pl.when(active & jnp.logical_not(whole))(lambda: work(True))
+
+
+def mask_of(start, rows, seq_len, diagonal):
+    key = lax.broadcasted_iota(jnp.int32, (rows, rows), 0)
+    bad = key + start >= seq_len
+    if diagonal:
+        bad = bad | (key > lax.broadcasted_iota(jnp.int32, (rows, rows), 1))
+    return jnp.where(bad, NEG, 0.0)
+
+
 def attend_blocks(info_ref, len_ref, base, q_ref, kv_refs, acc, top, low, diagonal):
     rows = q_ref.shape[0]
     seq_len = len_ref[0]
-    key = lax.broadcasted_iota(jnp.int32, (rows, rows), 0)
-    query = lax.broadcasted_iota(jnp.int32, (rows, rows), 1)
+
+    def work(role, start, masked):
+        if masked:
+            bias = mask_of(start, rows, seq_len, diagonal and role == 0)
+        for group in range(q_ref.shape[1] // 256):
+            lanes = slice(group * 128, group * 128 + 128)
+            keys = split_heads(kv_refs[role][0, :, lanes])
+            values = split_heads(kv_refs[role][1, :, lanes])
+            for pair in range(2):
+                at = 256 * group + 128 * pair
+                scores = dot(keys[pair], q_ref[:, at : at + 128], 1, 1)
+                weights, shrinks = [], []
+                for head in range(2):
+                    at = 2 * pair + head
+                    part = scores[head * rows : (head + 1) * rows]
+                    if masked:
+                        part = part + bias
+                    old = top[group, at : at + 1, :]
+                    new = jnp.maximum(old, jnp.max(part, 0, keepdims=True))
+                    prob = jnp.exp2(part - new)
+                    shrink = jnp.exp2(old - new)
+                    top[group, at : at + 1, :] = new
+                    fresh = jnp.sum(prob, 0, keepdims=True)
+                    low[group, at : at + 1, :] = low[group, at : at + 1, :] * shrink + fresh
+                    weights.append(prob.astype(BF16))
+                    shrinks.append(jnp.broadcast_to(shrink, (HEAD_DIM, rows)))
+                fresh = dot(values[pair], jnp.concatenate(weights, 0), 0, 0)
+                acc[group, pair] = acc[group, pair] * jnp.concatenate(shrinks, 0) + fresh
 
     for role in range(len(kv_refs)):
         start = info_ref[base + 2 * role]
         active = (info_ref[base + 2 * role + 1] > 0) & (start < seq_len)
-
-        @pl.when(active)
-        def _(role=role, start=start):
-            keys = split_heads(kv_refs[role][0])
-            values = split_heads(kv_refs[role][1])
-            bad = key + start >= seq_len
-            if diagonal and role == 0:
-                bad = bad | (key > query)
-            bias = jnp.where(bad, NEG, 0.0)
-            for pair in range(2):
-                q = q_ref[:, pair * 128 : pair * 128 + 128]
-                scores = dot(keys[pair], q, 1, 1)
-                weights, shrinks = [], []
-                for head in range(2):
-                    at = 2 * pair + head
-                    part = scores[head * rows : (head + 1) * rows] * LOG2E + bias
-                    old = top[0, at : at + 1, :]
-                    new = jnp.maximum(old, jnp.max(part, 0, keepdims=True))
-                    prob = jnp.exp2(part - new)
-                    shrink = jnp.exp2(old - new)
-                    top[0, at : at + 1, :] = new
-                    fresh = jnp.sum(prob, 0, keepdims=True)
-                    low[0, at : at + 1, :] = low[0, at : at + 1, :] * shrink + fresh
-                    weights.append(prob.astype(BF16))
-                    shrinks.append(jnp.broadcast_to(shrink, (HEAD_DIM, rows)))
-                fresh = dot(values[pair], jnp.concatenate(weights, 0), 0, 0)
-                acc[0, pair] = acc[0, pair] * jnp.concatenate(shrinks, 0) + fresh
+        with_mask(
+            active, start, rows, seq_len, diagonal and role == 0, functools.partial(work, role, start)
+        )
 
 
 def attend_start_body(base, roles, info_ref, len_ref, q_ref, *refs):
@@ -260,11 +280,13 @@
     top[...] = top_in[...]
     low[...] = low_in[...]
     attend_blocks(info_ref, len_ref, base, q_ref, refs[:roles], acc, top, low, False)
-    for pair in range(2):
-        sums = [low[0, 2 * pair + head : 2 * pair + head + 1, :] for head in range(2)]
-        total = [jnp.broadcast_to(1.0 / s, (HEAD_DIM, rows)) for s in sums]
-        att = acc[0, pair] * jnp.concatenate(total, 0)
-        att_ref[:, pair * 128 : pair * 128 + 128] = jnp.transpose(att).astype(BF16)
+    for group in range(q_ref.shape[1] // 256):
+        for pair in range(2):
+            sums = [low[group, 2 * pair + head : 2 * pair + head + 1, :] for head in range(2)]
+            total = [jnp.broadcast_to(1.0 / s, (HEAD_DIM, rows)) for s in sums]
+            att = acc[group, pair] * jnp.concatenate(total, 0)
+            at = 256 * group + 128 * pair
+            att_ref[:, at : at + 128] = jnp.transpose(att).astype(BF16)
     lse_ref[...] = top[...] + jnp.log2(jnp.maximum(low[...], 1e-30))
 
     @pl.when(step == 0)
@@ -283,16 +305,18 @@
 
 def attend(facts, base, q, blocks, state, wo=None, x=None, gain=None):
     rows, width = q.shape
-    steps = width // 256
+    groups = width // 256
+    per = PER_STEP
+    steps = groups // per
     roles = len(blocks)
     full = lambda shape: pl.BlockSpec(shape, lambda i, *s: (0, 0))
-    wide = pl.BlockSpec((rows, 256), lambda i, *s: (0, i))
-    heads = pl.BlockSpec((1, 8, rows), lambda i, *s: (i, 0, 0))
-    accs = pl.BlockSpec((1, 2, 128, rows), lambda i, *s: (i, 0, 0, 0))
-    in_specs = [wide] + [pl.BlockSpec((2, rows, 128), lambda i, *s: (0, 0, i))] * roles
+    wide = pl.BlockSpec((rows, 256 * per), lambda i, *s: (0, i))
+    heads = pl.BlockSpec((per, 8, rows), lambda i, *s: (i, 0, 0))
+    accs = pl.BlockSpec((per, 2, 128, rows), lambda i, *s: (i, 0, 0, 0))
+    in_specs = [wide] + [pl.BlockSpec((2, rows, 128 * per), lambda i, *s: (0, 0, i))] * roles
     state_specs = [accs, heads, heads]
-    state_shapes = [jax.ShapeDtypeStruct((steps, 2, 128, rows), F32)]
-    state_shapes += [jax.ShapeDtypeStruct((steps, 8, rows), F32)] * 2
+    state_shapes = [jax.ShapeDtypeStruct((groups, 2, 128, rows), F32)]
+    state_shapes += [jax.ShapeDtypeStruct((groups, 8, rows), F32)] * 2
     args = [*facts, q, *blocks]
     scratch = []
     if state is None:
@@ -302,21 +326,21 @@
         args += [*state, wo, x, gain]
         in_specs += state_specs
         in_specs += [
-            pl.BlockSpec((256, x.shape[1]), lambda i, *s: (i, 0)),
+            pl.BlockSpec((256 * per, x.shape[1]), lambda i, *s: (i, 0)),
             full(x.shape),
             full((1, x.shape[1])),
         ]
         out_specs = [wide, heads, full(x.shape), full(x.shape)]
         out_shape = [
             jax.ShapeDtypeStruct((rows, width), BF16),
-            jax.ShapeDtypeStruct((steps, 8, rows), F32),
+            jax.ShapeDtypeStruct((groups, 8, rows), F32),
             jax.ShapeDtypeStruct(x.shape, F32),
             jax.ShapeDtypeStruct(x.shape, BF16),
         ]
         scratch = [
-            pltpu.VMEM((1, 2, 128, rows), F32),
-            pltpu.VMEM((1, 8, rows), F32),
-            pltpu.VMEM((1, 8, rows), F32),
+            pltpu.VMEM((per, 2, 128, rows), F32),
+            pltpu.VMEM((per, 8, rows), F32),
+            pltpu.VMEM((per, 8, rows), F32),
             pltpu.VMEM(x.shape, F32),
         ]
     return pl.pallas_call(
@@ -343,61 +367,66 @@
         dq_ref[...] = start_ref[...]
     else:
         dq_ref[...] = jnp.zeros_like(dq_ref)
-    key = lax.broadcasted_iota(jnp.int32, (rows, rows), 0)
-    query = lax.broadcasted_iota(jnp.int32, (rows, rows), 1)
     lane = lax.broadcasted_iota(jnp.int32, (rows, 128), 1)
     low = lane < HEAD_DIM
 
-    for role in range(roles):
-        start = info_ref[base + 2 * role]
-        active = (info_ref[base + 2 * role + 1] > 0) & (start < seq_len)
-
-        @pl.when(jnp.logical_not(active))
-        def _(role=role):
-            dkv_refs[role][...] = jnp.zeros_like(dkv_refs[role])
-
-        @pl.when(active)
-        def _(role=role, start=start):
-            keys = split_heads(kv_refs[role][0])
-            values = split_heads(kv_refs[role][1])
-            bad = key + start >= seq_len
-            if diagonal and role == 0:
-                bad = bad | (key > query)
-            bias = jnp.where(bad, NEG, 0.0)
+    def work(role, start, masked):
+        if masked:
+            bias = mask_of(start, rows, seq_len, diagonal and role == 0)
+        for group in range(q_ref.shape[1] // 256):
+            lanes = slice(group * 128, group * 128 + 128)
+            keys = split_heads(kv_refs[role][0, :, lanes])
+            values = split_heads(kv_refs[role][1, :, lanes])
             dks, dvs = [], []
             for pair in range(2):
-                q = q_ref[:, pair * 128 : pair * 128 + 128]
-                do = do_ref[:, pair * 128 : pair * 128 + 128]
+                cols = slice(256 * group + 128 * pair, 256 * group + 128 * pair + 128)
+                q = q_ref[:, cols]
+                do = do_ref[:, cols]
                 scores = dot(keys[pair], q, 1, 1)
                 grads = dot(values[pair], do, 1, 1)
                 probs, raws = [], []
                 for head in range(2):
                     at = 2 * pair + head
-                    part = scores[head * rows : (head + 1) * rows] * LOG2E + bias
-                    prob = jnp.exp2(part - lse_ref[0, at : at + 1, :])
+                    part = scores[head * rows : (head + 1) * rows]
+                    if masked:
+                        part = part + bias
+                    prob = jnp.exp2(part - lse_ref[group, at : at + 1, :])
                     grad = grads[head * rows : (head + 1) * rows]
-                    raws.append((prob * (grad - delta_ref[0, at : at + 1, :])).astype(BF16))
+                    raws.append((prob * (grad - delta_ref[group, at : at + 1, :])).astype(BF16))
                     probs.append(prob.astype(BF16))
                 raw = jnp.concatenate(raws, 0)
-                dq_ref[:, pair * 128 : pair * 128 + 128] += dot(raw, keys[pair], 0, 0)
-                dks.append(dot(raw, q, 1, 0))
+                dq_ref[:, cols] += dot(raw, keys[pair], 0, 0)
+                dks.append(dot(raw, q, 1, 0) * (1.0 / LOG2E))
                 dvs.append(dot(jnp.concatenate(probs, 0), do, 1, 0))
             for which, parts in enumerate((dks, dvs)):
                 top_a, bottom_a = parts[0][:rows], parts[0][rows:]
                 top_b, bottom_b = parts[1][:rows], parts[1][rows:]
                 turn = pltpu.roll(jnp.where(low, top_b, bottom_a), HEAD_DIM, 1)
                 whole = jnp.where(low, top_a, bottom_b) + turn
-                dkv_refs[role][which] = whole.astype(dkv_refs[role].dtype)
+                dkv_refs[role][which, :, lanes] = whole.astype(dkv_refs[role].dtype)
+
+    for role in range(roles):
+        start = info_ref[base + 2 * role]
+        active = (info_ref[base + 2 * role + 1] > 0) & (start < seq_len)
+
+        @pl.when(jnp.logical_not(active))
+        def _(role=role):
+            dkv_refs[role][...] = jnp.zeros_like(dkv_refs[role])
+
+        with_mask(
+            active, start, rows, seq_len, diagonal and role == 0, functools.partial(work, role, start)
+        )
 
 
 def attend_back(facts, base, q, do, lse, delta, blocks, before, diagonal):
     rows, width = q.shape
-    steps = width // 256
+    per = PER_STEP
+    steps = width // (256 * per)
     roles = len(blocks)
     kvw = blocks[0].shape[2]
-    wide = pl.BlockSpec((rows, 256), lambda i, *s: (0, i))
-    heads = pl.BlockSpec((1, 8, rows), lambda i, *s: (i, 0, 0))
-    kv = pl.BlockSpec((2, rows, 128), lambda i, *s: (0, 0, i))
+    wide = pl.BlockSpec((rows, 256 * per), lambda i, *s: (0, i))
+    heads = pl.BlockSpec((per, 8, rows), lambda i, *s: (i, 0, 0))
+    kv = pl.BlockSpec((2, rows, 128 * per), lambda i, *s: (0, 0, i))
     more = [] if before is None else [before]
     return pl.pallas_call(
         functools.partial(attend_back_body, base, roles, diagonal),
@@ -422,6 +451,8 @@
     at += len(near)
     far = refs[at : at + remotes]
     at += remotes
+    lead = refs[at : at + (3 if own else 1)]
+    at += len(lead)
     before, out_before = (refs[at], refs[at + 1]) if carry else (None, None)
     outs = refs[-15 if first else -13 :]
     gm_ref, gate_ref, out_ref, inner_ref, dg_ref, du_ref = outs[:6]
@@ -454,10 +485,6 @@
             @pl.when(target == own + i)
             def _(i=i):
                 start([far[i].at[pl.ds(off, size)] for off, size in zip(offsets, sizes)])
-
-    @pl.when(step == 0)
-    def _():
-        fetch(jnp.int32(0), 0)
 
     @pl.when(step + 1 < total)
     def _():
@@ -494,36 +521,44 @@
             copies[0][0] = x_ref[...]
             copies[1][0] = cot_ref[pl.ds(0, rows), :]
 
-    for piece, (off, size) in enumerate(zip(offsets, sizes)):
-        place = wbuf.at[slot, pl.ds(off, size)]
-        pltpu.make_async_copy(place, place, sem.at[slot, piece]).wait()
-
-    wg = wbuf[slot, :width, :]
-    wu = wbuf[slot, width : 2 * width, :]
-    wd0 = wbuf[slot, 2 * width : 2 * width + ff, :]
-    wd1 = wbuf[slot, 2 * width + ff :, :]
-    which = info_ref[base + 2] + info_ref[base + 4 + step]
-    x = x_ref[...]
-    cot = cot_ref[pl.ds(0, rows), :]
-    g = dot(x, wg, 1, 0)
-    u = dot(x, wu, 1, 0)
-    raw = dot(cot[:, :ff], wd0, 1, 1) + dot(cot[:, ff:], wd1, 1, 1)
-    gate = jnp.sum(jnp.where(lane == which, gates[...], 0.0), 1, keepdims=True)
-    sig = 1.0 / (1.0 + jnp.exp(-g))
-    silu = g * sig
-    inner = silu * u
-    gg = jnp.sum(raw * inner, 1, keepdims=True)
-    back[...] += jnp.where(lane == which, gg, 0.0)
-    scaled = (gate * inner).astype(BF16)
-    gi = gate * raw
-    dg = (gi * u * (sig * (1.0 + g * (1.0 - sig)))).astype(BF16)
-    du = (gi * silu).astype(BF16)
-    inner_ref[0] = scaled
-    dg_ref[0] = dg
-    du_ref[0] = du
-    out_acc[:, :ff] += dot(scaled, wd0, 1, 0)
-    out_acc[:, ff:] += dot(scaled, wd1, 1, 0)
-    gm_acc[...] += dot(dg, wg, 1, 1) + dot(du, wu, 1, 1)
+    def expert(wg, wu, wd0, wd1):
+        which = info_ref[base + 2] + info_ref[base + 4 + step]
+        x = x_ref[...]
+        cot = cot_ref[pl.ds(0, rows), :]
+        g = dot(x, wg, 1, 0)
+        u = dot(x, wu, 1, 0)
+        raw = dot(cot[:, :ff], wd0, 1, 1) + dot(cot[:, ff:], wd1, 1, 1)
+        gate = jnp.sum(jnp.where(lane == which, gates[...], 0.0), 1, keepdims=True)
+        sig = 1.0 / (1.0 + jnp.exp(-g))
+        silu = g * sig
+        inner = silu * u
+        gg = jnp.sum(raw * inner, 1, keepdims=True)
+        back[...] += jnp.where(lane == which, gg, 0.0)
+        scaled = (gate * inner).astype(BF16)
+        gi = gate * raw
+        dg = (gi * u * (sig * (1.0 + g * (1.0 - sig)))).astype(BF16)
+        du = (gi * silu).astype(BF16)
+        inner_ref[0] = scaled
+        dg_ref[0] = dg
+        du_ref[0] = du
+        out_acc[:, :ff] += dot(scaled, wd0, 1, 0)
+        out_acc[:, ff:] += dot(scaled, wd1, 1, 0)
+        gm_acc[...] += dot(dg, wg, 1, 1) + dot(du, wu, 1, 1)
+
+    @pl.when(step == 0)
+    def _():
+        if own:
+            down = lead[2][0]
+            expert(lead[0][0], lead[1][0], down[:, :ff], down[:, ff:])
+        else:
+            expert(*(lead[0][off : off + size] for off, size in zip(offsets, sizes)))
+
+    @pl.when(step > 0)
+    def _():
+        for piece, (off, size) in enumerate(zip(offsets, sizes)):
+            place = wbuf.at[slot, pl.ds(off, size)]
+            pltpu.make_async_copy(place, place, sem.at[slot, piece]).wait()
+        expert(*(wbuf[slot, off : off + size, :] for off, size in zip(offsets, sizes)))
 
     @pl.when(step == total - 1)
     def _():
@@ -552,9 +587,11 @@
     count = 6 if first else 4
     fresh = isinstance(kept[0], jax.ShapeDtypeStruct)
     aliased = [] if fresh else list(kept[:count])
-    inputs = [*xs, *cots, wr, *own_weights, *far] + ([before] if carry else [])
+    lead = list(own_weights) if own else [far[0]]
+    inputs = [*xs, *cots, wr, *own_weights, *far, *lead] + ([before] if carry else [])
     specs = [full((rows, width))] * twins + [full(cots[0].shape)] * twins + [full(wr.shape)]
     specs += [anywhere] * (len(own_weights) + remotes)
+    specs += [full((1,) + w.shape[1:] if own else w.shape) for w in lead]
     specs += [full(before.shape)] if carry else []
     specs += [big if carry and k == 0 else anywhere for k in range(len(aliased))]
     gm_shape = (rows + experts, width)
@@ -723,7 +760,7 @@
 
 def middle(sums, gates, wr, hidden, cot_ext, attended, mixed, gain, wo, experts):
     rows, width = hidden.shape
-    steps = 3
+    steps = 1
     heads = attended.shape[1] // HEAD_DIM
     row = lambda w: pl.BlockSpec((rows // steps, w), lambda i: (i, 0))
     end = pl.BlockSpec((experts, width), lambda i: (rows // experts, 0))
@@ -788,13 +825,13 @@
 def early_grads(facts, attended, gb, router, ffn, experts):
     rows, width = gb.shape
     count = attended.shape[1]
-    col = lambda r: pl.BlockSpec((r, 256), lambda i, *s: (0, i))
+    col = lambda r: pl.BlockSpec((r, 512), lambda i, *s: (0, i))
     size = count // 2 + count // 8
     return pl.pallas_call(
         functools.partial(early_body, experts),
         grid_spec=pltpu.PrefetchScalarGridSpec(
             num_scalar_prefetch=2,
-            grid=(width // 256,),
+            grid=(width // 512,),
             in_specs=[
                 pl.BlockSpec(attended.shape, lambda i, *s: (0, 0)),
                 col(rows),
@@ -831,14 +868,14 @@
 
 def query_back(facts, dq, normed, cos, sin):
     rows, width = dq.shape
-    col = lambda r: pl.BlockSpec((r, 256), lambda i, *s: (0, i))
+    col = lambda r: pl.BlockSpec((r, 512), lambda i, *s: (0, i))
     full = lambda shape: pl.BlockSpec(shape, lambda i, *s: (0, 0))
     size = normed.shape[1] // 2
     return pl.pallas_call(
         query_back_body,
         grid_spec=pltpu.PrefetchScalarGridSpec(
             num_scalar_prefetch=2,
-            grid=(width // 256,),
+            grid=(width // 512,),
             in_specs=[col(rows), full(normed.shape), full(cos.shape), full(sin.shape)],
             out_specs=[col(rows), col(size), col(size)],
         ),
@@ -873,10 +910,10 @@
 
 def pair_back(facts, parts, normed, cos, sin):
     _, rows, kvw = parts[0].shape
-    half_steps = kvw // 256
-    col = lambda r: pl.BlockSpec((r, 256), lambda i, *s: (0, i))
+    half_steps = kvw // 512
+    col = lambda r: pl.BlockSpec((r, 512), lambda i, *s: (0, i))
     full = lambda shape: pl.BlockSpec(shape, lambda i, *s: (0, 0))
-    part = pl.BlockSpec((1, rows, 256), lambda i, *s: (i // half_steps, 0, i % half_steps))
+    part = pl.BlockSpec((1, rows, 512), lambda i, *s: (i // half_steps, 0, i % half_steps))
     size = normed.shape[1] // 2
     return pl.pallas_call(
         functools.partial(pair_back_body, len(parts), half_steps),
@@ -912,11 +949,11 @@
 
 def tokens_back(lq, lkv, wq, wk, wv, x, gh, gain):
     rows, width = x.shape
-    row = lambda w: pl.BlockSpec((rows // 4, w), lambda i: (i, 0))
+    row = lambda w: pl.BlockSpec((rows, w), lambda i: (i, 0))
     full = lambda shape: pl.BlockSpec(shape, lambda i: (0, 0))
     return pl.pallas_call(
         tokens_back_body,
-        grid=(4,),
+        grid=(1,),
         in_specs=[
             row(lq.shape[1]),
             row(lkv.shape[1]),
@@ -952,15 +989,15 @@
 
 def finish(facts, qa, qb, pa, pb, wq, wk, wv, gain):
     width = wq.shape[0]
-    part = width // 4
-    half = lambda w: pl.BlockSpec((part, w), lambda i, *s: (i % 2, 0))
+    part = width // 2
+    half = lambda w: pl.BlockSpec((part, w), lambda i, *s: (0, 0))
     row = lambda w: pl.BlockSpec((part, w), lambda i, *s: (i, 0))
     line = pl.BlockSpec((1, part), lambda i, *s: (0, i))
     return pl.pallas_call(
         finish_body,
         grid_spec=pltpu.PrefetchScalarGridSpec(
             num_scalar_prefetch=2,
-            grid=(4,),
+            grid=(2,),
             in_specs=[half(width)] * 4
             + [row(wq.shape[1]), row(wk.shape[1]), row(wv.shape[1]), line],
             out_specs=[row(wq.shape[1]), row(wk.shape[1]), row(wv.shape[1]), line],
@@ -1176,10 +1213,7 @@
         sums, gates, wr, hidden, cot_ext, attended, mixed, ffn_norm[None], w_out, experts
     )
     give, early = early_grads(facts, attended, gb, grad_router, grad_ffn, experts)
-    give, early, do, x_came, out_all = tie((give, early, do, x_came, kept[0]))
-    expert_sum = lax.psum_scatter(
-        line(out_all), "ep", scatter_dimension=0, axis_index_groups=z_groups, tiled=True
-    )
+    give, early, do, x_came = tie((give, early, do, x_came))
 
     y_parts = [scatter_start(total_of([total[0][0]] + x_came[0]), y_axis)]
     x_came.append(over_x(1))
@@ -1195,69 +1229,82 @@
         for k in range(ny - 1)
     ]
     x_came.append(over_x(2))
-    early = total_of(early)
+    early = scatter_start(total_of(early), z_axis)
     dq, *near_dkv = attend_back(facts, near_row, q, do, lse, delta, blocks[:2], dq, True)
-    dq, homeward, x_came, near_dkv, early = tie((dq, homeward, x_came, near_dkv, early))
+    dq, homeward, x_came, near_dkv, early, out_all = tie(
+        (dq, homeward, x_came, near_dkv, early, kept[0])
+    )
+    expert_sum = lax.psum_scatter(
+        line(out_all), "ep", scatter_dimension=0, axis_index_groups=z_groups, tiled=True
+    )
 
     parts = [near_dkv[0], lax.ppermute(near_dkv[1], "ctx", core_down), *homeward]
     y_parts.append(scatter_start(total_of([total[1][0]] + x_came[1]), y_axis))
-    early = scatter_start(early, x_axis)
+    early = scatter_start(total_of(early), x_axis)
     lin_q, give, keep = query_back(facts, dq, normed, cos, sin)
     parts, lin_q, give, keep = tie((parts, lin_q, give, keep))
 
     half_q = [keep, lax.ppermute(give, "ctx", core_swap)]
     lin_kv, give, keep = pair_back(facts, parts, normed, cos, sin)
-    half_q, lin_kv, give, keep, y_parts, early, expert_sum = tie(
-        (half_q, lin_kv, give, keep, y_parts, early, expert_sum)
-    )
+    half_q, lin_kv, give, keep, early = tie((half_q, lin_kv, give, keep, early))
 
     half_kv = [keep, lax.ppermute(give, "ctx", core_swap)]
     one = scatter_start(total_of(half_q), y_axis)
     two = scatter_start(total_of(half_kv), x_axis)
-    early = scatter_start(total_of(early), z_axis)
     grad_tokens = tokens_back(
         lin_q, lin_kv, w_query, w_key, w_value, tokens, gh, attn_norm[None]
     )
-    one, two, early, grad_tokens = tie((one, two, early, grad_tokens))
+    one, two, early, grad_tokens, y_parts, x_came = tie(
+        (one, two, early, grad_tokens, y_parts, x_came)
+    )
     one = scatter_start(total_of(one), x_axis)
     two = scatter_start(total_of(two), y_axis)
     early = scatter_start(total_of(early), y_axis)
     y_parts.append(scatter_start(total_of([total[2][0]] + x_came[2]), y_axis))
     one, two, early = tie((one, two, early))
+    early = gather_start(total_of(early), y_axis)
     both = scatter_start(jnp.concatenate([total_of(one), total_of(two)], 0), z_axis)
-    early = gather_start(total_of(early), y_axis)
     grads = [gather_start(total_of(y_parts[0]), y_axis)]
     both, early, y_parts = tie((both, early, y_parts))
     both = gather_start(total_of(both), z_axis)
+    early = gather_start(gather_end(early, y_axis), x_axis)
     grads.append(gather_start(total_of(y_parts[1]), y_axis))
-    both, early, grads[0] = tie((both, early, grads[0]))
+    both, early, grads[0], expert_sum = tie((both, early, grads[0], expert_sum))
+    early = gather_end(early, x_axis)
+    hop = [lax.ppermute(early, "ep", zx(swap)), lax.ppermute(early, "ep", zx(mid))]
     both = gather_end(both, z_axis)
     size = both.shape[0] // 2
     one, two = gather_start(both[:size], x_axis), gather_start(both[size:], y_axis)
-    early = gather_start(gather_end(early, y_axis), z_axis)
     result_out = (valid * (hidden + expert_sum.astype(F32))).astype(BF16)
-    one, two, result_out, grads = tie((one, two, result_out, grads))
+    one, two, result_out, grads, hop = tie((one, two, result_out, grads, hop))
+    hop2 = [lax.ppermute(hop[0], "ep", zx(mid)), lax.ppermute(hop[1], "ep", zx(out))]
     one = gather_start(gather_end(one, x_axis), y_axis)
     two = gather_start(gather_end(two, y_axis), x_axis)
     whole = lambda g: gather_end(gather_start(gather_end(g, y_axis)[None], core_axis), core_axis)
     ready = [whole(g).reshape(own, width, ff).astype(F32) for g in grads]
     grads = gather_start(total_of(y_parts[2]), y_axis)
-    one, two, ready, early = tie((one, two, ready, early))
+    one, two, ready, hop2 = tie((one, two, ready, hop2))
+    hop3 = lax.ppermute(hop2[0], "ep", zx(out))
     one, two = gather_end(one, y_axis), gather_end(two, x_axis)
     swapped = lax.ppermute(one, "ctx", core_swap), lax.ppermute(two, "ctx", core_swap)
-    early = gather_start(gather_end(early, z_axis), x_axis)
-    swapped, one, two = tie((swapped, one, two))
+    swapped, one, two, grads = tie((swapped, one, two, grads))
+    down = gather_start(gather_end(grads, y_axis)[None], core_axis)
     late_q, late_k, late_v, gain = finish(
         facts, one, swapped[0], two, swapped[1], w_query, w_key, w_value, attn_norm[None]
     )
-    early, late_q, grads = tie((early, late_q, grads))
-    early = gather_end(early, x_axis)
-    down = gather_end(grads, y_axis)
+    late_q, hop3, down = tie((late_q, hop3, down))
+    inner = (z == 1) | (z == 2)
+    came_c, came_d = jnp.where(inner, hop[1], hop2[1]), jnp.where(inner, hop2[0], hop3)
+    line_of = {0: (early, hop[0], came_c, came_d), 1: (hop[0], early, came_c, came_d)}
+    line_of |= {2: (came_d, came_c, early, hop[0]), 3: (came_d, came_c, hop[0], early)}
+    rows_of = [jnp.where(z == 0, line_of[0][k], line_of[1][k]) for k in range(NZ)]
+    back_of = [jnp.where(z == 2, line_of[2][k], line_of[3][k]) for k in range(NZ)]
+    early = jnp.concatenate([jnp.where(z < 2, a, b) for a, b in zip(rows_of, back_of)], 0)
     early = gather_end(gather_start(early[None], core_axis), core_axis)
+    down = gather_end(down, core_axis).reshape(own, width, ff)
+    down = jnp.concatenate([down[:, :ff], down[:, ff:]], -1).astype(F32)
     w_out_sum = early[:, : width // 2].reshape(width, width).astype(F32)
     small = early[0, width // 2 :].astype(F32)
-    down = gather_end(gather_start(down[None], core_axis), core_axis).reshape(own, width, ff)
-    down = jnp.concatenate([down[:, :ff], down[:, ff:]], -1).astype(F32)
     return (
         result_out[None],
         grad_tokens[None],

time: 505 us -> 509 us (level)
  Pallas kernels: 204 us -> 195 us
  starting transfers between devices: 95.3 us -> 103 us
  other arithmetic: 40.6 us -> 47.4 us
  waiting for transfers between devices: 123 us -> 117 us
    ppermute x3, waiting for transfers between devices: 20 us -> 5.9 us  [local(): lax.ppermute(total[k][s], 'ep', x_shift(s))]
    ppermute x0 -> x5, waiting for transfers between devices: none -> 7.79 us  [the longest x1 4.57 us: local(): lax.ppermute(hop[1], 'ep', zx(out))]
    ppermute x15, waiting for transfers between devices: 19 us -> 25 us  [scatter_start(): parts.append(lax.ppermute(take((pos + shift) % size), name, pairs(shift)))]
    ppermute x0 -> x5, starting transfers between devices: none -> 5.73 us  [the longest x1 1.39 us: local(): lax.ppermute(hop[0], 'ep', zx(mid))]
    ppermute x1, waiting for transfers between devices: 26.5 us -> 21.2 us  [local(): final = lax.ppermute(send, 'ep', zx(away))]
    unnamed x93 -> x99, local copies, waits for them, and re-layouts: 9.22 us -> 14 us
    ppermute x19 -> x16, waiting for transfers between devices: 28.4 us -> 24.1 us  [gather_start(): lax.ppermute(buf, name, pairs(shift))]
    convert_element_type x15 -> x16, other arithmetic: 13.3 us -> 11.7 us  [total_of(): return total.astype(BF16)]
  transfers between devices with their start and end apart: 68 -> 70, of which waited for: 23 -> 23; matrix products, arithmetic and copies ran while one was open for 8% -> 9% of each run, Pallas kernels for 40% -> 38%
where the time goes in v4:
time: 509 us; the launch traced here: 500 us
  Pallas kernels  195 us (38%)
  waiting for transfers between devices  117 us (23%)
  starting transfers between devices  103 us (20%)
  other arithmetic  47.4 us (9%)
  local copies, waits for them, and re-layouts  21.5 us (4%)
  between operations  16.2 us (3%)
    pallas_call x5, Pallas kernels, expert_call(): pl.pallas_call(functools.partial(expert_body, base, own, remotes, twins,...  77.2 us
    pallas_call x2, Pallas kernels, expert_grads(): pl.pallas_call(functools.partial(expert_grads_body, base), grid_spec=pltp...  30.6 us
    ppermute x15, starting transfers between devices, scatter_start(): parts.append(lax.ppermute(take((pos + shift) % size), name, pairs(shift)))  29.7 us
    ppermute x15, waiting for transfers between devices, scatter_start(): parts.append(lax.ppermute(take((pos + shift) % size), name, pairs(shift)))  25 us
    ppermute x16, waiting for transfers between devices, gather_start(): lax.ppermute(buf, name, pairs(shift))  24.1 us
    pallas_call x2, Pallas kernels, attend_back(): pl.pallas_call(functools.partial(attend_back_body, base, roles, diagonal)...  21.6 us
    ppermute x1, waiting for transfers between devices, local(): final = lax.ppermute(send, 'ep', zx(away))  21.2 us
    ppermute x16, starting transfers between devices, gather_start(): lax.ppermute(buf, name, pairs(shift))  17 us
  transfers between devices with their start and end apart: 70, of which 23 were waited for; matrix products, arithmetic and copies ran while one was open for 9% of the time, Pallas kernels for 38%

profile of v4, /device:TPU:0, one launch (start us, length us, event | category | flops | bytes accessed | tf_op | source)
XLA Modules:
  0.0 499.9 jit_solution(3732721737369748620)
XLA Ops:
  9.1 5.7 %prepare.1 = (bf16[400,1024]{1,0:T(8,128)(2,1)}, bf16[3072,512]{1,0:T(8,128)(2,1)}) custom-call(s32[160]{0:T(256)} %bitcast.80, s32[1]{0:T(128)} %copy.80.len_ref, s32[8,384]{1,0:T(8,128)} %bitcast.102, bf16[384,1024]{1,0:T(8,128)(2,1)} %bitcast.76, bf16[2,1024,512]{2,1,0:T(8,128)(2,1)} %refs_10_.5, bf16[2,1024,512]{2,1,0:T(8,128)(2,1)} %refs_11_.3, ...), custom_call_target="tpu_custom_call" | custom-call | flops 1048576 | bytes 1048576 | tf_op jit(solution)/shard_map/prepare/pallas_call | solution.py:97
  20.9 8.3 %project.1 = (bf16[384,1024]{1,0:T(8,128)(2,1)}, bf16[384,1024]{1,0:T(8,128)(2,1)}, bf16[2,384,512]{2,1,0:T(8,128)(2,1)}, f32[384,128]{1,0:T(8,128)}, f32[384,128]{1,0:T(8,128)}) custom-call(s32[160]{0:T(256)} %bitcast.81, s32[1]{0:T(128)} %copy.80.len_ref, bf16[384,1024]{1,0:T(8,128)(2,1)} %bitcast.69, f32[1,1024]{1,0:T(1,128)} %bitcast.97, ...), custom_call_target="tpu_custom_call" | custom-call | flops 1048576 | bytes 1048576 | tf_op jit(solution)/shard_map/project/pallas_call | solution.py:164
  34.9 7.9 %attend.2 = (f32[4,2,128,384]{3,2,1,0:T(8,128)}, f32[4,8,384]{2,1,0:T(8,128)}, f32[4,8,384]{2,1,0:T(8,128)}) custom-call(s32[160]{0:T(256)} %bitcast.82, s32[1]{0:T(128)} %copy.80.len_ref, bf16[384,1024]{1,0:T(8,128)(2,1)} %get-tuple-element.259.q_ref, bf16[2,384,512]{2,1,0:T(8,128)(2,1)} %get-tuple-element.260.refs_0_, bf16[2,384,512]{2,1,0:T(8,128)(2,1)} %copy-done.20), custom_call_target="tpu_custom_call" | custom-call | flops 1048576 | bytes 1048576 | tf_op jit(solution)/shard_map/attend/pallas_call | solution.py:346
  42.9 7.6 %collective-permute-done.refs_0_ = bf16[2,384,512]{2,1,0:T(8,128)(2,1)S(1)} collective-permute-done((bf16[2,384,512]{2,1,0:T(8,128)(2,1)}, bf16[2,384,512]{2,1,0:T(8,128)(2,1)S(1)}, u32[]{:S(2)}, u32[]{:S(2)}) %collective-permute-start) | collective-permute-done | bytes 786464 | tf_op jit(solution)/shard_map/ppermute | solution.py:1142
  54.5 7.0 %attend.3 = (bf16[384,1024]{1,0:T(8,128)(2,1)}, f32[4,8,384]{2,1,0:T(8,128)}, f32[384,1024]{1,0:T(8,128)}, bf16[384,1024]{1,0:T(8,128)(2,1)}) custom-call(s32[160]{0:T(256)} %bitcast.83, s32[1]{0:T(128)} %copy.80.len_ref, bf16[384,1024]{1,0:T(8,128)(2,1)} %get-tuple-element.259.q_ref, bf16[2,384,512]{2,1,0:T(8,128)(2,1)} %copy-done.25, ...), custom_call_target="tpu_custom_call" | custom-call | flops 1048576 | bytes 1048576 | tf_op jit(solution)/shard_map/attend/pallas_call | solution.py:346
  61.5 4.8 collective-permute-start.7
  69.2 7.4 %collective-permute-done.6.refs_3_ = bf16[400,1024]{1,0:T(8,128)(2,1)} collective-permute-done((bf16[400,1024]{1,0:T(8,128)(2,1)}, bf16[400,1024]{1,0:T(8,128)(2,1)}, u32[]{:S(2)}, u32[]{:S(2)}) %collective-permute-start.6) | collective-permute-done | bytes 819232 | tf_op jit(solution)/shard_map/ppermute | solution.py:1148
  76.6 11.6 %experts.5 = (bf16[400,1024]{1,0:T(8,128)(2,1)}, f32[384,128]{1,0:T(8,128)}, bf16[4,384,1024]{2,1,0:T(8,128)(2,1)}, bf16[4,384,2048]{2,1,0:T(8,128)(2,1)}, bf16[...) custom-call(s32[160]{0:T(256)} %bitcast.84, ...), custom_call_target="tpu_custom_call" | custom-call | flops 1048576 | bytes 1048576 | tf_op jit(solution)/shard_map/experts/pallas_call | solution.py:598
  88.2 4.8 collective-permute-done.7.refs_0_
  100.4 11.5 %experts.6 = (bf16[400,1024]{1,0:T(8,128)(2,1)}, f32[384,128]{1,0:T(8,128)}, bf16[4,384,1024]{2,1,0:T(8,128)(2,1)}, bf16[4,384,2048]{2,1,0:T(8,128)(2,1)}, bf16[...) custom-call(s32[160]{0:T(256)} %bitcast.85, ...), custom_call_target="tpu_custom_call", output_to_operand_aliasing={{2}: (9, {}), {3}: (10, {}), {4}: (11, {}), {5}: (12, {})} | custom-call | flops 4831838208 | bytes 6291456 | tf_op jit(solution)/shard_map/experts/pallas_call | solution.py:598
  117.3 17.6 %experts.7 = (bf16[400,1024]{1,0:T(8,128)(2,1)}, f32[384,128]{1,0:T(8,128)}, bf16[4,384,1024]{2,1,0:T(8,128)(2,1)}, bf16[4,384,2048]{2,1,0:T(8,128)(2,1)}, bf16[...) custom-call(s32[160]{0:T(256)} %bitcast.86, ...), custom_call_target="tpu_custom_call", output_to_operand_aliasing={{2}: (13, {}), {3}: (14, {}), {4}: (15, {}), {5}: (16, {}),... | custom-call | flops 9663676416 | bytes 12582912 | tf_op jit(solution)/shard_map/experts/pallas_call | solution.py:598
  135.0 4.6 collective-permute-start.13
  140.9 18.2 %experts.8 = (bf16[400,1024]{1,0:T(8,128)(2,1)}, f32[384,128]{1,0:T(8,128)}, bf16[4,384,1024]{2,1,0:T(8,128)(2,1)}, bf16[4,384,2048]{2,1,0:T(8,128)(2,1)}, bf16[...) custom-call(s32[160]{0:T(256)} %bitcast.87, ...), custom_call_target="tpu_custom_call", output_to_operand_aliasing={{2}: (15, {}), {3}: (16, {}), {4}: (17, {}), {5}: (18, {}),... | custom-call | flops 9663676416 | bytes 12582912 | tf_op jit(solution)/shard_map/experts/pallas_call | solution.py:598
  159.1 4.9 collective-permute-start.17
  165.0 18.3 %experts.9 = (bf16[400,1024]{1,0:T(8,128)(2,1)}, f32[384,128]{1,0:T(8,128)}, bf16[4,384,1024]{2,1,0:T(8,128)(2,1)}, bf16[4,384,2048]{2,1,0:T(8,128)(2,1)}, bf16[...) custom-call(s32[160]{0:T(256)} %bitcast.88, ...), custom_call_target="tpu_custom_call", output_to_operand_aliasing={{2}: (15, {}), {3}: (16, {}), {4}: (17, {}), {5}: (18, {}),... | custom-call | flops 9663676416 | bytes 12582912 | tf_op jit(solution)/shard_map/experts/pallas_call | solution.py:598
  188.9 15.2 %expert_grads.2 = bf16[2,3,1024,512]{3,2,1,0:T(8,128)(2,1)} custom-call(s32[160]{0:T(256)} %bitcast.89, s32[1]{0:T(128)} %copy.80.len_ref, bf16[1536,1024]{1,0:T(8,128)(2,1)} %bitcast.65, bf16[1536,1024]{1,0:T(8,128)(2,1)} %bitcast.67, bf16[1536,2048]{1,0:T(8,128)(2,1)} %bitcast.58, bf16[1536,2048]{1,0:T(8,128)(2,1)} %bitcast.60, bf16[1536,2048]{1,0:T(8,128)(2,1)} %bitcast.62), custom_call_target="tpu_custom_call" | custom-call | flops 9663676416 | bytes 16777216 | tf_op jit(solution)/shard_map/expert_grads/pallas_call | solution.py:678
  206.2 15.4 %expert_grads.3 = bf16[2,3,1024,512]{3,2,1,0:T(8,128)(2,1)} custom-call(s32[160]{0:T(256)} %bitcast.90, s32[1]{0:T(128)} %copy.80.len_ref, bf16[1536,1024]{1,0:T(8,128)(2,1)} %bitcast.66, bf16[1536,1024]{1,0:T(8,128)(2,1)} %bitcast.68, bf16[1536,2048]{1,0:T(8,128)(2,1)} %bitcast.59, bf16[1536,2048]{1,0:T(8,128)(2,1)} %bitcast.61, bf16[1536,2048]{1,0:T(8,128)(2,1)} %bitcast.63), custom_call_target="tpu_custom_call" | custom-call | flops 9663676416 | bytes 16777216 | tf_op jit(solution)/shard_map/expert_grads/pallas_call | solution.py:678
  232.8 21.2 %collective-permute-done.21.refs_3_.refs_7_ = bf16[400,1024]{1,0:T(8,128)(2,1)S(1)} collective-permute-done((bf16[400,1024]{1,0:T(8,128)(2,1)}, bf16[400,1024]{1,0:T(8,128)(2,1)S(1)}, u32[]{:S(2)}, u32[]{:S(2)}) %collective-permute-start.21) | collective-permute-done | bytes 819232 | tf_op jit(solution)/shard_map/ppermute | solution.py:1204
  254.9 6.9 %middle.1 = (f32[384,1024]{1,0:T(8,128)}, bf16[384,1024]{1,0:T(8,128)(2,1)}, bf16[384,1024]{1,0:T(8,128)(2,1)}, f32[4,8,384]{2,1,0:T(8,128)}, f32[1,1024]{1,0:T(1,128)}, /*index=5*/f32[128,1024]{1,0:T(8,128)}) custom-call(bf16[400,1024]{1,0:T(8,128)(2,1)} %get-tuple-element.286.refs_0_.refs_4_, bf16[400,1024]{1,0:T(8,128)(2,1)} %copy-done.5, ...), custom_call_target="tpu_custom_call" | custom-call | flops 1048576 | bytes 1048576 | tf_op jit(solution)/shard_map/middle/pallas_call | solution.py:768
  261.9 4.6 early_grads.1
  268.2 5.7 %collective-permute-start.23 = (bf16[512,512]{1,0:T(8,128)(2,1)S(1)}, bf16[512,512]{1,0:T(8,128)(2,1)S(1)}, u32[]{:S(2)}, u32[]{:S(2)}) collective-permute-start(bf16[512,512]{1,0:T(8,128)(2,1)S(1)} %get-tuple-element.522), channel_id=1, source_target_pairs={{0,2},{1,3},{2,0},{3,1},{4,6},{5,7},{6,4},{7,5},{8,10},{9,11},{10,... | collective-permute-start | bytes 1572872 | tf_op jit(solution)/shard_map/ppermute | solution.py:1030
  273.9 10.3 %attend_back.2 = (f32[384,1024]{1,0:T(8,128)}, bf16[2,384,512]{2,1,0:T(8,128)(2,1)}, bf16[2,384,512]{2,1,0:T(8,128)(2,1)}) custom-call(s32[160]{0:T(256)} %bitcast.92, s32[1]{0:T(128)} %copy.80.len_ref, bf16[384,1024]{1,0:T(8,128)(2,1)} %get-tuple-element.259.q_ref, bf16[384,1024]{1,0:T(8,128)(2,1)} %get-tuple-element.372.do_ref, ...), custom_call_target="tpu_custom_call" | custom-call | flops 12079595520 | bytes 16777216 | tf_op jit(solution)/shard_map/attend_back/pallas_call | solution.py:431
  295.9 11.3 %attend_back.3 = (f32[384,1024]{1,0:T(8,128)}, bf16[2,384,512]{2,1,0:T(8,128)(2,1)}, bf16[2,384,512]{2,1,0:T(8,128)(2,1)}) custom-call(s32[160]{0:T(256)} %bitcast.93, s32[1]{0:T(128)} %copy.80.len_ref, bf16[384,1024]{1,0:T(8,128)(2,1)} %get-tuple-element.259.q_ref, bf16[384,1024]{1,0:T(8,128)(2,1)} %get-tuple-element.372.do_ref, ...), custom_call_target="tpu_custom_call" | custom-call | flops 12079595520 | bytes 16777216 | tf_op jit(solution)/shard_map/attend_back/pallas_call | solution.py:431
  307.3 5.9 %collective-permute-done.28 = bf16[1024,512]{1,0:T(8,128)(2,1)} collective-permute-done((bf16[1024,512]{1,0:T(8,128)(2,1)}, bf16[1024,512]{1,0:T(8,128)(2,1)}, u32[]{:S(2)}, u32[]{:S(2)}) %collective-permute-start.28) | collective-permute-done | bytes 1048608 | tf_op jit(solution)/shard_map/ppermute | solution.py:1208
  321.2 5.4 %query_back.1 = (bf16[384,1024]{1,0:T(8,128)(2,1)}, bf16[512,1024]{1,0:T(8,128)(2,1)}, bf16[512,1024]{1,0:T(8,128)(2,1)}) custom-call(s32[160]{0:T(256)} %bitcast.94, s32[1]{0:T(128)} %copy.80.len_ref, f32[384,1024]{1,0:T(8,128)} %get-tuple-element.397.dq_ref, bf16[384,1024]{1,0:T(8,128)(2,1)} %get-tuple-element.398.n_ref.refs_3_, ...), custom_call_target="tpu_custom_call" | custom-call | flops 805306368 | bytes 8388608 | tf_op jit(solution)/shard_map/query_back/pallas_call | solution.py:874
  330.5 6.0 %pair_back.1 = (bf16[384,1024]{1,0:T(8,128)(2,1)}, bf16[512,1024]{1,0:T(8,128)(2,1)}, bf16[512,1024]{1,0:T(8,128)(2,1)}) custom-call(s32[160]{0:T(256)} %bitcast.95, s32[1]{0:T(128)} %copy.80.len_ref, bf16[2,384,512]{2,1,0:T(8,128)(2,1)} %get-tuple-element.406.refs_0_, bf16[2,384,512]{2,1,0:T(8,128)(2,1)} %copy-done.24, bf16[2,384,512]{2,1,0:T(8,128)(2,1)} %copy-done.23, ...), custom_call_target="tpu_custom_call" | custom-call | flops 1048576 | bytes 1048576 | tf_op jit(solution)/shard_map/pair_back/pallas_call | solution.py:918
  346.8 6.4 %tokens_back.1 = bf16[384,1024]{1,0:T(8,128)(2,1)} custom-call(bf16[384,1024]{1,0:T(8,128)(2,1)} %get-tuple-element.422.lq_ref, bf16[384,1024]{1,0:T(8,128)(2,1)} %get-tuple-element.423.lkv_ref, bf16[1024,1024]{1,0:T(8,128)(2,1)} %wq_ref.5, bf16[1024,512]{1,0:T(8,128)(2,1)} %wk_ref.5, bf16[1024,512]{1,0:T(8,128)(2,1)} %wv_ref.5, bf16[384,1024]{1,0:T(8,128)(2,1)} %bitcast.71, ...), custom_call_target="tpu_custom_call" | custom-call | flops 1048576 | bytes 1048576 | tf_op jit(solution)/shard_map/tokens_back/pallas_call | solution.py:954
  356.0 11.0 %collective-permute-done.35 = bf16[256,1024]{1,0:T(8,128)(2,1)} collective-permute-done((bf16[256,1024]{1,0:T(8,128)(2,1)}, bf16[256,1024]{1,0:T(8,128)(2,1)}, u32[]{:S(2)}, u32[]{:S(2)}) %collective-permute-start.35) | collective-permute-done | bytes 524320 | tf_op jit(solution)/shard_map/ppermute | solution.py:1030
  382.1 6.4 %collective-permute-start.42 = (bf16[64,1024]{1,0:T(8,128)(2,1)S(1)}, bf16[64,1024]{1,0:T(8,128)(2,1)S(1)}, u32[]{:S(2)}, u32[]{:S(2)}) collective-permute-start(bf16[64,1024]{1,0:T(8,128)(2,1)S(1)} %get-tuple-element.530), channel_id=1, source_target_pairs={{0,8},{4,12},{8,16},{12,20},{16,24},{20,28},{24,0},{28,4},{1,9},{5... | collective-permute-start | bytes 393224 | tf_op jit(solution)/shard_map/ppermute | solution.py:1030
  406.5 5.6 %collective-permute-done.48 = bf16[64,1024]{1,0:T(8,128)(2,1)S(1)} collective-permute-done((bf16[64,1024]{1,0:T(8,128)(2,1)S(1)}, bf16[64,1024]{1,0:T(8,128)(2,1)S(1)}, u32[]{:S(2)}, u32[]{:S(2)}) %collective-permute-start.48) | collective-permute-done | bytes 131104 | tf_op jit(solution)/shard_map/ppermute | solution.py:1036
  454.7 13.8 %collective-permute-done.65 = bf16[512,512]{1,0:T(8,128)(2,1)S(1)} collective-permute-done((bf16[512,512]{1,0:T(8,128)(2,1)S(1)}, bf16[512,512]{1,0:T(8,128)(2,1)S(1)}, u32[]{:S(2)}, u32[]{:S(2)}) %collective-permute-start.65) | collective-permute-done | bytes 524320 | tf_op jit(solution)/shard_map/ppermute | solution.py:1036
  471.5 7.7 %finish.1 = (f32[1024,1024]{1,0:T(8,128)}, f32[1024,512]{1,0:T(8,128)}, f32[1024,512]{1,0:T(8,128)}, f32[1,1024]{1,0:T(1,128)}) custom-call(s32[160]{0:T(256)} %bitcast.96, s32[1]{0:T(128)} %copy.80.len_ref, bf16[512,1024]{1,0:T(8,128)(2,1)} %copy-done.4, bf16[512,1024]{1,0:T(8,128)(2,1)} %copy-done.15, bf16[512,1024]{1,0:T(8,128)(2,1)} %copy-done.3, ...), custom_call_target="tpu_custom_call" | custom-call | flops 1048576 | bytes 1048576 | tf_op jit(solution)/shard_map/finish/pallas_call | solution.py:996
  (288 shorter events, 184.6 us)
Async XLA Ops:
  7.2 406.2 %reduce-scatter.2.cloned.1.call-start = ((), (), s32[]{:S(2)}) async-start(), calls=%async_computation.1 | async-start | bytes 3932160 | tf_op jit(solution)/shard_map/reduce_scatter | solution.py:1237
  14.8 78.2 %collective-permute-start.9 = (bf16[3072,512]{1,0:T(8,128)(2,1)}, bf16[3072,512]{1,0:T(8,128)(2,1)S(1)}, u32[]{:S(2)}, u32[]{:S(2)}) collective-permute-start(bf16[3072,512]{1,0:T(8,128)(2,1)} %get-tuple-element.257), channel_id=1, source_target_pairs={{0,4},{4,0},{8,12},{12,8},{16,20},{20,16},{24,28},{28,24},{1,5},{5... | collective-permute-start | bytes 9437192 | tf_op jit(solution)/shard_map/ppermute | solution.py:1128
  17.8 32.7 %collective-permute-start.2 = (bf16[400,1024]{1,0:T(8,128)(2,1)}, bf16[400,1024]{1,0:T(8,128)(2,1)}, u32[]{:S(2)}, u32[]{:S(2)}) collective-permute-start(bf16[400,1024]{1,0:T(8,128)(2,1)} %get-tuple-element.273.refs_1_.refs_11_), channel_id=1, source_target_pairs={{0,8},{4,12},{8,0},{12,4},{16,24},{20,28},{24,16},{28,20},{1,9},{5... | collective-permute-start | bytes 2457608 | tf_op jit(solution)/shard_map/ppermute | solution.py:1131
  19.4 31.1 %collective-permute-start.3 = (bf16[400,1024]{1,0:T(8,128)(2,1)}, bf16[400,1024]{1,0:T(8,128)(2,1)}, u32[]{:S(2)}, u32[]{:S(2)}) collective-permute-start(bf16[400,1024]{1,0:T(8,128)(2,1)} %get-tuple-element.273.refs_1_.refs_11_), channel_id=1, source_target_pairs={{8,16},{12,20},{16,8},{20,12},{9,17},{13,21},{17,9},{21,13},{10,18... | collective-permute-start | bytes 2457608 | tf_op jit(solution)/shard_map/ppermute | solution.py:1132
  30.5 19.9 %collective-permute-start = (bf16[2,384,512]{2,1,0:T(8,128)(2,1)}, bf16[2,384,512]{2,1,0:T(8,128)(2,1)S(1)}, u32[]{:S(2)}, u32[]{:S(2)}) collective-permute-start(bf16[2,384,512]{2,1,0:T(8,128)(2,1)} %get-tuple-element.260.refs_0_), channel_id=1, source_target_pairs={{0,2},{1,3},{4,6},{5,7},{8,10},{9,11},{12,14},{13,15},{16,18},{17,... | collective-permute-start | bytes 2359304 | tf_op jit(solution)/shard_map/ppermute | solution.py:1142
  50.5 18.7 %collective-permute-start.5 = (bf16[400,1024]{1,0:T(8,128)(2,1)}, bf16[400,1024]{1,0:T(8,128)(2,1)}, u32[]{:S(2)}, u32[]{:S(2)}) collective-permute-start(bf16[400,1024]{1,0:T(8,128)(2,1)} %collective-permute-done.2.refs_1_), channel_id=1, source_target_pairs={{8,16},{12,20},{16,8},{20,12},{9,17},{13,21},{17,9},{21,13},{10,18... | collective-permute-start | bytes 2457608 | tf_op jit(solution)/shard_map/ppermute | solution.py:1147
  52.1 24.5 %collective-permute-start.6 = (bf16[400,1024]{1,0:T(8,128)(2,1)}, bf16[400,1024]{1,0:T(8,128)(2,1)}, u32[]{:S(2)}, u32[]{:S(2)}) collective-permute-start(bf16[400,1024]{1,0:T(8,128)(2,1)} %collective-permute-done.3.refs_2_), channel_id=1, source_target_pairs={{8,0},{12,4},{16,24},{20,28},{9,1},{13,5},{17,25},{21,29},{10,2},{... | collective-permute-start | bytes 2457608 | tf_op jit(solution)/shard_map/ppermute | solution.py:1148
  61.5 31.5 %collective-permute-start.7 = (bf16[384,1024]{1,0:T(8,128)(2,1)}, bf16[384,1024]{1,0:T(8,128)(2,1)}, u32[]{:S(2)}, u32[]{:S(2)}) collective-permute-start(bf16[384,1024]{1,0:T(8,128)(2,1)} %get-tuple-element.272.refs_0_.refs_13_), channel_id=1, source_target_pairs={{0,8},{4,12},{8,0},{12,4},{16,24},{20,28},{24,16},{28,20},{1,9},{5... | collective-permute-start | bytes 2359304 | tf_op jit(solution)/shard_map/ppermute | solution.py:1167
  66.3 26.7 %collective-permute-start.8 = (bf16[384,1024]{1,0:T(8,128)(2,1)}, bf16[384,1024]{1,0:T(8,128)(2,1)}, u32[]{:S(2)}, u32[]{:S(2)}) collective-permute-start(bf16[384,1024]{1,0:T(8,128)(2,1)} %get-tuple-element.272.refs_0_.refs_13_), channel_id=1, source_target_pairs={{8,16},{12,20},{16,8},{20,12},{9,17},{13,21},{17,9},{21,13},{10,18... | collective-permute-start | bytes 2359304 | tf_op jit(solution)/shard_map/ppermute | solution.py:1168
  93.1 18.8 %collective-permute-start.11 = (bf16[384,1024]{1,0:T(8,128)(2,1)}, bf16[384,1024]{1,0:T(8,128)(2,1)S(1)}, u32[]{:S(2)}, u32[]{:S(2)}) collective-permute-start(bf16[384,1024]{1,0:T(8,128)(2,1)} %collective-permute-done.7.refs_0_), channel_id=1, source_target_pairs={{8,16},{12,20},{16,8},{20,12},{9,17},{13,21},{17,9},{21,13},{10,18... | collective-permute-start | bytes 2359304 | tf_op jit(solution)/shard_map/ppermute | solution.py:1172
  93.8 22.0 %collective-permute-start.12 = (bf16[384,1024]{1,0:T(8,128)(2,1)}, bf16[384,1024]{1,0:T(8,128)(2,1)S(1)}, u32[]{:S(2)}, u32[]{:S(2)}) collective-permute-start(bf16[384,1024]{1,0:T(8,128)(2,1)} %collective-permute-done.8.refs_0_), channel_id=1, source_target_pairs={{8,0},{12,4},{16,24},{20,28},{9,1},{13,5},{17,25},{21,29},{10,2},{... | collective-permute-start | bytes 2359304 | tf_op jit(solution)/shard_map/ppermute | solution.py:1173
  115.9 23.8 %collective-permute-start.14 = (bf16[384,1024]{1,0:T(8,128)(2,1)S(1)}, bf16[384,1024]{1,0:T(8,128)(2,1)S(1)}, u32[]{:S(2)}, u32[]{:S(2)}) collective-permute-start(bf16[384,1024]{1,0:T(8,128)(2,1)S(1)} %collective-permute-done.11.refs_0_), channel_id=1, source_target_pairs={{8,0},{12,4},{16,24},{20,28},{9,1},{13,5},{17,25},{21,29},{10,2},{... | collective-permute-start | bytes 2359304 | tf_op jit(solution)/shard_map/ppermute | solution.py:1179
  135.0 29.0 %collective-permute-start.13 = (bf16[400,1024]{1,0:T(8,128)(2,1)}, bf16[400,1024]{1,0:T(8,128)(2,1)S(1)}, u32[]{:S(2)}, u32[]{:S(2)}) collective-permute-start(bf16[400,1024]{1,0:T(8,128)(2,1)} %get-tuple-element.301), channel_id=1, source_target_pairs={{0,8},{4,12},{24,16},{28,20},{1,9},{5,13},{25,17},{29,21},{2,10},{... | collective-permute-start | bytes 2457608 | tf_op jit(solution)/shard_map/ppermute | solution.py:1181
  139.6 24.4 %collective-permute-start.15 = (bf16[400,1024]{1,0:T(8,128)(2,1)}, bf16[400,1024]{1,0:T(8,128)(2,1)S(1)}, u32[]{:S(2)}, u32[]{:S(2)}) collective-permute-start(bf16[400,1024]{1,0:T(8,128)(2,1)} %collective-permute-done.5.refs_2_), channel_id=1, source_target_pairs={{8,0},{12,4},{16,24},{20,28},{9,1},{13,5},{17,25},{21,29},{10,2},{... | collective-permute-start | bytes 2457608 | tf_op jit(solution)/shard_map/ppermute | solution.py:1183
  159.1 24.1 %collective-permute-start.17 = (bf16[400,1024]{1,0:T(8,128)(2,1)}, bf16[400,1024]{1,0:T(8,128)(2,1)S(1)}, u32[]{:S(2)}, u32[]{:S(2)}) collective-permute-start(bf16[400,1024]{1,0:T(8,128)(2,1)} %get-tuple-element.335), channel_id=1, source_target_pairs={{0,8},{4,12},{24,16},{28,20},{1,9},{5,13},{25,17},{29,21},{2,10},{... | collective-permute-start | bytes 2457608 | tf_op jit(solution)/shard_map/ppermute | solution.py:1186
  183.6 20.5 %collective-permute-start.18 = (bf16[400,1024]{1,0:T(8,128)(2,1)S(1)}, bf16[400,1024]{1,0:T(8,128)(2,1)S(1)}, u32[]{:S(2)}, u32[]{:S(2)}) collective-permute-start(bf16[400,1024]{1,0:T(8,128)(2,1)S(1)} %add_convert_fusion.12), channel_id=1, source_target_pairs={{8,16},{12,20},{16,8},{20,12},{9,17},{13,21},{17,9},{21,13},{10,18... | collective-permute-start | bytes 2457608 | tf_op jit(solution)/shard_map/ppermute | solution.py:1196
  184.4 20.3 %collective-permute-start.16 = (bf16[400,1024]{1,0:T(8,128)(2,1)S(1)}, bf16[400,1024]{1,0:T(8,128)(2,1)S(1)}, u32[]{:S(2)}, u32[]{:S(2)}) collective-permute-start(bf16[400,1024]{1,0:T(8,128)(2,1)S(1)} %copy-done.18), channel_id=1, source_target_pairs={{0,8},{4,12},{24,16},{28,20},{1,9},{5,13},{25,17},{29,21},{2,10},{... | collective-permute-start | bytes 2457608 | tf_op jit(solution)/shard_map/ppermute | solution.py:1190
  225.6 40.9 %collective-permute-start.22 = (bf16[1024,512]{1,0:T(8,128)(2,1)S(1)}, bf16[1024,512]{1,0:T(8,128)(2,1)}, u32[]{:S(2)}, u32[]{:S(2)}) collective-permute-start(bf16[1024,512]{1,0:T(8,128)(2,1)S(1)} %get-tuple-element.371), channel_id=1, source_target_pairs={{0,4},{4,0},{8,12},{12,8},{16,20},{20,16},{24,28},{28,24},{1,5},{5... | collective-permute-start | bytes 3145736 | tf_op jit(solution)/shard_map/ppermute | solution.py:1208
  226.2 27.8 %collective-permute-start.21 = (bf16[400,1024]{1,0:T(8,128)(2,1)}, bf16[400,1024]{1,0:T(8,128)(2,1)S(1)}, u32[]{:S(2)}, u32[]{:S(2)}) collective-permute-start(bf16[400,1024]{1,0:T(8,128)(2,1)} %add_convert_fusion.10), channel_id=1, source_target_pairs={{16,24},{20,28},{8,0},{12,4},{17,25},{21,29},{9,1},{13,5},{18,26},... | collective-permute-start | bytes 2457608 | tf_op jit(solution)/shard_map/ppermute | solution.py:1204
  231.3 52.9 %collective-permute-start.24 = (bf16[1024,512]{1,0:T(8,128)(2,1)S(1)}, bf16[1024,512]{1,0:T(8,128)(2,1)}, u32[]{:S(2)}, u32[]{:S(2)}) collective-permute-start(bf16[1024,512]{1,0:T(8,128)(2,1)S(1)} %get-tuple-element.501), channel_id=1, source_target_pairs={{0,4},{4,0},{8,12},{12,8},{16,20},{20,16},{24,28},{28,24},{1,5},{5... | collective-permute-start | bytes 3145736 | tf_op jit(solution)/shard_map/ppermute | solution.py:1208
  266.5 20.0 %collective-permute-start.25 = (bf16[640,1024]{1,0:T(8,128)(2,1)}, bf16[640,1024]{1,0:T(8,128)(2,1)S(1)}, u32[]{:S(2)}, u32[]{:S(2)}) collective-permute-start(bf16[640,1024]{1,0:T(8,128)(2,1)} %get-tuple-element.383), channel_id=1, source_target_pairs={{0,1},{1,0},{2,3},{3,2},{4,5},{5,4},{6,7},{7,6},{8,9},{9,8},{10,11... | collective-permute-start | bytes 3932168 | tf_op jit(solution)/shard_map/ppermute | solution.py:1220
  268.2 18.3 %collective-permute-start.23 = (bf16[512,512]{1,0:T(8,128)(2,1)S(1)}, bf16[512,512]{1,0:T(8,128)(2,1)S(1)}, u32[]{:S(2)}, u32[]{:S(2)}) collective-permute-start(bf16[512,512]{1,0:T(8,128)(2,1)S(1)} %get-tuple-element.522), channel_id=1, source_target_pairs={{0,2},{1,3},{2,0},{3,1},{4,6},{5,7},{6,4},{7,5},{8,10},{9,11},{10,... | collective-permute-start | bytes 1572872 | tf_op jit(solution)/shard_map/ppermute | solution.py:1030
  287.3 25.9 %collective-permute-start.28 = (bf16[1024,512]{1,0:T(8,128)(2,1)}, bf16[1024,512]{1,0:T(8,128)(2,1)}, u32[]{:S(2)}, u32[]{:S(2)}) collective-permute-start(bf16[1024,512]{1,0:T(8,128)(2,1)} %get-tuple-element.500), channel_id=1, source_target_pairs={{0,4},{4,0},{8,12},{12,8},{16,20},{20,16},{24,28},{28,24},{1,5},{5... | collective-permute-start | bytes 3145736 | tf_op jit(solution)/shard_map/ppermute | solution.py:1208
  289.4 23.8 %collective-permute-start.29 = (bf16[160,1024]{1,0:T(8,128)(2,1)S(1)}, bf16[160,1024]{1,0:T(8,128)(2,1)S(1)}, u32[]{:S(2)}, u32[]{:S(2)}) collective-permute-start(bf16[160,1024]{1,0:T(8,128)(2,1)S(1)} %get-tuple-element.512), channel_id=1, source_target_pairs={{0,8},{4,12},{8,16},{12,20},{16,24},{20,28},{24,0},{28,4},{1,9},{5... | collective-permute-start | bytes 983048 | tf_op jit(solution)/shard_map/ppermute | solution.py:1030
  289.5 25.8 %collective-permute-start.30 = (bf16[160,1024]{1,0:T(8,128)(2,1)S(1)}, bf16[160,1024]{1,0:T(8,128)(2,1)S(1)}, u32[]{:S(2)}, u32[]{:S(2)}) collective-permute-start(bf16[160,1024]{1,0:T(8,128)(2,1)S(1)} %get-tuple-element.511), channel_id=1, source_target_pairs={{0,16},{4,20},{8,24},{12,28},{16,0},{20,4},{24,8},{28,12},{1,17},{... | collective-permute-start | bytes 983048 | tf_op jit(solution)/shard_map/ppermute | solution.py:1030
  292.6 22.6 %collective-permute-start.31 = (bf16[160,1024]{1,0:T(8,128)(2,1)S(1)}, bf16[160,1024]{1,0:T(8,128)(2,1)S(1)}, u32[]{:S(2)}, u32[]{:S(2)}) collective-permute-start(bf16[160,1024]{1,0:T(8,128)(2,1)S(1)} %get-tuple-element.510), channel_id=1, source_target_pairs={{0,24},{4,28},{8,0},{12,4},{16,8},{20,12},{24,16},{28,20},{1,25},{... | collective-permute-start | bytes 983048 | tf_op jit(solution)/shard_map/ppermute | solution.py:1030
  294.6 25.2 %collective-permute-start.27 = (bf16[2,384,512]{2,1,0:T(8,128)(2,1)S(1)}, bf16[2,384,512]{2,1,0:T(8,128)(2,1)S(1)}, u32[]{:S(2)}, u32[]{:S(2)}) collective-permute-start(bf16[2,384,512]{2,1,0:T(8,128)(2,1)S(1)} %add_convert_fusion.13), channel_id=1, source_target_pairs={{2,0},{3,1},{6,4},{7,5},{10,8},{11,9},{14,12},{15,13},{18,16},{19,... | collective-permute-start | bytes 2359304 | tf_op jit(solution)/shard_map/ppermute | solution.py:1228
  344.2 22.9 %collective-permute-start.35 = (bf16[256,1024]{1,0:T(8,128)(2,1)}, bf16[256,1024]{1,0:T(8,128)(2,1)}, u32[]{:S(2)}, u32[]{:S(2)}) collective-permute-start(bf16[256,1024]{1,0:T(8,128)(2,1)} %get-tuple-element.520), channel_id=1, source_target_pairs={{0,2},{1,3},{2,0},{3,1},{4,6},{5,7},{6,4},{7,5},{8,10},{9,11},{10,... | collective-permute-start | bytes 1572872 | tf_op jit(solution)/shard_map/ppermute | solution.py:1030
  345.2 21.8 %collective-permute-start.37 = (bf16[256,1024]{1,0:T(8,128)(2,1)S(1)}, bf16[256,1024]{1,0:T(8,128)(2,1)S(1)}, u32[]{:S(2)}, u32[]{:S(2)}) collective-permute-start(bf16[256,1024]{1,0:T(8,128)(2,1)S(1)} %get-tuple-element.518), channel_id=1, source_target_pairs={{0,4},{4,0},{8,12},{12,8},{16,20},{20,16},{24,28},{28,24},{1,5},{5... | collective-permute-start | bytes 1572872 | tf_op jit(solution)/shard_map/ppermute | solution.py:1030
  375.5 21.7 %collective-permute-start.46 = (bf16[512,512]{1,0:T(8,128)(2,1)S(1)}, bf16[512,512]{1,0:T(8,128)(2,1)S(1)}, u32[]{:S(2)}, u32[]{:S(2)}) collective-permute-start(bf16[512,512]{1,0:T(8,128)(2,1)S(1)} %get-tuple-element.514), channel_id=1, source_target_pairs={{0,2},{1,3},{2,0},{3,1},{4,6},{5,7},{6,4},{7,5},{8,10},{9,11},{10,... | collective-permute-start | bytes 1572872 | tf_op jit(solution)/shard_map/ppermute | solution.py:1030
  405.0 19.2 %collective-permute-start.54 = (bf16[512,512]{1,0:T(8,128)(2,1)S(1)}, bf16[512,512]{1,0:T(8,128)(2,1)}, u32[]{:S(2)}, u32[]{:S(2)}) collective-permute-start(bf16[512,512]{1,0:T(8,128)(2,1)S(1)} %add_convert_fusion.15), channel_id=1, source_target_pairs={{0,2},{1,3},{2,0},{3,1},{4,6},{5,7},{6,4},{7,5},{8,10},{9,11},{10,... | collective-permute-start | bytes 1572872 | tf_op jit(solution)/shard_map/ppermute | solution.py:1036
  432.0 18.1 %collective-permute-start.58 = (bf16[256,1024]{1,0:T(8,128)(2,1)S(1)}, bf16[256,1024]{1,0:T(8,128)(2,1)}, u32[]{:S(2)}, u32[]{:S(2)}) collective-permute-start(bf16[256,1024]{1,0:T(8,128)(2,1)S(1)} %maximum_select_fusion.10), channel_id=1, source_target_pairs={{0,4},{4,0},{8,12},{12,8},{16,20},{20,16},{24,28},{28,24},{1,5},{5... | collective-permute-start | bytes 1572872 | tf_op jit(solution)/shard_map/ppermute | solution.py:1036
  (84 other events, 766.7 us)
Sparse Core Ops, SparseCore 0:
  321.3 65.8 reduce-scatter.1

commit v5 on v4

--- a/solution.py
+++ b/solution.py
@@ -1213,7 +1213,10 @@
         sums, gates, wr, hidden, cot_ext, attended, mixed, ffn_norm[None], w_out, experts
     )
     give, early = early_grads(facts, attended, gb, grad_router, grad_ffn, experts)
-    give, early, do, x_came = tie((give, early, do, x_came))
+    give, early, do, x_came, out_all = tie((give, early, do, x_came, kept[0]))
+    expert_sum = lax.psum_scatter(
+        line(out_all), "ep", scatter_dimension=0, axis_index_groups=z_groups, tiled=True
+    )
 
     y_parts = [scatter_start(total_of([total[0][0]] + x_came[0]), y_axis)]
     x_came.append(over_x(1))
@@ -1229,24 +1232,19 @@
         for k in range(ny - 1)
     ]
     x_came.append(over_x(2))
-    early = scatter_start(total_of(early), z_axis)
+    early = total_of(early)
     dq, *near_dkv = attend_back(facts, near_row, q, do, lse, delta, blocks[:2], dq, True)
-    dq, homeward, x_came, near_dkv, early, out_all = tie(
-        (dq, homeward, x_came, near_dkv, early, kept[0])
-    )
-    expert_sum = lax.psum_scatter(
-        line(out_all), "ep", scatter_dimension=0, axis_index_groups=z_groups, tiled=True
-    )
+    dq, homeward, x_came, near_dkv, early = tie((dq, homeward, x_came, near_dkv, early))
 
     parts = [near_dkv[0], lax.ppermute(near_dkv[1], "ctx", core_down), *homeward]
     y_parts.append(scatter_start(total_of([total[1][0]] + x_came[1]), y_axis))
-    early = scatter_start(total_of(early), x_axis)
+    early = scatter_start(early, x_axis)
     lin_q, give, keep = query_back(facts, dq, normed, cos, sin)
     parts, lin_q, give, keep = tie((parts, lin_q, give, keep))
 
     half_q = [keep, lax.ppermute(give, "ctx", core_swap)]
     lin_kv, give, keep = pair_back(facts, parts, normed, cos, sin)
-    half_q, lin_kv, give, keep, early = tie((half_q, lin_kv, give, keep, early))
+    half_q, lin_kv, give, keep, expert_sum = tie((half_q, lin_kv, give, keep, expert_sum))
 
     half_kv = [keep, lax.ppermute(give, "ctx", core_swap)]
     one = scatter_start(total_of(half_q), y_axis)
@@ -1259,52 +1257,44 @@
     )
     one = scatter_start(total_of(one), x_axis)
     two = scatter_start(total_of(two), y_axis)
-    early = scatter_start(total_of(early), y_axis)
+    early = scatter_start(total_of(early), z_axis)
     y_parts.append(scatter_start(total_of([total[2][0]] + x_came[2]), y_axis))
-    one, two, early = tie((one, two, early))
-    early = gather_start(total_of(early), y_axis)
+    one, two = tie((one, two))
     both = scatter_start(jnp.concatenate([total_of(one), total_of(two)], 0), z_axis)
     grads = [gather_start(total_of(y_parts[0]), y_axis)]
     both, early, y_parts = tie((both, early, y_parts))
     both = gather_start(total_of(both), z_axis)
-    early = gather_start(gather_end(early, y_axis), x_axis)
+    early = scatter_start(total_of(early), y_axis)
     grads.append(gather_start(total_of(y_parts[1]), y_axis))
-    both, early, grads[0], expert_sum = tie((both, early, grads[0], expert_sum))
-    early = gather_end(early, x_axis)
-    hop = [lax.ppermute(early, "ep", zx(swap)), lax.ppermute(early, "ep", zx(mid))]
+    both, early, grads[0] = tie((both, early, grads[0]))
+    early = gather_start(total_of(early), y_axis)
     both = gather_end(both, z_axis)
     size = both.shape[0] // 2
     one, two = gather_start(both[:size], x_axis), gather_start(both[size:], y_axis)
     result_out = (valid * (hidden + expert_sum.astype(F32))).astype(BF16)
-    one, two, result_out, grads, hop = tie((one, two, result_out, grads, hop))
-    hop2 = [lax.ppermute(hop[0], "ep", zx(mid)), lax.ppermute(hop[1], "ep", zx(out))]
+    one, two, result_out, grads, early = tie((one, two, result_out, grads, early))
+    early = gather_start(gather_end(early, y_axis), z_axis)
     one = gather_start(gather_end(one, x_axis), y_axis)
     two = gather_start(gather_end(two, y_axis), x_axis)
     whole = lambda g: gather_end(gather_start(gather_end(g, y_axis)[None], core_axis), core_axis)
     ready = [whole(g).reshape(own, width, ff).astype(F32) for g in grads]
     grads = gather_start(total_of(y_parts[2]), y_axis)
-    one, two, ready, hop2 = tie((one, two, ready, hop2))
-    hop3 = lax.ppermute(hop2[0], "ep", zx(out))
+    one, two, ready, early = tie((one, two, ready, early))
     one, two = gather_end(one, y_axis), gather_end(two, x_axis)
     swapped = lax.ppermute(one, "ctx", core_swap), lax.ppermute(two, "ctx", core_swap)
-    swapped, one, two, grads = tie((swapped, one, two, grads))
-    down = gather_start(gather_end(grads, y_axis)[None], core_axis)
+    early = gather_start(gather_end(early, z_axis), x_axis)
+    swapped, one, two = tie((swapped, one, two))
     late_q, late_k, late_v, gain = finish(
         facts, one, swapped[0], two, swapped[1], w_query, w_key, w_value, attn_norm[None]
     )
-    late_q, hop3, down = tie((late_q, hop3, down))
-    inner = (z == 1) | (z == 2)
-    came_c, came_d = jnp.where(inner, hop[1], hop2[1]), jnp.where(inner, hop2[0], hop3)
-    line_of = {0: (early, hop[0], came_c, came_d), 1: (hop[0], early, came_c, came_d)}
-    line_of |= {2: (came_d, came_c, early, hop[0]), 3: (came_d, came_c, hop[0], early)}
-    rows_of = [jnp.where(z == 0, line_of[0][k], line_of[1][k]) for k in range(NZ)]
-    back_of = [jnp.where(z == 2, line_of[2][k], line_of[3][k]) for k in range(NZ)]
-    early = jnp.concatenate([jnp.where(z < 2, a, b) for a, b in zip(rows_of, back_of)], 0)
+    early, late_q, grads = tie((early, late_q, grads))
+    early = gather_end(early, x_axis)
+    down = gather_end(grads, y_axis)
     early = gather_end(gather_start(early[None], core_axis), core_axis)
-    down = gather_end(down, core_axis).reshape(own, width, ff)
-    down = jnp.concatenate([down[:, :ff], down[:, ff:]], -1).astype(F32)
     w_out_sum = early[:, : width // 2].reshape(width, width).astype(F32)
     small = early[0, width // 2 :].astype(F32)
+    down = gather_end(gather_start(down[None], core_axis), core_axis).reshape(own, width, ff)
+    down = jnp.concatenate([down[:, :ff], down[:, ff:]], -1).astype(F32)
     return (
         result_out[None],
         grad_tokens[None],

time: 509 us -> 504 us (level)
  waiting for transfers between devices: 117 us -> 133 us
  other arithmetic: 47.4 us -> 38.3 us
  starting transfers between devices: 103 us -> 96.9 us
    ppermute x3, waiting for transfers between devices: 5.9 us -> 16.4 us  [local(): lax.ppermute(total[k][s], 'ep', x_shift(s))]
    ppermute x15, waiting for transfers between devices: 25 us -> 35.2 us  [scatter_start(): parts.append(lax.ppermute(take((pos + shift) % size), name, pairs(shift)))]
    ppermute x5 -> x0, waiting for transfers between devices: 7.79 us -> none  [the longest x1 4.57 us: local(): lax.ppermute(hop[1], 'ep', zx(out))]
    ppermute x5 -> x0, starting transfers between devices: 5.73 us -> none  [the longest x1 1.39 us: local(): lax.ppermute(hop[0], 'ep', zx(mid))]
    ppermute x1, waiting for transfers between devices: 21.2 us -> 26.3 us  [local(): final = lax.ppermute(send, 'ep', zx(away))]
    unnamed x99 -> x95, local copies, waits for them, and re-layouts: 14 us -> 9.19 us
    ppermute x16 -> x19, starting transfers between devices: 17 us -> 19.6 us  [gather_start(): lax.ppermute(buf, name, pairs(shift))]
    ppermute x16 -> x19, waiting for transfers between devices: 24.1 us -> 23.6 us  [gather_start(): lax.ppermute(buf, name, pairs(shift))]
  transfers between devices with their start and end apart: 70 -> 68, of which waited for: 23 -> 28; matrix products, arithmetic and copies ran while one was open for 9% -> 7% of each run, Pallas kernels for 38% -> 38%
where the time goes in v5:
time: 504 us; the launch traced here: 495 us
  Pallas kernels  195 us (39%)
  waiting for transfers between devices  133 us (26%)
  starting transfers between devices  96.9 us (19%)
  other arithmetic  38.3 us (8%)
  local copies, waits for them, and re-layouts  16.7 us (3%)
  between operations  16.1 us (3%)
    pallas_call x5, Pallas kernels, expert_call(): pl.pallas_call(functools.partial(expert_body, base, own, remotes, twins,...  77.2 us
    ppermute x15, waiting for transfers between devices, scatter_start(): parts.append(lax.ppermute(take((pos + shift) % size), name, pairs(shift)))  35.2 us
    pallas_call x2, Pallas kernels, expert_grads(): pl.pallas_call(functools.partial(expert_grads_body, base), grid_spec=pltp...  30.6 us
    ppermute x15, starting transfers between devices, scatter_start(): parts.append(lax.ppermute(take((pos + shift) % size), name, pairs(shift)))  26.4 us
    ppermute x1, waiting for transfers between devices, local(): final = lax.ppermute(send, 'ep', zx(away))  26.3 us
    ppermute x19, waiting for transfers between devices, gather_start(): lax.ppermute(buf, name, pairs(shift))  23.6 us
    pallas_call x2, Pallas kernels, attend_back(): pl.pallas_call(functools.partial(attend_back_body, base, roles, diagonal)...  21.3 us
    ppermute x19, starting transfers between devices, gather_start(): lax.ppermute(buf, name, pairs(shift))  19.6 us
  transfers between devices with their start and end apart: 68, of which 28 were waited for; matrix products, arithmetic and copies ran while one was open for 7% of the time, Pallas kernels for 38%

profile of v5, /device:TPU:0, one launch (start us, length us, event | category | flops | bytes accessed | tf_op | source)
XLA Modules:
  0.0 495.3 jit_solution(14397918492832607213)
XLA Ops:
  9.1 5.7 %prepare.1 = (bf16[400,1024]{1,0:T(8,128)(2,1)}, bf16[3072,512]{1,0:T(8,128)(2,1)}) custom-call(s32[160]{0:T(256)} %bitcast.82, s32[1]{0:T(128)} %copy.86.len_ref, s32[8,384]{1,0:T(8,128)} %bitcast.104, bf16[384,1024]{1,0:T(8,128)(2,1)} %bitcast.77, bf16[2,1024,512]{2,1,0:T(8,128)(2,1)} %refs_10_.5, bf16[2,1024,512]{2,1,0:T(8,128)(2,1)} %refs_11_.3, ...), custom_call_target="tpu_custom_call" | custom-call | flops 1048576 | bytes 1048576 | tf_op jit(solution)/shard_map/prepare/pallas_call | solution.py:97
  21.0 8.3 %project.1 = (bf16[384,1024]{1,0:T(8,128)(2,1)}, bf16[384,1024]{1,0:T(8,128)(2,1)}, bf16[2,384,512]{2,1,0:T(8,128)(2,1)}, f32[384,128]{1,0:T(8,128)}, f32[384,128]{1,0:T(8,128)}) custom-call(s32[160]{0:T(256)} %bitcast.83, s32[1]{0:T(128)} %copy.86.len_ref, bf16[384,1024]{1,0:T(8,128)(2,1)} %bitcast.69, f32[1,1024]{1,0:T(1,128)} %bitcast.99, ...), custom_call_target="tpu_custom_call" | custom-call | flops 1048576 | bytes 1048576 | tf_op jit(solution)/shard_map/project/pallas_call | solution.py:164
  35.0 7.9 %attend.2 = (f32[4,2,128,384]{3,2,1,0:T(8,128)}, f32[4,8,384]{2,1,0:T(8,128)}, f32[4,8,384]{2,1,0:T(8,128)}) custom-call(s32[160]{0:T(256)} %bitcast.84, s32[1]{0:T(128)} %copy.86.len_ref, bf16[384,1024]{1,0:T(8,128)(2,1)} %get-tuple-element.255.q_ref, bf16[2,384,512]{2,1,0:T(8,128)(2,1)} %get-tuple-element.256.refs_0_, bf16[2,384,512]{2,1,0:T(8,128)(2,1)} %copy-done.22), custom_call_target="tpu_custom_call" | custom-call | flops 1048576 | bytes 1048576 | tf_op jit(solution)/shard_map/attend/pallas_call | solution.py:346
  42.9 7.6 %collective-permute-done.refs_0_ = bf16[2,384,512]{2,1,0:T(8,128)(2,1)S(1)} collective-permute-done((bf16[2,384,512]{2,1,0:T(8,128)(2,1)}, bf16[2,384,512]{2,1,0:T(8,128)(2,1)S(1)}, u32[]{:S(2)}, u32[]{:S(2)}) %collective-permute-start) | collective-permute-done | bytes 786464 | tf_op jit(solution)/shard_map/ppermute | solution.py:1142
  54.6 6.9 %attend.3 = (bf16[384,1024]{1,0:T(8,128)(2,1)}, f32[4,8,384]{2,1,0:T(8,128)}, f32[384,1024]{1,0:T(8,128)}, bf16[384,1024]{1,0:T(8,128)(2,1)}) custom-call(s32[160]{0:T(256)} %bitcast.85, s32[1]{0:T(128)} %copy.86.len_ref, bf16[384,1024]{1,0:T(8,128)(2,1)} %get-tuple-element.255.q_ref, bf16[2,384,512]{2,1,0:T(8,128)(2,1)} %copy-done.26, ...), custom_call_target="tpu_custom_call" | custom-call | flops 1048576 | bytes 1048576 | tf_op jit(solution)/shard_map/attend/pallas_call | solution.py:346
  61.5 4.8 collective-permute-start.7
  69.2 7.4 %collective-permute-done.6.refs_3_ = bf16[400,1024]{1,0:T(8,128)(2,1)} collective-permute-done((bf16[400,1024]{1,0:T(8,128)(2,1)}, bf16[400,1024]{1,0:T(8,128)(2,1)}, u32[]{:S(2)}, u32[]{:S(2)}) %collective-permute-start.6) | collective-permute-done | bytes 819232 | tf_op jit(solution)/shard_map/ppermute | solution.py:1148
  76.7 11.6 %experts.5 = (bf16[400,1024]{1,0:T(8,128)(2,1)}, f32[384,128]{1,0:T(8,128)}, bf16[4,384,1024]{2,1,0:T(8,128)(2,1)}, bf16[4,384,2048]{2,1,0:T(8,128)(2,1)}, bf16[...) custom-call(s32[160]{0:T(256)} %bitcast.86, ...), custom_call_target="tpu_custom_call" | custom-call | flops 1048576 | bytes 1048576 | tf_op jit(solution)/shard_map/experts/pallas_call | solution.py:598
  88.3 4.8 collective-permute-done.7.refs_0_
  100.5 11.5 %experts.6 = (bf16[400,1024]{1,0:T(8,128)(2,1)}, f32[384,128]{1,0:T(8,128)}, bf16[4,384,1024]{2,1,0:T(8,128)(2,1)}, bf16[4,384,2048]{2,1,0:T(8,128)(2,1)}, bf16[...) custom-call(s32[160]{0:T(256)} %bitcast.87, ...), custom_call_target="tpu_custom_call", output_to_operand_aliasing={{2}: (9, {}), {3}: (10, {}), {4}: (11, {}), {5}: (12, {})} | custom-call | flops 4831838208 | bytes 6291456 | tf_op jit(solution)/shard_map/experts/pallas_call | solution.py:598
  117.4 17.6 %experts.7 = (bf16[400,1024]{1,0:T(8,128)(2,1)}, f32[384,128]{1,0:T(8,128)}, bf16[4,384,1024]{2,1,0:T(8,128)(2,1)}, bf16[4,384,2048]{2,1,0:T(8,128)(2,1)}, bf16[...) custom-call(s32[160]{0:T(256)} %bitcast.88, ...), custom_call_target="tpu_custom_call", output_to_operand_aliasing={{2}: (13, {}), {3}: (14, {}), {4}: (15, {}), {5}: (16, {}),... | custom-call | flops 9663676416 | bytes 12582912 | tf_op jit(solution)/shard_map/experts/pallas_call | solution.py:598
  141.0 18.2 %experts.8 = (bf16[400,1024]{1,0:T(8,128)(2,1)}, f32[384,128]{1,0:T(8,128)}, bf16[4,384,1024]{2,1,0:T(8,128)(2,1)}, bf16[4,384,2048]{2,1,0:T(8,128)(2,1)}, bf16[...) custom-call(s32[160]{0:T(256)} %bitcast.89, ...), custom_call_target="tpu_custom_call", output_to_operand_aliasing={{2}: (15, {}), {3}: (16, {}), {4}: (17, {}), {5}: (18, {}),... | custom-call | flops 9663676416 | bytes 12582912 | tf_op jit(solution)/shard_map/experts/pallas_call | solution.py:598
  159.2 4.9 collective-permute-start.17
  165.0 18.3 %experts.9 = (bf16[400,1024]{1,0:T(8,128)(2,1)}, f32[384,128]{1,0:T(8,128)}, bf16[4,384,1024]{2,1,0:T(8,128)(2,1)}, bf16[4,384,2048]{2,1,0:T(8,128)(2,1)}, bf16[...) custom-call(s32[160]{0:T(256)} %bitcast.90, ...), custom_call_target="tpu_custom_call", output_to_operand_aliasing={{2}: (15, {}), {3}: (16, {}), {4}: (17, {}), {5}: (18, {}),... | custom-call | flops 9663676416 | bytes 12582912 | tf_op jit(solution)/shard_map/experts/pallas_call | solution.py:598
  189.0 15.2 %expert_grads.2 = bf16[2,3,1024,512]{3,2,1,0:T(8,128)(2,1)} custom-call(s32[160]{0:T(256)} %bitcast.91, s32[1]{0:T(128)} %copy.86.len_ref, bf16[1536,1024]{1,0:T(8,128)(2,1)} %bitcast.65, bf16[1536,1024]{1,0:T(8,128)(2,1)} %bitcast.67, bf16[1536,2048]{1,0:T(8,128)(2,1)} %bitcast.58, bf16[1536,2048]{1,0:T(8,128)(2,1)} %bitcast.60, bf16[1536,2048]{1,0:T(8,128)(2,1)} %bitcast.62), custom_call_target="tpu_custom_call" | custom-call | flops 9663676416 | bytes 16777216 | tf_op jit(solution)/shard_map/expert_grads/pallas_call | solution.py:678
  206.3 15.4 %expert_grads.3 = bf16[2,3,1024,512]{3,2,1,0:T(8,128)(2,1)} custom-call(s32[160]{0:T(256)} %bitcast.92, s32[1]{0:T(128)} %copy.86.len_ref, bf16[1536,1024]{1,0:T(8,128)(2,1)} %bitcast.66, bf16[1536,1024]{1,0:T(8,128)(2,1)} %bitcast.68, bf16[1536,2048]{1,0:T(8,128)(2,1)} %bitcast.59, bf16[1536,2048]{1,0:T(8,128)(2,1)} %bitcast.61, bf16[1536,2048]{1,0:T(8,128)(2,1)} %bitcast.63), custom_call_target="tpu_custom_call" | custom-call | flops 9663676416 | bytes 16777216 | tf_op jit(solution)/shard_map/expert_grads/pallas_call | solution.py:678
  226.7 26.3 %collective-permute-done.21.refs_3_.refs_7_ = bf16[400,1024]{1,0:T(8,128)(2,1)S(1)} collective-permute-done((bf16[400,1024]{1,0:T(8,128)(2,1)S(1)}, bf16[400,1024]{1,0:T(8,128)(2,1)S(1)}, u32[]{:S(2)}, u32[]{:S(2)}) %collective-permute-start.21) | collective-permute-done | bytes 819232 | tf_op jit(solution)/shard_map/ppermute | solution.py:1204
  253.9 6.9 %middle.1 = (f32[384,1024]{1,0:T(8,128)}, bf16[384,1024]{1,0:T(8,128)(2,1)}, bf16[384,1024]{1,0:T(8,128)(2,1)}, f32[4,8,384]{2,1,0:T(8,128)}, f32[1,1024]{1,0:T(1,128)}, /*index=5*/f32[128,1024]{1,0:T(8,128)}) custom-call(bf16[400,1024]{1,0:T(8,128)(2,1)} %get-tuple-element.282.refs_0_.refs_4_, bf16[400,1024]{1,0:T(8,128)(2,1)} %copy-done.5, ...), custom_call_target="tpu_custom_call" | custom-call | flops 1048576 | bytes 1048576 | tf_op jit(solution)/shard_map/middle/pallas_call | solution.py:768
  271.1 5.9 %collective-permute-start.23 = (bf16[512,512]{1,0:T(8,128)(2,1)S(1)}, bf16[512,512]{1,0:T(8,128)(2,1)S(1)}, u32[]{:S(2)}, u32[]{:S(2)}) collective-permute-start(bf16[512,512]{1,0:T(8,128)(2,1)S(1)} %get-tuple-element.508), channel_id=1, source_target_pairs={{0,2},{1,3},{2,0},{3,1},{4,6},{5,7},{6,4},{7,5},{8,10},{9,11},{10,... | collective-permute-start | bytes 1572872 | tf_op jit(solution)/shard_map/ppermute | solution.py:1030
  277.0 10.0 %attend_back.2 = (f32[384,1024]{1,0:T(8,128)}, bf16[2,384,512]{2,1,0:T(8,128)(2,1)}, bf16[2,384,512]{2,1,0:T(8,128)(2,1)}) custom-call(s32[160]{0:T(256)} %bitcast.94, s32[1]{0:T(128)} %copy.86.len_ref, bf16[384,1024]{1,0:T(8,128)(2,1)} %get-tuple-element.255.q_ref, bf16[384,1024]{1,0:T(8,128)(2,1)} %get-tuple-element.369.do_ref, ...), custom_call_target="tpu_custom_call" | custom-call | flops 12079595520 | bytes 16777216 | tf_op jit(solution)/shard_map/attend_back/pallas_call | solution.py:431
  287.0 6.3 %collective-permute-done.24 = bf16[1024,512]{1,0:T(8,128)(2,1)} collective-permute-done((bf16[1024,512]{1,0:T(8,128)(2,1)S(1)}, bf16[1024,512]{1,0:T(8,128)(2,1)}, u32[]{:S(2)}, u32[]{:S(2)}) %collective-permute-start.24) | collective-permute-done | bytes 1048608 | tf_op jit(solution)/shard_map/ppermute | solution.py:1208
  297.6 11.3 %attend_back.3 = (f32[384,1024]{1,0:T(8,128)}, bf16[2,384,512]{2,1,0:T(8,128)(2,1)}, bf16[2,384,512]{2,1,0:T(8,128)(2,1)}) custom-call(s32[160]{0:T(256)} %bitcast.95, s32[1]{0:T(128)} %copy.86.len_ref, bf16[384,1024]{1,0:T(8,128)(2,1)} %get-tuple-element.255.q_ref, bf16[384,1024]{1,0:T(8,128)(2,1)} %get-tuple-element.369.do_ref, ...), custom_call_target="tpu_custom_call" | custom-call | flops 12079595520 | bytes 16777216 | tf_op jit(solution)/shard_map/attend_back/pallas_call | solution.py:431
  309.0 10.2 %collective-permute-done.28 = bf16[1024,512]{1,0:T(8,128)(2,1)S(1)} collective-permute-done((bf16[1024,512]{1,0:T(8,128)(2,1)}, bf16[1024,512]{1,0:T(8,128)(2,1)S(1)}, u32[]{:S(2)}, u32[]{:S(2)}) %collective-permute-start.28) | collective-permute-done | bytes 1048608 | tf_op jit(solution)/shard_map/ppermute | solution.py:1208
  322.1 5.4 %query_back.1 = (bf16[384,1024]{1,0:T(8,128)(2,1)}, bf16[512,1024]{1,0:T(8,128)(2,1)}, bf16[512,1024]{1,0:T(8,128)(2,1)}) custom-call(s32[160]{0:T(256)} %bitcast.96, s32[1]{0:T(128)} %copy.86.len_ref, f32[384,1024]{1,0:T(8,128)} %get-tuple-element.393.dq_ref, bf16[384,1024]{1,0:T(8,128)(2,1)} %get-tuple-element.394.n_ref.refs_3_, ...), custom_call_target="tpu_custom_call" | custom-call | flops 805306368 | bytes 8388608 | tf_op jit(solution)/shard_map/query_back/pallas_call | solution.py:874
  329.6 5.9 %pair_back.1 = (bf16[384,1024]{1,0:T(8,128)(2,1)}, bf16[512,1024]{1,0:T(8,128)(2,1)}, bf16[512,1024]{1,0:T(8,128)(2,1)}) custom-call(s32[160]{0:T(256)} %bitcast.97, s32[1]{0:T(128)} %copy.86.len_ref, bf16[2,384,512]{2,1,0:T(8,128)(2,1)} %get-tuple-element.402.refs_0_, bf16[2,384,512]{2,1,0:T(8,128)(2,1)} %copy-done.24, bf16[2,384,512]{2,1,0:T(8,128)(2,1)} %copy-done.23, ...), custom_call_target="tpu_custom_call" | custom-call | flops 1048576 | bytes 1048576 | tf_op jit(solution)/shard_map/pair_back/pallas_call | solution.py:918
  349.1 6.4 %tokens_back.1 = bf16[384,1024]{1,0:T(8,128)(2,1)} custom-call(bf16[384,1024]{1,0:T(8,128)(2,1)} %get-tuple-element.414.lq_ref, bf16[384,1024]{1,0:T(8,128)(2,1)} %get-tuple-element.415.lkv_ref, bf16[1024,1024]{1,0:T(8,128)(2,1)} %wq_ref.5, bf16[1024,512]{1,0:T(8,128)(2,1)} %wk_ref.5, bf16[1024,512]{1,0:T(8,128)(2,1)} %wv_ref.5, bf16[384,1024]{1,0:T(8,128)(2,1)} %bitcast.71, ...), custom_call_target="tpu_custom_call" | custom-call | flops 1048576 | bytes 1048576 | tf_op jit(solution)/shard_map/tokens_back/pallas_call | solution.py:954
  356.5 5.9 %collective-permute-done.34 = bf16[320,1024]{1,0:T(8,128)(2,1)} collective-permute-done((bf16[320,1024]{1,0:T(8,128)(2,1)}, bf16[320,1024]{1,0:T(8,128)(2,1)}, u32[]{:S(2)}, u32[]{:S(2)}) %collective-permute-start.34) | collective-permute-done | bytes 655392 | tf_op jit(solution)/shard_map/ppermute | solution.py:1030
  367.2 5.2 %collective-permute-done.33 = bf16[256,1024]{1,0:T(8,128)(2,1)} collective-permute-done((bf16[256,1024]{1,0:T(8,128)(2,1)}, bf16[256,1024]{1,0:T(8,128)(2,1)}, u32[]{:S(2)}, u32[]{:S(2)}) %collective-permute-start.33) | collective-permute-done | bytes 524320 | tf_op jit(solution)/shard_map/ppermute | solution.py:1030
  384.5 8.3 %collective-permute-done.37 = bf16[128,1024]{1,0:T(8,128)(2,1)S(1)} collective-permute-done((bf16[128,1024]{1,0:T(8,128)(2,1)S(1)}, bf16[128,1024]{1,0:T(8,128)(2,1)S(1)}, u32[]{:S(2)}, u32[]{:S(2)}) %collective-permute-start.37) | collective-permute-done | bytes 262176 | tf_op jit(solution)/shard_map/ppermute | solution.py:1030
  417.8 5.2 %collective-permute-done.46 = bf16[64,1024]{1,0:T(8,128)(2,1)S(1)} collective-permute-done((bf16[64,1024]{1,0:T(8,128)(2,1)S(1)}, bf16[64,1024]{1,0:T(8,128)(2,1)S(1)}, u32[]{:S(2)}, u32[]{:S(2)}) %collective-permute-start.46) | collective-permute-done | bytes 131104 | tf_op jit(solution)/shard_map/ppermute | solution.py:1036
  452.8 5.9 %collective-permute-done.59 = bf16[80,1024]{1,0:T(8,128)(2,1)S(1)} collective-permute-done((bf16[80,1024]{1,0:T(8,128)(2,1)S(1)}, bf16[80,1024]{1,0:T(8,128)(2,1)S(1)}, u32[]{:S(2)}, u32[]{:S(2)}) %collective-permute-start.59) | collective-permute-done | bytes 163872 | tf_op jit(solution)/shard_map/ppermute | solution.py:1036
  464.5 7.6 %finish.1 = (f32[1024,1024]{1,0:T(8,128)}, f32[1024,512]{1,0:T(8,128)}, f32[1024,512]{1,0:T(8,128)}, f32[1,1024]{1,0:T(1,128)}) custom-call(s32[160]{0:T(256)} %bitcast.98, s32[1]{0:T(128)} %copy.86.len_ref, bf16[512,1024]{1,0:T(8,128)(2,1)} %copy-done.4, bf16[512,1024]{1,0:T(8,128)(2,1)} %copy-done.16, bf16[512,1024]{1,0:T(8,128)(2,1)} %copy-done.3, ...), custom_call_target="tpu_custom_call" | custom-call | flops 1048576 | bytes 1048576 | tf_op jit(solution)/shard_map/finish/pallas_call | solution.py:996
  (280 shorter events, 180.4 us)
Async XLA Ops:
  7.2 328.3 %reduce-scatter.2.cloned.1.call-start = ((), (), s32[]{:S(2)}) async-start(), calls=%async_computation.1 | async-start | bytes 3932160 | tf_op jit(solution)/shard_map/reduce_scatter | solution.py:1217
  14.9 78.2 %collective-permute-start.9 = (bf16[3072,512]{1,0:T(8,128)(2,1)}, bf16[3072,512]{1,0:T(8,128)(2,1)S(1)}, u32[]{:S(2)}, u32[]{:S(2)}) collective-permute-start(bf16[3072,512]{1,0:T(8,128)(2,1)} %get-tuple-element.253), channel_id=1, source_target_pairs={{0,4},{4,0},{8,12},{12,8},{16,20},{20,16},{24,28},{28,24},{1,5},{5... | collective-permute-start | bytes 9437192 | tf_op jit(solution)/shard_map/ppermute | solution.py:1128
  17.9 32.7 %collective-permute-start.2 = (bf16[400,1024]{1,0:T(8,128)(2,1)}, bf16[400,1024]{1,0:T(8,128)(2,1)}, u32[]{:S(2)}, u32[]{:S(2)}) collective-permute-start(bf16[400,1024]{1,0:T(8,128)(2,1)} %get-tuple-element.269.refs_1_.refs_11_), channel_id=1, source_target_pairs={{0,8},{4,12},{8,0},{12,4},{16,24},{20,28},{24,16},{28,20},{1,9},{5... | collective-permute-start | bytes 2457608 | tf_op jit(solution)/shard_map/ppermute | solution.py:1131
  19.4 31.1 %collective-permute-start.3 = (bf16[400,1024]{1,0:T(8,128)(2,1)}, bf16[400,1024]{1,0:T(8,128)(2,1)}, u32[]{:S(2)}, u32[]{:S(2)}) collective-permute-start(bf16[400,1024]{1,0:T(8,128)(2,1)} %get-tuple-element.269.refs_1_.refs_11_), channel_id=1, source_target_pairs={{8,16},{12,20},{16,8},{20,12},{9,17},{13,21},{17,9},{21,13},{10,18... | collective-permute-start | bytes 2457608 | tf_op jit(solution)/shard_map/ppermute | solution.py:1132
  30.6 19.9 %collective-permute-start = (bf16[2,384,512]{2,1,0:T(8,128)(2,1)}, bf16[2,384,512]{2,1,0:T(8,128)(2,1)S(1)}, u32[]{:S(2)}, u32[]{:S(2)}) collective-permute-start(bf16[2,384,512]{2,1,0:T(8,128)(2,1)} %get-tuple-element.256.refs_0_), channel_id=1, source_target_pairs={{0,2},{1,3},{4,6},{5,7},{8,10},{9,11},{12,14},{13,15},{16,18},{17,... | collective-permute-start | bytes 2359304 | tf_op jit(solution)/shard_map/ppermute | solution.py:1142
  50.6 18.6 %collective-permute-start.5 = (bf16[400,1024]{1,0:T(8,128)(2,1)}, bf16[400,1024]{1,0:T(8,128)(2,1)}, u32[]{:S(2)}, u32[]{:S(2)}) collective-permute-start(bf16[400,1024]{1,0:T(8,128)(2,1)} %collective-permute-done.2.refs_1_), channel_id=1, source_target_pairs={{8,16},{12,20},{16,8},{20,12},{9,17},{13,21},{17,9},{21,13},{10,18... | collective-permute-start | bytes 2457608 | tf_op jit(solution)/shard_map/ppermute | solution.py:1147
  52.2 24.5 %collective-permute-start.6 = (bf16[400,1024]{1,0:T(8,128)(2,1)}, bf16[400,1024]{1,0:T(8,128)(2,1)}, u32[]{:S(2)}, u32[]{:S(2)}) collective-permute-start(bf16[400,1024]{1,0:T(8,128)(2,1)} %collective-permute-done.3.refs_2_), channel_id=1, source_target_pairs={{8,0},{12,4},{16,24},{20,28},{9,1},{13,5},{17,25},{21,29},{10,2},{... | collective-permute-start | bytes 2457608 | tf_op jit(solution)/shard_map/ppermute | solution.py:1148
  61.5 31.6 %collective-permute-start.7 = (bf16[384,1024]{1,0:T(8,128)(2,1)}, bf16[384,1024]{1,0:T(8,128)(2,1)}, u32[]{:S(2)}, u32[]{:S(2)}) collective-permute-start(bf16[384,1024]{1,0:T(8,128)(2,1)} %get-tuple-element.268.refs_0_.refs_13_), channel_id=1, source_target_pairs={{0,8},{4,12},{8,0},{12,4},{16,24},{20,28},{24,16},{28,20},{1,9},{5... | collective-permute-start | bytes 2359304 | tf_op jit(solution)/shard_map/ppermute | solution.py:1167
  66.4 26.7 %collective-permute-start.8 = (bf16[384,1024]{1,0:T(8,128)(2,1)}, bf16[384,1024]{1,0:T(8,128)(2,1)}, u32[]{:S(2)}, u32[]{:S(2)}) collective-permute-start(bf16[384,1024]{1,0:T(8,128)(2,1)} %get-tuple-element.268.refs_0_.refs_13_), channel_id=1, source_target_pairs={{8,16},{12,20},{16,8},{20,12},{9,17},{13,21},{17,9},{21,13},{10,18... | collective-permute-start | bytes 2359304 | tf_op jit(solution)/shard_map/ppermute | solution.py:1168
  93.2 18.8 %collective-permute-start.11 = (bf16[384,1024]{1,0:T(8,128)(2,1)}, bf16[384,1024]{1,0:T(8,128)(2,1)S(1)}, u32[]{:S(2)}, u32[]{:S(2)}) collective-permute-start(bf16[384,1024]{1,0:T(8,128)(2,1)} %collective-permute-done.7.refs_0_), channel_id=1, source_target_pairs={{8,16},{12,20},{16,8},{20,12},{9,17},{13,21},{17,9},{21,13},{10,18... | collective-permute-start | bytes 2359304 | tf_op jit(solution)/shard_map/ppermute | solution.py:1172
  93.9 22.0 %collective-permute-start.12 = (bf16[384,1024]{1,0:T(8,128)(2,1)}, bf16[384,1024]{1,0:T(8,128)(2,1)S(1)}, u32[]{:S(2)}, u32[]{:S(2)}) collective-permute-start(bf16[384,1024]{1,0:T(8,128)(2,1)} %collective-permute-done.8.refs_0_), channel_id=1, source_target_pairs={{8,0},{12,4},{16,24},{20,28},{9,1},{13,5},{17,25},{21,29},{10,2},{... | collective-permute-start | bytes 2359304 | tf_op jit(solution)/shard_map/ppermute | solution.py:1173
  115.9 23.8 %collective-permute-start.14 = (bf16[384,1024]{1,0:T(8,128)(2,1)S(1)}, bf16[384,1024]{1,0:T(8,128)(2,1)S(1)}, u32[]{:S(2)}, u32[]{:S(2)}) collective-permute-start(bf16[384,1024]{1,0:T(8,128)(2,1)S(1)} %collective-permute-done.11.refs_0_), channel_id=1, source_target_pairs={{8,0},{12,4},{16,24},{20,28},{9,1},{13,5},{17,25},{21,29},{10,2},{... | collective-permute-start | bytes 2359304 | tf_op jit(solution)/shard_map/ppermute | solution.py:1179
  135.0 29.0 %collective-permute-start.13 = (bf16[400,1024]{1,0:T(8,128)(2,1)}, bf16[400,1024]{1,0:T(8,128)(2,1)S(1)}, u32[]{:S(2)}, u32[]{:S(2)}) collective-permute-start(bf16[400,1024]{1,0:T(8,128)(2,1)} %get-tuple-element.297), channel_id=1, source_target_pairs={{0,8},{4,12},{24,16},{28,20},{1,9},{5,13},{25,17},{29,21},{2,10},{... | collective-permute-start | bytes 2457608 | tf_op jit(solution)/shard_map/ppermute | solution.py:1181
  139.7 24.4 %collective-permute-start.15 = (bf16[400,1024]{1,0:T(8,128)(2,1)}, bf16[400,1024]{1,0:T(8,128)(2,1)S(1)}, u32[]{:S(2)}, u32[]{:S(2)}) collective-permute-start(bf16[400,1024]{1,0:T(8,128)(2,1)} %collective-permute-done.5.refs_2_), channel_id=1, source_target_pairs={{8,0},{12,4},{16,24},{20,28},{9,1},{13,5},{17,25},{21,29},{10,2},{... | collective-permute-start | bytes 2457608 | tf_op jit(solution)/shard_map/ppermute | solution.py:1183
  159.2 24.1 %collective-permute-start.17 = (bf16[400,1024]{1,0:T(8,128)(2,1)}, bf16[400,1024]{1,0:T(8,128)(2,1)S(1)}, u32[]{:S(2)}, u32[]{:S(2)}) collective-permute-start(bf16[400,1024]{1,0:T(8,128)(2,1)} %get-tuple-element.331), channel_id=1, source_target_pairs={{0,8},{4,12},{24,16},{28,20},{1,9},{5,13},{25,17},{29,21},{2,10},{... | collective-permute-start | bytes 2457608 | tf_op jit(solution)/shard_map/ppermute | solution.py:1186
  183.7 20.5 %collective-permute-start.18 = (bf16[400,1024]{1,0:T(8,128)(2,1)S(1)}, bf16[400,1024]{1,0:T(8,128)(2,1)S(1)}, u32[]{:S(2)}, u32[]{:S(2)}) collective-permute-start(bf16[400,1024]{1,0:T(8,128)(2,1)S(1)} %add_convert_fusion.12), channel_id=1, source_target_pairs={{8,16},{12,20},{16,8},{20,12},{9,17},{13,21},{17,9},{21,13},{10,18... | collective-permute-start | bytes 2457608 | tf_op jit(solution)/shard_map/ppermute | solution.py:1196
  184.5 20.3 %collective-permute-start.16 = (bf16[400,1024]{1,0:T(8,128)(2,1)S(1)}, bf16[400,1024]{1,0:T(8,128)(2,1)S(1)}, u32[]{:S(2)}, u32[]{:S(2)}) collective-permute-start(bf16[400,1024]{1,0:T(8,128)(2,1)S(1)} %copy-done.19), channel_id=1, source_target_pairs={{0,8},{4,12},{24,16},{28,20},{1,9},{5,13},{25,17},{29,21},{2,10},{... | collective-permute-start | bytes 2457608 | tf_op jit(solution)/shard_map/ppermute | solution.py:1190
  224.8 40.7 %collective-permute-start.22 = (bf16[1024,512]{1,0:T(8,128)(2,1)S(1)}, bf16[1024,512]{1,0:T(8,128)(2,1)S(1)}, u32[]{:S(2)}, u32[]{:S(2)}) collective-permute-start(bf16[1024,512]{1,0:T(8,128)(2,1)S(1)} %get-tuple-element.367), channel_id=1, source_target_pairs={{0,4},{4,0},{8,12},{12,8},{16,20},{20,16},{24,28},{28,24},{1,5},{5... | collective-permute-start | bytes 3145736 | tf_op jit(solution)/shard_map/ppermute | solution.py:1208
  225.4 27.6 %collective-permute-start.21 = (bf16[400,1024]{1,0:T(8,128)(2,1)S(1)}, bf16[400,1024]{1,0:T(8,128)(2,1)S(1)}, u32[]{:S(2)}, u32[]{:S(2)}) collective-permute-start(bf16[400,1024]{1,0:T(8,128)(2,1)S(1)} %add_convert_fusion.10), channel_id=1, source_target_pairs={{16,24},{20,28},{8,0},{12,4},{17,25},{21,29},{9,1},{13,5},{18,26},... | collective-permute-start | bytes 2457608 | tf_op jit(solution)/shard_map/ppermute | solution.py:1204
  269.2 24.0 %collective-permute-start.24 = (bf16[1024,512]{1,0:T(8,128)(2,1)S(1)}, bf16[1024,512]{1,0:T(8,128)(2,1)}, u32[]{:S(2)}, u32[]{:S(2)}) collective-permute-start(bf16[1024,512]{1,0:T(8,128)(2,1)S(1)} %get-tuple-element.493), channel_id=1, source_target_pairs={{0,4},{4,0},{8,12},{12,8},{16,20},{20,16},{24,28},{28,24},{1,5},{5... | collective-permute-start | bytes 3145736 | tf_op jit(solution)/shard_map/ppermute | solution.py:1208
  270.7 22.5 %collective-permute-start.25 = (bf16[640,1024]{1,0:T(8,128)(2,1)}, bf16[640,1024]{1,0:T(8,128)(2,1)S(1)}, u32[]{:S(2)}, u32[]{:S(2)}) collective-permute-start(bf16[640,1024]{1,0:T(8,128)(2,1)} %get-tuple-element.380), channel_id=1, source_target_pairs={{0,1},{1,0},{2,3},{3,2},{4,5},{5,4},{6,7},{7,6},{8,9},{9,8},{10,11... | collective-permute-start | bytes 3932168 | tf_op jit(solution)/shard_map/ppermute | solution.py:1223
  271.1 22.1 %collective-permute-start.23 = (bf16[512,512]{1,0:T(8,128)(2,1)S(1)}, bf16[512,512]{1,0:T(8,128)(2,1)S(1)}, u32[]{:S(2)}, u32[]{:S(2)}) collective-permute-start(bf16[512,512]{1,0:T(8,128)(2,1)S(1)} %get-tuple-element.508), channel_id=1, source_target_pairs={{0,2},{1,3},{2,0},{3,1},{4,6},{5,7},{6,4},{7,5},{8,10},{9,11},{10,... | collective-permute-start | bytes 1572872 | tf_op jit(solution)/shard_map/ppermute | solution.py:1030
  294.1 25.0 %collective-permute-start.28 = (bf16[1024,512]{1,0:T(8,128)(2,1)}, bf16[1024,512]{1,0:T(8,128)(2,1)S(1)}, u32[]{:S(2)}, u32[]{:S(2)}) collective-permute-start(bf16[1024,512]{1,0:T(8,128)(2,1)} %get-tuple-element.492), channel_id=1, source_target_pairs={{0,4},{4,0},{8,12},{12,8},{16,20},{20,16},{24,28},{28,24},{1,5},{5... | collective-permute-start | bytes 3145736 | tf_op jit(solution)/shard_map/ppermute | solution.py:1208
  296.3 24.5 %collective-permute-start.27 = (bf16[2,384,512]{2,1,0:T(8,128)(2,1)S(1)}, bf16[2,384,512]{2,1,0:T(8,128)(2,1)S(1)}, u32[]{:S(2)}, u32[]{:S(2)}) collective-permute-start(bf16[2,384,512]{2,1,0:T(8,128)(2,1)S(1)} %add_convert_fusion.13), channel_id=1, source_target_pairs={{2,0},{3,1},{6,4},{7,5},{10,8},{11,9},{14,12},{15,13},{18,16},{19,... | collective-permute-start | bytes 2359304 | tf_op jit(solution)/shard_map/ppermute | solution.py:1231
  344.5 18.0 %collective-permute-start.34 = (bf16[320,1024]{1,0:T(8,128)(2,1)}, bf16[320,1024]{1,0:T(8,128)(2,1)}, u32[]{:S(2)}, u32[]{:S(2)}) collective-permute-start(bf16[320,1024]{1,0:T(8,128)(2,1)} %get-tuple-element.498), channel_id=1, source_target_pairs={{0,4},{4,0},{8,12},{12,8},{16,20},{20,16},{24,28},{28,24},{1,5},{5... | collective-permute-start | bytes 1966088 | tf_op jit(solution)/shard_map/ppermute | solution.py:1030
  347.5 19.8 %collective-permute-start.31 = (bf16[256,1024]{1,0:T(8,128)(2,1)}, bf16[256,1024]{1,0:T(8,128)(2,1)}, u32[]{:S(2)}, u32[]{:S(2)}) collective-permute-start(bf16[256,1024]{1,0:T(8,128)(2,1)} %get-tuple-element.506), channel_id=1, source_target_pairs={{0,2},{1,3},{2,0},{3,1},{4,6},{5,7},{6,4},{7,5},{8,10},{9,11},{10,... | collective-permute-start | bytes 1572872 | tf_op jit(solution)/shard_map/ppermute | solution.py:1030
  348.8 23.7 %collective-permute-start.33 = (bf16[256,1024]{1,0:T(8,128)(2,1)}, bf16[256,1024]{1,0:T(8,128)(2,1)}, u32[]{:S(2)}, u32[]{:S(2)}) collective-permute-start(bf16[256,1024]{1,0:T(8,128)(2,1)} %get-tuple-element.504), channel_id=1, source_target_pairs={{0,4},{4,0},{8,12},{12,8},{16,20},{20,16},{24,28},{28,24},{1,5},{5... | collective-permute-start | bytes 1572872 | tf_op jit(solution)/shard_map/ppermute | solution.py:1030
  374.5 32.8 %collective-permute-start.44 = (bf16[512,512]{1,0:T(8,128)(2,1)S(1)}, bf16[512,512]{1,0:T(8,128)(2,1)S(1)}, u32[]{:S(2)}, u32[]{:S(2)}) collective-permute-start(bf16[512,512]{1,0:T(8,128)(2,1)S(1)} %get-tuple-element.500), channel_id=1, source_target_pairs={{0,2},{1,3},{2,0},{3,1},{4,6},{5,7},{6,4},{7,5},{8,10},{9,11},{10,... | collective-permute-start | bytes 1572872 | tf_op jit(solution)/shard_map/ppermute | solution.py:1030
  378.3 17.1 %collective-permute-start.36 = (bf16[128,1024]{1,0:T(8,128)(2,1)S(1)}, bf16[128,1024]{1,0:T(8,128)(2,1)S(1)}, u32[]{:S(2)}, u32[]{:S(2)}) collective-permute-start(bf16[128,1024]{1,0:T(8,128)(2,1)S(1)} %get-tuple-element.522), channel_id=1, source_target_pairs={{0,4},{4,0},{8,12},{12,8},{16,20},{20,16},{24,28},{28,24},{1,5},{5... | collective-permute-start | bytes 786440 | tf_op jit(solution)/shard_map/ppermute | solution.py:1030
  413.5 21.4 %collective-permute-start.52 = (bf16[512,512]{1,0:T(8,128)(2,1)S(1)}, bf16[512,512]{1,0:T(8,128)(2,1)S(1)}, u32[]{:S(2)}, u32[]{:S(2)}) collective-permute-start(bf16[512,512]{1,0:T(8,128)(2,1)S(1)} %add_convert_fusion.16), channel_id=1, source_target_pairs={{0,2},{1,3},{2,0},{3,1},{4,6},{5,7},{6,4},{7,5},{8,10},{9,11},{10,... | collective-permute-start | bytes 1572872 | tf_op jit(solution)/shard_map/ppermute | solution.py:1036
  437.7 21.1 %collective-permute-start.55 = (bf16[256,1024]{1,0:T(8,128)(2,1)S(1)}, bf16[256,1024]{1,0:T(8,128)(2,1)S(1)}, u32[]{:S(2)}, u32[]{:S(2)}) collective-permute-start(bf16[256,1024]{1,0:T(8,128)(2,1)S(1)} %maximum_select_fusion.11), channel_id=1, source_target_pairs={{0,4},{4,0},{8,12},{12,8},{16,20},{20,16},{24,28},{28,24},{1,5},{5... | collective-permute-start | bytes 1572872 | tf_op jit(solution)/shard_map/ppermute | solution.py:1036
  439.3 19.4 %collective-permute-start.54 = (bf16[256,1024]{1,0:T(8,128)(2,1)S(1)}, bf16[256,1024]{1,0:T(8,128)(2,1)S(1)}, u32[]{:S(2)}, u32[]{:S(2)}) collective-permute-start(bf16[256,1024]{1,0:T(8,128)(2,1)S(1)} %maximum_select_fusion.10), channel_id=1, source_target_pairs={{0,2},{1,3},{2,0},{3,1},{4,6},{5,7},{6,4},{7,5},{8,10},{9,11},{10,... | collective-permute-start | bytes 1572872 | tf_op jit(solution)/shard_map/ppermute | solution.py:1036
  (77 other events, 722.3 us)
Sparse Core Ops, SparseCore 0:
  265.6 64.6 reduce-scatter.1
